TPU v7x, 256 devices: a whole 4x4x8 slice. The times are simulated.
256 devices in a mesh: slab: 4 (over x), space: 64 (over y, z, core).
Axes of the slice: x: 4, y: 4, z: 8, core: 2. Of those that a mesh axis runs over, the one named last changes fastest.
Arguments:
- dipoles: float32 [3, 131072], P(None, ('slab', 'space')), may hold values from -3 to 3
- residual: float32 [3, 131072], P(None, ('slab', 'space')), may hold values from -12 to 12, as said below
- cells: int32 [3, 131072], P(None, ('slab', 'space')), may hold values from 0 to 255, as said below
- fraction: float32 [3, 131072], P(None, ('slab', 'space')), may hold values from 0.25 to 0.75
- polarizability: float32 [131072], P(('slab', 'space')), may hold values from 0.3 to 2.5
- tile_order: int32 [256, 512], P(('slab', 'space')), may hold values from 0 to 511, as said below
- send_tiles: int32 [256, 2], P(('slab', 'space')), may hold values from 0 to 3, as said below
- tile_lists: int32 [256, 4, 8], P(('slab', 'space')), may hold values from 0 to 19, as said below
- tile_counts: int32 [256, 4], P(('slab', 'space')), may hold values from 1 to 8, as said below
Outputs:
- dipoles_next: float32 [3, 131072], P(None, ('slab', 'space'))
- residual_next: float32 [3, 131072], P(None, ('slab', 'space'))
- direction: float32 [3, 131072], P(None, ('slab', 'space'))
Inputs may be any that keep to these rules, and one draw needn't show every extreme that they name: The residual's entries stay within the stated range. `cells`: the first component is below 64 and the second below 4; no two atoms of one device share a cell. `tile_order`: each device's row holds every number of 0 to 511 once. `send_tiles`: the 2 tile numbers of each device are distinct. `tile_lists`: entry 0 of the list of tile t is t itself; the 8 entries of one list are distinct. `tile_counts`: on some devices every tile has 8 live entries.
All inputs are finite; a program needn't handle non-finite values.
Results may differ from a plain program's by a relative error of at most 0.0003.
Values sent between devices are 32-bit elements; how exact they have to be, the bound alone decides.
No kernel may reach another device: no remote copies, remote signals or barrier semaphores. Data moves between devices by JAX's collectives and lax.ppermute only.
A program may use at most 64 MiB of HBM per device.

v0:
```python
import functools
import math

import jax
import jax.numpy as jnp
from jax import lax
from jax.sharding import Mesh
from jax.sharding import PartitionSpec as P

G = 256
SLAB_SPACE = ("slab", "space_0", "space_1", "space_2")
SPACE = ("space_0", "space_1", "space_2")


EWALD_BETA = 0.4
THOLE_SCALE = 0.39
SELF_FIELD = 4.0 * EWALD_BETA**3 / (3.0 * math.sqrt(math.pi))
HIGHEST = lax.Precision.HIGHEST


def with_halo(array, sides, width):
    for axis, dim in sides:
        devices, length = (lax.axis_size(axis), array.shape[dim])
        up = [(i, (i + 1) % devices) for i in range(devices)]
        down = [(j, i) for i, j in up]
        last = lax.slice_in_dim(array, length - width, length, axis=dim)
        initial = lax.slice_in_dim(array, 0, width, axis=dim)
        before = lax.ppermute(last, axis, up)
        after = lax.ppermute(initial, axis, down)
        array = jnp.concatenate([before, array, after], axis=dim)
    return array


def over_axes(array, axes):
    return functools.reduce(lax.psum, axes, array)


def split_up(array, dim, devices):
    dims = array.shape
    pieces = array.reshape(*dims[:dim], devices, dims[dim] // devices, *dims[dim + 1 :])
    return jnp.moveaxis(pieces, dim, 0)


def summed_on_arrival(array, axis, dim):
    pieces = split_up(array, dim, lax.axis_size(axis))
    arrived = lax.all_to_all(pieces, axis, split_axis=0, concat_axis=0, tiled=True)
    return arrived.sum(axis=0)


def spline(fraction):
    centre_arg = fraction - 0.5
    lower_one = fraction + 0.5
    upper_one = 1.5 - fraction
    lower_two = fraction + 1.5
    upper_two = 2.5 - fraction

    def middle(amount):
        return (
            55.0 + 20.0 * amount - 120.0 * amount**2 + 80.0 * amount**3 - 16.0 * amount**4
        ) / 96.0

    def middle_slope(amount):
        return (20.0 - 240.0 * amount + 240.0 * amount**2 - 64.0 * amount**3) / 96.0

    def outer_piece(amount):
        return (5.0 - 2.0 * amount) ** 4 / 384.0

    def outer_slope(amount):
        return -((5.0 - 2.0 * amount) ** 3) / 48.0

    centre = 115.0 / 192.0 - 0.625 * centre_arg**2 + 0.25 * centre_arg**4
    centre_slope = -1.25 * centre_arg + centre_arg**3
    weights = jnp.stack(
        [
            outer_piece(lower_two),
            middle(lower_one),
            centre,
            middle(upper_one),
            outer_piece(upper_two),
        ]
    )
    slopes = jnp.stack(
        [
            outer_slope(lower_two),
            middle_slope(lower_one),
            centre_slope,
            -middle_slope(upper_one),
            -outer_slope(upper_two),
        ]
    )
    return (weights, slopes)


def wave_factors(freq_ids):
    wrapped = jnp.where(freq_ids > G // 2, freq_ids - G, freq_ids).astype(jnp.float32) / G
    angles = 2.0 * math.pi / G * freq_ids.astype(jnp.float32)
    modulus = 115.0 / 192.0 + 19.0 / 48.0 * jnp.cos(angles) + 1.0 / 192.0 * jnp.cos(2.0 * angles)
    return (
        wrapped * wrapped,
        jnp.exp(-((math.pi / EWALD_BETA) ** 2) * wrapped * wrapped) / (modulus * modulus),
    )


def multiplier(freq_x, freq_y, freq_z):
    square_x, factor_x = wave_factors(freq_x)
    square_y, factor_y = wave_factors(freq_y)
    square_z, factor_z = wave_factors(freq_z)
    square_sum = square_x + square_y + square_z
    anchor = ((freq_x == 0) & (freq_y == 0) & (freq_z == 0)).astype(jnp.float32)
    return (
        (1.0 - anchor)
        * factor_x
        * factor_y
        * factor_z
        / (math.pi * float(G) ** 3 * (square_sum + anchor))
    )


def separation(own_tile, geometry):
    displacement = geometry[:, :3, None, :] - own_tile[None, :3, :, None]
    half_box = 0.5 * G
    depth_z = displacement[:, 2]
    depth_z = jnp.where(
        depth_z > half_box, depth_z - G, jnp.where(depth_z < -half_box, depth_z + G, depth_z)
    )
    return jnp.stack([displacement[:, 0], displacement[:, 1], depth_z], 1)


def grouped(values, group_count):
    return values.reshape((group_count, -1) + values.shape[1:])


def pair_coefficients(own_geometry, pool_geometry, neighbour_ids, neighbour_counts):
    count_tiles = own_geometry.shape[0]
    tile_width = own_geometry.shape[2]
    slots = neighbour_ids.shape[1]
    group_count = count_tiles // math.gcd(count_tiles, 4)
    tile_ids = jnp.arange(count_tiles, dtype=jnp.int32)
    diagonal = (jnp.arange(tile_width)[:, None] == jnp.arange(tile_width)[None, :]).astype(
        jnp.float32
    )
    slot_ids = jnp.arange(slots, dtype=jnp.int32)

    def pair_per_tile(tile_id, own_tile, picked, live_count):
        geometry = pool_geometry[picked]
        displacement = separation(own_tile, geometry)
        itself = (picked == tile_id).astype(jnp.float32)[:, None, None] * diagonal[None]
        square = jnp.sum(displacement * displacement, 1) + itself
        distance = jnp.sqrt(square)
        inverse = 1.0 / distance
        inverse_sq = inverse * inverse
        gauss = jnp.exp(-(EWALD_BETA**2) * square)
        bare_zero = lax.erfc(EWALD_BETA * distance) * inverse
        bare_one = (bare_zero + 2.0 * EWALD_BETA / math.sqrt(math.pi) * gauss) * inverse_sq
        bare_two = (3.0 * bare_one + 4.0 * EWALD_BETA**3 / math.sqrt(math.pi) * gauss) * inverse_sq
        damping = (
            THOLE_SCALE
            * square
            * distance
            * lax.rsqrt(own_tile[3][None, :, None] * geometry[:, 3][:, None, :])
        )
        decay = jnp.exp(-damping)
        rank_three = bare_one - decay * inverse * inverse_sq
        rank_five = bare_two - 3.0 * (1.0 + damping) * decay * inverse * inverse_sq * inverse_sq
        weight_pair = (slot_ids < live_count).astype(jnp.float32)[:, None, None] * (1.0 - itself)
        return (weight_pair * rank_five, weight_pair * rank_three)

    def pair_per_group(inputs):
        return jax.vmap(pair_per_tile)(*inputs)

    fives, threes = lax.map(
        pair_per_group,
        (
            grouped(tile_ids, group_count),
            grouped(own_geometry, group_count),
            grouped(neighbour_ids, group_count),
            grouped(neighbour_counts, group_count),
        ),
    )
    return (
        fives.reshape((count_tiles,) + fives.shape[2:]),
        threes.reshape((count_tiles,) + threes.shape[2:]),
    )


def short_field(own_geometry, pool_geometry, pool_dipoles, neighbour_ids, coefficients):
    count_tiles = own_geometry.shape[0]
    group_count = count_tiles // math.gcd(count_tiles, 4)
    fives, threes = coefficients

    def short_per_tile(own_tile, picked, rank_five, rank_three):
        geometry = pool_geometry[picked]
        dipole = pool_dipoles[picked]
        displacement = separation(own_tile, geometry)
        projection = jnp.sum(displacement * dipole[:, :, None, :], 1)
        terms = (
            rank_five[:, None] * displacement * projection[:, None]
            - rank_three[:, None] * dipole[:, :, None, :]
        )
        return jnp.sum(terms, (0, 3))

    def short_per_group(inputs):
        return jax.vmap(short_per_tile)(*inputs)

    fields = lax.map(
        short_per_group,
        (
            grouped(own_geometry, group_count),
            grouped(neighbour_ids, group_count),
            grouped(fives, group_count),
            grouped(threes, group_count),
        ),
    )
    return fields.reshape((count_tiles,) + fields.shape[2:])


def fold_rims(padded, axis_id, length):
    core = lax.slice_in_dim(padded, 4, length + 4, axis=axis_id)
    lower_rim = lax.slice_in_dim(padded, 0, 2, axis=axis_id)
    upper_rim = lax.slice_in_dim(padded, length + 6, length + 8, axis=axis_id)
    lower_pad = [(0, 0)] * padded.ndim
    lower_pad[axis_id] = (0, length - 2)
    upper_pad = [(0, 0)] * padded.ndim
    upper_pad[axis_id] = (length - 2, 0)
    return core + jnp.pad(lower_rim, lower_pad) + jnp.pad(upper_rim, upper_pad)


def to_tiles(values, count_tiles):
    return values.reshape(values.shape[0], count_tiles, -1).transpose(1, 0, 2)


def from_tiles(tile_values):
    return tile_values.transpose(1, 0, 2).reshape(tile_values.shape[1], -1)


def tile_rims(payload):
    return with_halo(payload, (("slab", 0), (SPACE, 1)), 1)


def grid_rims(values):
    return with_halo(values, (("slab", 0), (SPACE, 1)), 2)


def pool_from(received):
    flattened = received.reshape((9,) + received.shape[2:])
    picked = flattened[jnp.array([0, 1, 2, 3, 5, 6, 7, 8], dtype=jnp.int32)]
    return picked.reshape((-1,) + received.shape[3:])


def point_tables(cell_row, frac_row, length, wrapped):
    weights, slopes = spline(frac_row)
    step_ids = jnp.arange(5, dtype=jnp.int32)[:, None]
    if wrapped:
        targets = (cell_row[None] + step_ids - 2 + length) % length
    else:
        targets = cell_row[None] + step_ids
    matches = (jnp.arange(length, dtype=jnp.int32)[:, None, None] == targets[None]).astype(
        jnp.float32
    )
    return (jnp.sum(matches * weights[None], 1), jnp.sum(matches * slopes[None], 1))


def local(
    dipoles,
    residual,
    cells,
    fraction,
    polarizability,
    tile_order,
    send_tiles,
    tile_lists,
    tile_counts,
):
    atom_order = tile_order[0]
    sending = send_tiles[0]
    neighbour_ids = tile_lists[0]
    counts = tile_counts[0]
    count_tiles = neighbour_ids.shape[0]
    atom_count = atom_order.shape[0]
    send_count = sending.shape[0]
    n_slab = lax.axis_size("slab")
    n_space = lax.axis_size(SPACE)
    extent_x = G // n_slab
    extent_y = G // n_space
    extent_k = G // n_space
    slab_index = lax.axis_index("slab")
    space_index = lax.axis_index(SPACE)
    cell_rows = cells[:, atom_order]
    frac_rows = fraction[:, atom_order]
    alphas = polarizability[atom_order][None]
    target = residual[:, atom_order]
    moments = dipoles[:, atom_order]
    positions = cell_rows.astype(jnp.float32) + frac_rows
    geometry = to_tiles(jnp.concatenate([positions, alphas], 0), count_tiles)
    shift_rows = []
    for step_a in range(3):
        for step_b in range(3):
            if step_a != 1 or step_b != 1:
                shift_rows.append(
                    [float((step_a - 1) * extent_x), float((step_b - 1) * extent_y), 0.0, 0.0]
                )
    shifts = jnp.repeat(jnp.array(shift_rows, jnp.float32), send_count, 0)[:, :, None]
    search = alphas * target
    search_tiles = to_tiles(search, count_tiles)
    first_pool = pool_from(
        tile_rims(jnp.concatenate([geometry, search_tiles], 1)[sending][None, None])
    )
    pool_geometry = jnp.concatenate([geometry, first_pool[:, :4] + shifts], 0)
    coefficients = pair_coefficients(geometry, pool_geometry, neighbour_ids, counts)

    def short_from(values_tiles, received_dipoles):
        pool_dipoles = jnp.concatenate([values_tiles, received_dipoles], 0)
        return from_tiles(
            short_field(geometry, pool_geometry, pool_dipoles, neighbour_ids, coefficients)
        )

    def short_apply(values):
        values_tiles = to_tiles(values, count_tiles)
        return short_from(values_tiles, pool_from(tile_rims(values_tiles[sending][None, None])))

    search = alphas * (target + short_from(search_tiles, first_pool[:, 4:]))
    for sweep_id in range(2):
        search = alphas * (target + short_apply(search))
    search_dot = jnp.sum(target * search)
    search_total = over_axes(search_dot, SLAB_SPACE)
    weight_x, slope_x = point_tables(cell_rows[0], frac_rows[0], extent_x + 4, False)
    weight_y, slope_y = point_tables(cell_rows[1], frac_rows[1], extent_y + 4, False)
    weight_z, slope_z = point_tables(cell_rows[2], frac_rows[2], G, True)
    plane_xs = (slope_x[:, None] * weight_y[None]).reshape(-1, atom_count)
    plane_ys = (weight_x[:, None] * slope_y[None]).reshape(-1, atom_count)
    plane_ww = (weight_x[:, None] * weight_y[None]).reshape(-1, atom_count)
    left_side = jnp.concatenate(
        [search[0][None] * plane_xs + search[1][None] * plane_ys, plane_ww], 1
    )
    right_side = jnp.concatenate([weight_z.T, (search[2][None] * slope_z).T], 0)
    spread = jnp.dot(left_side, right_side, precision=HIGHEST).reshape(
        extent_x + 4, extent_y + 4, G
    )
    planes = fold_rims(fold_rims(grid_rims(spread), 0, extent_x), 1, extent_y)
    grid_ids = jnp.arange(G, dtype=jnp.int32)
    angles = 2.0 * math.pi / G * (grid_ids[:, None] * grid_ids[None, :] % G).astype(jnp.float32)
    cas_table = jnp.cos(angles) + jnp.sin(angles)
    freq_z = space_index * extent_k + jnp.arange(extent_k, dtype=jnp.int32)
    along_z = jnp.einsum(
        "xvz,zsk->sxvk", planes, cas_table.reshape(G, n_space, extent_k), precision=HIGHEST
    )
    columns = lax.all_to_all(
        along_z.reshape(n_space, -1), SPACE, split_axis=0, concat_axis=0, tiled=True
    )
    columns = columns.reshape(n_space, extent_x, extent_y, extent_k)
    first_x = slab_index * extent_x

    def x_transform(source):
        flattened = source.reshape(extent_x, -1)
        cas_rows = lax.dynamic_slice(
            cas_table, (0, first_x), (extent_x * lax.axis_size("slab"), extent_x)
        )
        return summed_on_arrival(
            jnp.dot(cas_rows, flattened, precision=HIGHEST), "slab", 0
        ).reshape(source.shape)

    along_y = jnp.einsum(
        "sxvk,svl->xkl", columns, cas_table.reshape(n_space, extent_y, G), precision=HIGHEST
    )
    spectrum = x_transform(along_y)
    freq_x = first_x + jnp.arange(extent_x, dtype=jnp.int32)
    scaled = spectrum * multiplier(
        freq_x[:, None, None], grid_ids[None, None, :], freq_z[None, :, None]
    )
    back_x = x_transform(scaled)
    planes_send = jnp.einsum(
        "xkl,lsv->sxvk", back_x, cas_table.reshape(G, n_space, extent_y), precision=HIGHEST
    )
    planes_back = lax.all_to_all(
        planes_send.reshape(n_space, -1), SPACE, split_axis=0, concat_axis=0, tiled=True
    )
    planes_back = planes_back.reshape(n_space, extent_x, extent_y, extent_k)
    potential = jnp.einsum(
        "sxvk,skz->xvz", planes_back, cas_table.reshape(n_space, extent_k, G), precision=HIGHEST
    )
    beside_all = grid_rims(potential)
    probed = jnp.dot(
        beside_all.reshape(-1, G), jnp.concatenate([weight_z, slope_z], 1), precision=HIGHEST
    )
    probed_w = probed[:, :atom_count]
    probed_s = probed[:, atom_count:]
    recip_field = -jnp.stack(
        [
            jnp.sum(plane_xs * probed_w, 0),
            jnp.sum(plane_ys * probed_w, 0),
            jnp.sum(plane_ww * probed_s, 0),
        ]
    )
    applied = search / alphas - short_apply(search) - SELF_FIELD * search - recip_field
    curve_local = jnp.sum(search * applied)
    curve_total = over_axes(curve_local, SLAB_SPACE)
    step_size = search_total / curve_total

    def restore(values):
        return jnp.zeros_like(values).at[:, atom_order].set(values)

    return (
        restore(moments + step_size * search),
        restore(target - step_size * applied),
        restore(search),
    )


def solution(mesh):
    finer = Mesh(
        mesh.devices.reshape(mesh.shape["slab"], 4, 8, 2), ("slab", "space_0", "space_1", "space_2")
    )
    in_specs = (
        P(None, SLAB_SPACE),
        P(None, SLAB_SPACE),
        P(None, SLAB_SPACE),
        P(None, SLAB_SPACE),
        P(SLAB_SPACE),
        P(SLAB_SPACE, None),
        P(SLAB_SPACE, None),
        P(SLAB_SPACE, None, None),
        P(SLAB_SPACE, None),
    )
    out_specs = (P(None, SLAB_SPACE), P(None, SLAB_SPACE), P(None, SLAB_SPACE))
    return jax.shard_map(local, mesh=finer, in_specs=in_specs, out_specs=out_specs, check_vma=False)
```

profile of v0, /device:TPU:1, one launch (start us, length us, event | category | flops | bytes accessed | tf_op | source)
XLA Modules:
  0.0 282.9 jit_solution(14055221000330609133)
XLA Ops:
  6.0 3.5 %gather_fusion.1 = f32[512]{0:T(512)S(1)} fusion(f32[512]{0:T(512)S(1)} %copy-done, s32[1024]{0:T(1024)S(1)} %pad_clamp_fusion.3), kind=kCustom, calls=%fused_computation.2 | custom fusion | bytes 6144 | tf_op jit(solution)/shard_map/gather | solution.py:290
  11.5 2.1 collective-permute-start
  13.7 1.4 collective-permute-start.1
  16.3 3.5 %collective-permute-start.2 = (f32[3,1,2,7,128]{4,3,2,1,0:T(8,128)S(1)}, f32[3,1,2,7,128]{4,3,2,1,0:T(8,128)S(1)}, u32[]{:S(2)}, u32[]{:S(2)}) collective-permute-start(f32[3,1,2,7,128]{4,3,2,1,0:T(8,128)S(1)} %pad_maximum_fusion.16), channel_id=1, source_target_pairs={{0,1},{1,2},{2,3},{3,4},{4,5},{5,6},{6,7},{7,8},{8,9},{9,10},{10,1... | collective-permute-start | bytes 64520 | tf_op jit(solution)/shard_map/ppermute | solution.py:28
  20.7 2.5 collective-permute-done.3
  25.7 2.2 slice.239
  29.0 3.3 %multiply_reduce_fusion.3 = (f32[4,8,128,128]{3,2,1,0:T(8,128)S(1)}, f32[4,8,128,128]{3,2,1,0:T(8,128)S(1)}) fusion(f32[4,8,3,128]{3,2,1,0:T(4,128)S(1)} %bitcast.221, f32[4,8,1,128,128]{4,3,2,1,0:T(8,128)S(1)} %fusion.12, f32[4,8,2,128,128]{4,3,2,1,0:T(8,128)} %slice.239), kind=kLoop, calls=%fused_computation.29 | loop fusion | flops 6815744 | bytes 10534912 | tf_op jit(solution)/shard_map/while/body/eval_jaxpr/vmap()/reduce_sum | solution.py:195
  32.3 7.3 %fusion.6 = (f32[4,8,128,128]{3,2,1,0:T(8,128)S(1)}, f32[4,8,128,128]{3,2,1,0:T(8,128)S(1)}) fusion(f32[4,8,128,128]{3,2,1,0:T(8,128)S(1)} %get-tuple-element.127, f32[4,8,128]{2,1,0:T(8,128)S(1)} %bitcast.242, f32[4,128]{1,0:T(4,128)S(1)} %bitcast.272, f32[128,128]{1,0:T(8,128)S(1)} %fusion.146, f32[4,8]{1,0:T(4,128)S(1)} %get-tuple-element.218, ...), kind=kLoop, calls=%fused_computation.46 | loop fusion | flops 46661632 | bytes 6375680 | tf_op jit(solution)/shard_map/while/body/eval_jaxpr/vmap()/mul | solution.py:166
  39.6 1.8 fusion.5
  41.4 1.6 copy-done.1
  43.0 2.0 subtract_reduce_fusion.3
  45.6 1.3 collective-permute-start.4
  46.9 1.6 collective-permute-start.5
  49.4 1.4 collective-permute-start.6
  50.8 3.9 %collective-permute-start.7 = (f32[3,1,2,3,128]{4,3,2,1,0:T(4,128)S(1)}, f32[3,1,2,3,128]{4,3,2,1,0:T(4,128)S(1)}, u32[]{:S(2)}, u32[]{:S(2)}) collective-permute-start(f32[3,1,2,3,128]{4,3,2,1,0:T(4,128)S(1)} %pad_maximum_fusion.18), channel_id=1, source_target_pairs={{1,0},{2,1},{3,2},{4,3},{5,4},{6,5},{7,6},{8,7},{9,8},{10,9},{11,1... | collective-permute-start | bytes 27656 | tf_op jit(solution)/shard_map/ppermute | solution.py:29
  54.7 1.2 multiply_bitcast_fusion
  57.3 3.7 %multiply_reduce_fusion.2 = f32[4,8,128,128]{3,2,1,0:T(8,128)S(1)} fusion(f32[4,8,3,128]{3,2,1,0:T(4,128)S(1)} %bitcast.223, f32[4,8,1,128,128]{4,3,2,1,0:T(8,128)S(1)} %fusion.12, f32[4,8,2,128,128]{4,3,2,1,0:T(8,128)} %slice.239), kind=kLoop, calls=%fused_computation.27 | loop fusion | flops 4194304 | bytes 8437760 | tf_op jit(solution)/shard_map/while/body/eval_jaxpr/vmap()/reduce_sum | solution.py:195
  62.0 2.0 subtract_reduce_fusion.2
  65.4 2.1 collective-permute-start.9
  68.5 6.2 %collective-permute-start.11 = (f32[3,1,2,3,128]{4,3,2,1,0:T(4,128)S(1)}, f32[3,1,2,3,128]{4,3,2,1,0:T(4,128)S(1)}, u32[]{:S(2)}, u32[]{:S(2)}) collective-permute-start(f32[3,1,2,3,128]{4,3,2,1,0:T(4,128)S(1)} %pad_maximum_fusion.19), channel_id=1, source_target_pairs={{1,0},{2,1},{3,2},{4,3},{5,4},{6,5},{7,6},{8,7},{9,8},{10,9},{11,1... | collective-permute-start | bytes 27656 | tf_op jit(solution)/shard_map/ppermute | solution.py:29
  77.1 3.7 %multiply_reduce_fusion.1 = f32[4,8,128,128]{3,2,1,0:T(8,128)S(1)} fusion(f32[4,8,3,128]{3,2,1,0:T(4,128)S(1)} %bitcast.225, f32[4,8,1,128,128]{4,3,2,1,0:T(8,128)S(1)} %fusion.12, f32[4,8,2,128,128]{4,3,2,1,0:T(8,128)} %slice.239), kind=kLoop, calls=%fused_computation.25 | loop fusion | flops 4194304 | bytes 8437760 | tf_op jit(solution)/shard_map/while/body/eval_jaxpr/vmap()/reduce_sum | solution.py:195
  81.8 2.0 subtract_reduce_fusion.1
  84.6 1.3 broadcast_multiply_fusion
  86.4 1.2 fusion.20
  87.6 1.9 fusion
  89.6 1.7 collective-permute-start.16
  91.3 1.5 collective-permute-start.17
  94.8 7.0 %collective-permute-start.19 = (f32[72,2,256]{2,0,1:T(8,128)}, f32[72,2,256]{2,0,1:T(8,128)}, u32[]{:S(2)}, u32[]{:S(2)}) collective-permute-start(f32[72,2,256]{2,0,1:T(8,128)} %get-tuple-element.177), channel_id=1, source_target_pairs={{1,0},{2,1},{3,2},{4,3},{5,4},{6,5},{7,6},{8,7},{9,8},{10,9},{11,1... | collective-permute-start | bytes 442376 | tf_op jit(solution)/shard_map/ppermute | solution.py:29
  104.2 1.2 fusion.30
  105.4 2.5 convolution_bitcast_fusion.1
  108.0 1.4 copy.379
  110.3 13.8 %all-to-all-start = ((f32[64,1,1024]{2,1,0:T(1,128)}), f32[64,1,1024]{2,1,0:T(1,128)S(1)}, u32[]{:S(2)}, u32[]{:S(2)}) async-start(f32[64,1,1024]{2,1,0:T(1,128)} %copy.380), calls=%async_computation | async-start | bytes 524288 | tf_op jit(solution)/shard_map/all_to_all | solution.py:347
  126.0 10.0 %all-to-all-done = f32[64,1,1024]{2,1,0:T(1,128)S(1)} async-done(((f32[64,1,1024]{2,1,0:T(1,128)}), f32[64,1,1024]{2,1,0:T(1,128)S(1)}, u32[]{:S(2)}, u32[]{:S(2)}) %all-to-all-start) | async-done | bytes 262176 | tf_op jit(solution)/shard_map/all_to_all | solution.py:347
  136.0 1.1 copy.381
  137.1 2.8 convolution_bitcast_fusion.3
  140.2 1.9 fusion.222
  142.1 4.3 %all-to-all-start.1 = ((f32[4,64,1024]{2,1,0:T(8,128)}), f32[4,64,1024]{2,1,0:T(8,128)}, u32[]{:S(2)}, u32[]{:S(2)}) async-start(f32[4,64,1024]{2,1,0:T(8,128)} %fusion.222), calls=%async_computation.1 | async-start | bytes 2097152 | tf_op jit(solution)/shard_map/all_to_all | solution.py:46
  148.4 12.8 %all-to-all-done.1 = f32[4,64,1024]{2,1,0:T(8,128)} async-done(((f32[4,64,1024]{2,1,0:T(8,128)}), f32[4,64,1024]{2,1,0:T(8,128)}, u32[]{:S(2)}, u32[]{:S(2)}) %all-to-all-start.1) | async-done | bytes 1048608 | tf_op jit(solution)/shard_map/all_to_all | solution.py:46
  161.3 1.3 reduce_sum.225
  162.7 1.1 fusion.45
  165.0 16.9 %all_to_all.28 = f32[4,64,1024]{2,1,0:T(8,128)} all-to-all(f32[4,64,1024]{2,1,0:T(8,128)S(1)} %fusion.223), channel_id=1, replica_groups=mesh['slab'=4,'space_0'=4,'space_1'=8,'space_2'=2] {'slab'}, dimensions={0} | all-to-all | bytes 2097152 | tf_op jit(solution)/shard_map/all_to_all | solution.py:46
  181.9 1.3 reduce_sum.227
  183.3 2.9 %convolution_bitcast_fusion = f32[64,64,4,4]{1,0,3,2:T(8,128)} fusion(f32[8,4,8,256]{3,2,1,0:T(8,128)S(1)} %bitcast.232, s32[64,4]{0,1:T(4,128)S(1)} %copy-done.43), kind=kOutput, calls=%fused_computation.70 | convolution fusion | flops 202309632 | bytes 525312 | tf_op jit(solution)/shard_map/xkl,lsv->sxvk/dot_general | solution.py:371
  186.2 1.4 copy.385
  188.6 8.0 %all-to-all-start.3 = ((f32[64,1,1024]{2,1,0:T(1,128)}), f32[64,1,1024]{2,1,0:T(1,128)S(1)}, u32[]{:S(2)}, u32[]{:S(2)}) async-start(f32[64,1,1024]{2,1,0:T(1,128)} %copy.386), calls=%async_computation.3 | async-start | bytes 524288 | tf_op jit(solution)/shard_map/all_to_all | solution.py:374
  197.7 2.4 collective-permute-start.13
  200.1 1.3 collective-permute-done.12
  201.4 2.6 collective-permute-start.14
  204.8 1.9 scatter_custom_fusion.2
  208.9 1.1 copy.387
  210.0 2.8 convolution_bitcast_fusion.2
  212.9 2.9 %collective-permute-start.21 = (f32[2,4,256]{2,0,1:T(2,128)S(1)}, f32[2,4,256]{2,0,1:T(2,128)S(1)}, u32[]{:S(2)}, u32[]{:S(2)}) collective-permute-start(f32[2,4,256]{2,0,1:T(2,128)S(1)} %get-tuple-element.183), channel_id=1, source_target_pairs={{64,0},{128,64},{192,128},{0,192},{65,1},{129,65},{193,129},{1,193... | collective-permute-start | bytes 24584 | tf_op jit(solution)/shard_map/ppermute | solution.py:29
  215.8 3.7 %multiply_reduce_fusion = f32[4,8,128,128]{3,2,1,0:T(8,128)S(1)} fusion(f32[4,8,3,128]{3,2,1,0:T(4,128)S(1)} %bitcast.219, f32[4,8,1,128,128]{4,3,2,1,0:T(8,128)S(1)} %fusion.12, f32[4,8,2,128,128]{4,3,2,1,0:T(8,128)} %slice.239), kind=kLoop, calls=%fused_computation.23 | loop fusion | flops 4194304 | bytes 8437760 | tf_op jit(solution)/shard_map/while/body/eval_jaxpr/vmap()/reduce_sum | solution.py:195
  220.3 2.3 collective-permute-start.22
  222.6 2.2 collective-permute-start.23
  224.8 2.0 subtract_reduce_fusion
  227.4 1.1 pad_maximum_fusion.2
  228.6 2.1 fusion.26
  232.0 8.3 %all-reduce.4 = (f32[]{:T(128)}, f32[]{:T(128)}) all-reduce(f32[]{:T(128)} %get-tuple-element.143, f32[]{:T(128)} %get-tuple-element.142), channel_id=1, replica_groups=mesh['slab'=4,'space_0'=4,'space_1'=8,'space_2'=2] {'slab'}, use_global_device_ids=true, to_apply=%region_8.9 | all-reduce | flops 2 | bytes 16 | tf_op jit(solution)/shard_map/psum | solution.py:35
  240.2 9.2 %all-reduce.3 = (f32[]{:T(128)}, f32[]{:T(128)}) all-reduce(f32[]{:T(128)} %get-tuple-element.170, f32[]{:T(128)} %get-tuple-element.171), channel_id=1, replica_groups=mesh['slab'=4,'space_0'=4,'space_1'=8,'space_2'=2] {'space_0'}, use_global_device_ids=true, to_apply=%region_9.10 | all-reduce | flops 2 | bytes 16 | tf_op jit(solution)/shard_map/psum | solution.py:35
  249.4 19.1 %all-reduce.2 = (f32[]{:T(128)}, f32[]{:T(128)}) all-reduce(f32[]{:T(128)} %get-tuple-element.168, f32[]{:T(128)} %get-tuple-element.169), channel_id=1, replica_groups=mesh['slab'=4,'space_0'=4,'space_1'=8,'space_2'=2] {'space_1'}, use_global_device_ids=true, to_apply=%region_10.11 | all-reduce | flops 2 | bytes 16 | tf_op jit(solution)/shard_map/psum | solution.py:35
  268.5 5.6 %all-reduce.5 = (f32[]{:T(128)}, f32[]{:T(128)}) all-reduce(f32[]{:T(128)} %get-tuple-element.158, f32[]{:T(128)} %get-tuple-element.159), channel_id=1, replica_groups=mesh['slab'=4,'space_0'=4,'space_1'=8,'space_2'=2] {'space_2'}, use_global_device_ids=true, to_apply=%region_11.12 | all-reduce | flops 2 | bytes 16 | tf_op jit(solution)/shard_map/psum | solution.py:35
  275.7 1.9 scatter_custom_fusion.1
  278.3 3.4 %scatter_custom_fusion = f32[3,512]{0,1:T(8,128)S(1)} fusion(s32[512]{0:T(512)} %bitcast.283, f32[3,512]{0,1:T(8,128)S(1)} %broadcast_multiply_fusion, f32[]{:T(128)S(6)} %div.175, f32[]{:T(128)} %constant.342.clone.1, f32[3,512]{0,1:T(8,128)S(1)} %copy-done.23, s32[1024]{0:T(1024)S(1)} %copy-done.31), kind=kCustom, calls=%fused_computation.169 | custom fusion | flops 3072 | bytes 23044 | tf_op jit(solution)/shard_map/scatter | solution.py:400
  (259 shorter events, 43.8 us)
Async XLA Ops:
  0.6 5.4 %copy-start = (f32[512]{0:T(512)S(1)}, f32[512]{0:T(512)}, u32[]{:S(2)}) copy-start(f32[512]{0:T(512)} %param.18) | copy-start | bytes 6148
  0.6 8.9 %copy-start.37 = (f32[3,512]{1,0:T(4,128)S(1)}, f32[3,512]{1,0:T(4,128)}, u32[]{:S(2)}) copy-start(f32[3,512]{1,0:T(4,128)} %param.15) | copy-start | bytes 18436
  0.7 10.2 %copy-start.48 = (s32[1,2]{1,0:T(1,128)S(1)}, s32[1,2]{1,0:T(1,128)}, u32[]{:S(2)}) copy-start(s32[1,2]{1,0:T(1,128)} %param.20) | copy-start | bytes 28
  2.0 13.2 %copy-start.30 = (s32[1024]{0:T(1024)}, s32[1024]{0:T(1024)S(1)}, u32[]{:S(2)}) copy-start(s32[1024]{0:T(1024)S(1)} %pad_clamp_fusion.3) | copy-start | bytes 12292
  2.0 13.2 %copy-start.40 = (s32[1,4,8]{2,1,0:T(4,128)S(1)}, s32[1,4,8]{2,1,0:T(4,128)}, u32[]{:S(2)}) copy-start(s32[1,4,8]{2,1,0:T(4,128)} %param.21) | copy-start | bytes 388
  2.0 13.2 %copy-start.47 = (s32[1,4]{1,0:T(1,128)S(1)}, s32[1,4]{1,0:T(1,128)}, u32[]{:S(2)}) copy-start(s32[1,4]{1,0:T(1,128)} %param.22) | copy-start | bytes 52
  4.0 12.2 %copy-start.45 = (s32[8]{0:T(128)S(1)}, s32[8]{0:T(128)}, u32[]{:S(2)}) copy-start(s32[8]{0:T(128)} %constant.441) | copy-start | bytes 100
  6.0 17.9 %copy-start.41 = (f32[8,4]{1,0:T(8,128)S(1)}, f32[8,4]{1,0:T(8,128)}, u32[]{:S(2)}) copy-start(f32[8,4]{1,0:T(8,128)} %constant.427.clone) | copy-start | bytes 388
  10.8 14.9 %copy-start.16 = (f32[512,3]{1,0:T(8,128)}, f32[512,3]{1,0:T(8,128)S(1)}, u32[]{:S(2)}) copy-start(f32[512,3]{1,0:T(8,128)S(1)} %gather_fusion) | copy-start | bytes 18436
  10.9 53.1 %copy-start.36 = (s32[1024]{0:T(1024)}, s32[1024]{0:T(1024)S(1)}, u32[]{:S(2)}) copy-start(s32[1024]{0:T(1024)S(1)} %pad_clamp_fusion.2) | copy-start | bytes 12292
  11.5 4.8 %collective-permute-start = (f32[1,1,2,7,128]{4,3,2,1,0:T(8,128)S(1)}, f32[1,1,2,7,128]{4,3,2,1,0:T(8,128)S(1)}, u32[]{:S(2)}, u32[]{:S(2)}) collective-permute-start(f32[1,1,2,7,128]{4,3,2,1,0:T(8,128)S(1)} %bitcast.253), channel_id=1, source_target_pairs={{0,64},{64,128},{128,192},{192,0},{1,65},{65,129},{129,193},{193,1... | collective-permute-start | bytes 21512 | tf_op jit(solution)/shard_map/ppermute | solution.py:28
  13.7 2.6 collective-permute-start.1
  16.2 38.5 %copy-start.18 = (f32[68,512]{1,0:T(8,128)}, f32[68,512]{1,0:T(8,128)S(1)}, u32[]{:S(2)}) copy-start(f32[68,512]{1,0:T(8,128)S(1)} %get-tuple-element.153) | copy-start | bytes 417796
  16.2 39.8 %copy-start.35 = (s32[1024]{0:T(1024)}, s32[1024]{0:T(1024)S(1)}, u32[]{:S(2)}) copy-start(s32[1024]{0:T(1024)S(1)} %pad_clamp_fusion.1) | copy-start | bytes 12292
  16.3 4.4 %collective-permute-start.2 = (f32[3,1,2,7,128]{4,3,2,1,0:T(8,128)S(1)}, f32[3,1,2,7,128]{4,3,2,1,0:T(8,128)S(1)}, u32[]{:S(2)}, u32[]{:S(2)}) collective-permute-start(f32[3,1,2,7,128]{4,3,2,1,0:T(8,128)S(1)} %pad_maximum_fusion.16), channel_id=1, source_target_pairs={{0,1},{1,2},{2,3},{3,4},{4,5},{5,6},{6,7},{7,8},{8,9},{9,10},{10,1... | collective-permute-start | bytes 64520 | tf_op jit(solution)/shard_map/ppermute | solution.py:28
  19.8 3.4 %collective-permute-start.3 = (f32[3,1,2,7,128]{4,3,2,1,0:T(8,128)S(1)}, f32[3,1,2,7,128]{4,3,2,1,0:T(8,128)S(1)}, u32[]{:S(2)}, u32[]{:S(2)}) collective-permute-start(f32[3,1,2,7,128]{4,3,2,1,0:T(8,128)S(1)} %pad_maximum_fusion.16), channel_id=1, source_target_pairs={{1,0},{2,1},{3,2},{4,3},{5,4},{6,5},{7,6},{8,7},{9,8},{10,9},{11,1... | collective-permute-start | bytes 64520 | tf_op jit(solution)/shard_map/ppermute | solution.py:29
  20.1 36.5 %copy-start.32 = (s32[1024]{0:T(1024)}, s32[1024]{0:T(1024)S(1)}, u32[]{:S(2)}) copy-start(s32[1024]{0:T(1024)S(1)} %pad_clamp_fusion) | copy-start | bytes 12292
  45.6 3.7 %collective-permute-start.4 = (f32[1,1,2,3,128]{4,3,2,1,0:T(4,128)S(1)}, f32[1,1,2,3,128]{4,3,2,1,0:T(4,128)S(1)}, u32[]{:S(2)}, u32[]{:S(2)}) collective-permute-start(f32[1,1,2,3,128]{4,3,2,1,0:T(4,128)S(1)} %bitcast.263), channel_id=1, source_target_pairs={{0,64},{64,128},{128,192},{192,0},{1,65},{65,129},{129,193},{193,1... | collective-permute-start | bytes 9224 | tf_op jit(solution)/shard_map/ppermute | solution.py:28
  46.9 2.5 collective-permute-start.5
  48.5 37.9 %copy-start.24 = (f32[8,512]{1,0:T(8,128)}, f32[8,512]{1,0:T(8,128)S(1)}, u32[]{:S(2)}) copy-start(f32[8,512]{1,0:T(8,128)S(1)} %get-tuple-element.155) | copy-start | bytes 49156
  48.5 37.9 %copy-start.26 = (f32[8,512]{1,0:T(8,128)}, f32[8,512]{1,0:T(8,128)S(1)}, u32[]{:S(2)}) copy-start(f32[8,512]{1,0:T(8,128)S(1)} %get-tuple-element.154) | copy-start | bytes 49156
  49.4 6.5 %collective-permute-start.6 = (f32[3,1,2,3,128]{4,3,2,1,0:T(4,128)S(1)}, f32[3,1,2,3,128]{4,3,2,1,0:T(4,128)S(1)}, u32[]{:S(2)}, u32[]{:S(2)}) collective-permute-start(f32[3,1,2,3,128]{4,3,2,1,0:T(4,128)S(1)} %pad_maximum_fusion.18), channel_id=1, source_target_pairs={{0,1},{1,2},{2,3},{3,4},{4,5},{5,6},{6,7},{7,8},{8,9},{9,10},{10,1... | collective-permute-start | bytes 27656 | tf_op jit(solution)/shard_map/ppermute | solution.py:28
  50.8 5.1 %collective-permute-start.7 = (f32[3,1,2,3,128]{4,3,2,1,0:T(4,128)S(1)}, f32[3,1,2,3,128]{4,3,2,1,0:T(4,128)S(1)}, u32[]{:S(2)}, u32[]{:S(2)}) collective-permute-start(f32[3,1,2,3,128]{4,3,2,1,0:T(4,128)S(1)} %pad_maximum_fusion.18), channel_id=1, source_target_pairs={{1,0},{2,1},{3,2},{4,3},{5,4},{6,5},{7,6},{8,7},{9,8},{10,9},{11,1... | collective-permute-start | bytes 27656 | tf_op jit(solution)/shard_map/ppermute | solution.py:29
  57.3 4.1 %copy-start.6 = (f32[4,8,128,128]{3,2,1,0:T(8,128)S(1)}, f32[4,8,128,128]{3,2,1,0:T(8,128)}, u32[]{:S(2)}) copy-start(f32[4,8,128,128]{3,2,1,0:T(8,128)} %copy-done.5) | copy-start | bytes 6291460
  57.3 4.7 %copy-start.10 = (f32[4,8,128,128]{3,2,1,0:T(8,128)S(1)}, f32[4,8,128,128]{3,2,1,0:T(8,128)}, u32[]{:S(2)}) copy-start(f32[4,8,128,128]{3,2,1,0:T(8,128)} %copy-done.9) | copy-start | bytes 6291460
  62.0 14.4 %copy-start.33 = (s32[1024]{0:T(1024)S(1)}, s32[1024]{0:T(1024)}, u32[]{:S(2)}) copy-start(s32[1024]{0:T(1024)} %copy-done.32) | copy-start | bytes 12292
  64.6 3.9 %collective-permute-start.8 = (f32[1,1,2,3,128]{4,3,2,1,0:T(4,128)S(1)}, f32[1,1,2,3,128]{4,3,2,1,0:T(4,128)S(1)}, u32[]{:S(2)}, u32[]{:S(2)}) collective-permute-start(f32[1,1,2,3,128]{4,3,2,1,0:T(4,128)S(1)} %bitcast.259), channel_id=1, source_target_pairs={{0,64},{64,128},{128,192},{192,0},{1,65},{65,129},{129,193},{193,1... | collective-permute-start | bytes 9224 | tf_op jit(solution)/shard_map/ppermute | solution.py:28
  65.4 3.0 %collective-permute-start.9 = (f32[1,1,2,3,128]{4,3,2,1,0:T(4,128)S(1)}, f32[1,1,2,3,128]{4,3,2,1,0:T(4,128)S(1)}, u32[]{:S(2)}, u32[]{:S(2)}) collective-permute-start(f32[1,1,2,3,128]{4,3,2,1,0:T(4,128)S(1)} %bitcast.260), channel_id=1, source_target_pairs={{64,0},{128,64},{192,128},{0,192},{65,1},{129,65},{193,129},{1,193... | collective-permute-start | bytes 9224 | tf_op jit(solution)/shard_map/ppermute | solution.py:29
  68.4 6.9 %collective-permute-start.10 = (f32[3,1,2,3,128]{4,3,2,1,0:T(4,128)S(1)}, f32[3,1,2,3,128]{4,3,2,1,0:T(4,128)S(1)}, u32[]{:S(2)}, u32[]{:S(2)}) collective-permute-start(f32[3,1,2,3,128]{4,3,2,1,0:T(4,128)S(1)} %pad_maximum_fusion.19), channel_id=1, source_target_pairs={{0,1},{1,2},{2,3},{3,4},{4,5},{5,6},{6,7},{7,8},{8,9},{9,10},{10,1... | collective-permute-start | bytes 27656 | tf_op jit(solution)/shard_map/ppermute | solution.py:28
  68.5 7.1 %collective-permute-start.11 = (f32[3,1,2,3,128]{4,3,2,1,0:T(4,128)S(1)}, f32[3,1,2,3,128]{4,3,2,1,0:T(4,128)S(1)}, u32[]{:S(2)}, u32[]{:S(2)}) collective-permute-start(f32[3,1,2,3,128]{4,3,2,1,0:T(4,128)S(1)} %pad_maximum_fusion.19), channel_id=1, source_target_pairs={{1,0},{2,1},{3,2},{4,3},{5,4},{6,5},{7,6},{8,7},{9,8},{10,9},{11,1... | collective-permute-start | bytes 27656 | tf_op jit(solution)/shard_map/ppermute | solution.py:29
  75.4 12.2 %copy-start.13 = (f32[256,512]{1,0:T(8,128)}, f32[256,512]{1,0:T(8,128)S(1)}, u32[]{:S(2)}) copy-start(f32[256,512]{1,0:T(8,128)S(1)} %get-tuple-element.156) | copy-start | bytes 1572868
  77.0 4.1 %copy-start.7 = (f32[4,8,128,128]{3,2,1,0:T(8,128)S(1)}, f32[4,8,128,128]{3,2,1,0:T(8,128)}, u32[]{:S(2)}) copy-start(f32[4,8,128,128]{3,2,1,0:T(8,128)} %copy-done.5) | copy-start | bytes 6291460
  77.0 4.7 %copy-start.11 = (f32[4,8,128,128]{3,2,1,0:T(8,128)S(1)}, f32[4,8,128,128]{3,2,1,0:T(8,128)}, u32[]{:S(2)}) copy-start(f32[4,8,128,128]{3,2,1,0:T(8,128)} %copy-done.9) | copy-start | bytes 6291460
  83.8 3.8 %copy-start.28 = (f32[4,3,128]{2,1,0:T(4,128)}, f32[4,3,128]{2,1,0:T(4,128)S(1)}, u32[]{:S(2)}) copy-start(f32[4,3,128]{2,1,0:T(4,128)S(1)} %subtract_reduce_fusion.1) | copy-start | bytes 18436
  89.6 4.2 %collective-permute-start.16 = (f32[2,8,256]{2,0,1:T(2,128)S(1)}, f32[2,8,256]{2,0,1:T(2,128)S(1)}, u32[]{:S(2)}, u32[]{:S(2)}) collective-permute-start(f32[2,8,256]{2,0,1:T(2,128)S(1)} %copy.376), channel_id=1, source_target_pairs={{0,64},{64,128},{128,192},{192,0},{1,65},{65,129},{129,193},{193,1... | collective-permute-start | bytes 49160 | tf_op jit(solution)/shard_map/ppermute | solution.py:28
  91.3 2.7 collective-permute-start.17
  94.8 8.2 %collective-permute-start.18 = (f32[72,2,256]{2,0,1:T(8,128)}, f32[72,2,256]{2,0,1:T(8,128)}, u32[]{:S(2)}, u32[]{:S(2)}) collective-permute-start(f32[72,2,256]{2,0,1:T(8,128)} %get-tuple-element.176), channel_id=1, source_target_pairs={{0,1},{1,2},{2,3},{3,4},{4,5},{5,6},{6,7},{7,8},{8,9},{9,10},{10,1... | collective-permute-start | bytes 442376 | tf_op jit(solution)/shard_map/ppermute | solution.py:28
  94.8 8.3 %collective-permute-start.19 = (f32[72,2,256]{2,0,1:T(8,128)}, f32[72,2,256]{2,0,1:T(8,128)}, u32[]{:S(2)}, u32[]{:S(2)}) collective-permute-start(f32[72,2,256]{2,0,1:T(8,128)} %get-tuple-element.177), channel_id=1, source_target_pairs={{1,0},{2,1},{3,2},{4,3},{5,4},{6,5},{7,6},{8,7},{9,8},{10,9},{11,1... | collective-permute-start | bytes 442376 | tf_op jit(solution)/shard_map/ppermute | solution.py:29
  110.3 25.8 %all-to-all-start = ((f32[64,1,1024]{2,1,0:T(1,128)}), f32[64,1,1024]{2,1,0:T(1,128)S(1)}, u32[]{:S(2)}, u32[]{:S(2)}) async-start(f32[64,1,1024]{2,1,0:T(1,128)} %copy.380), calls=%async_computation | async-start | bytes 524288 | tf_op jit(solution)/shard_map/all_to_all | solution.py:347
  140.2 6.9 %copy-start.46 = (pred[64]{0:T(512)(128)(4,1)S(1)}, pred[64]{0:T(512)(128)(4,1)}, u32[]{:S(2)}) copy-start(pred[64]{0:T(512)(128)(4,1)} %fusion.200) | copy-start | bytes 196
  140.2 7.5 %copy-start.44 = (f32[64]{0:T(128)S(1)}, f32[64]{0:T(128)}, u32[]{:S(2)}) copy-start(f32[64]{0:T(128)} %get-tuple-element.220) | copy-start | bytes 772
  142.1 19.1 %all-to-all-start.1 = ((f32[4,64,1024]{2,1,0:T(8,128)}), f32[4,64,1024]{2,1,0:T(8,128)}, u32[]{:S(2)}, u32[]{:S(2)}) async-start(f32[4,64,1024]{2,1,0:T(8,128)} %fusion.222), calls=%async_computation.1 | async-start | bytes 2097152 | tf_op jit(solution)/shard_map/all_to_all | solution.py:46
  164.0 19.3 %copy-start.43 = (s32[64,4]{0,1:T(4,128)S(1)}, s32[64,4]{0,1:T(4,128)}, u32[]{:S(2)}) copy-start(s32[64,4]{0,1:T(4,128)} %copy-done.42) | copy-start | bytes 3076
  183.3 13.3 %copy-start.29 = (f32[4,3,128]{2,1,0:T(4,128)S(1)}, f32[4,3,128]{2,1,0:T(4,128)}, u32[]{:S(2)}) copy-start(f32[4,3,128]{2,1,0:T(4,128)} %copy-done.28) | copy-start | bytes 18436
  183.3 20.7 %copy-start.38 = (f32[3,512]{1,0:T(4,128)S(1)}, f32[3,512]{1,0:T(4,128)}, u32[]{:S(2)}) copy-start(f32[3,512]{1,0:T(4,128)} %param.14) | copy-start | bytes 18436
  186.2 22.0 %copy-start.34 = (s32[1024]{0:T(1024)S(1)}, s32[1024]{0:T(1024)}, u32[]{:S(2)}) copy-start(s32[1024]{0:T(1024)} %copy-done.32) | copy-start | bytes 12292
  188.6 20.3 %all-to-all-start.3 = ((f32[64,1,1024]{2,1,0:T(1,128)}), f32[64,1,1024]{2,1,0:T(1,128)S(1)}, u32[]{:S(2)}, u32[]{:S(2)}) async-start(f32[64,1,1024]{2,1,0:T(1,128)} %copy.386), calls=%async_computation.3 | async-start | bytes 524288 | tf_op jit(solution)/shard_map/all_to_all | solution.py:374
  197.3 4.0 %collective-permute-start.12 = (f32[1,1,2,3,128]{4,3,2,1,0:T(4,128)S(1)}, f32[1,1,2,3,128]{4,3,2,1,0:T(4,128)S(1)}, u32[]{:S(2)}, u32[]{:S(2)}) collective-permute-start(f32[1,1,2,3,128]{4,3,2,1,0:T(4,128)S(1)} %bitcast.267), channel_id=1, source_target_pairs={{0,64},{64,128},{128,192},{192,0},{1,65},{65,129},{129,193},{193,1... | collective-permute-start | bytes 9224 | tf_op jit(solution)/shard_map/ppermute | solution.py:28
  197.7 3.7 %collective-permute-start.13 = (f32[1,1,2,3,128]{4,3,2,1,0:T(4,128)S(1)}, f32[1,1,2,3,128]{4,3,2,1,0:T(4,128)S(1)}, u32[]{:S(2)}, u32[]{:S(2)}) collective-permute-start(f32[1,1,2,3,128]{4,3,2,1,0:T(4,128)S(1)} %bitcast.268), channel_id=1, source_target_pairs={{64,0},{128,64},{192,128},{0,192},{65,1},{129,65},{193,129},{1,193... | collective-permute-start | bytes 9224 | tf_op jit(solution)/shard_map/ppermute | solution.py:29
  201.4 6.1 %collective-permute-start.14 = (f32[3,1,2,3,128]{4,3,2,1,0:T(4,128)S(1)}, f32[3,1,2,3,128]{4,3,2,1,0:T(4,128)S(1)}, u32[]{:S(2)}, u32[]{:S(2)}) collective-permute-start(f32[3,1,2,3,128]{4,3,2,1,0:T(4,128)S(1)} %pad_maximum_fusion.20), channel_id=1, source_target_pairs={{0,1},{1,2},{2,3},{3,4},{4,5},{5,6},{6,7},{7,8},{8,9},{9,10},{10,1... | collective-permute-start | bytes 27656 | tf_op jit(solution)/shard_map/ppermute | solution.py:28
  203.9 3.5 %collective-permute-start.15 = (f32[3,1,2,3,128]{4,3,2,1,0:T(4,128)S(1)}, f32[3,1,2,3,128]{4,3,2,1,0:T(4,128)S(1)}, u32[]{:S(2)}, u32[]{:S(2)}) collective-permute-start(f32[3,1,2,3,128]{4,3,2,1,0:T(4,128)S(1)} %pad_maximum_fusion.20), channel_id=1, source_target_pairs={{1,0},{2,1},{3,2},{4,3},{5,4},{6,5},{7,6},{8,7},{9,8},{10,9},{11,1... | collective-permute-start | bytes 27656 | tf_op jit(solution)/shard_map/ppermute | solution.py:29
  212.7 6.8 %copy-start.22 = (f32[64,4,256]{2,0,1:T(8,128)}, f32[64,4,256]{2,0,1:T(8,128)S(1)}, u32[]{:S(2)}) copy-start(f32[64,4,256]{2,0,1:T(8,128)S(1)} %convolution_bitcast_fusion.2) | copy-start | bytes 786436
  212.8 6.7 %collective-permute-start.20 = (f32[2,4,256]{2,0,1:T(2,128)S(1)}, f32[2,4,256]{2,0,1:T(2,128)S(1)}, u32[]{:S(2)}, u32[]{:S(2)}) collective-permute-start(f32[2,4,256]{2,0,1:T(2,128)S(1)} %get-tuple-element.182), channel_id=1, source_target_pairs={{0,64},{64,128},{128,192},{192,0},{1,65},{65,129},{129,193},{193,1... | collective-permute-start | bytes 24584 | tf_op jit(solution)/shard_map/ppermute | solution.py:28
  212.9 6.6 %collective-permute-start.21 = (f32[2,4,256]{2,0,1:T(2,128)S(1)}, f32[2,4,256]{2,0,1:T(2,128)S(1)}, u32[]{:S(2)}, u32[]{:S(2)}) collective-permute-start(f32[2,4,256]{2,0,1:T(2,128)S(1)} %get-tuple-element.183), channel_id=1, source_target_pairs={{64,0},{128,64},{192,128},{0,192},{65,1},{129,65},{193,129},{1,193... | collective-permute-start | bytes 24584 | tf_op jit(solution)/shard_map/ppermute | solution.py:29
  215.8 9.0 %copy-start.4 = (f32[4,8,2,128,128]{4,3,2,1,0:T(8,128)S(1)}, f32[4,8,2,128,128]{4,3,2,1,0:T(8,128)}, u32[]{:S(2)}) copy-start(f32[4,8,2,128,128]{4,3,2,1,0:T(8,128)} %slice.239) | copy-start | bytes 12582916
  215.8 9.0 %copy-start.8 = (f32[4,8,128,128]{3,2,1,0:T(8,128)S(1)}, f32[4,8,128,128]{3,2,1,0:T(8,128)}, u32[]{:S(2)}) copy-start(f32[4,8,128,128]{3,2,1,0:T(8,128)} %copy-done.5) | copy-start | bytes 6291460
  215.8 9.0 %copy-start.12 = (f32[4,8,128,128]{3,2,1,0:T(8,128)S(1)}, f32[4,8,128,128]{3,2,1,0:T(8,128)}, u32[]{:S(2)}) copy-start(f32[4,8,128,128]{3,2,1,0:T(8,128)} %copy-done.9) | copy-start | bytes 6291460
  220.3 6.7 %collective-permute-start.22 = (f32[68,2,256]{2,0,1:T(8,128)}, f32[68,2,256]{2,0,1:T(8,128)}, u32[]{:S(2)}, u32[]{:S(2)}) collective-permute-start(f32[68,2,256]{2,0,1:T(8,128)} %get-tuple-element.180), channel_id=1, source_target_pairs={{0,1},{1,2},{2,3},{3,4},{4,5},{5,6},{6,7},{7,8},{8,9},{9,10},{10,1... | collective-permute-start | bytes 417800 | tf_op jit(solution)/shard_map/ppermute | solution.py:28
  222.6 6.0 %copy-start.14 = (f32[256,512]{1,0:T(8,128)S(1)}, f32[256,512]{1,0:T(8,128)}, u32[]{:S(2)}) copy-start(f32[256,512]{1,0:T(8,128)} %copy-done.13) | copy-start | bytes 1572868
  222.6 4.9 %collective-permute-start.23 = (f32[68,2,256]{2,0,1:T(8,128)}, f32[68,2,256]{2,0,1:T(8,128)}, u32[]{:S(2)}, u32[]{:S(2)}) collective-permute-start(f32[68,2,256]{2,0,1:T(8,128)} %get-tuple-element.181), channel_id=1, source_target_pairs={{1,0},{2,1},{3,2},{4,3},{5,4},{6,5},{7,6},{8,7},{9,8},{10,9},{11,1... | collective-permute-start | bytes 417800 | tf_op jit(solution)/shard_map/ppermute | solution.py:29
  230.7 44.8 %copy-start.17 = (f32[512,3]{1,0:T(8,128)S(1)}, f32[512,3]{1,0:T(8,128)}, u32[]{:S(2)}) copy-start(f32[512,3]{1,0:T(8,128)} %copy-done.16) | copy-start | bytes 18436
  230.7 44.8 %copy-start.20 = (f32[3,4,128]{0,2,1:T(8,128)S(1)}, f32[3,4,128]{0,2,1:T(8,128)}, u32[]{:S(2)}) copy-start(f32[3,4,128]{0,2,1:T(8,128)} %copy.375) | copy-start | bytes 18436
  230.7 47.6 %copy-start.23 = (f32[3,512]{0,1:T(8,128)S(1)}, f32[3,512]{0,1:T(8,128)}, u32[]{:S(2)}) copy-start(f32[3,512]{0,1:T(8,128)} %copy.348) | copy-start | bytes 18436
  230.7 47.6 %copy-start.31 = (s32[1024]{0:T(1024)S(1)}, s32[1024]{0:T(1024)}, u32[]{:S(2)}) copy-start(s32[1024]{0:T(1024)} %copy-done.30) | copy-start | bytes 12292
  (13 other events, 32.5 us)
where the time goes:
time: 288 us; the launch traced here: 283 us
  starting transfers between devices  73.8 us (26%)
  blocking collectives  59.1 us (21%)
  other arithmetic  56.9 us (20%)
  local copies, waits for them, and re-layouts  40.7 us (14%)
  waiting for transfers between devices  30.7 us (11%)
  matrix products  17.9 us (6%)
  between operations  3.82 us (1%)
    psum x4, blocking collectives, over_axes(): return functools.reduce(lax.psum, axes, array)  42.2 us
    ppermute x12, starting transfers between devices, with_halo(): after = lax.ppermute(initial, axis, down)  31.5 us
    all_to_all x1, blocking collectives, summed_on_arrival(): lax.all_to_all(pieces, axis, split_axis=0, concat_axis=0, tiled=True)  16.9 us
    ppermute x12, starting transfers between devices, with_halo(): before = lax.ppermute(last, axis, up)  16.3 us
    reduce_sum x4, other arithmetic, short_per_tile(): projection = jnp.sum(displacement * dipole[:, :, None, :], 1)  14.4 us
    all_to_all x1, starting transfers between devices, local(): lax.all_to_all(along_z.reshape(n_space, -1), SPACE, split_axis=0, concat_...  13.8 us
    all_to_all x1, waiting for transfers between devices, summed_on_arrival(): lax.all_to_all(pieces, axis, split_axis=0, concat_axis=0, tiled=True)  12.8 us
    all_to_all x1, waiting for transfers between devices, local(): lax.all_to_all(along_z.reshape(n_space, -1), SPACE, split_axis=0, concat_...  10 us
  transfers between devices with their start and end apart: 27, of which 13 were waited for; matrix products, arithmetic and copies ran while one was open for 7% of the time, Pallas kernels for 0%

commit v1 on v0

v1 whole, which is shorter than its diff:
```python
import functools
import math

import jax
import jax.numpy as jnp
import ml_dtypes
import numpy as np
from jax import lax
from jax.experimental import pallas as pl
from jax.experimental.pallas import tpu as pltpu
from jax.sharding import PartitionSpec as P

G = 256
TILE = 128
BOTH = ("slab", "space")
BETA = 0.4
THOLE = 0.39
ROOT_PI = math.sqrt(math.pi)
SELF_FIELD = 4.0 * BETA**3 / (3.0 * ROOT_PI)
F32 = jnp.float32
BF16 = jnp.bfloat16
SCALED_ERFC_T = 0.45
SCALED_ERFC = (
    0.25388532876968384,
    0.25388309359550476,
    0.22827406227588654,
    0.17522020637989044,
    0.1201537474989891,
    -0.023065825924277306,
    0.14381752908229828,
    -0.3022053837776184,
    0.19167575240135193,
    -0.04163854941725731,
)
NT = (((1,), (1,)), ((), ()))
NN = (((1,), (0,)), ((), ()))
TN = (((0,), (0,)), ((), ()))
VMEM_LIMIT = 48 * 1024 * 1024


def halves(values):
    high = values.astype(BF16)
    return (high, (values - high.astype(F32)).astype(BF16))


def product(left, right, dims):
    def one(a, b):
        return lax.dot_general(a, b, dims, preferred_element_type=F32)

    return one(left[0], right[0]) + (one(left[0], right[1]) + one(left[1], right[0]))


def thirds(values):
    high = values.astype(BF16).astype(F32)
    rest = values - high
    middle = rest.astype(BF16).astype(F32)
    return jnp.concatenate([high, middle, rest - middle], 0).astype(BF16)


def selected(values, one_hot, dims):
    rows = values.shape[0]
    picked = lax.dot_general(thirds(values), one_hot, dims, preferred_element_type=F32)
    return picked[:rows] + (picked[rows : 2 * rows] + picked[2 * rows :])


def order_matrix(order_row, count):
    ids = lax.broadcasted_iota(jnp.int32, (count, count), 0)
    return jnp.where(ids == order_row, 1.0, 0.0).astype(BF16)


COUNTS_AT = 32
SEND_AT = 36
PARITY_AT = 38


def tile_at(meta, place):
    first, second = (meta[SEND_AT], meta[SEND_AT + 1])
    if place == 0:
        return first
    if place == 1:
        return second
    third = jnp.where(
        (first != 0) & (second != 0), 0, jnp.where((first != 1) & (second != 1), 1, 2)
    )
    return third if place == 2 else 6 - first - second - third


def pool_slot(meta, entry):
    remote = entry - 4
    pair = remote // 2
    pair = pair + jnp.where(pair >= 4, 1, 0)
    along = jnp.where(pair >= 3, 1, 0) + jnp.where(pair >= 6, 1, 0)
    across = pair - 3 * along
    inner_side = jnp.where(meta[PARITY_AT] == 0, 2, 0)
    base = jnp.where(across == 1, 4, jnp.where(across == inner_side, 10, 16))
    return jnp.where(entry < 4, entry, base + along * 2 + remote % 2)


def call(kernel, outs, flops, smem=0, scratch=()):
    def run(*args):
        in_specs = [pl.BlockSpec(memory_space=pltpu.SMEM)] * smem
        in_specs += [pl.BlockSpec(memory_space=pltpu.VMEM)] * (len(args) - smem)
        return pl.pallas_call(
            kernel,
            out_shape=[jax.ShapeDtypeStruct(shape, dtype) for shape, dtype in outs],
            in_specs=in_specs,
            out_specs=[pl.BlockSpec(memory_space=pltpu.VMEM)] * len(outs),
            scratch_shapes=list(scratch),
            compiler_params=pltpu.CompilerParams(vmem_limit_bytes=VMEM_LIMIT),
            cost_estimate=pl.CostEstimate(
                flops=flops, bytes_accessed=1 << 20, transcendentals=0
            ),
        )(*args)

    return run


def gather_kernel(meta, residual, cells, fraction, alphas, order, own, sent):
    atoms = residual.shape[1]
    position = cells[...].astype(F32) + fraction[...]
    rows = jnp.concatenate(
        [position, alphas[...], residual[...], jnp.zeros((1, atoms), F32)], 0
    )
    picked = selected(rows, order_matrix(order[...], atoms), NN)
    for tile in range(atoms // TILE):
        own[tile] = picked[:, tile * TILE : (tile + 1) * TILE]
    for place in range(2):
        sent[place] = own[meta[SEND_AT + place]]


def search_rows(block):
    return block[3:4] * block[4:7]


def fill_pool(pool, extents, own, straight, inner, outer, meta):
    inner_step = jnp.where(meta[PARITY_AT] == 0, 1.0, -1.0)
    rows = lax.broadcasted_iota(jnp.int32, (8, TILE), 0)
    for tile in range(4):
        pool[tile] = own[tile]
    for base, source, step in ((4, straight, 0.0), (10, inner, inner_step), (16, outer, -inner_step)):
        for along in range(3):
            shift = jnp.where(
                rows == 0,
                float((along - 1) * extents[0]),
                jnp.where(rows == 1, step * float(extents[1]), 0.0),
            )
            for member in range(2):
                pool[base + 2 * along + member] = source[along, member] + shift


def own_columns(columns, block):
    turned = block.T
    for row in range(columns.shape[0]):
        columns[row] = jnp.broadcast_to(turned[:, row : row + 1], (TILE, TILE))


def wrap_depth(depth):
    half = 0.5 * G
    return jnp.where(depth > half, depth - G, jnp.where(depth < -half, depth + G, depth))


PAIR_ROWS = 64


def pair_kernel(places, extents, meta, own, straight, inner, outer, pool, pairs, found, columns, totals):
    fill_pool(pool, extents, own, straight, inner, outer, meta)
    for at, place in enumerate(places):
        tile = tile_at(meta, place)
        block = own[tile]
        own_columns(columns, jnp.concatenate([block[:3], lax.rsqrt(block[3:4]), block[4:]], 0))
        live = meta[COUNTS_AT + tile]
        for chunk in range(TILE // PAIR_ROWS):
            rows = slice(chunk * PAIR_ROWS, (chunk + 1) * PAIR_ROWS)
            shape = (PAIR_ROWS, TILE)
            same = lax.broadcasted_iota(jnp.int32, shape, 0) + chunk * PAIR_ROWS
            diagonal = jnp.where(same == lax.broadcasted_iota(jnp.int32, shape, 1), 1.0, 0.0)

            def step(entry, sums):
                listed = meta[tile * 8 + entry]
                other = pool[pool_slot(meta, listed)]
                itself = diagonal * jnp.where(listed == tile, 1.0, 0.0)
                d_x = other[0:1] - columns[0, rows]
                d_y = other[1:2] - columns[1, rows]
                d_z = wrap_depth(other[2:3] - columns[2, rows])
                square = d_x * d_x + d_y * d_y + d_z * d_z + itself
                inverse = lax.rsqrt(square)
                distance = square * inverse
                inverse_sq = inverse * inverse
                gauss = jnp.exp(-(BETA**2) * square)
                t = 1.0 / (1.0 + (SCALED_ERFC_T * BETA) * distance)
                series = jnp.full(shape, SCALED_ERFC[-1], F32)
                for term in SCALED_ERFC[-2::-1]:
                    series = series * t + term
                bare_one = gauss * (series * t * inverse + 2.0 * BETA / ROOT_PI) * inverse_sq
                bare_two = (3.0 * bare_one + (4.0 * BETA**3 / ROOT_PI) * gauss) * inverse_sq
                damping = (square * distance) * (THOLE * columns[3, rows] * lax.rsqrt(other[3:4]))
                decay = jnp.exp(-damping) * inverse * inverse_sq
                keep = 1.0 - itself
                three = keep * (bare_one - decay)
                five = keep * (bare_two - 3.0 * (1.0 + damping) * decay * inverse_sq)
                pairs[0, at * 8 + entry, rows] = five
                pairs[1, at * 8 + entry, rows] = three
                v = search_rows(other)
                along = five * (d_x * v[0:1] + d_y * v[1:2] + d_z * v[2:3])
                return (
                    sums[0] + (along * d_x - three * v[0:1]),
                    sums[1] + (along * d_y - three * v[1:2]),
                    sums[2] + (along * d_z - three * v[2:3]),
                )

            zero = jnp.zeros(shape, F32)
            sums = lax.fori_loop(0, live, step, (zero, zero, zero))
            for part in range(3):
                totals[part, rows] = sums[part]
        found[at] = updated(block, totals)


def field_rows(totals):
    return [jnp.sum(totals[part].T, axis=0, keepdims=True) for part in range(3)]


def updated(block, totals):
    alpha = block[3:4]
    field = field_rows(totals)
    rows = [alpha * (block[4 + part : 5 + part] + field[part]) for part in range(3)]
    return jnp.concatenate(rows + [jnp.zeros((5, TILE), F32)], 0)


APPLY_ROWS = 32


def fill_search(pool, own_first, own_rest, straight, inner, outer, meta):
    for place in range(4):
        pool[tile_at(meta, place)] = own_first[place] if place < 2 else own_rest[place - 2]
    for base, source in ((4, straight), (10, inner), (16, outer)):
        for along in range(3):
            for member in range(2):
                pool[base + 2 * along + member] = source[along, member]


def apply_tile(meta, tile, at, pairs, geometry, pool, columns, totals):
    block = geometry[tile]
    own_columns(columns, block)
    live = meta[COUNTS_AT + tile]
    for chunk in range(TILE // APPLY_ROWS):
        rows = slice(chunk * APPLY_ROWS, (chunk + 1) * APPLY_ROWS)
        x_i, y_i, z_i = (columns[0, rows], columns[1, rows], columns[2, rows])

        def step(entry, sums):
            slot = pool_slot(meta, meta[tile * 8 + entry])
            other = geometry[slot]
            v = pool[slot]
            d_x = other[0:1] - x_i
            d_y = other[1:2] - y_i
            d_z = wrap_depth(other[2:3] - z_i)
            three = pairs[1, at * 8 + entry, rows]
            along = pairs[0, at * 8 + entry, rows] * (d_x * v[0:1] + d_y * v[1:2] + d_z * v[2:3])
            return (
                sums[0] + (along * d_x - three * v[0:1]),
                sums[1] + (along * d_y - three * v[1:2]),
                sums[2] + (along * d_z - three * v[2:3]),
            )

        zero = jnp.zeros((APPLY_ROWS, TILE), F32)
        sums = lax.fori_loop(0, live, step, (zero, zero, zero))
        for part in range(3):
            totals[part, rows] = sums[part]


def sweep_kernel(places, meta, geometry, own_first, own_rest, straight, inner, outer, *rest):
    banks = len(places) // 2
    pairs, found = (rest[:banks], rest[banks])
    pool, columns, totals = rest[banks + 1 :]
    fill_search(pool, own_first, own_rest, straight, inner, outer, meta)
    for at, place in enumerate(places):
        tile = tile_at(meta, place)
        apply_tile(meta, tile, at % 2, pairs[at // 2], geometry, pool, columns, totals)
        found[at] = updated(geometry[tile], totals)


def final_field_kernel(
    meta, geometry, direction, straight, inner, outer, pairs_a, pairs_b, order, applied, sums, pool, columns, totals, local
):
    atoms = order.shape[1]
    fill_search(pool, direction, direction.at[2:4], straight, inner, outer, meta)
    curve = jnp.zeros((1, TILE), F32)
    dots = jnp.zeros((1, TILE), F32)
    for place in range(4):
        tile = tile_at(meta, place)
        apply_tile(meta, tile, place % 2, (pairs_a, pairs_b)[place // 2], geometry, pool, columns, totals)
        block = geometry[tile]
        ahead = direction[place]
        field = field_rows(totals)
        rows = []
        for part in range(3):
            d = ahead[part : part + 1]
            value = d / block[3:4] - field[part] - SELF_FIELD * d
            curve = curve + d * value
            dots = dots + d * block[4 + part : 5 + part]
            rows.append(value)
        local[tile] = jnp.concatenate(rows + [jnp.zeros((5, TILE), F32)], 0)
    in_tiles = jnp.concatenate([local[tile] for tile in range(4)], 1)
    applied[...] = selected(in_tiles, order_matrix(order[...], atoms), NT)
    lane = lax.broadcasted_iota(jnp.int32, (8, TILE), 1)
    curve_sum = jnp.sum(curve, axis=1, keepdims=True)
    dot_sum = jnp.sum(dots, axis=1, keepdims=True)
    sums[...] = jnp.where(lane == 1, curve_sum, jnp.where(lane == 2, dot_sum, 0.0))


def spline(fraction):
    centre_arg = fraction - 0.5

    def middle(u):
        return (55.0 + u * (20.0 + u * (-120.0 + u * (80.0 - 16.0 * u)))) / 96.0

    def middle_slope(u):
        return (20.0 + u * (-240.0 + u * (240.0 - 64.0 * u))) / 96.0

    def outer(u):
        w = 5.0 - 2.0 * u
        return (w * w) * (w * w) / 384.0

    def outer_slope(u):
        w = 5.0 - 2.0 * u
        return -(w * w * w) / 48.0

    sq = centre_arg * centre_arg
    weights = (
        outer(fraction + 1.5),
        middle(fraction + 0.5),
        115.0 / 192.0 - 0.625 * sq + 0.25 * sq * sq,
        middle(1.5 - fraction),
        outer(2.5 - fraction),
    )
    slopes = (
        outer_slope(fraction + 1.5),
        middle_slope(fraction + 0.5),
        -1.25 * centre_arg + centre_arg * sq,
        -middle_slope(1.5 - fraction),
        -outer_slope(2.5 - fraction),
    )
    return (weights, slopes)


def table(cell_row, values, length, wrapped):
    atoms = cell_row.shape[1]
    ids = lax.broadcasted_iota(jnp.int32, (length, atoms), 0)
    if wrapped:
        ahead = ids - cell_row + 2
        ahead = jnp.where(ahead >= G, ahead - G, jnp.where(ahead < 0, ahead + G, ahead))
    else:
        ahead = ids - cell_row
    total = jnp.zeros((length, atoms), F32)
    for step in range(5):
        total = jnp.where(ahead == step, values[step], total)
    return total


def tables_kernel(cells, fraction, cas_high, cas_low, tab_x, tab_y, w_high, w_low, slope_z):
    for dim, out in ((0, tab_x), (1, tab_y)):
        weights, slopes = spline(fraction[dim : dim + 1])
        out[0] = table(cells[dim : dim + 1], weights, out.shape[1], False)
        out[1] = table(cells[dim : dim + 1], slopes, out.shape[1], False)
    weights, slopes = spline(fraction[2:3])
    cas = (cas_high[...], cas_low[...])
    waves = product(cas, halves(table(cells[2:3], weights, G, True)), NN)
    high, low = halves(waves)
    w_high[...] = high
    w_low[...] = low
    slope_z[...] = product(cas, halves(table(cells[2:3], slopes, G, True)), NN)


def spread_kernel(x_rows, meta, direction, order, tab_x, tab_y, w_high, w_low, slope_z, ordered, out, local):
    atoms = order.shape[1]
    y_rows = tab_y.shape[1]
    for place in range(4):
        local[tile_at(meta, place)] = direction[place]
    in_tiles = jnp.concatenate([local[tile] for tile in range(4)], 1)
    d = selected(in_tiles, order_matrix(order[...], atoms), NT)
    ordered[...] = d
    w_z = (w_high[...], w_low[...])
    s_z = halves(slope_z[...] * d[2:3])
    slope_part = tab_x[1] * d[0:1]
    weight_part = tab_x[0] * d[1:2]
    sides = []
    for y in range(y_rows):
        w_y, s_y = (tab_y[0, y : y + 1], tab_y[1, y : y + 1])
        sides.append((slope_part * w_y + weight_part * s_y, tab_x[0] * w_y))
    side = halves(jnp.concatenate([pair[0] for pair in sides], 0))
    flat = halves(jnp.concatenate([pair[1] for pair in sides], 0))
    width = y_rows * x_rows
    out[:, :width] = product(w_z, side, NT) + product(s_z, flat, NT)
    out[:, width:] = jnp.zeros((G, out.shape[1] - width), F32)


def plane_kernel(
    shapes, grid, factor, sums, x_high, x_low, y_high, y_low, yt_high, yt_low, xt_high, xt_low, out, along_x
):
    n_slab, n_space, x_rows, y_rows = shapes
    width = x_rows * y_rows
    for y in range(y_rows):
        total = None
        for s in range(n_slab):
            block = halves(grid[s * n_space : (s + 1) * n_space, y * x_rows : (y + 1) * x_rows])
            rows = slice(s * x_rows, (s + 1) * x_rows)
            term = product(block, (x_high[rows], x_low[rows]), NN)
            total = term if total is None else total + term
        along_x[y * n_space : (y + 1) * n_space] = total
    spectrum = product((yt_high[...], yt_low[...]), halves(along_x[...]), NN)
    scaled = spectrum * factor[...]
    energy = jnp.sum(jnp.sum(spectrum * scaled, axis=0, keepdims=True), axis=1, keepdims=True)
    back = halves(product((y_high[...], y_low[...]), halves(scaled), NN))
    planes = product(back, (xt_high[...], xt_low[...]), NN)
    for s in range(n_slab):
        for y in range(y_rows):
            out[s * n_space : (s + 1) * n_space, y * x_rows : (y + 1) * x_rows] = planes[
                y * n_space : (y + 1) * n_space, s * TILE : s * TILE + x_rows
            ]
    spare = out.shape[1] - width
    lane = lax.broadcasted_iota(jnp.int32, (1, spare), 1)
    tail = jnp.where(lane == 0, energy, sums[0:1, :spare])
    out[:, width:] = jnp.broadcast_to(tail, (out.shape[0], spare))


def finish_kernel(
    x_rows, grid, w_high, w_low, slope_z, tab_x, tab_y, ordered, applied, dipoles, residual, next_dipoles, next_residual, direction
):
    y_rows = tab_y.shape[1]
    width = y_rows * x_rows
    planes = halves(grid[:, :width])
    tail = jnp.sum(grid[:, width:], axis=0, keepdims=True)
    step = tail[:, 2:3] / (tail[:, 0:1] + tail[:, 1:2])
    by_weight = product(planes, (w_high[...], w_low[...]), TN)
    by_slope = product(planes, halves(slope_z[...]), TN)
    fields = [0.0, 0.0, 0.0]
    for y in range(y_rows):
        rows = slice(y * x_rows, (y + 1) * x_rows)
        w_y, s_y = (tab_y[0, y : y + 1], tab_y[1, y : y + 1])
        weighted = by_weight[rows]
        fields[0] += w_y * jnp.sum(tab_x[1] * weighted, axis=0, keepdims=True)
        fields[1] += s_y * jnp.sum(tab_x[0] * weighted, axis=0, keepdims=True)
        fields[2] += w_y * jnp.sum(tab_x[0] * by_slope[rows], axis=0, keepdims=True)
    total = applied[0:3] + jnp.concatenate(fields, 0)
    d = ordered[0:3]
    next_dipoles[...] = dipoles[...] + step * d
    next_residual[...] = residual[...] - step * total
    direction[...] = d


def cas_matrix(first, second):
    angles = 2.0 * np.pi / G * (np.outer(first, second) % G)
    return np.cos(angles) + np.sin(angles)


def split_constant(values):
    whole = values.astype(np.float32)
    high = whole.astype(ml_dtypes.bfloat16)
    low = (values - high.astype(np.float64)).astype(ml_dtypes.bfloat16)
    return (jnp.asarray(high), jnp.asarray(low))


def wave_factors(freq_ids):
    wrapped = jnp.where(freq_ids > G // 2, freq_ids - G, freq_ids).astype(F32) / G
    angles = 2.0 * math.pi / G * freq_ids.astype(F32)
    modulus = 115.0 / 192.0 + 19.0 / 48.0 * jnp.cos(angles) + 1.0 / 192.0 * jnp.cos(2.0 * angles)
    return (
        wrapped * wrapped,
        jnp.exp(-((math.pi / BETA) ** 2) * wrapped * wrapped) / (modulus * modulus),
    )


def multiplier(freq_x, freq_y, freq_z):
    square_x, factor_x = wave_factors(freq_x)
    square_y, factor_y = wave_factors(freq_y)
    square_z, factor_z = wave_factors(freq_z)
    square_sum = square_x + square_y + square_z
    anchor = ((freq_x == 0) & (freq_y == 0) & (freq_z == 0)).astype(F32)
    return (
        (1.0 - anchor)
        * factor_x
        * factor_y
        * factor_z
        / (math.pi * float(G) ** 3 * (square_sum + anchor))
    )


def swap_pairs(n_slab, n_space, odd):
    pairs = []
    for s in range(n_slab):
        for q in range(n_space):
            partner = (q + 1 if (q % 2 == 1) == odd else q - 1) % n_space
            pairs.append((s * n_space + q, s * n_space + partner))
    return pairs


def around(block):
    n_slab, n_space = (lax.axis_size("slab"), lax.axis_size("space"))
    up = [(i, (i + 1) % n_slab) for i in range(n_slab)]
    down = [(j, i) for i, j in up]
    before = lax.ppermute(block, "slab", up)
    after = lax.ppermute(block, "slab", down)
    straight = jnp.stack([before, block, after])
    inner = lax.ppermute(straight, BOTH, swap_pairs(n_slab, n_space, False))
    outer = lax.ppermute(straight, BOTH, swap_pairs(n_slab, n_space, True))
    return (straight, inner, outer)


def local(
    dipoles, residual, cells, fraction, polarizability, tile_order, send_tiles, tile_lists, tile_counts
):
    n_slab, n_space = (lax.axis_size("slab"), lax.axis_size("space"))
    atoms = residual.shape[1]
    extents = (G // n_slab, G // n_space)
    x_rows = -(-(extents[0] + 4) // 8) * 8
    y_rows = extents[1] + 4
    width = x_rows * y_rows
    lanes = -(-(width + 3) // TILE) * TILE
    slab_index, space_index = (lax.axis_index("slab"), lax.axis_index("space"))
    meta = jnp.concatenate(
        [
            tile_lists.reshape(-1),
            tile_counts.reshape(-1),
            send_tiles.reshape(-1),
            (space_index % 2).reshape(1).astype(jnp.int32),
        ]
    )
    tile_shape = ((4, 8, TILE), F32)
    two_shape = ((2, 8, TILE), F32)
    bank_shape = ((2, 16, TILE, TILE), F32)
    pool_scratch = pltpu.VMEM((22, 8, TILE), F32)
    total_scratch = pltpu.VMEM((3, TILE, TILE), F32)
    own, sent = call(gather_kernel, [tile_shape, two_shape], 10**8, smem=1)(
        meta, residual, cells, fraction, polarizability.reshape(1, atoms), tile_order
    )
    first = around(sent)

    def pairs_of(places):
        return call(
            functools.partial(pair_kernel, places, extents),
            [((22, 8, TILE), F32), bank_shape, two_shape],
            10**9,
            smem=1,
            scratch=(pltpu.VMEM((8, TILE, TILE), F32), total_scratch),
        )(meta, own, *first)

    geometry, pairs_a, search_a = pairs_of((0, 1))
    _, pairs_b, search_b = pairs_of((2, 3))
    sweep_scratch = (pool_scratch, pltpu.VMEM((3, TILE, TILE), F32), total_scratch)
    second = around(search_a)

    def sweep(places, mine, others, received, banks):
        return call(
            functools.partial(sweep_kernel, places),
            [((len(places), 8, TILE), F32)],
            10**8,
            smem=1,
            scratch=sweep_scratch,
        )(meta, geometry, mine, others, *received, *banks)[0]

    next_a = sweep((0, 1), search_a, search_b, second, (pairs_a,))
    next_b = sweep((2, 3), search_a, search_b, second, (pairs_b,))
    third = around(next_a)
    direction = sweep((0, 1, 2, 3), next_a, next_b, third, (pairs_a, pairs_b))
    freq = np.arange(G)
    padded_x = np.stack([(s * extents[0] + np.arange(x_rows) - 2) % G for s in range(n_slab)])
    real_x = np.tile(np.arange(x_rows) < extents[0] + 4, n_slab)
    cas_x = cas_matrix(padded_x.reshape(-1), freq) * real_x[:, None]
    rows_y = (np.arange(n_space)[None] * extents[1] + np.arange(y_rows)[:, None] - 2) % G
    cas_y = cas_matrix(rows_y.reshape(-1), freq)
    wide_x = np.zeros((G, n_slab, TILE))
    wide_x[:, :, :x_rows] = cas_x.reshape(n_slab, x_rows, G).transpose(2, 0, 1)
    tab_x, tab_y, w_high, w_low, slope_z = call(
        tables_kernel,
        [
            ((2, x_rows, atoms), F32),
            ((2, y_rows, atoms), F32),
            ((G, atoms), BF16),
            ((G, atoms), BF16),
            ((G, atoms), F32),
        ],
        10**8,
    )(cells, fraction, *split_constant(cas_matrix(freq, freq)))
    ordered, spread = call(
        functools.partial(spread_kernel, x_rows),
        [((8, atoms), F32), ((G, lanes), F32)],
        10**9,
        smem=1,
        scratch=(pltpu.VMEM((4, 8, TILE), F32),),
    )(meta, direction, tile_order, tab_x, tab_y, w_high, w_low, slope_z)
    grid = lax.all_to_all(spread, BOTH, 0, 0, tiled=True)
    last = around(direction[:2])
    applied, sums = call(
        final_field_kernel,
        [((8, atoms), F32), ((8, TILE), F32)],
        10**9,
        smem=1,
        scratch=sweep_scratch + (pltpu.VMEM((4, 8, TILE), F32),),
    )(meta, geometry, direction, *last, pairs_a, pairs_b, tile_order)
    ids = jnp.arange(G, dtype=jnp.int32)
    factor = multiplier(ids[None, :], ids[:, None], slab_index * n_space + space_index)
    planes = call(
        functools.partial(plane_kernel, (n_slab, n_space, x_rows, y_rows)),
        [((G, lanes), F32)],
        10**9,
        scratch=(pltpu.VMEM((y_rows * n_space, G), F32),),
    )(
        grid,
        factor,
        sums,
        *split_constant(cas_x),
        *split_constant(cas_y),
        *split_constant(cas_y.T),
        *split_constant(wide_x.reshape(G, -1)),
    )[0]
    returned = lax.all_to_all(planes, BOTH, 0, 0, tiled=True)
    three = ((3, atoms), F32)
    return tuple(
        call(functools.partial(finish_kernel, x_rows), [three, three, three], 10**9)(
            returned, w_high, w_low, slope_z, tab_x, tab_y, ordered, applied, dipoles, residual
        )
    )


def solution(mesh):
    in_specs = (
        P(None, BOTH),
        P(None, BOTH),
        P(None, BOTH),
        P(None, BOTH),
        P(BOTH),
        P(BOTH, None),
        P(BOTH, None),
        P(BOTH, None, None),
        P(BOTH, None),
    )
    out_specs = (P(None, BOTH), P(None, BOTH), P(None, BOTH))
    return jax.shard_map(local, mesh=mesh, in_specs=in_specs, out_specs=out_specs, check_vma=False)
```

time: 288 us -> 146 us (0.51); the launches traced: 283 us -> 145 us
  other arithmetic: 56.9 us -> 1.01 us
  Pallas kernels: 0 us -> 27.7 us
  local copies, waits for them, and re-layouts: 40.7 us -> 13.6 us
  starting transfers between devices: 73.8 us -> 47.1 us
  blocking collectives: 59.1 us -> 36 us
  matrix products: 17.9 us -> 0 us
  waiting for transfers between devices: 30.7 us -> 18.1 us
    psum x4 -> x0, blocking collectives: 42.2 us -> none  [over_axes(): return functools.reduce(lax.psum, axes, array)]
    pallas_call x0 -> x11, Pallas kernels: none -> 27.7 us  [run(): pl.pallas_call(kernel, out_shape=[jax.ShapeDtypeStruct(shape, dtype) for...]
    reduce_sum x15 -> x0, other arithmetic: 27.5 us -> none  [the longest x4 14.4 us: short_per_tile(): projection = jnp.sum(displacement * dipole[:, :, None, :], 1)]
    all_to_all x3 -> x1, waiting for transfers between devices: 22.8 us -> 3.36 us  [local(): grid = lax.all_to_all(spread, BOTH, 0, 0, tiled=True)]
    all_to_all x1, blocking collectives: 16.9 us -> 36 us  [local(): returned = lax.all_to_all(planes, BOTH, 0, 0, tiled=True)]
    dot_general x8 -> x0, matrix products: 17.9 us -> none  [the longest x1 2.93 us: local(): jnp.einsum('xkl,lsv->sxvk', back_x, cas_table.reshape(G, n_space, extent_...]
    gather x24 -> x0, local copies, waits for them, and re-layouts: 15 us -> none  [the longest x1 3.52 us: local(): alphas = polarizability[atom_order][None]]
    all_to_all x3 -> x1, starting transfers between devices: 26.1 us -> 12.7 us  [local(): grid = lax.all_to_all(spread, BOTH, 0, 0, tiled=True)]
  transfers between devices with their start and end apart: 27 -> 17, of which waited for: 13 -> 11; matrix products, arithmetic and copies ran while one was open for 7% -> 0% of each run, Pallas kernels for 0% -> 8%
where the time goes in v1:
time: 146 us; the launch traced here: 145 us
  starting transfers between devices  47.1 us (32%)
  blocking collectives  36 us (25%)
  Pallas kernels  27.7 us (19%)
  waiting for transfers between devices  18.1 us (12%)
  local copies, waits for them, and re-layouts  13.6 us (9%)
    all_to_all x1, blocking collectives, local(): returned = lax.all_to_all(planes, BOTH, 0, 0, tiled=True)  36 us
    pallas_call x11, Pallas kernels, run(): pl.pallas_call(kernel, out_shape=[jax.ShapeDtypeStruct(shape, dtype) for...  27.7 us
    ppermute x4, starting transfers between devices, around(): inner = lax.ppermute(straight, BOTH, swap_pairs(n_slab, n_space, False))  21.5 us
    all_to_all x1, starting transfers between devices, local(): grid = lax.all_to_all(spread, BOTH, 0, 0, tiled=True)  12.7 us
    unnamed x70, local copies, waits for them, and re-layouts  10.6 us
    ppermute x4, starting transfers between devices, around(): after = lax.ppermute(block, 'slab', down)  9.06 us
    ppermute x4, waiting for transfers between devices, around(): outer = lax.ppermute(straight, BOTH, swap_pairs(n_slab, n_space, True))  8.9 us
    ppermute x4, waiting for transfers between devices, around(): before = lax.ppermute(block, 'slab', up)  4.06 us
  transfers between devices with their start and end apart: 17, of which 11 were waited for; matrix products, arithmetic and copies ran while one was open for 0% of the time, Pallas kernels for 8%

profile of v1, /device:TPU:1, one launch (start us, length us, event | category | flops | bytes accessed | tf_op | source)
XLA Modules:
  0.0 144.8 jit_solution(4942671165519077332)
XLA Ops:
  0.6 0.8 reshape.135
  1.4 0.7 pad_add_fusion.meta
  2.2 0.7 copy-done.2
  2.8 0.7 copy-done.4
  3.5 0.7 copy-done.6
  4.2 0.7 copy-done.8
  4.9 0.7 copy-done.11
  5.6 0.7 shard_map.202
  6.3 2.1 %collective-permute-start = (f32[2,8,128]{2,1,0:T(8,128)S(1)}, f32[2,8,128]{2,1,0:T(8,128)S(1)}, u32[]{:S(2)}, u32[]{:S(2)}) collective-permute-start(f32[2,8,128]{2,1,0:T(8,128)S(1)} %get-tuple-element.20), channel_id=1, source_target_pairs={{0,64},{64,128},{128,192},{192,0},{1,65},{65,129},{129,193},{193,1... | collective-permute-start | bytes 24584 | tf_op jit(solution)/shard_map/ppermute | solution.py:500
  8.4 1.4 collective-permute-start.1
  9.8 0.9 collective-permute-done
  10.8 0.2 collective-permute-done.1
  10.9 3.6 %collective-permute-start.2 = (f32[3,2,8,128]{3,2,1,0:T(8,128)S(1)}, f32[3,2,8,128]{3,2,1,0:T(8,128)S(1)}, u32[]{:S(2)}, u32[]{:S(2)}) collective-permute-start(f32[3,2,8,128]{3,2,1,0:T(8,128)S(1)} %pad_maximum_fusion.straight), channel_id=1, source_target_pairs={{0,1},{1,0},{2,3},{3,2},{4,5},{5,4},{6,7},{7,6},{8,9},{9,8},{10,11... | collective-permute-start | bytes 73736 | tf_op jit(solution)/shard_map/ppermute | solution.py:503
  14.5 0.1 collective-permute-start.3
  14.6 0.8 collective-permute-done.2.inner
  15.4 2.4 %collective-permute-done.3.outer = f32[3,2,8,128]{3,2,1,0:T(8,128)S(1)} collective-permute-done((f32[3,2,8,128]{3,2,1,0:T(8,128)S(1)}, f32[3,2,8,128]{3,2,1,0:T(8,128)S(1)}, u32[]{:S(2)}, u32[]{:S(2)}) %collective-permute-start.3) | collective-permute-done | bytes 24608 | tf_op jit(solution)/shard_map/ppermute | solution.py:504
  17.8 2.9 %shard_map.203 = (f32[22,8,128]{2,1,0:T(8,128)S(1)}, f32[2,16,128,128]{3,2,1,0:T(8,128)S(1)}, f32[2,8,128]{2,1,0:T(8,128)S(1)}) custom-call(s32[39]{0:T(128)S(1)} %pad_add_fusion.meta, f32[4,8,128]{2,1,0:T(8,128)S(1)} %get-tuple-element.19.own, f32[3,2,8,128]{3,2,1,0:T(8,128)S(1)} %pad_maximum_fusion.straight, ...), custom_call_target="tpu_custom_call" | custom-call | flops 1000000000 | bytes 1048576 | tf_op jit(solution)/shard_map/pallas_call | solution.py:103
  20.6 0.1 collective-permute-start.4
  20.7 3.6 %collective-permute-start.5 = (f32[2,8,128]{2,1,0:T(8,128)S(1)}, f32[2,8,128]{2,1,0:T(8,128)S(1)}, u32[]{:S(2)}, u32[]{:S(2)}) collective-permute-start(f32[2,8,128]{2,1,0:T(8,128)S(1)} %get-tuple-element.22.own_first), channel_id=1, source_target_pairs={{64,0},{128,64},{192,128},{0,192},{65,1},{129,65},{193,129},{1,193... | collective-permute-start | bytes 24584 | tf_op jit(solution)/shard_map/ppermute | solution.py:501
  24.3 0.9 collective-permute-done.4
  25.3 0.0 collective-permute-done.5
  25.3 8.7 %collective-permute-start.6 = (f32[3,2,8,128]{3,2,1,0:T(8,128)S(1)}, f32[3,2,8,128]{3,2,1,0:T(8,128)S(1)}, u32[]{:S(2)}, u32[]{:S(2)}) collective-permute-start(f32[3,2,8,128]{3,2,1,0:T(8,128)S(1)} %pad_maximum_fusion.1.straight), channel_id=1, source_target_pairs={{0,1},{1,0},{2,3},{3,2},{4,5},{5,4},{6,7},{7,6},{8,9},{9,8},{10,11... | collective-permute-start | bytes 73736 | tf_op jit(solution)/shard_map/ppermute | solution.py:503
  34.0 0.0 collective-permute-start.7
  34.0 3.9 %shard_map.204 = (f32[22,8,128]{2,1,0:T(8,128)}, f32[2,16,128,128]{3,2,1,0:T(8,128)S(1)}, f32[2,8,128]{2,1,0:T(8,128)S(1)}) custom-call(s32[39]{0:T(128)S(1)} %pad_add_fusion.meta, f32[4,8,128]{2,1,0:T(8,128)S(1)} %get-tuple-element.19.own, f32[3,2,8,128]{3,2,1,0:T(8,128)S(1)} %pad_maximum_fusion.straight, ...), custom_call_target="tpu_custom_call" | custom-call | flops 1000000000 | bytes 1048576 | tf_op jit(solution)/shard_map/pallas_call | solution.py:103
  38.0 0.0 copy-start.21
  38.0 0.0 collective-permute-done.7.outer
  38.0 2.0 %shard_map.205.own_first = f32[2,8,128]{2,1,0:T(8,128)S(1)} custom-call(s32[39]{0:T(128)S(1)} %pad_add_fusion.meta, f32[22,8,128]{2,1,0:T(8,128)S(1)} %get-tuple-element.21.geometry, f32[2,8,128]{2,1,0:T(8,128)S(1)} %get-tuple-element.22.own_first, f32[2,8,128]{2,1,0:T(8,128)S(1)} %get-tuple-element.23.own_rest, ...), custom_call_target="tpu_custom_call" | custom-call | flops 100000000 | bytes 1048576 | tf_op jit(solution)/shard_map/pallas_call | solution.py:103
  40.0 0.1 collective-permute-start.8
  40.1 2.8 %collective-permute-start.9 = (f32[2,8,128]{2,1,0:T(8,128)S(1)}, f32[2,8,128]{2,1,0:T(8,128)S(1)}, u32[]{:S(2)}, u32[]{:S(2)}) collective-permute-start(f32[2,8,128]{2,1,0:T(8,128)S(1)} %shard_map.205.own_first), channel_id=1, source_target_pairs={{64,0},{128,64},{192,128},{0,192},{65,1},{129,65},{193,129},{1,193... | collective-permute-start | bytes 24584 | tf_op jit(solution)/shard_map/ppermute | solution.py:501
  42.8 0.9 collective-permute-done.8
  43.8 6.2 %collective-permute-start.10 = (f32[3,2,8,128]{3,2,1,0:T(8,128)S(1)}, f32[3,2,8,128]{3,2,1,0:T(8,128)S(1)}, u32[]{:S(2)}, u32[]{:S(2)}) collective-permute-start(f32[3,2,8,128]{3,2,1,0:T(8,128)S(1)} %pad_maximum_fusion.2.straight), channel_id=1, source_target_pairs={{0,1},{1,0},{2,3},{3,2},{4,5},{5,4},{6,7},{7,6},{8,9},{9,8},{10,11... | collective-permute-start | bytes 73736 | tf_op jit(solution)/shard_map/ppermute | solution.py:503
  50.0 0.0 collective-permute-start.11
  50.1 1.3 shard_map.208
  51.4 2.3 %shard_map.206.own_rest = f32[2,8,128]{2,1,0:T(8,128)S(1)} custom-call(s32[39]{0:T(128)S(1)} %pad_add_fusion.meta, f32[22,8,128]{2,1,0:T(8,128)S(1)} %get-tuple-element.21.geometry, f32[2,8,128]{2,1,0:T(8,128)S(1)} %get-tuple-element.22.own_first, f32[2,8,128]{2,1,0:T(8,128)S(1)} %get-tuple-element.23.own_rest, ...), custom_call_target="tpu_custom_call" | custom-call | flops 100000000 | bytes 1048576 | tf_op jit(solution)/shard_map/pallas_call | solution.py:103
  53.7 0.0 copy-start.3
  53.7 3.6 %shard_map.207.direction = f32[4,8,128]{2,1,0:T(8,128)S(1)} custom-call(s32[39]{0:T(128)S(1)} %pad_add_fusion.meta, f32[22,8,128]{2,1,0:T(8,128)S(1)} %get-tuple-element.21.geometry, f32[2,8,128]{2,1,0:T(8,128)S(1)} %shard_map.205.own_first, f32[2,8,128]{2,1,0:T(8,128)S(1)} %shard_map.206.own_rest, f32[3,2,8,128]{3,2,1,0:T(8,128)S(1)} %pad_maximum_fusion.2.straight, ...), custom_call_target="tpu_custom_call" | custom-call | flops 100000000 | bytes 1048576 | tf_op jit(solution)/shard_map/pallas_call | solution.py:103
  57.4 2.5 %shard_map.209 = (f32[8,512]{1,0:T(8,128)S(1)}, f32[256,640]{1,0:T(8,128)S(1)}) custom-call(s32[39]{0:T(128)S(1)} %pad_add_fusion.meta, f32[4,8,128]{2,1,0:T(8,128)S(1)} %shard_map.207.direction, s32[1,512]{1,0:T(1,128)S(1)} %copy-done.3, f32[2,72,512]{2,1,0:T(8,128)S(1)} %get-tuple-element.26.tab_x, f32[2,8,512]{2,1,0:T(8,128)S(1)} %get-tuple-element.27.tab_y, ...), custom_call_target="tpu_custom_call" | custom-call | flops 1000000000 | bytes 1048576 | tf_op jit(solution)/shard_map/pallas_call | solution.py:103
  59.9 0.6 copy-done.32
  60.5 1.5 %copy.22 = f32[256,1,640]{2,1,0:T(1,128)} copy(f32[256,1,640]{2,0,1:T(8,128)S(1)} %bitcast.28) | data formatting | bytes 1310720 | tf_op jit(solution)/shard_map/all_to_all | solution.py:590
  62.0 12.7 %all-to-all-start = ((f32[256,1,640]{2,1,0:T(1,128)}), f32[256,1,640]{2,1,0:T(1,128)}, u32[]{:S(2)}, u32[]{:S(2)}) async-start(f32[256,1,640]{2,1,0:T(1,128)} %copy.22), calls=%async_computation | async-start | bytes 1310720 | tf_op jit(solution)/shard_map/all_to_all | solution.py:590
  74.8 0.1 fusion.12
  74.8 1.5 %collective-permute-start.12 = (f32[2,8,128]{2,1,0:T(8,128)S(1)}, f32[2,8,128]{2,1,0:T(8,128)S(1)}, u32[]{:S(2)}, u32[]{:S(2)}) collective-permute-start(f32[2,8,128]{2,1,0:T(8,128)S(1)} %get-tuple-element.36), channel_id=1, source_target_pairs={{0,64},{64,128},{128,192},{192,0},{1,65},{65,129},{129,193},{193,1... | collective-permute-start | bytes 24584 | tf_op jit(solution)/shard_map/ppermute | solution.py:500
  76.3 1.3 collective-permute-start.13
  77.9 1.2 collective-permute-done.12
  79.1 0.1 collective-permute-done.13
  79.2 2.9 %collective-permute-start.14 = (f32[3,2,8,128]{3,2,1,0:T(8,128)S(1)}, f32[3,2,8,128]{3,2,1,0:T(8,128)S(1)}, u32[]{:S(2)}, u32[]{:S(2)}) collective-permute-start(f32[3,2,8,128]{3,2,1,0:T(8,128)S(1)} %pad_maximum_fusion.3.straight), channel_id=1, source_target_pairs={{0,1},{1,0},{2,3},{3,2},{4,5},{5,4},{6,7},{7,6},{8,9},{9,8},{10,11... | collective-permute-start | bytes 73736 | tf_op jit(solution)/shard_map/ppermute | solution.py:503
  82.2 0.2 fusion.3.factor
  82.4 0.7 collective-permute-done.14.inner
  83.0 6.5 %collective-permute-done.15.outer = f32[3,2,8,128]{3,2,1,0:T(8,128)S(1)} collective-permute-done((f32[3,2,8,128]{3,2,1,0:T(8,128)S(1)}, f32[3,2,8,128]{3,2,1,0:T(8,128)S(1)}, u32[]{:S(2)}, u32[]{:S(2)}) %collective-permute-start.15) | collective-permute-done | bytes 24608 | tf_op jit(solution)/shard_map/ppermute | solution.py:504
  89.5 1.6 %copy-done.1 = f32[2,16,128,128]{3,2,1,0:T(8,128)S(1)} copy-done((f32[2,16,128,128]{3,2,1,0:T(8,128)S(1)}, f32[2,16,128,128]{3,2,1,0:T(8,128)}, u32[]{:S(2)}) %copy-start.1) | copy-done | bytes 2097176
  91.1 4.0 %shard_map.210 = (f32[8,512]{1,0:T(8,128)S(1)}, f32[8,128]{1,0:T(8,128)S(1)}) custom-call(s32[39]{0:T(128)S(1)} %pad_add_fusion.meta, f32[22,8,128]{2,1,0:T(8,128)S(1)} %get-tuple-element.21.geometry, f32[4,8,128]{2,1,0:T(8,128)S(1)} %shard_map.207.direction, f32[3,2,8,128]{3,2,1,0:T(8,128)S(1)} %pad_maximum_fusion.3.straight, ...), custom_call_target="tpu_custom_call" | custom-call | flops 1000000000 | bytes 1048576 | tf_op jit(solution)/shard_map/pallas_call | solution.py:103
  95.1 3.4 %all-to-all-done = f32[256,1,640]{2,1,0:T(1,128)} async-done(((f32[256,1,640]{2,1,0:T(1,128)}), f32[256,1,640]{2,1,0:T(1,128)}, u32[]{:S(2)}, u32[]{:S(2)}) %all-to-all-start) | async-done | bytes 655392 | tf_op jit(solution)/shard_map/all_to_all | solution.py:590
  98.5 1.1 copy.29
  99.7 0.0 copy-start.16
  99.7 0.9 copy-done.16
  100.6 0.9 copy-done.17
  101.6 0.9 copy-done.18
  102.5 0.9 copy-done.19
  103.4 2.6 %shard_map.211 = f32[256,640]{1,0:T(8,128)S(1)} custom-call(f32[256,640]{1,0:T(8,128)S(1)} %bitcast.26, f32[256,256]{1,0:T(8,128)S(1)} %fusion.3.factor, f32[8,128]{1,0:T(8,128)S(1)} %get-tuple-element.32.sums, bf16[288,256]{1,0:T(8,128)(2,1)S(1)} %copy-done.18, bf16[288,256]{1,0:T(8,128)(2,1)S(1)} %copy-done.19, bf16[512,256]{1,0:T(8,128)(2,1)S(1)} %copy-done.12, ...), custom_call_target="tpu_custom_call" | custom-call | flops 1000000000 | bytes 1048576 | tf_op jit(solution)/shard_map/pallas_call | solution.py:103
  106.0 0.0 copy-start.9
  106.0 0.0 copy-start.10
  106.1 0.7 copy.23
  106.8 36.0 %all_to_all.22 = f32[256,1,640]{2,1,0:T(1,128)S(1)} all-to-all(f32[256,1,640]{2,1,0:T(1,128)S(1)} %copy.23), channel_id=1, replica_groups=mesh['slab'=4,'space'=64] {'slab','space'}, dimensions={0} | all-to-all | bytes 1310720 | tf_op jit(solution)/shard_map/all_to_all | solution.py:615
  142.9 1.9 %shard_map.212 = (f32[3,512]{1,0:T(4,128)}, f32[3,512]{1,0:T(4,128)}, f32[3,512]{1,0:T(4,128)}) custom-call(f32[256,640]{1,0:T(8,128)S(1)} %bitcast.25, bf16[256,512]{1,0:T(8,128)(2,1)S(1)} %copy-done.27, bf16[256,512]{1,0:T(8,128)(2,1)S(1)} %copy-done.29, f32[256,512]{1,0:T(8,128)S(1)} %copy-done.23, f32[2,72,512]{2,1,0:T(8,128)S(1)} %copy-done.25, ...), custom_call_target="tpu_custom_call" | custom-call | flops 1000000000 | bytes 1048576 | tf_op jit(solution)/shard_map/pallas_call | solution.py:103
  (64 shorter events, 0.2 us)
Async XLA Ops:
  2.2 0.7 copy-start.2
  2.8 0.7 copy-start.4
  3.5 0.7 copy-start.6
  4.2 0.7 copy-start.8
  4.9 0.7 copy-start.11
  6.3 4.4 %collective-permute-start = (f32[2,8,128]{2,1,0:T(8,128)S(1)}, f32[2,8,128]{2,1,0:T(8,128)S(1)}, u32[]{:S(2)}, u32[]{:S(2)}) collective-permute-start(f32[2,8,128]{2,1,0:T(8,128)S(1)} %get-tuple-element.20), channel_id=1, source_target_pairs={{0,64},{64,128},{128,192},{192,0},{1,65},{65,129},{129,193},{193,1... | collective-permute-start | bytes 24584 | tf_op jit(solution)/shard_map/ppermute | solution.py:500
  8.4 2.5 %collective-permute-start.1 = (f32[2,8,128]{2,1,0:T(8,128)S(1)}, f32[2,8,128]{2,1,0:T(8,128)S(1)}, u32[]{:S(2)}, u32[]{:S(2)}) collective-permute-start(f32[2,8,128]{2,1,0:T(8,128)S(1)} %get-tuple-element.20), channel_id=1, source_target_pairs={{64,0},{128,64},{192,128},{0,192},{65,1},{129,65},{193,129},{1,193... | collective-permute-start | bytes 24584 | tf_op jit(solution)/shard_map/ppermute | solution.py:501
  10.9 4.4 %collective-permute-start.2 = (f32[3,2,8,128]{3,2,1,0:T(8,128)S(1)}, f32[3,2,8,128]{3,2,1,0:T(8,128)S(1)}, u32[]{:S(2)}, u32[]{:S(2)}) collective-permute-start(f32[3,2,8,128]{3,2,1,0:T(8,128)S(1)} %pad_maximum_fusion.straight), channel_id=1, source_target_pairs={{0,1},{1,0},{2,3},{3,2},{4,5},{5,4},{6,7},{7,6},{8,9},{9,8},{10,11... | collective-permute-start | bytes 73736 | tf_op jit(solution)/shard_map/ppermute | solution.py:503
  14.5 3.3 %collective-permute-start.3 = (f32[3,2,8,128]{3,2,1,0:T(8,128)S(1)}, f32[3,2,8,128]{3,2,1,0:T(8,128)S(1)}, u32[]{:S(2)}, u32[]{:S(2)}) collective-permute-start(f32[3,2,8,128]{3,2,1,0:T(8,128)S(1)} %pad_maximum_fusion.straight), channel_id=1, source_target_pairs={{0,63},{1,2},{2,1},{3,4},{4,3},{5,6},{6,5},{7,8},{8,7},{9,10},{10,... | collective-permute-start | bytes 73736 | tf_op jit(solution)/shard_map/ppermute | solution.py:504
  20.6 4.7 %collective-permute-start.4 = (f32[2,8,128]{2,1,0:T(8,128)S(1)}, f32[2,8,128]{2,1,0:T(8,128)S(1)}, u32[]{:S(2)}, u32[]{:S(2)}) collective-permute-start(f32[2,8,128]{2,1,0:T(8,128)S(1)} %get-tuple-element.22.own_first), channel_id=1, source_target_pairs={{0,64},{64,128},{128,192},{192,0},{1,65},{65,129},{129,193},{193,1... | collective-permute-start | bytes 24584 | tf_op jit(solution)/shard_map/ppermute | solution.py:500
  20.7 4.6 %collective-permute-start.5 = (f32[2,8,128]{2,1,0:T(8,128)S(1)}, f32[2,8,128]{2,1,0:T(8,128)S(1)}, u32[]{:S(2)}, u32[]{:S(2)}) collective-permute-start(f32[2,8,128]{2,1,0:T(8,128)S(1)} %get-tuple-element.22.own_first), channel_id=1, source_target_pairs={{64,0},{128,64},{192,128},{0,192},{65,1},{129,65},{193,129},{1,193... | collective-permute-start | bytes 24584 | tf_op jit(solution)/shard_map/ppermute | solution.py:501
  25.3 12.7 %collective-permute-start.6 = (f32[3,2,8,128]{3,2,1,0:T(8,128)S(1)}, f32[3,2,8,128]{3,2,1,0:T(8,128)S(1)}, u32[]{:S(2)}, u32[]{:S(2)}) collective-permute-start(f32[3,2,8,128]{3,2,1,0:T(8,128)S(1)} %pad_maximum_fusion.1.straight), channel_id=1, source_target_pairs={{0,1},{1,0},{2,3},{3,2},{4,5},{5,4},{6,7},{7,6},{8,9},{9,8},{10,11... | collective-permute-start | bytes 73736 | tf_op jit(solution)/shard_map/ppermute | solution.py:503
  34.0 4.0 %collective-permute-start.7 = (f32[3,2,8,128]{3,2,1,0:T(8,128)S(1)}, f32[3,2,8,128]{3,2,1,0:T(8,128)S(1)}, u32[]{:S(2)}, u32[]{:S(2)}) collective-permute-start(f32[3,2,8,128]{3,2,1,0:T(8,128)S(1)} %pad_maximum_fusion.1.straight), channel_id=1, source_target_pairs={{0,63},{1,2},{2,1},{3,4},{4,3},{5,6},{6,5},{7,8},{8,7},{9,10},{10,... | collective-permute-start | bytes 73736 | tf_op jit(solution)/shard_map/ppermute | solution.py:504
  38.0 15.8 %copy-start = (f32[2,16,128,128]{3,2,1,0:T(8,128)}, f32[2,16,128,128]{3,2,1,0:T(8,128)S(1)}, u32[]{:S(2)}) copy-start(f32[2,16,128,128]{3,2,1,0:T(8,128)S(1)} %get-tuple-element.25.rest_0_.rest_1_.pairs_b) | copy-start | bytes 6291460
  38.0 12.1 %copy-start.5 = (s32[3,512]{1,0:T(4,128)S(1)}, s32[3,512]{1,0:T(4,128)}, u32[]{:S(2)}) copy-start(s32[3,512]{1,0:T(4,128)} %cells.3) | copy-start | bytes 18436
  38.0 12.1 %copy-start.7 = (f32[3,512]{1,0:T(4,128)S(1)}, f32[3,512]{1,0:T(4,128)}, u32[]{:S(2)}) copy-start(f32[3,512]{1,0:T(4,128)} %fraction.3) | copy-start | bytes 18436
  38.0 12.1 %copy-start.20 = (bf16[256,256]{1,0:T(8,128)(2,1)S(1)}, bf16[256,256]{1,0:T(8,128)(2,1)}, u32[]{:S(2)}) copy-start(bf16[256,256]{1,0:T(8,128)(2,1)} %constant.103.clone.cas_high) | copy-start | bytes 393220
  38.0 12.1 %copy-start.21 = (bf16[256,256]{1,0:T(8,128)(2,1)S(1)}, bf16[256,256]{1,0:T(8,128)(2,1)}, u32[]{:S(2)}) copy-start(bf16[256,256]{1,0:T(8,128)(2,1)} %constant.104.clone.cas_low) | copy-start | bytes 393220
  40.0 3.8 %collective-permute-start.8 = (f32[2,8,128]{2,1,0:T(8,128)S(1)}, f32[2,8,128]{2,1,0:T(8,128)S(1)}, u32[]{:S(2)}, u32[]{:S(2)}) collective-permute-start(f32[2,8,128]{2,1,0:T(8,128)S(1)} %shard_map.205.own_first), channel_id=1, source_target_pairs={{0,64},{64,128},{128,192},{192,0},{1,65},{65,129},{129,193},{193,1... | collective-permute-start | bytes 24584 | tf_op jit(solution)/shard_map/ppermute | solution.py:500
  40.1 3.7 %collective-permute-start.9 = (f32[2,8,128]{2,1,0:T(8,128)S(1)}, f32[2,8,128]{2,1,0:T(8,128)S(1)}, u32[]{:S(2)}, u32[]{:S(2)}) collective-permute-start(f32[2,8,128]{2,1,0:T(8,128)S(1)} %shard_map.205.own_first), channel_id=1, source_target_pairs={{64,0},{128,64},{192,128},{0,192},{65,1},{129,65},{193,129},{1,193... | collective-permute-start | bytes 24584 | tf_op jit(solution)/shard_map/ppermute | solution.py:501
  43.8 9.9 %collective-permute-start.10 = (f32[3,2,8,128]{3,2,1,0:T(8,128)S(1)}, f32[3,2,8,128]{3,2,1,0:T(8,128)S(1)}, u32[]{:S(2)}, u32[]{:S(2)}) collective-permute-start(f32[3,2,8,128]{3,2,1,0:T(8,128)S(1)} %pad_maximum_fusion.2.straight), channel_id=1, source_target_pairs={{0,1},{1,0},{2,3},{3,2},{4,5},{5,4},{6,7},{7,6},{8,9},{9,8},{10,11... | collective-permute-start | bytes 73736 | tf_op jit(solution)/shard_map/ppermute | solution.py:503
  50.0 3.7 %collective-permute-start.11 = (f32[3,2,8,128]{3,2,1,0:T(8,128)S(1)}, f32[3,2,8,128]{3,2,1,0:T(8,128)S(1)}, u32[]{:S(2)}, u32[]{:S(2)}) collective-permute-start(f32[3,2,8,128]{3,2,1,0:T(8,128)S(1)} %pad_maximum_fusion.2.straight), channel_id=1, source_target_pairs={{0,63},{1,2},{2,1},{3,4},{4,3},{5,6},{6,5},{7,8},{8,7},{9,10},{10,... | collective-permute-start | bytes 73736 | tf_op jit(solution)/shard_map/ppermute | solution.py:504
  51.3 6.0 %copy-start.22 = (f32[256,512]{1,0:T(8,128)}, f32[256,512]{1,0:T(8,128)S(1)}, u32[]{:S(2)}) copy-start(f32[256,512]{1,0:T(8,128)S(1)} %get-tuple-element.30.slope_z) | copy-start | bytes 1572868
  51.4 6.0 %copy-start.24 = (f32[2,72,512]{2,1,0:T(8,128)}, f32[2,72,512]{2,1,0:T(8,128)S(1)}, u32[]{:S(2)}) copy-start(f32[2,72,512]{2,1,0:T(8,128)S(1)} %get-tuple-element.26.tab_x) | copy-start | bytes 884740
  51.4 6.0 %copy-start.26 = (bf16[256,512]{1,0:T(8,128)(2,1)}, bf16[256,512]{1,0:T(8,128)(2,1)S(1)}, u32[]{:S(2)}) copy-start(bf16[256,512]{1,0:T(8,128)(2,1)S(1)} %get-tuple-element.28.w_high) | copy-start | bytes 786436
  51.4 6.0 %copy-start.28 = (bf16[256,512]{1,0:T(8,128)(2,1)}, bf16[256,512]{1,0:T(8,128)(2,1)S(1)}, u32[]{:S(2)}) copy-start(bf16[256,512]{1,0:T(8,128)(2,1)S(1)} %get-tuple-element.29.w_low) | copy-start | bytes 786436
  51.4 6.0 %copy-start.30 = (f32[2,8,512]{2,1,0:T(8,128)}, f32[2,8,512]{2,1,0:T(8,128)S(1)}, u32[]{:S(2)}) copy-start(f32[2,8,512]{2,1,0:T(8,128)S(1)} %get-tuple-element.27.tab_y) | copy-start | bytes 98308
  53.7 3.7 %copy-start.3 = (s32[1,512]{1,0:T(1,128)S(1)}, s32[1,512]{1,0:T(1,128)}, u32[]{:S(2)}) copy-start(s32[1,512]{1,0:T(1,128)} %order.5) | copy-start | bytes 6148
  59.9 0.6 copy-start.32
  62.0 36.5 %all-to-all-start = ((f32[256,1,640]{2,1,0:T(1,128)}), f32[256,1,640]{2,1,0:T(1,128)}, u32[]{:S(2)}, u32[]{:S(2)}) async-start(f32[256,1,640]{2,1,0:T(1,128)} %copy.22), calls=%async_computation | async-start | bytes 1310720 | tf_op jit(solution)/shard_map/all_to_all | solution.py:590
  74.8 4.3 %collective-permute-start.12 = (f32[2,8,128]{2,1,0:T(8,128)S(1)}, f32[2,8,128]{2,1,0:T(8,128)S(1)}, u32[]{:S(2)}, u32[]{:S(2)}) collective-permute-start(f32[2,8,128]{2,1,0:T(8,128)S(1)} %get-tuple-element.36), channel_id=1, source_target_pairs={{0,64},{64,128},{128,192},{192,0},{1,65},{65,129},{129,193},{193,1... | collective-permute-start | bytes 24584 | tf_op jit(solution)/shard_map/ppermute | solution.py:500
  76.3 2.9 %collective-permute-start.13 = (f32[2,8,128]{2,1,0:T(8,128)S(1)}, f32[2,8,128]{2,1,0:T(8,128)S(1)}, u32[]{:S(2)}, u32[]{:S(2)}) collective-permute-start(f32[2,8,128]{2,1,0:T(8,128)S(1)} %get-tuple-element.36), channel_id=1, source_target_pairs={{64,0},{128,64},{192,128},{0,192},{65,1},{129,65},{193,129},{1,193... | collective-permute-start | bytes 24584 | tf_op jit(solution)/shard_map/ppermute | solution.py:501
  79.2 3.8 %collective-permute-start.14 = (f32[3,2,8,128]{3,2,1,0:T(8,128)S(1)}, f32[3,2,8,128]{3,2,1,0:T(8,128)S(1)}, u32[]{:S(2)}, u32[]{:S(2)}) collective-permute-start(f32[3,2,8,128]{3,2,1,0:T(8,128)S(1)} %pad_maximum_fusion.3.straight), channel_id=1, source_target_pairs={{0,1},{1,0},{2,3},{3,2},{4,5},{5,4},{6,7},{7,6},{8,9},{9,8},{10,11... | collective-permute-start | bytes 73736 | tf_op jit(solution)/shard_map/ppermute | solution.py:503
  82.2 7.3 %collective-permute-start.15 = (f32[3,2,8,128]{3,2,1,0:T(8,128)S(1)}, f32[3,2,8,128]{3,2,1,0:T(8,128)S(1)}, u32[]{:S(2)}, u32[]{:S(2)}) collective-permute-start(f32[3,2,8,128]{3,2,1,0:T(8,128)S(1)} %pad_maximum_fusion.3.straight), channel_id=1, source_target_pairs={{0,63},{1,2},{2,1},{3,4},{4,3},{5,6},{6,5},{7,8},{8,7},{9,10},{10,... | collective-permute-start | bytes 73736 | tf_op jit(solution)/shard_map/ppermute | solution.py:504
  82.2 17.4 %copy-start.12 = (bf16[512,256]{1,0:T(8,128)(2,1)S(1)}, bf16[512,256]{1,0:T(8,128)(2,1)}, u32[]{:S(2)}) copy-start(bf16[512,256]{1,0:T(8,128)(2,1)} %constant.107.clone.y_high) | copy-start | bytes 786436
  89.5 1.6 %copy-start.1 = (f32[2,16,128,128]{3,2,1,0:T(8,128)S(1)}, f32[2,16,128,128]{3,2,1,0:T(8,128)}, u32[]{:S(2)}) copy-start(f32[2,16,128,128]{3,2,1,0:T(8,128)} %copy-done) | copy-start | bytes 6291460
  91.1 8.5 %copy-start.13 = (bf16[512,256]{1,0:T(8,128)(2,1)S(1)}, bf16[512,256]{1,0:T(8,128)(2,1)}, u32[]{:S(2)}) copy-start(bf16[512,256]{1,0:T(8,128)(2,1)} %constant.108.clone.y_low) | copy-start | bytes 786436
  91.1 8.5 %copy-start.14 = (bf16[256,512]{1,0:T(8,128)(2,1)S(1)}, bf16[256,512]{1,0:T(8,128)(2,1)}, u32[]{:S(2)}) copy-start(bf16[256,512]{1,0:T(8,128)(2,1)} %constant.109.clone.yt_high) | copy-start | bytes 786436
  91.1 8.5 %copy-start.15 = (bf16[256,512]{1,0:T(8,128)(2,1)S(1)}, bf16[256,512]{1,0:T(8,128)(2,1)}, u32[]{:S(2)}) copy-start(bf16[256,512]{1,0:T(8,128)(2,1)} %constant.110.clone.yt_low) | copy-start | bytes 786436
  99.7 1.0 copy-start.16
  100.6 0.9 copy-start.17
  101.6 0.9 copy-start.18
  102.5 0.9 copy-start.19
  106.0 36.8 %copy-start.9 = (f32[3,512]{1,0:T(4,128)S(1)}, f32[3,512]{1,0:T(4,128)}, u32[]{:S(2)}) copy-start(f32[3,512]{1,0:T(4,128)} %residual.3) | copy-start | bytes 18436
  106.0 36.8 %copy-start.10 = (f32[3,512]{1,0:T(4,128)S(1)}, f32[3,512]{1,0:T(4,128)}, u32[]{:S(2)}) copy-start(f32[3,512]{1,0:T(4,128)} %dipoles.1) | copy-start | bytes 18436
  106.0 36.8 %copy-start.23 = (f32[256,512]{1,0:T(8,128)S(1)}, f32[256,512]{1,0:T(8,128)}, u32[]{:S(2)}) copy-start(f32[256,512]{1,0:T(8,128)} %copy-done.22) | copy-start | bytes 1572868
  106.0 36.8 %copy-start.25 = (f32[2,72,512]{2,1,0:T(8,128)S(1)}, f32[2,72,512]{2,1,0:T(8,128)}, u32[]{:S(2)}) copy-start(f32[2,72,512]{2,1,0:T(8,128)} %copy-done.24) | copy-start | bytes 884740
  106.0 36.8 %copy-start.27 = (bf16[256,512]{1,0:T(8,128)(2,1)S(1)}, bf16[256,512]{1,0:T(8,128)(2,1)}, u32[]{:S(2)}) copy-start(bf16[256,512]{1,0:T(8,128)(2,1)} %copy-done.26) | copy-start | bytes 786436
  106.1 36.8 %copy-start.29 = (bf16[256,512]{1,0:T(8,128)(2,1)S(1)}, bf16[256,512]{1,0:T(8,128)(2,1)}, u32[]{:S(2)}) copy-start(bf16[256,512]{1,0:T(8,128)(2,1)} %copy-done.28) | copy-start | bytes 786436
  106.1 36.8 %copy-start.31 = (f32[2,8,512]{2,1,0:T(8,128)S(1)}, f32[2,8,512]{2,1,0:T(8,128)}, u32[]{:S(2)}) copy-start(f32[2,8,512]{2,1,0:T(8,128)} %copy-done.30) | copy-start | bytes 98308
  106.1 36.8 %copy-start.33 = (f32[8,512]{1,0:T(8,128)S(1)}, f32[8,512]{1,0:T(8,128)}, u32[]{:S(2)}) copy-start(f32[8,512]{1,0:T(8,128)} %copy-done.32) | copy-start | bytes 49156

commit v2 on v1

--- a/solution.py
+++ b/solution.py
@@ -35,7 +35,7 @@
 NT = (((1,), (1,)), ((), ()))
 NN = (((1,), (0,)), ((), ()))
 TN = (((0,), (0,)), ((), ()))
-VMEM_LIMIT = 48 * 1024 * 1024
+VMEM_LIMIT = 20 * 1024 * 1024
 
 
 def halves(values):
@@ -69,31 +69,25 @@
 
 
 COUNTS_AT = 32
-SEND_AT = 36
-PARITY_AT = 38
-
-
-def tile_at(meta, place):
-    first, second = (meta[SEND_AT], meta[SEND_AT + 1])
-    if place == 0:
-        return first
-    if place == 1:
-        return second
+ORDER_AT = 36
+PARITY_AT = 40
+
+
+def meta_of(tile_lists, tile_counts, send_tiles, parity):
+    entry = tile_lists.reshape(-1)
+    remote = entry - 4
+    pair = remote // 2
+    pair = pair + (pair >= 4)
+    along = pair // 3
+    across = pair % 3
+    base = jnp.where(across == 1, 4, jnp.where(across == 2 - 2 * parity, 10, 16))
+    slots = jnp.where(entry < 4, entry, base + along * 2 + remote % 2)
+    first, second = (send_tiles[0, 0], send_tiles[0, 1])
     third = jnp.where(
         (first != 0) & (second != 0), 0, jnp.where((first != 1) & (second != 1), 1, 2)
     )
-    return third if place == 2 else 6 - first - second - third
-
-
-def pool_slot(meta, entry):
-    remote = entry - 4
-    pair = remote // 2
-    pair = pair + jnp.where(pair >= 4, 1, 0)
-    along = jnp.where(pair >= 3, 1, 0) + jnp.where(pair >= 6, 1, 0)
-    across = pair - 3 * along
-    inner_side = jnp.where(meta[PARITY_AT] == 0, 2, 0)
-    base = jnp.where(across == 1, 4, jnp.where(across == inner_side, 10, 16))
-    return jnp.where(entry < 4, entry, base + along * 2 + remote % 2)
+    rest = jnp.stack([first, second, third, 6 - first - second - third, parity])
+    return jnp.concatenate([slots, tile_counts.reshape(-1), rest]).astype(jnp.int32)
 
 
 def call(kernel, outs, flops, smem=0, scratch=()):
@@ -115,17 +109,27 @@
     return run
 
 
-def gather_kernel(meta, residual, cells, fraction, alphas, order, own, sent):
+def gather_kernel(send, *refs):
+    sources, own, sent, held, sems = (refs[:5], refs[5], refs[6], refs[7:12], refs[12])
+    copies = [
+        pltpu.make_async_copy(source, target, sems.at[at])
+        for at, (source, target) in enumerate(zip(sources, held))
+    ]
+    for copy in copies:
+        copy.start()
+    for copy in copies:
+        copy.wait()
+    residual, cells, fraction, alphas, order = held
     atoms = residual.shape[1]
     position = cells[...].astype(F32) + fraction[...]
     rows = jnp.concatenate(
-        [position, alphas[...], residual[...], jnp.zeros((1, atoms), F32)], 0
+        [position, alphas[...].reshape(1, atoms), residual[...], jnp.zeros((1, atoms), F32)], 0
     )
     picked = selected(rows, order_matrix(order[...], atoms), NN)
     for tile in range(atoms // TILE):
         own[tile] = picked[:, tile * TILE : (tile + 1) * TILE]
     for place in range(2):
-        sent[place] = own[meta[SEND_AT + place]]
+        sent[place] = own[send[0, place]]
 
 
 def search_rows(block):
@@ -148,9 +152,9 @@
                 pool[base + 2 * along + member] = source[along, member] + shift
 
 
-def own_columns(columns, block):
+def own_columns(columns, block, count):
     turned = block.T
-    for row in range(columns.shape[0]):
+    for row in range(count):
         columns[row] = jnp.broadcast_to(turned[:, row : row + 1], (TILE, TILE))
 
 
@@ -159,60 +163,76 @@
     return jnp.where(depth > half, depth - G, jnp.where(depth < -half, depth + G, depth))
 
 
-PAIR_ROWS = 64
-
-
-def pair_kernel(places, extents, meta, own, straight, inner, outer, pool, pairs, found, columns, totals):
+PAIR_ROWS = 32
+GROUP = 4
+
+
+def pair_kernel(first_place, extents, meta, own, straight, inner, outer, pool, pairs, found, columns, totals):
     fill_pool(pool, extents, own, straight, inner, outer, meta)
-    for at, place in enumerate(places):
-        tile = tile_at(meta, place)
+
+    def tile_step(at, carry):
+        tile = meta[ORDER_AT + first_place + at]
         block = own[tile]
-        own_columns(columns, jnp.concatenate([block[:3], lax.rsqrt(block[3:4]), block[4:]], 0))
+        own_columns(columns, jnp.concatenate([block[:3], lax.rsqrt(block[3:4]), block[4:]], 0), 4)
         live = meta[COUNTS_AT + tile]
-        for chunk in range(TILE // PAIR_ROWS):
-            rows = slice(chunk * PAIR_ROWS, (chunk + 1) * PAIR_ROWS)
+
+        def chunk_step(chunk, carry):
+            start = pl.multiple_of(chunk * PAIR_ROWS, PAIR_ROWS)
+            rows = pl.ds(start, PAIR_ROWS)
             shape = (PAIR_ROWS, TILE)
-            same = lax.broadcasted_iota(jnp.int32, shape, 0) + chunk * PAIR_ROWS
-            diagonal = jnp.where(same == lax.broadcasted_iota(jnp.int32, shape, 1), 1.0, 0.0)
-
-            def step(entry, sums):
-                listed = meta[tile * 8 + entry]
-                other = pool[pool_slot(meta, listed)]
-                itself = diagonal * jnp.where(listed == tile, 1.0, 0.0)
-                d_x = other[0:1] - columns[0, rows]
-                d_y = other[1:2] - columns[1, rows]
-                d_z = wrap_depth(other[2:3] - columns[2, rows])
-                square = d_x * d_x + d_y * d_y + d_z * d_z + itself
-                inverse = lax.rsqrt(square)
-                distance = square * inverse
-                inverse_sq = inverse * inverse
-                gauss = jnp.exp(-(BETA**2) * square)
-                t = 1.0 / (1.0 + (SCALED_ERFC_T * BETA) * distance)
-                series = jnp.full(shape, SCALED_ERFC[-1], F32)
-                for term in SCALED_ERFC[-2::-1]:
-                    series = series * t + term
-                bare_one = gauss * (series * t * inverse + 2.0 * BETA / ROOT_PI) * inverse_sq
-                bare_two = (3.0 * bare_one + (4.0 * BETA**3 / ROOT_PI) * gauss) * inverse_sq
-                damping = (square * distance) * (THOLE * columns[3, rows] * lax.rsqrt(other[3:4]))
-                decay = jnp.exp(-damping) * inverse * inverse_sq
-                keep = 1.0 - itself
-                three = keep * (bare_one - decay)
-                five = keep * (bare_two - 3.0 * (1.0 + damping) * decay * inverse_sq)
-                pairs[0, at * 8 + entry, rows] = five
-                pairs[1, at * 8 + entry, rows] = three
-                v = search_rows(other)
-                along = five * (d_x * v[0:1] + d_y * v[1:2] + d_z * v[2:3])
-                return (
-                    sums[0] + (along * d_x - three * v[0:1]),
-                    sums[1] + (along * d_y - three * v[1:2]),
-                    sums[2] + (along * d_z - three * v[2:3]),
-                )
+            ahead = lax.broadcasted_iota(jnp.int32, shape, 0) - lax.broadcasted_iota(
+                jnp.int32, shape, 1
+            )
+            diagonal = jnp.where(ahead == -start, 1.0, 0.0)
+
+            def group_step(group, sums):
+                for member in range(GROUP):
+                    entry = group * GROUP + member
+                    slot = meta[tile * 8 + entry]
+                    other = pool[slot]
+                    itself = diagonal * jnp.where(slot == tile, 1.0, 0.0)
+                    d_x = other[0:1] - columns[0, rows]
+                    d_y = other[1:2] - columns[1, rows]
+                    d_z = wrap_depth(other[2:3] - columns[2, rows])
+                    square = d_x * d_x + d_y * d_y + d_z * d_z + itself
+                    inverse = lax.rsqrt(square)
+                    distance = square * inverse
+                    inverse_sq = inverse * inverse
+                    gauss = jnp.exp(-(BETA**2) * square)
+                    stretch = 1.0 + (SCALED_ERFC_T * BETA) * distance
+                    t = lax.rsqrt(stretch * stretch)
+                    series = SCALED_ERFC[-1] * t + SCALED_ERFC[-2]
+                    for term in SCALED_ERFC[-3::-1]:
+                        series = series * t + term
+                    bare_one = gauss * (series * t * inverse + 2.0 * BETA / ROOT_PI) * inverse_sq
+                    bare_two = (3.0 * bare_one + (4.0 * BETA**3 / ROOT_PI) * gauss) * inverse_sq
+                    damping = (square * distance) * columns[3, rows] * (THOLE * lax.rsqrt(other[3:4]))
+                    decay = jnp.exp(-damping) * inverse * inverse_sq
+                    keep = jnp.where(entry < live, 1.0, 0.0) * (1.0 - itself)
+                    three = keep * (bare_one - decay)
+                    five = keep * (bare_two - (3.0 + 3.0 * damping) * decay * inverse_sq)
+                    pairs[0, at * 8 + entry, rows] = five
+                    pairs[1, at * 8 + entry, rows] = three
+                    v = search_rows(other)
+                    along = five * (d_x * v[0:1] + d_y * v[1:2] + d_z * v[2:3])
+                    sums = (
+                        sums[0] + (along * d_x - three * v[0:1]),
+                        sums[1] + (along * d_y - three * v[1:2]),
+                        sums[2] + (along * d_z - three * v[2:3]),
+                    )
+                return sums
 
             zero = jnp.zeros(shape, F32)
-            sums = lax.fori_loop(0, live, step, (zero, zero, zero))
+            sums = lax.fori_loop(0, (live + GROUP - 1) // GROUP, group_step, (zero, zero, zero))
             for part in range(3):
                 totals[part, rows] = sums[part]
+            return carry
+
+        lax.fori_loop(0, TILE // PAIR_ROWS, chunk_step, 0)
         found[at] = updated(block, totals)
+        return carry
+
+    lax.fori_loop(0, 2, tile_step, 0)
 
 
 def field_rows(totals):
@@ -226,12 +246,12 @@
     return jnp.concatenate(rows + [jnp.zeros((5, TILE), F32)], 0)
 
 
-APPLY_ROWS = 32
+APPLY_ROWS = 64
 
 
 def fill_search(pool, own_first, own_rest, straight, inner, outer, meta):
     for place in range(4):
-        pool[tile_at(meta, place)] = own_first[place] if place < 2 else own_rest[place - 2]
+        pool[meta[ORDER_AT + place]] = own_first[place] if place < 2 else own_rest[place - 2]
     for base, source in ((4, straight), (10, inner), (16, outer)):
         for along in range(3):
             for member in range(2):
@@ -240,42 +260,53 @@
 
 def apply_tile(meta, tile, at, pairs, geometry, pool, columns, totals):
     block = geometry[tile]
-    own_columns(columns, block)
+    own_columns(columns, block, 3)
     live = meta[COUNTS_AT + tile]
-    for chunk in range(TILE // APPLY_ROWS):
-        rows = slice(chunk * APPLY_ROWS, (chunk + 1) * APPLY_ROWS)
-        x_i, y_i, z_i = (columns[0, rows], columns[1, rows], columns[2, rows])
-
-        def step(entry, sums):
-            slot = pool_slot(meta, meta[tile * 8 + entry])
-            other = geometry[slot]
-            v = pool[slot]
-            d_x = other[0:1] - x_i
-            d_y = other[1:2] - y_i
-            d_z = wrap_depth(other[2:3] - z_i)
-            three = pairs[1, at * 8 + entry, rows]
-            along = pairs[0, at * 8 + entry, rows] * (d_x * v[0:1] + d_y * v[1:2] + d_z * v[2:3])
-            return (
-                sums[0] + (along * d_x - three * v[0:1]),
-                sums[1] + (along * d_y - three * v[1:2]),
-                sums[2] + (along * d_z - three * v[2:3]),
-            )
+
+    def chunk_step(chunk, carry):
+        rows = pl.ds(pl.multiple_of(chunk * APPLY_ROWS, APPLY_ROWS), APPLY_ROWS)
+
+        def group_step(group, sums):
+            for member in range(GROUP):
+                entry = group * GROUP + member
+                slot = meta[tile * 8 + entry]
+                other = geometry[slot]
+                v = pool[slot]
+                d_x = other[0:1] - columns[0, rows]
+                d_y = other[1:2] - columns[1, rows]
+                d_z = wrap_depth(other[2:3] - columns[2, rows])
+                three = pairs[1, at * 8 + entry, rows]
+                along = pairs[0, at * 8 + entry, rows] * (d_x * v[0:1] + d_y * v[1:2] + d_z * v[2:3])
+                sums = (
+                    sums[0] + (along * d_x - three * v[0:1]),
+                    sums[1] + (along * d_y - three * v[1:2]),
+                    sums[2] + (along * d_z - three * v[2:3]),
+                )
+            return sums
 
         zero = jnp.zeros((APPLY_ROWS, TILE), F32)
-        sums = lax.fori_loop(0, live, step, (zero, zero, zero))
+        sums = lax.fori_loop(0, (live + GROUP - 1) // GROUP, group_step, (zero, zero, zero))
         for part in range(3):
             totals[part, rows] = sums[part]
-
-
-def sweep_kernel(places, meta, geometry, own_first, own_rest, straight, inner, outer, *rest):
-    banks = len(places) // 2
+        return carry
+
+    lax.fori_loop(0, TILE // APPLY_ROWS, chunk_step, 0)
+
+
+def sweep_kernel(first_place, meta, geometry, own_first, own_rest, straight, inner, outer, *rest):
+    banks = len(rest) - 4
     pairs, found = (rest[:banks], rest[banks])
     pool, columns, totals = rest[banks + 1 :]
     fill_search(pool, own_first, own_rest, straight, inner, outer, meta)
-    for at, place in enumerate(places):
-        tile = tile_at(meta, place)
-        apply_tile(meta, tile, at % 2, pairs[at // 2], geometry, pool, columns, totals)
-        found[at] = updated(geometry[tile], totals)
+    for bank in range(banks):
+
+        def tile_step(at, carry):
+            tile = meta[ORDER_AT + first_place + 2 * bank + at]
+            apply_tile(meta, tile, at, pairs[bank], geometry, pool, columns, totals)
+            found[2 * bank + at] = updated(geometry[tile], totals)
+            return carry
+
+        lax.fori_loop(0, 2, tile_step, 0)
 
 
 def final_field_kernel(
@@ -283,27 +314,33 @@
 ):
     atoms = order.shape[1]
     fill_search(pool, direction, direction.at[2:4], straight, inner, outer, meta)
-    curve = jnp.zeros((1, TILE), F32)
-    dots = jnp.zeros((1, TILE), F32)
-    for place in range(4):
-        tile = tile_at(meta, place)
-        apply_tile(meta, tile, place % 2, (pairs_a, pairs_b)[place // 2], geometry, pool, columns, totals)
-        block = geometry[tile]
-        ahead = direction[place]
-        field = field_rows(totals)
-        rows = []
-        for part in range(3):
-            d = ahead[part : part + 1]
-            value = d / block[3:4] - field[part] - SELF_FIELD * d
-            curve = curve + d * value
-            dots = dots + d * block[4 + part : 5 + part]
-            rows.append(value)
-        local[tile] = jnp.concatenate(rows + [jnp.zeros((5, TILE), F32)], 0)
+    both = (jnp.zeros((1, TILE), F32), jnp.zeros((1, TILE), F32))
+    for bank, pairs in enumerate((pairs_a, pairs_b)):
+
+        def tile_step(at, both):
+            curve, dots = both
+            place = 2 * bank + at
+            tile = meta[ORDER_AT + place]
+            apply_tile(meta, tile, at, pairs, geometry, pool, columns, totals)
+            block = geometry[tile]
+            ahead = direction[place]
+            field = field_rows(totals)
+            rows = []
+            for part in range(3):
+                d = ahead[part : part + 1]
+                value = d / block[3:4] - field[part] - SELF_FIELD * d
+                curve = curve + d * value
+                dots = dots + d * block[4 + part : 5 + part]
+                rows.append(value)
+            local[tile] = jnp.concatenate(rows + [jnp.zeros((5, TILE), F32)], 0)
+            return (curve, dots)
+
+        both = lax.fori_loop(0, 2, tile_step, both)
     in_tiles = jnp.concatenate([local[tile] for tile in range(4)], 1)
     applied[...] = selected(in_tiles, order_matrix(order[...], atoms), NT)
     lane = lax.broadcasted_iota(jnp.int32, (8, TILE), 1)
-    curve_sum = jnp.sum(curve, axis=1, keepdims=True)
-    dot_sum = jnp.sum(dots, axis=1, keepdims=True)
+    curve_sum = jnp.sum(both[0], axis=1, keepdims=True)
+    dot_sum = jnp.sum(both[1], axis=1, keepdims=True)
     sums[...] = jnp.where(lane == 1, curve_sum, jnp.where(lane == 2, dot_sum, 0.0))
 
 
@@ -374,7 +411,7 @@
     atoms = order.shape[1]
     y_rows = tab_y.shape[1]
     for place in range(4):
-        local[tile_at(meta, place)] = direction[place]
+        local[meta[ORDER_AT + place]] = direction[place]
     in_tiles = jnp.concatenate([local[tile] for tile in range(4)], 1)
     d = selected(in_tiles, order_matrix(order[...], atoms), NT)
     ordered[...] = d
@@ -393,24 +430,23 @@
     out[:, width:] = jnp.zeros((G, out.shape[1] - width), F32)
 
 
-def plane_kernel(
-    shapes, grid, factor, sums, x_high, x_low, y_high, y_low, yt_high, yt_low, xt_high, xt_low, out, along_x
-):
+def plane_kernel(shapes, grid, factor, sums, x_high, x_low, y_high, y_low, out, along_x):
     n_slab, n_space, x_rows, y_rows = shapes
     width = x_rows * y_rows
     for y in range(y_rows):
         total = None
         for s in range(n_slab):
             block = halves(grid[s * n_space : (s + 1) * n_space, y * x_rows : (y + 1) * x_rows])
-            rows = slice(s * x_rows, (s + 1) * x_rows)
+            rows = slice(s * TILE, s * TILE + x_rows)
             term = product(block, (x_high[rows], x_low[rows]), NN)
             total = term if total is None else total + term
         along_x[y * n_space : (y + 1) * n_space] = total
-    spectrum = product((yt_high[...], yt_low[...]), halves(along_x[...]), NN)
+    cas_y = (y_high[...], y_low[...])
+    spectrum = product(cas_y, halves(along_x[...]), TN)
     scaled = spectrum * factor[...]
     energy = jnp.sum(jnp.sum(spectrum * scaled, axis=0, keepdims=True), axis=1, keepdims=True)
-    back = halves(product((y_high[...], y_low[...]), halves(scaled), NN))
-    planes = product(back, (xt_high[...], xt_low[...]), NN)
+    back = halves(product(cas_y, halves(scaled), NN))
+    planes = product(back, (x_high[...], x_low[...]), NT)
     for s in range(n_slab):
         for y in range(y_rows):
             out[s * n_space : (s + 1) * n_space, y * x_rows : (y + 1) * x_rows] = planes[
@@ -516,59 +552,65 @@
     width = x_rows * y_rows
     lanes = -(-(width + 3) // TILE) * TILE
     slab_index, space_index = (lax.axis_index("slab"), lax.axis_index("space"))
-    meta = jnp.concatenate(
-        [
-            tile_lists.reshape(-1),
-            tile_counts.reshape(-1),
-            send_tiles.reshape(-1),
-            (space_index % 2).reshape(1).astype(jnp.int32),
-        ]
-    )
     tile_shape = ((4, 8, TILE), F32)
     two_shape = ((2, 8, TILE), F32)
     bank_shape = ((2, 16, TILE, TILE), F32)
     pool_scratch = pltpu.VMEM((22, 8, TILE), F32)
     total_scratch = pltpu.VMEM((3, TILE, TILE), F32)
-    own, sent = call(gather_kernel, [tile_shape, two_shape], 10**8, smem=1)(
-        meta, residual, cells, fraction, polarizability.reshape(1, atoms), tile_order
-    )
+    own, sent = pl.pallas_call(
+        gather_kernel,
+        out_shape=[jax.ShapeDtypeStruct(*tile_shape), jax.ShapeDtypeStruct(*two_shape)],
+        in_specs=[pl.BlockSpec(memory_space=pltpu.SMEM)] + [pl.BlockSpec(memory_space=pltpu.HBM)] * 5,
+        out_specs=[pl.BlockSpec(memory_space=pltpu.VMEM)] * 2,
+        scratch_shapes=[
+            pltpu.VMEM((3, atoms), F32),
+            pltpu.VMEM((3, atoms), jnp.int32),
+            pltpu.VMEM((3, atoms), F32),
+            pltpu.VMEM((atoms,), F32),
+            pltpu.VMEM((1, atoms), jnp.int32),
+            pltpu.SemaphoreType.DMA((5,)),
+        ],
+        compiler_params=pltpu.CompilerParams(vmem_limit_bytes=VMEM_LIMIT),
+    )(send_tiles, residual, cells, fraction, polarizability, tile_order)
+    later = lax.optimization_barrier((tile_lists, tile_counts, send_tiles, sent))
+    meta = meta_of(*later[:3], space_index % 2)
     first = around(sent)
 
-    def pairs_of(places):
+    def pairs_of(first_place):
         return call(
-            functools.partial(pair_kernel, places, extents),
+            functools.partial(pair_kernel, first_place, extents),
             [((22, 8, TILE), F32), bank_shape, two_shape],
             10**9,
             smem=1,
-            scratch=(pltpu.VMEM((8, TILE, TILE), F32), total_scratch),
+            scratch=(pltpu.VMEM((4, TILE, TILE), F32), total_scratch),
         )(meta, own, *first)
 
-    geometry, pairs_a, search_a = pairs_of((0, 1))
-    _, pairs_b, search_b = pairs_of((2, 3))
+    geometry, pairs_a, search_a = pairs_of(0)
+    _, pairs_b, search_b = pairs_of(2)
     sweep_scratch = (pool_scratch, pltpu.VMEM((3, TILE, TILE), F32), total_scratch)
     second = around(search_a)
 
-    def sweep(places, mine, others, received, banks):
+    def sweep(first_place, mine, others, received, banks):
         return call(
-            functools.partial(sweep_kernel, places),
-            [((len(places), 8, TILE), F32)],
+            functools.partial(sweep_kernel, first_place),
+            [((2 * len(banks), 8, TILE), F32)],
             10**8,
             smem=1,
             scratch=sweep_scratch,
         )(meta, geometry, mine, others, *received, *banks)[0]
 
-    next_a = sweep((0, 1), search_a, search_b, second, (pairs_a,))
-    next_b = sweep((2, 3), search_a, search_b, second, (pairs_b,))
+    next_a = sweep(0, search_a, search_b, second, (pairs_a,))
+    next_b = sweep(2, search_a, search_b, second, (pairs_b,))
     third = around(next_a)
-    direction = sweep((0, 1, 2, 3), next_a, next_b, third, (pairs_a, pairs_b))
+    direction = sweep(0, next_a, next_b, third, (pairs_a, pairs_b))
     freq = np.arange(G)
     padded_x = np.stack([(s * extents[0] + np.arange(x_rows) - 2) % G for s in range(n_slab)])
     real_x = np.tile(np.arange(x_rows) < extents[0] + 4, n_slab)
     cas_x = cas_matrix(padded_x.reshape(-1), freq) * real_x[:, None]
     rows_y = (np.arange(n_space)[None] * extents[1] + np.arange(y_rows)[:, None] - 2) % G
     cas_y = cas_matrix(rows_y.reshape(-1), freq)
-    wide_x = np.zeros((G, n_slab, TILE))
-    wide_x[:, :, :x_rows] = cas_x.reshape(n_slab, x_rows, G).transpose(2, 0, 1)
+    wide_x = np.zeros((n_slab, TILE, G))
+    wide_x[:, :x_rows] = cas_x.reshape(n_slab, x_rows, G)
     tab_x, tab_y, w_high, w_low, slope_z = call(
         tables_kernel,
         [
@@ -607,10 +649,8 @@
         grid,
         factor,
         sums,
-        *split_constant(cas_x),
+        *split_constant(wide_x.reshape(-1, G)),
         *split_constant(cas_y),
-        *split_constant(cas_y.T),
-        *split_constant(wide_x.reshape(G, -1)),
     )[0]
     returned = lax.all_to_all(planes, BOTH, 0, 0, tiled=True)
     three = ((3, atoms), F32)

time: 146 us -> 141 us (0.966)
  between operations: 1.34 us -> 5.22 us
  starting transfers between devices: 47.1 us -> 44 us
  blocking collectives: 36 us -> 33.6 us
    unnamed x70 -> x64, local copies, waits for them, and re-layouts: 10.6 us -> 7.56 us
    all_to_all x1, starting transfers between devices: 12.7 us -> 10.1 us  [local(): grid = lax.all_to_all(spread, BOTH, 0, 0, tiled=True)]
    all_to_all x1, blocking collectives: 36 us -> 33.6 us  [local(): returned = lax.all_to_all(planes, BOTH, 0, 0, tiled=True)]
    ppermute x4, waiting for transfers between devices: 8.9 us -> 6.5 us  [around(): outer = lax.ppermute(straight, BOTH, swap_pairs(n_slab, n_space, True))]
    concatenate x0 -> x1, local copies, waits for them, and re-layouts: none -> 2.02 us  [meta_of(): jnp.concatenate([slots, tile_counts.reshape(-1), rest]).astype(jnp.int32)]
    pallas_call x11 -> x10, Pallas kernels: 27.7 us -> 26 us  [run(): pl.pallas_call(kernel, out_shape=[jax.ShapeDtypeStruct(shape, dtype) for...]
  transfers between devices with their start and end apart: 17 -> 17, of which waited for: 11 -> 10; matrix products, arithmetic and copies ran while one was open for 0% -> 3% of each run, Pallas kernels for 8% -> 7%
where the time goes in v2:
time: 141 us
  starting transfers between devices  44 us (31%)
  blocking collectives  33.6 us (24%)
  Pallas kernels  26.8 us (19%)
  waiting for transfers between devices  17.3 us (12%)
  local copies, waits for them, and re-layouts  13.8 us (10%)
  between operations  5.22 us (4%)
    all_to_all x1, blocking collectives, local(): returned = lax.all_to_all(planes, BOTH, 0, 0, tiled=True)  33.6 us
    pallas_call x10, Pallas kernels, run(): pl.pallas_call(kernel, out_shape=[jax.ShapeDtypeStruct(shape, dtype) for...  26 us
    ppermute x4, starting transfers between devices, around(): inner = lax.ppermute(straight, BOTH, swap_pairs(n_slab, n_space, False))  20.9 us
    all_to_all x1, starting transfers between devices, local(): grid = lax.all_to_all(spread, BOTH, 0, 0, tiled=True)  10.1 us
    ppermute x4, starting transfers between devices, around(): after = lax.ppermute(block, 'slab', down)  8.32 us
    unnamed x64, local copies, waits for them, and re-layouts  7.56 us
    ppermute x4, waiting for transfers between devices, around(): outer = lax.ppermute(straight, BOTH, swap_pairs(n_slab, n_space, True))  6.5 us
    ppermute x4, waiting for transfers between devices, around(): before = lax.ppermute(block, 'slab', up)  5.32 us
  transfers between devices with their start and end apart: 17, of which 10 were waited for; matrix products, arithmetic and copies ran while one was open for 3% of the time, Pallas kernels for 7%

profile of v2, /device:TPU:1, one launch (start us, length us, event | category | flops | bytes accessed | tf_op | source)
XLA Modules:
  0.0 141.1 jit_solution(18186565415957630227)
XLA Ops:
  0.6 0.0 copy-start.2
  0.6 0.7 copy-done.2
  1.3 0.7 copy-done.4
  2.0 0.7 copy-done.6
  2.7 0.7 copy-done.8
  3.4 0.7 copy-done.10
  4.1 0.7 copy-done.11
  4.7 0.8 shard_map.166
  5.6 2.1 %collective-permute-start = (f32[2,8,128]{2,1,0:T(8,128)S(1)}, f32[2,8,128]{2,1,0:T(8,128)S(1)}, u32[]{:S(2)}, u32[]{:S(2)}) collective-permute-start(f32[2,8,128]{2,1,0:T(8,128)S(1)} %get-tuple-element.22), channel_id=1, source_target_pairs={{0,64},{64,128},{128,192},{192,0},{1,65},{65,129},{129,193},{193,1... | collective-permute-start | bytes 24584 | tf_op jit(solution)/shard_map/ppermute | solution.py:536
  7.7 1.4 collective-permute-start.1
  9.1 0.8 reshape.142
  9.9 0.2 collective-permute-done
  10.0 0.2 collective-permute-done.1
  10.2 3.6 %collective-permute-start.2 = (f32[3,2,8,128]{3,2,1,0:T(8,128)S(1)}, f32[3,2,8,128]{3,2,1,0:T(8,128)S(1)}, u32[]{:S(2)}, u32[]{:S(2)}) collective-permute-start(f32[3,2,8,128]{3,2,1,0:T(8,128)S(1)} %pad_maximum_fusion.straight), channel_id=1, source_target_pairs={{0,1},{1,0},{2,3},{3,2},{4,5},{5,4},{6,7},{7,6},{8,9},{9,8},{10,11... | collective-permute-start | bytes 73736 | tf_op jit(solution)/shard_map/ppermute | solution.py:539
  13.8 0.1 collective-permute-start.3
  13.8 1.3 fusion.21
  19.0 2.0 %concatenate.3.meta = s32[41]{0:T(128)S(1)} concatenate(s32[32]{0:T(128)S(1)} %compare_select_fusion.1, s32[4]{0:T(128)} %bitcast.42, s32[1]{0:T(128)} %bitcast.1, s32[1]{0:T(128)} %bitcast.2, s32[1]{0:T(128)} %bitcast.3, s32[1]{0:T(128)} %bitcast.4, s32[1]{0:T(128)} %bitcast.5), dimensions={0} | concatenate | bytes 328 | tf_op jit(solution)/shard_map/concatenate | solution.py:90
  21.1 0.0 collective-permute-done.2.inner
  21.1 0.0 collective-permute-done.3.outer
  21.1 3.3 %shard_map.167 = (f32[22,8,128]{2,1,0:T(8,128)S(1)}, f32[2,16,128,128]{3,2,1,0:T(8,128)S(1)}, f32[2,8,128]{2,1,0:T(8,128)S(1)}) custom-call(s32[41]{0:T(128)S(1)} %concatenate.3.meta, f32[4,8,128]{2,1,0:T(8,128)S(1)} %get-tuple-element.26.own, f32[3,2,8,128]{3,2,1,0:T(8,128)S(1)} %pad_maximum_fusion.straight, ...), custom_call_target="tpu_custom_call" | custom-call | flops 1000000000 | bytes 1048576 | tf_op jit(solution)/shard_map/pallas_call | solution.py:97
  24.3 3.0 %collective-permute-start.5 = (f32[2,8,128]{2,1,0:T(8,128)S(1)}, f32[2,8,128]{2,1,0:T(8,128)S(1)}, u32[]{:S(2)}, u32[]{:S(2)}) collective-permute-start(f32[2,8,128]{2,1,0:T(8,128)S(1)} %get-tuple-element.28.own_first), channel_id=1, source_target_pairs={{64,0},{128,64},{192,128},{0,192},{65,1},{129,65},{193,129},{1,193... | collective-permute-start | bytes 24584 | tf_op jit(solution)/shard_map/ppermute | solution.py:537
  27.3 0.0 collective-permute-start.4
  27.3 0.8 collective-permute-done.5
  28.1 2.9 %collective-permute-done.4 = f32[2,8,128]{2,1,0:T(8,128)S(1)} collective-permute-done((f32[2,8,128]{2,1,0:T(8,128)S(1)}, f32[2,8,128]{2,1,0:T(8,128)S(1)}, u32[]{:S(2)}, u32[]{:S(2)}) %collective-permute-start.4) | collective-permute-done | bytes 8224 | tf_op jit(solution)/shard_map/ppermute | solution.py:536
  31.0 9.9 %collective-permute-start.6 = (f32[3,2,8,128]{3,2,1,0:T(8,128)S(1)}, f32[3,2,8,128]{3,2,1,0:T(8,128)S(1)}, u32[]{:S(2)}, u32[]{:S(2)}) collective-permute-start(f32[3,2,8,128]{3,2,1,0:T(8,128)S(1)} %pad_maximum_fusion.1.straight), channel_id=1, source_target_pairs={{0,1},{1,0},{2,3},{3,2},{4,5},{5,4},{6,7},{7,6},{8,9},{9,8},{10,11... | collective-permute-start | bytes 73736 | tf_op jit(solution)/shard_map/ppermute | solution.py:539
  40.9 0.0 collective-permute-start.7
  40.9 3.8 %shard_map.168 = (f32[22,8,128]{2,1,0:T(8,128)}, f32[2,16,128,128]{3,2,1,0:T(8,128)S(1)}, f32[2,8,128]{2,1,0:T(8,128)S(1)}) custom-call(s32[41]{0:T(128)S(1)} %concatenate.3.meta, f32[4,8,128]{2,1,0:T(8,128)S(1)} %get-tuple-element.26.own, f32[3,2,8,128]{3,2,1,0:T(8,128)S(1)} %pad_maximum_fusion.straight, f32[3,2,8,128]{3,2,1,0:T(8,128)S(1)} %collective-permute-done.2.inner, ...), custom_call_target="tpu_custom_call" | custom-call | flops 1000000000 | bytes 1048576 | tf_op jit(solution)/shard_map/pallas_call | solution.py:97
  44.7 0.0 copy-start.18
  44.7 1.9 %shard_map.169.own_first = f32[2,8,128]{2,1,0:T(8,128)S(1)} custom-call(s32[41]{0:T(128)S(1)} %concatenate.3.meta, f32[22,8,128]{2,1,0:T(8,128)S(1)} %get-tuple-element.27.geometry, f32[2,8,128]{2,1,0:T(8,128)S(1)} %get-tuple-element.28.own_first, f32[2,8,128]{2,1,0:T(8,128)S(1)} %get-tuple-element.29.own_rest, ...), custom_call_target="tpu_custom_call" | custom-call | flops 100000000 | bytes 1048576 | tf_op jit(solution)/shard_map/pallas_call | solution.py:97
  46.6 0.1 collective-permute-start.8
  46.7 2.7 %collective-permute-start.9 = (f32[2,8,128]{2,1,0:T(8,128)S(1)}, f32[2,8,128]{2,1,0:T(8,128)S(1)}, u32[]{:S(2)}, u32[]{:S(2)}) collective-permute-start(f32[2,8,128]{2,1,0:T(8,128)S(1)} %shard_map.169.own_first), channel_id=1, source_target_pairs={{64,0},{128,64},{192,128},{0,192},{65,1},{129,65},{193,129},{1,193... | collective-permute-start | bytes 24584 | tf_op jit(solution)/shard_map/ppermute | solution.py:537
  49.4 1.0 collective-permute-done.8
  50.4 0.0 collective-permute-done.9
  50.4 4.5 %collective-permute-start.10 = (f32[3,2,8,128]{3,2,1,0:T(8,128)S(1)}, f32[3,2,8,128]{3,2,1,0:T(8,128)S(1)}, u32[]{:S(2)}, u32[]{:S(2)}) collective-permute-start(f32[3,2,8,128]{3,2,1,0:T(8,128)S(1)} %pad_maximum_fusion.2.straight), channel_id=1, source_target_pairs={{0,1},{1,0},{2,3},{3,2},{4,5},{5,4},{6,7},{7,6},{8,9},{9,8},{10,11... | collective-permute-start | bytes 73736 | tf_op jit(solution)/shard_map/ppermute | solution.py:539
  54.9 1.0 collective-permute-start.11
  56.0 1.3 shard_map.172
  57.3 1.9 %shard_map.170.own_rest = f32[2,8,128]{2,1,0:T(8,128)S(1)} custom-call(s32[41]{0:T(128)S(1)} %concatenate.3.meta, f32[22,8,128]{2,1,0:T(8,128)S(1)} %get-tuple-element.27.geometry, f32[2,8,128]{2,1,0:T(8,128)S(1)} %get-tuple-element.28.own_first, f32[2,8,128]{2,1,0:T(8,128)S(1)} %get-tuple-element.29.own_rest, ...), custom_call_target="tpu_custom_call" | custom-call | flops 100000000 | bytes 1048576 | tf_op jit(solution)/shard_map/pallas_call | solution.py:97
  59.2 0.0 copy-start.3
  59.2 0.0 collective-permute-done.10.inner
  59.3 3.3 %shard_map.171.direction = f32[4,8,128]{2,1,0:T(8,128)S(1)} custom-call(s32[41]{0:T(128)S(1)} %concatenate.3.meta, f32[22,8,128]{2,1,0:T(8,128)S(1)} %get-tuple-element.27.geometry, f32[2,8,128]{2,1,0:T(8,128)S(1)} %shard_map.169.own_first, f32[2,8,128]{2,1,0:T(8,128)S(1)} %shard_map.170.own_rest, f32[3,2,8,128]{3,2,1,0:T(8,128)S(1)} %pad_maximum_fusion.2.straight, ...), custom_call_target="tpu_custom_call" | custom-call | flops 100000000 | bytes 1048576 | tf_op jit(solution)/shard_map/pallas_call | solution.py:97
  62.6 2.5 %shard_map.173 = (f32[8,512]{1,0:T(8,128)S(1)}, f32[256,640]{1,0:T(8,128)S(1)}) custom-call(s32[41]{0:T(128)S(1)} %concatenate.3.meta, f32[4,8,128]{2,1,0:T(8,128)S(1)} %shard_map.171.direction, s32[1,512]{1,0:T(1,128)S(1)} %copy-done.3, f32[2,72,512]{2,1,0:T(8,128)S(1)} %get-tuple-element.32.tab_x, f32[2,8,512]{2,1,0:T(8,128)S(1)} %get-tuple-element.33.tab_y, ...), custom_call_target="tpu_custom_call" | custom-call | flops 1000000000 | bytes 1048576 | tf_op jit(solution)/shard_map/pallas_call | solution.py:97
  65.1 0.6 copy-done.29
  65.7 1.5 %copy.18 = f32[256,1,640]{2,1,0:T(1,128)} copy(f32[256,1,640]{2,0,1:T(8,128)S(1)} %bitcast.30) | data formatting | bytes 1310720 | tf_op jit(solution)/shard_map/all_to_all | solution.py:632
  67.2 10.1 %all-to-all-start = ((f32[256,1,640]{2,1,0:T(1,128)}), f32[256,1,640]{2,1,0:T(1,128)}, u32[]{:S(2)}, u32[]{:S(2)}) async-start(f32[256,1,640]{2,1,0:T(1,128)} %copy.18), calls=%async_computation | async-start | bytes 1310720 | tf_op jit(solution)/shard_map/all_to_all | solution.py:632
  77.3 0.1 fusion.12
  77.4 1.5 %collective-permute-start.12 = (f32[2,8,128]{2,1,0:T(8,128)S(1)}, f32[2,8,128]{2,1,0:T(8,128)S(1)}, u32[]{:S(2)}, u32[]{:S(2)}) collective-permute-start(f32[2,8,128]{2,1,0:T(8,128)S(1)} %get-tuple-element.42), channel_id=1, source_target_pairs={{0,64},{64,128},{128,192},{192,0},{1,65},{65,129},{129,193},{193,1... | collective-permute-start | bytes 24584 | tf_op jit(solution)/shard_map/ppermute | solution.py:536
  78.8 1.3 collective-permute-start.13
  80.4 1.2 collective-permute-done.12
  81.6 0.1 collective-permute-done.13
  81.8 2.9 %collective-permute-start.14 = (f32[3,2,8,128]{3,2,1,0:T(8,128)S(1)}, f32[3,2,8,128]{3,2,1,0:T(8,128)S(1)}, u32[]{:S(2)}, u32[]{:S(2)}) collective-permute-start(f32[3,2,8,128]{3,2,1,0:T(8,128)S(1)} %pad_maximum_fusion.3.straight), channel_id=1, source_target_pairs={{0,1},{1,0},{2,3},{3,2},{4,5},{5,4},{6,7},{7,6},{8,9},{9,8},{10,11... | collective-permute-start | bytes 73736 | tf_op jit(solution)/shard_map/ppermute | solution.py:539
  84.7 0.0 collective-permute-start.15
  84.7 0.2 fusion.3.factor
  84.9 0.7 collective-permute-done.14.inner
  85.6 6.5 %collective-permute-done.15.outer = f32[3,2,8,128]{3,2,1,0:T(8,128)S(1)} collective-permute-done((f32[3,2,8,128]{3,2,1,0:T(8,128)S(1)}, f32[3,2,8,128]{3,2,1,0:T(8,128)S(1)}, u32[]{:S(2)}, u32[]{:S(2)}) %collective-permute-start.15) | collective-permute-done | bytes 24608 | tf_op jit(solution)/shard_map/ppermute | solution.py:540
  92.1 1.6 %copy-done.1 = f32[2,16,128,128]{3,2,1,0:T(8,128)S(1)} copy-done((f32[2,16,128,128]{3,2,1,0:T(8,128)S(1)}, f32[2,16,128,128]{3,2,1,0:T(8,128)}, u32[]{:S(2)}) %copy-start.1) | copy-done | bytes 2097176
  93.7 3.6 %shard_map.174 = (f32[8,512]{1,0:T(8,128)S(1)}, f32[8,128]{1,0:T(8,128)S(1)}) custom-call(s32[41]{0:T(128)S(1)} %concatenate.3.meta, f32[22,8,128]{2,1,0:T(8,128)S(1)} %get-tuple-element.27.geometry, f32[4,8,128]{2,1,0:T(8,128)S(1)} %shard_map.171.direction, f32[3,2,8,128]{3,2,1,0:T(8,128)S(1)} %pad_maximum_fusion.3.straight, ...), custom_call_target="tpu_custom_call" | custom-call | flops 1000000000 | bytes 1048576 | tf_op jit(solution)/shard_map/pallas_call | solution.py:97
  97.3 3.7 %all-to-all-done = f32[256,1,640]{2,1,0:T(1,128)} async-done(((f32[256,1,640]{2,1,0:T(1,128)}), f32[256,1,640]{2,1,0:T(1,128)}, u32[]{:S(2)}, u32[]{:S(2)}) %all-to-all-start) | async-done | bytes 655392 | tf_op jit(solution)/shard_map/all_to_all | solution.py:632
  101.0 1.1 copy.25
  102.2 2.6 %shard_map.175 = f32[256,640]{1,0:T(8,128)S(1)} custom-call(f32[256,640]{1,0:T(8,128)S(1)} %bitcast.28, f32[256,256]{1,0:T(8,128)S(1)} %fusion.3.factor, f32[8,128]{1,0:T(8,128)S(1)} %get-tuple-element.38.sums, bf16[512,256]{1,0:T(8,128)(2,1)S(1)} %copy-done.13, bf16[512,256]{1,0:T(8,128)(2,1)S(1)} %copy-done.14, bf16[512,256]{1,0:T(8,128)(2,1)S(1)} %copy-done.15, ...), custom_call_target="tpu_custom_call" | custom-call | flops 1000000000 | bytes 1048576 | tf_op jit(solution)/shard_map/pallas_call | solution.py:97
  104.8 0.0 copy-start.9
  104.8 0.0 copy-start.12
  104.9 0.7 copy.19
  105.6 33.6 %all_to_all.22 = f32[256,1,640]{2,1,0:T(1,128)S(1)} all-to-all(f32[256,1,640]{2,1,0:T(1,128)S(1)} %copy.19), channel_id=1, replica_groups=mesh['slab'=4,'space'=64] {'slab','space'}, dimensions={0} | all-to-all | bytes 1310720 | tf_op jit(solution)/shard_map/all_to_all | solution.py:655
  139.3 1.9 %shard_map.176 = (f32[3,512]{1,0:T(4,128)}, f32[3,512]{1,0:T(4,128)}, f32[3,512]{1,0:T(4,128)}) custom-call(f32[256,640]{1,0:T(8,128)S(1)} %bitcast.27, bf16[256,512]{1,0:T(8,128)(2,1)S(1)} %copy-done.24, bf16[256,512]{1,0:T(8,128)(2,1)S(1)} %copy-done.26, f32[256,512]{1,0:T(8,128)S(1)} %copy-done.20, f32[2,72,512]{2,1,0:T(8,128)S(1)} %copy-done.22, ...), custom_call_target="tpu_custom_call" | custom-call | flops 1000000000 | bytes 1048576 | tf_op jit(solution)/shard_map/pallas_call | solution.py:97
  (60 shorter events, 0.2 us)
Async XLA Ops:
  0.6 0.7 copy-start.2
  1.3 0.7 copy-start.4
  2.0 0.7 copy-start.6
  2.7 0.7 copy-start.8
  3.4 0.7 copy-start.10
  4.1 0.7 copy-start.11
  5.6 4.4 %collective-permute-start = (f32[2,8,128]{2,1,0:T(8,128)S(1)}, f32[2,8,128]{2,1,0:T(8,128)S(1)}, u32[]{:S(2)}, u32[]{:S(2)}) collective-permute-start(f32[2,8,128]{2,1,0:T(8,128)S(1)} %get-tuple-element.22), channel_id=1, source_target_pairs={{0,64},{64,128},{128,192},{192,0},{1,65},{65,129},{129,193},{193,1... | collective-permute-start | bytes 24584 | tf_op jit(solution)/shard_map/ppermute | solution.py:536
  7.7 2.5 %collective-permute-start.1 = (f32[2,8,128]{2,1,0:T(8,128)S(1)}, f32[2,8,128]{2,1,0:T(8,128)S(1)}, u32[]{:S(2)}, u32[]{:S(2)}) collective-permute-start(f32[2,8,128]{2,1,0:T(8,128)S(1)} %get-tuple-element.22), channel_id=1, source_target_pairs={{64,0},{128,64},{192,128},{0,192},{65,1},{129,65},{193,129},{1,193... | collective-permute-start | bytes 24584 | tf_op jit(solution)/shard_map/ppermute | solution.py:537
  10.2 10.9 %collective-permute-start.2 = (f32[3,2,8,128]{3,2,1,0:T(8,128)S(1)}, f32[3,2,8,128]{3,2,1,0:T(8,128)S(1)}, u32[]{:S(2)}, u32[]{:S(2)}) collective-permute-start(f32[3,2,8,128]{3,2,1,0:T(8,128)S(1)} %pad_maximum_fusion.straight), channel_id=1, source_target_pairs={{0,1},{1,0},{2,3},{3,2},{4,5},{5,4},{6,7},{7,6},{8,9},{9,8},{10,11... | collective-permute-start | bytes 73736 | tf_op jit(solution)/shard_map/ppermute | solution.py:539
  13.8 7.3 %collective-permute-start.3 = (f32[3,2,8,128]{3,2,1,0:T(8,128)S(1)}, f32[3,2,8,128]{3,2,1,0:T(8,128)S(1)}, u32[]{:S(2)}, u32[]{:S(2)}) collective-permute-start(f32[3,2,8,128]{3,2,1,0:T(8,128)S(1)} %pad_maximum_fusion.straight), channel_id=1, source_target_pairs={{0,63},{1,2},{2,1},{3,4},{4,3},{5,6},{6,5},{7,8},{8,7},{9,10},{10,... | collective-permute-start | bytes 73736 | tf_op jit(solution)/shard_map/ppermute | solution.py:540
  24.3 3.8 %collective-permute-start.5 = (f32[2,8,128]{2,1,0:T(8,128)S(1)}, f32[2,8,128]{2,1,0:T(8,128)S(1)}, u32[]{:S(2)}, u32[]{:S(2)}) collective-permute-start(f32[2,8,128]{2,1,0:T(8,128)S(1)} %get-tuple-element.28.own_first), channel_id=1, source_target_pairs={{64,0},{128,64},{192,128},{0,192},{65,1},{129,65},{193,129},{1,193... | collective-permute-start | bytes 24584 | tf_op jit(solution)/shard_map/ppermute | solution.py:537
  27.3 3.7 %collective-permute-start.4 = (f32[2,8,128]{2,1,0:T(8,128)S(1)}, f32[2,8,128]{2,1,0:T(8,128)S(1)}, u32[]{:S(2)}, u32[]{:S(2)}) collective-permute-start(f32[2,8,128]{2,1,0:T(8,128)S(1)} %get-tuple-element.28.own_first), channel_id=1, source_target_pairs={{0,64},{64,128},{128,192},{192,0},{1,65},{65,129},{129,193},{193,1... | collective-permute-start | bytes 24584 | tf_op jit(solution)/shard_map/ppermute | solution.py:536
  31.0 13.7 %collective-permute-start.6 = (f32[3,2,8,128]{3,2,1,0:T(8,128)S(1)}, f32[3,2,8,128]{3,2,1,0:T(8,128)S(1)}, u32[]{:S(2)}, u32[]{:S(2)}) collective-permute-start(f32[3,2,8,128]{3,2,1,0:T(8,128)S(1)} %pad_maximum_fusion.1.straight), channel_id=1, source_target_pairs={{0,1},{1,0},{2,3},{3,2},{4,5},{5,4},{6,7},{7,6},{8,9},{9,8},{10,11... | collective-permute-start | bytes 73736 | tf_op jit(solution)/shard_map/ppermute | solution.py:539
  40.9 3.8 %collective-permute-start.7 = (f32[3,2,8,128]{3,2,1,0:T(8,128)S(1)}, f32[3,2,8,128]{3,2,1,0:T(8,128)S(1)}, u32[]{:S(2)}, u32[]{:S(2)}) collective-permute-start(f32[3,2,8,128]{3,2,1,0:T(8,128)S(1)} %pad_maximum_fusion.1.straight), channel_id=1, source_target_pairs={{0,63},{1,2},{2,1},{3,4},{4,3},{5,6},{6,5},{7,8},{8,7},{9,10},{10,... | collective-permute-start | bytes 73736 | tf_op jit(solution)/shard_map/ppermute | solution.py:540
  44.7 14.6 %copy-start = (f32[2,16,128,128]{3,2,1,0:T(8,128)}, f32[2,16,128,128]{3,2,1,0:T(8,128)S(1)}, u32[]{:S(2)}) copy-start(f32[2,16,128,128]{3,2,1,0:T(8,128)S(1)} %get-tuple-element.31.rest_0_.rest_1_.pairs_b) | copy-start | bytes 6291460
  44.7 11.3 %copy-start.5 = (s32[3,512]{1,0:T(4,128)S(1)}, s32[3,512]{1,0:T(4,128)}, u32[]{:S(2)}) copy-start(s32[3,512]{1,0:T(4,128)} %cells.1) | copy-start | bytes 18436
  44.7 11.3 %copy-start.7 = (f32[3,512]{1,0:T(4,128)S(1)}, f32[3,512]{1,0:T(4,128)}, u32[]{:S(2)}) copy-start(f32[3,512]{1,0:T(4,128)} %fraction.1) | copy-start | bytes 18436
  44.7 11.3 %copy-start.17 = (bf16[256,256]{1,0:T(8,128)(2,1)S(1)}, bf16[256,256]{1,0:T(8,128)(2,1)}, u32[]{:S(2)}) copy-start(bf16[256,256]{1,0:T(8,128)(2,1)} %constant.150.clone.cas_high) | copy-start | bytes 393220
  44.7 11.3 %copy-start.18 = (bf16[256,256]{1,0:T(8,128)(2,1)S(1)}, bf16[256,256]{1,0:T(8,128)(2,1)}, u32[]{:S(2)}) copy-start(bf16[256,256]{1,0:T(8,128)(2,1)} %constant.151.clone.cas_low) | copy-start | bytes 393220
  46.6 3.8 %collective-permute-start.8 = (f32[2,8,128]{2,1,0:T(8,128)S(1)}, f32[2,8,128]{2,1,0:T(8,128)S(1)}, u32[]{:S(2)}, u32[]{:S(2)}) collective-permute-start(f32[2,8,128]{2,1,0:T(8,128)S(1)} %shard_map.169.own_first), channel_id=1, source_target_pairs={{0,64},{64,128},{128,192},{192,0},{1,65},{65,129},{129,193},{193,1... | collective-permute-start | bytes 24584 | tf_op jit(solution)/shard_map/ppermute | solution.py:536
  46.7 3.7 %collective-permute-start.9 = (f32[2,8,128]{2,1,0:T(8,128)S(1)}, f32[2,8,128]{2,1,0:T(8,128)S(1)}, u32[]{:S(2)}, u32[]{:S(2)}) collective-permute-start(f32[2,8,128]{2,1,0:T(8,128)S(1)} %shard_map.169.own_first), channel_id=1, source_target_pairs={{64,0},{128,64},{192,128},{0,192},{65,1},{129,65},{193,129},{1,193... | collective-permute-start | bytes 24584 | tf_op jit(solution)/shard_map/ppermute | solution.py:537
  50.4 8.8 %collective-permute-start.10 = (f32[3,2,8,128]{3,2,1,0:T(8,128)S(1)}, f32[3,2,8,128]{3,2,1,0:T(8,128)S(1)}, u32[]{:S(2)}, u32[]{:S(2)}) collective-permute-start(f32[3,2,8,128]{3,2,1,0:T(8,128)S(1)} %pad_maximum_fusion.2.straight), channel_id=1, source_target_pairs={{0,1},{1,0},{2,3},{3,2},{4,5},{5,4},{6,7},{7,6},{8,9},{9,8},{10,11... | collective-permute-start | bytes 73736 | tf_op jit(solution)/shard_map/ppermute | solution.py:539
  54.9 4.3 %collective-permute-start.11 = (f32[3,2,8,128]{3,2,1,0:T(8,128)S(1)}, f32[3,2,8,128]{3,2,1,0:T(8,128)S(1)}, u32[]{:S(2)}, u32[]{:S(2)}) collective-permute-start(f32[3,2,8,128]{3,2,1,0:T(8,128)S(1)} %pad_maximum_fusion.2.straight), channel_id=1, source_target_pairs={{0,63},{1,2},{2,1},{3,4},{4,3},{5,6},{6,5},{7,8},{8,7},{9,10},{10,... | collective-permute-start | bytes 73736 | tf_op jit(solution)/shard_map/ppermute | solution.py:540
  57.2 5.3 %copy-start.19 = (f32[256,512]{1,0:T(8,128)}, f32[256,512]{1,0:T(8,128)S(1)}, u32[]{:S(2)}) copy-start(f32[256,512]{1,0:T(8,128)S(1)} %get-tuple-element.36.slope_z) | copy-start | bytes 1572868
  57.3 5.3 %copy-start.21 = (f32[2,72,512]{2,1,0:T(8,128)}, f32[2,72,512]{2,1,0:T(8,128)S(1)}, u32[]{:S(2)}) copy-start(f32[2,72,512]{2,1,0:T(8,128)S(1)} %get-tuple-element.32.tab_x) | copy-start | bytes 884740
  57.3 5.3 %copy-start.23 = (bf16[256,512]{1,0:T(8,128)(2,1)}, bf16[256,512]{1,0:T(8,128)(2,1)S(1)}, u32[]{:S(2)}) copy-start(bf16[256,512]{1,0:T(8,128)(2,1)S(1)} %get-tuple-element.34.w_high) | copy-start | bytes 786436
  57.3 5.3 %copy-start.25 = (bf16[256,512]{1,0:T(8,128)(2,1)}, bf16[256,512]{1,0:T(8,128)(2,1)S(1)}, u32[]{:S(2)}) copy-start(bf16[256,512]{1,0:T(8,128)(2,1)S(1)} %get-tuple-element.35.w_low) | copy-start | bytes 786436
  57.3 5.3 %copy-start.27 = (f32[2,8,512]{2,1,0:T(8,128)}, f32[2,8,512]{2,1,0:T(8,128)S(1)}, u32[]{:S(2)}) copy-start(f32[2,8,512]{2,1,0:T(8,128)S(1)} %get-tuple-element.33.tab_y) | copy-start | bytes 98308
  59.2 3.4 %copy-start.3 = (s32[1,512]{1,0:T(1,128)S(1)}, s32[1,512]{1,0:T(1,128)}, u32[]{:S(2)}) copy-start(s32[1,512]{1,0:T(1,128)} %order.3) | copy-start | bytes 6148
  65.1 0.6 copy-start.29
  67.2 33.8 %all-to-all-start = ((f32[256,1,640]{2,1,0:T(1,128)}), f32[256,1,640]{2,1,0:T(1,128)}, u32[]{:S(2)}, u32[]{:S(2)}) async-start(f32[256,1,640]{2,1,0:T(1,128)} %copy.18), calls=%async_computation | async-start | bytes 1310720 | tf_op jit(solution)/shard_map/all_to_all | solution.py:632
  77.4 4.3 %collective-permute-start.12 = (f32[2,8,128]{2,1,0:T(8,128)S(1)}, f32[2,8,128]{2,1,0:T(8,128)S(1)}, u32[]{:S(2)}, u32[]{:S(2)}) collective-permute-start(f32[2,8,128]{2,1,0:T(8,128)S(1)} %get-tuple-element.42), channel_id=1, source_target_pairs={{0,64},{64,128},{128,192},{192,0},{1,65},{65,129},{129,193},{193,1... | collective-permute-start | bytes 24584 | tf_op jit(solution)/shard_map/ppermute | solution.py:536
  78.8 2.9 %collective-permute-start.13 = (f32[2,8,128]{2,1,0:T(8,128)S(1)}, f32[2,8,128]{2,1,0:T(8,128)S(1)}, u32[]{:S(2)}, u32[]{:S(2)}) collective-permute-start(f32[2,8,128]{2,1,0:T(8,128)S(1)} %get-tuple-element.42), channel_id=1, source_target_pairs={{64,0},{128,64},{192,128},{0,192},{65,1},{129,65},{193,129},{1,193... | collective-permute-start | bytes 24584 | tf_op jit(solution)/shard_map/ppermute | solution.py:537
  81.8 3.8 %collective-permute-start.14 = (f32[3,2,8,128]{3,2,1,0:T(8,128)S(1)}, f32[3,2,8,128]{3,2,1,0:T(8,128)S(1)}, u32[]{:S(2)}, u32[]{:S(2)}) collective-permute-start(f32[3,2,8,128]{3,2,1,0:T(8,128)S(1)} %pad_maximum_fusion.3.straight), channel_id=1, source_target_pairs={{0,1},{1,0},{2,3},{3,2},{4,5},{5,4},{6,7},{7,6},{8,9},{9,8},{10,11... | collective-permute-start | bytes 73736 | tf_op jit(solution)/shard_map/ppermute | solution.py:539
  84.7 7.3 %collective-permute-start.15 = (f32[3,2,8,128]{3,2,1,0:T(8,128)S(1)}, f32[3,2,8,128]{3,2,1,0:T(8,128)S(1)}, u32[]{:S(2)}, u32[]{:S(2)}) collective-permute-start(f32[3,2,8,128]{3,2,1,0:T(8,128)S(1)} %pad_maximum_fusion.3.straight), channel_id=1, source_target_pairs={{0,63},{1,2},{2,1},{3,4},{4,3},{5,6},{6,5},{7,8},{8,7},{9,10},{10,... | collective-permute-start | bytes 73736 | tf_op jit(solution)/shard_map/ppermute | solution.py:540
  84.7 17.4 %copy-start.13 = (bf16[512,256]{1,0:T(8,128)(2,1)S(1)}, bf16[512,256]{1,0:T(8,128)(2,1)}, u32[]{:S(2)}) copy-start(bf16[512,256]{1,0:T(8,128)(2,1)} %constant.152.clone.x_high) | copy-start | bytes 786436
  92.1 1.6 %copy-start.1 = (f32[2,16,128,128]{3,2,1,0:T(8,128)S(1)}, f32[2,16,128,128]{3,2,1,0:T(8,128)}, u32[]{:S(2)}) copy-start(f32[2,16,128,128]{3,2,1,0:T(8,128)} %copy-done) | copy-start | bytes 6291460
  93.6 8.5 %copy-start.14 = (bf16[512,256]{1,0:T(8,128)(2,1)S(1)}, bf16[512,256]{1,0:T(8,128)(2,1)}, u32[]{:S(2)}) copy-start(bf16[512,256]{1,0:T(8,128)(2,1)} %constant.153.clone.x_low) | copy-start | bytes 786436
  93.6 8.5 %copy-start.15 = (bf16[512,256]{1,0:T(8,128)(2,1)S(1)}, bf16[512,256]{1,0:T(8,128)(2,1)}, u32[]{:S(2)}) copy-start(bf16[512,256]{1,0:T(8,128)(2,1)} %constant.154.clone.y_high) | copy-start | bytes 786436
  93.7 8.5 %copy-start.16 = (bf16[512,256]{1,0:T(8,128)(2,1)S(1)}, bf16[512,256]{1,0:T(8,128)(2,1)}, u32[]{:S(2)}) copy-start(bf16[512,256]{1,0:T(8,128)(2,1)} %constant.155.clone.y_low) | copy-start | bytes 786436
  104.8 34.4 %copy-start.9 = (f32[3,512]{1,0:T(4,128)S(1)}, f32[3,512]{1,0:T(4,128)}, u32[]{:S(2)}) copy-start(f32[3,512]{1,0:T(4,128)} %residual.1) | copy-start | bytes 18436
  104.8 34.4 %copy-start.12 = (f32[3,512]{1,0:T(4,128)S(1)}, f32[3,512]{1,0:T(4,128)}, u32[]{:S(2)}) copy-start(f32[3,512]{1,0:T(4,128)} %dipoles.1) | copy-start | bytes 18436
  104.8 34.4 %copy-start.20 = (f32[256,512]{1,0:T(8,128)S(1)}, f32[256,512]{1,0:T(8,128)}, u32[]{:S(2)}) copy-start(f32[256,512]{1,0:T(8,128)} %copy-done.19) | copy-start | bytes 1572868
  104.8 34.4 %copy-start.22 = (f32[2,72,512]{2,1,0:T(8,128)S(1)}, f32[2,72,512]{2,1,0:T(8,128)}, u32[]{:S(2)}) copy-start(f32[2,72,512]{2,1,0:T(8,128)} %copy-done.21) | copy-start | bytes 884740
  104.8 34.4 %copy-start.24 = (bf16[256,512]{1,0:T(8,128)(2,1)S(1)}, bf16[256,512]{1,0:T(8,128)(2,1)}, u32[]{:S(2)}) copy-start(bf16[256,512]{1,0:T(8,128)(2,1)} %copy-done.23) | copy-start | bytes 786436
  104.9 34.4 %copy-start.26 = (bf16[256,512]{1,0:T(8,128)(2,1)S(1)}, bf16[256,512]{1,0:T(8,128)(2,1)}, u32[]{:S(2)}) copy-start(bf16[256,512]{1,0:T(8,128)(2,1)} %copy-done.25) | copy-start | bytes 786436
  104.9 34.4 %copy-start.28 = (f32[2,8,512]{2,1,0:T(8,128)S(1)}, f32[2,8,512]{2,1,0:T(8,128)}, u32[]{:S(2)}) copy-start(f32[2,8,512]{2,1,0:T(8,128)} %copy-done.27) | copy-start | bytes 98308
  104.9 34.4 %copy-start.30 = (f32[8,512]{1,0:T(8,128)S(1)}, f32[8,512]{1,0:T(8,128)}, u32[]{:S(2)}) copy-start(f32[8,512]{1,0:T(8,128)} %copy-done.29) | copy-start | bytes 49156

commit v3 on v2

--- a/solution.py
+++ b/solution.py
@@ -8,11 +8,14 @@
 from jax import lax
 from jax.experimental import pallas as pl
 from jax.experimental.pallas import tpu as pltpu
+from jax.sharding import Mesh
 from jax.sharding import PartitionSpec as P
 
 G = 256
 TILE = 128
-BOTH = ("slab", "space")
+SPACE = ("pair", "core")
+BOTH = ("slab", "pair", "core")
+CHIPS = ("slab", "pair")
 BETA = 0.4
 THOLE = 0.39
 ROOT_PI = math.sqrt(math.pi)
@@ -110,7 +113,7 @@
 
 
 def gather_kernel(send, *refs):
-    sources, own, sent, held, sems = (refs[:5], refs[5], refs[6], refs[7:12], refs[12])
+    sources, (own, sent, statics), held, sems = (refs[:5], refs[5:8], refs[8:13], refs[13])
     copies = [
         pltpu.make_async_copy(source, target, sems.at[at])
         for at, (source, target) in enumerate(zip(sources, held))
@@ -121,7 +124,11 @@
         copy.wait()
     residual, cells, fraction, alphas, order = held
     atoms = residual.shape[1]
-    position = cells[...].astype(F32) + fraction[...]
+    in_cells = cells[...].astype(F32)
+    statics[0:3] = in_cells
+    statics[3:6] = fraction[...]
+    statics[6:8] = jnp.zeros((2, atoms), F32)
+    position = in_cells + fraction[...]
     rows = jnp.concatenate(
         [position, alphas[...].reshape(1, atoms), residual[...], jnp.zeros((1, atoms), F32)], 0
     )
@@ -293,20 +300,35 @@
     lax.fori_loop(0, TILE // APPLY_ROWS, chunk_step, 0)
 
 
-def sweep_kernel(first_place, meta, geometry, own_first, own_rest, straight, inner, outer, *rest):
-    banks = len(rest) - 4
-    pairs, found = (rest[:banks], rest[banks])
-    pool, columns, totals = rest[banks + 1 :]
-    fill_search(pool, own_first, own_rest, straight, inner, outer, meta)
-    for bank in range(banks):
+def sweep_tiles(first_place, meta, geometry, banks, found, pool, columns, totals, local=None):
+    for bank, pairs in enumerate(banks):
 
         def tile_step(at, carry):
             tile = meta[ORDER_AT + first_place + 2 * bank + at]
-            apply_tile(meta, tile, at, pairs[bank], geometry, pool, columns, totals)
-            found[2 * bank + at] = updated(geometry[tile], totals)
+            apply_tile(meta, tile, at, pairs, geometry, pool, columns, totals)
+            rows = updated(geometry[tile], totals)
+            found[2 * bank + at] = rows
+            if local is not None:
+                local[tile] = rows
             return carry
 
         lax.fori_loop(0, 2, tile_step, 0)
+
+
+def sweep_kernel(
+    first_place, meta, geometry, own_first, own_rest, straight, inner, outer, pairs, found, pool, columns, totals
+):
+    fill_search(pool, own_first, own_rest, straight, inner, outer, meta)
+    sweep_tiles(first_place, meta, geometry, (pairs,), found, pool, columns, totals)
+
+
+def direction_kernel(
+    meta, geometry, own_first, own_rest, straight, inner, outer, pairs_a, pairs_b, order, found, ordered, pool, columns, totals, local
+):
+    fill_search(pool, own_first, own_rest, straight, inner, outer, meta)
+    sweep_tiles(0, meta, geometry, (pairs_a, pairs_b), found, pool, columns, totals, local)
+    in_tiles = jnp.concatenate([local[tile] for tile in range(4)], 1)
+    ordered[...] = selected(in_tiles, order_matrix(order[...], order.shape[1]), NT)
 
 
 def final_field_kernel(
@@ -393,93 +415,134 @@
     return total
 
 
-def tables_kernel(cells, fraction, cas_high, cas_low, tab_x, tab_y, w_high, w_low, slope_z):
-    for dim, out in ((0, tab_x), (1, tab_y)):
-        weights, slopes = spline(fraction[dim : dim + 1])
-        out[0] = table(cells[dim : dim + 1], weights, out.shape[1], False)
-        out[1] = table(cells[dim : dim + 1], slopes, out.shape[1], False)
-    weights, slopes = spline(fraction[2:3])
-    cas = (cas_high[...], cas_low[...])
-    waves = product(cas, halves(table(cells[2:3], weights, G, True)), NN)
-    high, low = halves(waves)
-    w_high[...] = high
-    w_low[...] = low
-    slope_z[...] = product(cas, halves(table(cells[2:3], slopes, G, True)), NN)
-
-
-def spread_kernel(x_rows, meta, direction, order, tab_x, tab_y, w_high, w_low, slope_z, ordered, out, local):
-    atoms = order.shape[1]
-    y_rows = tab_y.shape[1]
-    for place in range(4):
-        local[meta[ORDER_AT + place]] = direction[place]
-    in_tiles = jnp.concatenate([local[tile] for tile in range(4)], 1)
-    d = selected(in_tiles, order_matrix(order[...], atoms), NT)
-    ordered[...] = d
-    w_z = (w_high[...], w_low[...])
-    s_z = halves(slope_z[...] * d[2:3])
-    slope_part = tab_x[1] * d[0:1]
-    weight_part = tab_x[0] * d[1:2]
+def tables_kernel(meta, mine, beside, cas_high, cas_low, tab_x, tab_y, w_high, w_low, slope_z):
+    cas = (cas_high[meta[PARITY_AT]], cas_low[meta[PARITY_AT]])
+    for side, statics in enumerate((mine, beside)):
+        cells = statics[0:3].astype(jnp.int32)
+        for dim, out in ((0, tab_x), (1, tab_y)):
+            weights, slopes = spline(statics[3 + dim : 4 + dim])
+            out[side, 0] = table(cells[dim : dim + 1], weights, out.shape[2], False)
+            out[side, 1] = table(cells[dim : dim + 1], slopes, out.shape[2], False)
+        weights, slopes = spline(statics[5:6])
+        high, low = halves(product(cas, halves(table(cells[2:3], weights, G, True)), NN))
+        w_high[side] = high
+        w_low[side] = low
+        slope_z[side] = product(cas, halves(table(cells[2:3], slopes, G, True)), NN)
+
+
+def spread_part(side, d, tab_x, tab_y, w_high, w_low, slope_z):
+    w_z = (w_high[side], w_low[side])
+    s_z = halves(slope_z[side] * d[2:3])
+    weight_x = tab_x[side, 0]
+    slope_part = tab_x[side, 1] * d[0:1]
+    weight_part = weight_x * d[1:2]
     sides = []
-    for y in range(y_rows):
-        w_y, s_y = (tab_y[0, y : y + 1], tab_y[1, y : y + 1])
-        sides.append((slope_part * w_y + weight_part * s_y, tab_x[0] * w_y))
-    side = halves(jnp.concatenate([pair[0] for pair in sides], 0))
+    for y in range(tab_y.shape[2]):
+        w_y, s_y = (tab_y[side, 0, y : y + 1], tab_y[side, 1, y : y + 1])
+        sides.append((slope_part * w_y + weight_part * s_y, weight_x * w_y))
+    rows = halves(jnp.concatenate([pair[0] for pair in sides], 0))
     flat = halves(jnp.concatenate([pair[1] for pair in sides], 0))
-    width = y_rows * x_rows
-    out[:, :width] = product(w_z, side, NT) + product(s_z, flat, NT)
-    out[:, width:] = jnp.zeros((G, out.shape[1] - width), F32)
-
-
-def plane_kernel(shapes, grid, factor, sums, x_high, x_low, y_high, y_low, out, along_x):
-    n_slab, n_space, x_rows, y_rows = shapes
+    return product(w_z, rows, NT) + product(s_z, flat, NT)
+
+
+def spread_own_kernel(ordered, tab_x, tab_y, w_high, w_low, slope_z, out):
+    out[...] = spread_part(0, ordered[...], tab_x, tab_y, w_high, w_low, slope_z)
+
+
+def put_lanes(out, flat):
+    for row in range(8):
+        out[:, row, :] = flat[:, row * TILE : (row + 1) * TILE]
+
+
+def get_lanes(grid):
+    return jnp.concatenate([grid[:, row, :] for row in range(8)], 1)
+
+
+def spread_both_kernel(shift, meta, ordered, mine, tab_x, tab_y, w_high, w_low, slope_z, out, flat):
+    theirs = spread_part(1, ordered[...], tab_x, tab_y, w_high, w_low, slope_z)
+    ours = mine[...]
+    width = ours.shape[1]
+    even = meta[PARITY_AT] == 0
+    lower = jnp.where(even, ours, theirs)
+    upper = jnp.where(even, theirs, ours)
+    flat[:, :shift] = lower[:, :shift]
+    flat[:, shift:width] = lower[:, shift:] + upper[:, : width - shift]
+    flat[:, width : width + shift] = upper[:, width - shift :]
+    flat[:, width + shift :] = jnp.zeros((flat.shape[0], flat.shape[1] - width - shift), F32)
+    put_lanes(out, flat)
+
+
+def plane_kernel(shapes, grid, factor, sums, x_high, x_low, y_high, y_low, out, flat):
+    n_slab, n_pair, x_rows, y_rows = shapes
     width = x_rows * y_rows
-    for y in range(y_rows):
-        total = None
-        for s in range(n_slab):
-            block = halves(grid[s * n_space : (s + 1) * n_space, y * x_rows : (y + 1) * x_rows])
-            rows = slice(s * TILE, s * TILE + x_rows)
-            term = product(block, (x_high[rows], x_low[rows]), NN)
-            total = term if total is None else total + term
-        along_x[y * n_space : (y + 1) * n_space] = total
+    flat[...] = get_lanes(grid)
+    along_x = None
+    for s in range(n_slab):
+        block = jnp.concatenate(
+            [
+                flat[s * n_pair : (s + 1) * n_pair, y * x_rows : (y + 1) * x_rows]
+                for y in range(y_rows)
+            ],
+            0,
+        )
+        rows = slice(s * TILE, s * TILE + x_rows)
+        term = product(halves(block), (x_high[rows], x_low[rows]), NN)
+        along_x = term if along_x is None else along_x + term
     cas_y = (y_high[...], y_low[...])
-    spectrum = product(cas_y, halves(along_x[...]), TN)
+    spectrum = product(cas_y, halves(along_x), TN)
     scaled = spectrum * factor[...]
     energy = jnp.sum(jnp.sum(spectrum * scaled, axis=0, keepdims=True), axis=1, keepdims=True)
     back = halves(product(cas_y, halves(scaled), NN))
     planes = product(back, (x_high[...], x_low[...]), NT)
     for s in range(n_slab):
         for y in range(y_rows):
-            out[s * n_space : (s + 1) * n_space, y * x_rows : (y + 1) * x_rows] = planes[
-                y * n_space : (y + 1) * n_space, s * TILE : s * TILE + x_rows
+            flat[s * n_pair : (s + 1) * n_pair, y * x_rows : (y + 1) * x_rows] = planes[
+                y * n_pair : (y + 1) * n_pair, s * TILE : s * TILE + x_rows
             ]
-    spare = out.shape[1] - width
+    spare = flat.shape[1] - width
     lane = lax.broadcasted_iota(jnp.int32, (1, spare), 1)
-    tail = jnp.where(lane == 0, energy, sums[0:1, :spare])
-    out[:, width:] = jnp.broadcast_to(tail, (out.shape[0], spare))
-
-
-def finish_kernel(
-    x_rows, grid, w_high, w_low, slope_z, tab_x, tab_y, ordered, applied, dipoles, residual, next_dipoles, next_residual, direction
-):
-    y_rows = tab_y.shape[1]
-    width = y_rows * x_rows
-    planes = halves(grid[:, :width])
-    tail = jnp.sum(grid[:, width:], axis=0, keepdims=True)
-    step = tail[:, 2:3] / (tail[:, 0:1] + tail[:, 1:2])
-    by_weight = product(planes, (w_high[...], w_low[...]), TN)
-    by_slope = product(planes, halves(slope_z[...]), TN)
+    known = jnp.concatenate([sums[0:1], jnp.zeros((1, spare - TILE), F32)], 1)
+    tail = jnp.where(lane == 0, energy, known)
+    flat[:, width:] = jnp.broadcast_to(tail, (flat.shape[0], spare))
+    put_lanes(out, flat)
+
+
+def probe_part(side, planes, tab_x, tab_y, w_high, w_low, slope_z):
+    x_rows = tab_x.shape[2]
+    by_weight = product(planes, (w_high[side], w_low[side]), TN)
+    by_slope = product(planes, halves(slope_z[side]), TN)
+    weight_x, slope_x = (tab_x[side, 0], tab_x[side, 1])
     fields = [0.0, 0.0, 0.0]
-    for y in range(y_rows):
+    for y in range(tab_y.shape[2]):
         rows = slice(y * x_rows, (y + 1) * x_rows)
-        w_y, s_y = (tab_y[0, y : y + 1], tab_y[1, y : y + 1])
+        w_y, s_y = (tab_y[side, 0, y : y + 1], tab_y[side, 1, y : y + 1])
         weighted = by_weight[rows]
-        fields[0] += w_y * jnp.sum(tab_x[1] * weighted, axis=0, keepdims=True)
-        fields[1] += s_y * jnp.sum(tab_x[0] * weighted, axis=0, keepdims=True)
-        fields[2] += w_y * jnp.sum(tab_x[0] * by_slope[rows], axis=0, keepdims=True)
-    total = applied[0:3] + jnp.concatenate(fields, 0)
+        fields[0] += w_y * jnp.sum(slope_x * weighted, axis=0, keepdims=True)
+        fields[1] += s_y * jnp.sum(weight_x * weighted, axis=0, keepdims=True)
+        fields[2] += w_y * jnp.sum(weight_x * by_slope[rows], axis=0, keepdims=True)
+    return fields
+
+
+def probe_kernel(side, shift, meta, grid, tab_x, tab_y, w_high, w_low, slope_z, out):
+    matrix = get_lanes(grid)
+    width = tab_x.shape[2] * tab_y.shape[2]
+    low_side = 0 if side == 0 else 1
+    planes = jnp.where(
+        meta[PARITY_AT] == low_side, matrix[:, :width], matrix[:, shift : shift + width]
+    )
+    fields = probe_part(side, halves(planes), tab_x, tab_y, w_high, w_low, slope_z)
+    atoms = out.shape[1]
+    scalars = jnp.sum(matrix[:, width + shift :], axis=0, keepdims=True)[:, :TILE]
+    padded = jnp.concatenate([scalars, jnp.zeros((1, atoms - TILE), F32)], 1)
+    out[...] = jnp.concatenate(fields + [padded, jnp.zeros((4, atoms), F32)], 0)
+
+
+def finish_kernel(mine, theirs, ordered, applied, dipoles, residual, next_dipoles, next_residual, direction):
+    total = mine[...] + theirs[...]
+    step = total[3:4, 2:3] / (total[3:4, 0:1] + total[3:4, 1:2])
     d = ordered[0:3]
     next_dipoles[...] = dipoles[...] + step * d
-    next_residual[...] = residual[...] - step * total
+    next_residual[...] = residual[...] - step * (applied[0:3] + total[0:3])
     direction[...] = d
 
 
@@ -530,7 +593,7 @@
 
 
 def around(block):
-    n_slab, n_space = (lax.axis_size("slab"), lax.axis_size("space"))
+    n_slab, n_space = (lax.axis_size("slab"), lax.axis_size(SPACE))
     up = [(i, (i + 1) % n_slab) for i in range(n_slab)]
     down = [(j, i) for i, j in up]
     before = lax.ppermute(block, "slab", up)
@@ -541,27 +604,39 @@
     return (straight, inner, outer)
 
 
+def from_core_beside(block):
+    return lax.ppermute(
+        block, BOTH, swap_pairs(lax.axis_size("slab"), lax.axis_size(SPACE), False)
+    )
+
+
 def local(
     dipoles, residual, cells, fraction, polarizability, tile_order, send_tiles, tile_lists, tile_counts
 ):
-    n_slab, n_space = (lax.axis_size("slab"), lax.axis_size("space"))
+    n_slab, n_space = (lax.axis_size("slab"), lax.axis_size(SPACE))
+    n_pair = n_space // 2
     atoms = residual.shape[1]
     extents = (G // n_slab, G // n_space)
     x_rows = -(-(extents[0] + 4) // 8) * 8
     y_rows = extents[1] + 4
-    width = x_rows * y_rows
-    lanes = -(-(width + 3) // TILE) * TILE
-    slab_index, space_index = (lax.axis_index("slab"), lax.axis_index("space"))
+    pair_rows = 2 * extents[1] + 4
+    shift = extents[1] * x_rows
+    half = G // 2
+    slab_index, space_index = (lax.axis_index("slab"), lax.axis_index(SPACE))
     tile_shape = ((4, 8, TILE), F32)
     two_shape = ((2, 8, TILE), F32)
     bank_shape = ((2, 16, TILE, TILE), F32)
     pool_scratch = pltpu.VMEM((22, 8, TILE), F32)
     total_scratch = pltpu.VMEM((3, TILE, TILE), F32)
-    own, sent = pl.pallas_call(
+    own, sent, statics = pl.pallas_call(
         gather_kernel,
-        out_shape=[jax.ShapeDtypeStruct(*tile_shape), jax.ShapeDtypeStruct(*two_shape)],
+        out_shape=[
+            jax.ShapeDtypeStruct(*tile_shape),
+            jax.ShapeDtypeStruct(*two_shape),
+            jax.ShapeDtypeStruct((8, atoms), F32),
+        ],
         in_specs=[pl.BlockSpec(memory_space=pltpu.SMEM)] + [pl.BlockSpec(memory_space=pltpu.HBM)] * 5,
-        out_specs=[pl.BlockSpec(memory_space=pltpu.VMEM)] * 2,
+        out_specs=[pl.BlockSpec(memory_space=pltpu.VMEM)] * 3,
         scratch_shapes=[
             pltpu.VMEM((3, atoms), F32),
             pltpu.VMEM((3, atoms), jnp.int32),
@@ -590,61 +665,76 @@
     sweep_scratch = (pool_scratch, pltpu.VMEM((3, TILE, TILE), F32), total_scratch)
     second = around(search_a)
 
-    def sweep(first_place, mine, others, received, banks):
+    def sweep(first_place, pairs):
         return call(
             functools.partial(sweep_kernel, first_place),
-            [((2 * len(banks), 8, TILE), F32)],
+            [two_shape],
             10**8,
             smem=1,
             scratch=sweep_scratch,
-        )(meta, geometry, mine, others, *received, *banks)[0]
-
-    next_a = sweep(0, search_a, search_b, second, (pairs_a,))
-    next_b = sweep(2, search_a, search_b, second, (pairs_b,))
+        )(meta, geometry, search_a, search_b, *second, pairs)[0]
+
+    next_a = sweep(0, pairs_a)
+    next_b = sweep(2, pairs_b)
     third = around(next_a)
-    direction = sweep(0, next_a, next_b, third, (pairs_a, pairs_b))
+    local_scratch = pltpu.VMEM((4, 8, TILE), F32)
+    direction, ordered = call(
+        direction_kernel,
+        [tile_shape, ((8, atoms), F32)],
+        10**8,
+        smem=1,
+        scratch=sweep_scratch + (local_scratch,),
+    )(meta, geometry, next_a, next_b, *third, pairs_a, pairs_b, tile_order)
+    ordered_beside = from_core_beside(ordered)
     freq = np.arange(G)
     padded_x = np.stack([(s * extents[0] + np.arange(x_rows) - 2) % G for s in range(n_slab)])
     real_x = np.tile(np.arange(x_rows) < extents[0] + 4, n_slab)
     cas_x = cas_matrix(padded_x.reshape(-1), freq) * real_x[:, None]
-    rows_y = (np.arange(n_space)[None] * extents[1] + np.arange(y_rows)[:, None] - 2) % G
+    rows_y = (np.arange(n_pair)[None] * 2 * extents[1] + np.arange(pair_rows)[:, None] - 2) % G
     cas_y = cas_matrix(rows_y.reshape(-1), freq)
+    freq_by_core = np.stack([freq[0::2], freq[1::2]])
+    cas_z = cas_matrix(freq_by_core.reshape(-1), freq).reshape(2, half, G)
     wide_x = np.zeros((n_slab, TILE, G))
     wide_x[:, :x_rows] = cas_x.reshape(n_slab, x_rows, G)
-    tab_x, tab_y, w_high, w_low, slope_z = call(
+    statics, _ = lax.optimization_barrier((statics, first[1]))
+    tables = call(
         tables_kernel,
         [
-            ((2, x_rows, atoms), F32),
-            ((2, y_rows, atoms), F32),
-            ((G, atoms), BF16),
-            ((G, atoms), BF16),
-            ((G, atoms), F32),
+            ((2, 2, x_rows, atoms), F32),
+            ((2, 2, y_rows, atoms), F32),
+            ((2, half, atoms), BF16),
+            ((2, half, atoms), BF16),
+            ((2, half, atoms), F32),
         ],
         10**8,
-    )(cells, fraction, *split_constant(cas_matrix(freq, freq)))
-    ordered, spread = call(
-        functools.partial(spread_kernel, x_rows),
-        [((8, atoms), F32), ((G, lanes), F32)],
+        smem=1,
+    )(meta, statics, from_core_beside(statics), *split_constant(cas_z))
+    message = ((half, 8, TILE), F32)
+    flat_scratch = pltpu.VMEM((half, 8 * TILE), F32)
+    spread_own = call(spread_own_kernel, [((half, x_rows * y_rows), F32)], 10**9)(ordered, *tables)[0]
+    spread = call(
+        functools.partial(spread_both_kernel, shift),
+        [message],
         10**9,
         smem=1,
-        scratch=(pltpu.VMEM((4, 8, TILE), F32),),
-    )(meta, direction, tile_order, tab_x, tab_y, w_high, w_low, slope_z)
-    grid = lax.all_to_all(spread, BOTH, 0, 0, tiled=True)
+        scratch=(flat_scratch,),
+    )(meta, ordered_beside, spread_own, *tables)[0]
+    grid = lax.all_to_all(spread, CHIPS, 0, 0, tiled=True)
     last = around(direction[:2])
     applied, sums = call(
         final_field_kernel,
         [((8, atoms), F32), ((8, TILE), F32)],
         10**9,
         smem=1,
-        scratch=sweep_scratch + (pltpu.VMEM((4, 8, TILE), F32),),
+        scratch=sweep_scratch + (local_scratch,),
     )(meta, geometry, direction, *last, pairs_a, pairs_b, tile_order)
     ids = jnp.arange(G, dtype=jnp.int32)
     factor = multiplier(ids[None, :], ids[:, None], slab_index * n_space + space_index)
     planes = call(
-        functools.partial(plane_kernel, (n_slab, n_space, x_rows, y_rows)),
-        [((G, lanes), F32)],
+        functools.partial(plane_kernel, (n_slab, n_pair, x_rows, pair_rows)),
+        [message],
         10**9,
-        scratch=(pltpu.VMEM((y_rows * n_space, G), F32),),
+        scratch=(flat_scratch,),
     )(
         grid,
         factor,
@@ -652,16 +742,25 @@
         *split_constant(wide_x.reshape(-1, G)),
         *split_constant(cas_y),
     )[0]
-    returned = lax.all_to_all(planes, BOTH, 0, 0, tiled=True)
+    returned = lax.all_to_all(planes, CHIPS, 0, 0, tiled=True)
+
+    def probe(side):
+        return call(
+            functools.partial(probe_kernel, side, shift), [((8, atoms), F32)], 10**9, smem=1
+        )(meta, returned, *tables)[0]
+
+    beside = from_core_beside(probe(1))
     three = ((3, atoms), F32)
     return tuple(
-        call(functools.partial(finish_kernel, x_rows), [three, three, three], 10**9)(
-            returned, w_high, w_low, slope_z, tab_x, tab_y, ordered, applied, dipoles, residual
+        call(finish_kernel, [three, three, three], 10**6)(
+            probe(0), beside, ordered, applied, dipoles, residual
         )
     )
 
 
 def solution(mesh):
+    slab, space = (mesh.shape["slab"], mesh.shape["space"])
+    mesh = Mesh(mesh.devices.reshape(slab, space // 2, 2), BOTH)
     in_specs = (
         P(None, BOTH),
         P(None, BOTH),

time: 141 us -> 139 us (0.986)
  Pallas kernels: 26.8 us -> 33.6 us
  waiting for transfers between devices: 17.3 us -> 12.1 us
  local copies, waits for them, and re-layouts: 13.8 us -> 11.7 us
    ppermute x0 -> x3, starting transfers between devices: none -> 7.66 us  [from_core_beside(): lax.ppermute(block, BOTH, swap_pairs(lax.axis_size('slab'), lax.axis_size...]
    pallas_call x10 -> x13, Pallas kernels: 26 us -> 32.7 us  [run(): pl.pallas_call(kernel, out_shape=[jax.ShapeDtypeStruct(shape, dtype) for...]
    ppermute x4, starting transfers between devices: 20.9 us -> 15.1 us  [around(): inner = lax.ppermute(straight, BOTH, swap_pairs(n_slab, n_space, False))]
    all_to_all x1, starting transfers between devices: 10.1 us -> 7.39 us  [local(): grid = lax.all_to_all(spread, CHIPS, 0, 0, tiled=True)]
    all_to_all x1, waiting for transfers between devices: 3.75 us -> 1.5 us  [local(): grid = lax.all_to_all(spread, CHIPS, 0, 0, tiled=True)]
    all_to_all x2 -> x0, local copies, waits for them, and re-layouts: 2.18 us -> none  [the longest x1 1.51 us: local(): grid = lax.all_to_all(spread, BOTH, 0, 0, tiled=True)]
    unnamed x64 -> x54, local copies, waits for them, and re-layouts: 7.56 us -> 7.64 us
  transfers between devices with their start and end apart: 17 -> 20, of which waited for: 10 -> 7; matrix products, arithmetic and copies ran while one was open for 3% -> 3% of each run, Pallas kernels for 7% -> 11%
where the time goes in v3:
time: 139 us
  starting transfers between devices  43.2 us (31%)
  Pallas kernels  33.6 us (24%)
  blocking collectives  32.8 us (24%)
  waiting for transfers between devices  12.1 us (9%)
  local copies, waits for them, and re-layouts  11.7 us (8%)
  between operations  5.11 us (4%)
    all_to_all x1, blocking collectives, local(): returned = lax.all_to_all(planes, CHIPS, 0, 0, tiled=True)  32.8 us
    pallas_call x13, Pallas kernels, run(): pl.pallas_call(kernel, out_shape=[jax.ShapeDtypeStruct(shape, dtype) for...  32.7 us
    ppermute x4, starting transfers between devices, around(): inner = lax.ppermute(straight, BOTH, swap_pairs(n_slab, n_space, False))  15.1 us
    ppermute x4, starting transfers between devices, around(): after = lax.ppermute(block, 'slab', down)  8.99 us
    ppermute x3, starting transfers between devices, from_core_beside(): lax.ppermute(block, BOTH, swap_pairs(lax.axis_size('slab'), lax.axis_size...  7.66 us
    unnamed x54, local copies, waits for them, and re-layouts  7.64 us
    all_to_all x1, starting transfers between devices, local(): grid = lax.all_to_all(spread, CHIPS, 0, 0, tiled=True)  7.39 us
    ppermute x4, waiting for transfers between devices, around(): outer = lax.ppermute(straight, BOTH, swap_pairs(n_slab, n_space, True))  5.38 us
  transfers between devices with their start and end apart: 20, of which 7 were waited for; matrix products, arithmetic and copies ran while one was open for 3% of the time, Pallas kernels for 11%

profile of v3, /device:TPU:1, one launch (start us, length us, event | category | flops | bytes accessed | tf_op | source)
XLA Modules:
  0.0 138.9 jit_solution(17408696921010421337)
XLA Ops:
  0.6 0.0 copy-start.2
  0.6 0.7 copy-done.2
  1.3 0.7 copy-done.4
  2.0 0.7 copy-done.6
  2.7 0.7 copy-done.7
  3.4 0.7 copy-done.9
  4.1 0.7 copy-done.10
  4.7 0.8 shard_map.166
  5.6 2.1 %collective-permute-start = (f32[2,8,128]{2,1,0:T(8,128)S(1)}, f32[2,8,128]{2,1,0:T(8,128)S(1)}, u32[]{:S(2)}, u32[]{:S(2)}) collective-permute-start(f32[2,8,128]{2,1,0:T(8,128)S(1)} %get-tuple-element.24), channel_id=1, source_target_pairs={{0,64},{64,128},{128,192},{192,0},{1,65},{65,129},{129,193},{193,1... | collective-permute-start | bytes 24584 | tf_op jit(solution)/shard_map/ppermute | solution.py:599
  7.7 1.4 collective-permute-start.1
  9.1 0.8 reshape.138
  9.9 0.2 collective-permute-done
  10.0 0.2 collective-permute-done.1
  10.2 3.6 %collective-permute-start.2 = (f32[3,2,8,128]{3,2,1,0:T(8,128)S(1)}, f32[3,2,8,128]{3,2,1,0:T(8,128)S(1)}, u32[]{:S(2)}, u32[]{:S(2)}) collective-permute-start(f32[3,2,8,128]{3,2,1,0:T(8,128)S(1)} %pad_maximum_fusion.straight), channel_id=1, source_target_pairs={{0,1},{1,0},{2,3},{3,2},{4,5},{5,4},{6,7},{7,6},{8,9},{9,8},{10,11... | collective-permute-start | bytes 73736 | tf_op jit(solution)/shard_map/ppermute | solution.py:602
  13.8 0.1 collective-permute-start.3
  13.8 1.3 fusion.21
  19.1 2.0 %concatenate.3.meta = s32[41]{0:T(128)S(1)} concatenate(s32[32]{0:T(128)S(1)} %compare_select_fusion.1, s32[4]{0:T(128)} %bitcast.30, s32[1]{0:T(128)} %bitcast.1, s32[1]{0:T(128)} %bitcast.2, s32[1]{0:T(128)} %bitcast.3, s32[1]{0:T(128)} %bitcast.4, s32[1]{0:T(128)} %bitcast.5), dimensions={0} | concatenate | bytes 328 | tf_op jit(solution)/shard_map/concatenate | solution.py:93
  21.1 0.0 collective-permute-done.2.inner
  21.1 3.3 %shard_map.167 = (f32[22,8,128]{2,1,0:T(8,128)S(1)}, f32[2,16,128,128]{3,2,1,0:T(8,128)S(1)}, f32[2,8,128]{2,1,0:T(8,128)S(1)}) custom-call(s32[41]{0:T(128)S(1)} %concatenate.3.meta, f32[4,8,128]{2,1,0:T(8,128)S(1)} %get-tuple-element.28.own, f32[3,2,8,128]{3,2,1,0:T(8,128)S(1)} %pad_maximum_fusion.straight, ...), custom_call_target="tpu_custom_call" | custom-call | flops 1000000000 | bytes 1048576 | tf_op jit(solution)/shard_map/pallas_call | solution.py:100
  24.3 3.0 %collective-permute-start.5 = (f32[2,8,128]{2,1,0:T(8,128)S(1)}, f32[2,8,128]{2,1,0:T(8,128)S(1)}, u32[]{:S(2)}, u32[]{:S(2)}) collective-permute-start(f32[2,8,128]{2,1,0:T(8,128)S(1)} %get-tuple-element.30.own_first), channel_id=1, source_target_pairs={{64,0},{128,64},{192,128},{0,192},{65,1},{129,65},{193,129},{1,193... | collective-permute-start | bytes 24584 | tf_op jit(solution)/shard_map/ppermute | solution.py:600
  27.3 0.8 collective-permute-done.5
  28.1 2.9 %collective-permute-done.4 = f32[2,8,128]{2,1,0:T(8,128)S(1)} collective-permute-done((f32[2,8,128]{2,1,0:T(8,128)S(1)}, f32[2,8,128]{2,1,0:T(8,128)S(1)}, u32[]{:S(2)}, u32[]{:S(2)}) %collective-permute-start.4) | collective-permute-done | bytes 8224 | tf_op jit(solution)/shard_map/ppermute | solution.py:599
  31.0 8.1 %collective-permute-start.6 = (f32[3,2,8,128]{3,2,1,0:T(8,128)S(1)}, f32[3,2,8,128]{3,2,1,0:T(8,128)S(1)}, u32[]{:S(2)}, u32[]{:S(2)}) collective-permute-start(f32[3,2,8,128]{3,2,1,0:T(8,128)S(1)} %pad_maximum_fusion.1.straight), channel_id=1, source_target_pairs={{0,1},{1,0},{2,3},{3,2},{4,5},{5,4},{6,7},{7,6},{8,9},{9,8},{10,11... | collective-permute-start | bytes 73736 | tf_op jit(solution)/shard_map/ppermute | solution.py:602
  39.1 0.0 collective-permute-start.7
  39.1 3.8 %shard_map.168 = (f32[22,8,128]{2,1,0:T(8,128)}, f32[2,16,128,128]{3,2,1,0:T(8,128)S(1)}, f32[2,8,128]{2,1,0:T(8,128)S(1)}) custom-call(s32[41]{0:T(128)S(1)} %concatenate.3.meta, f32[4,8,128]{2,1,0:T(8,128)S(1)} %get-tuple-element.28.own, f32[3,2,8,128]{3,2,1,0:T(8,128)S(1)} %pad_maximum_fusion.straight, f32[3,2,8,128]{3,2,1,0:T(8,128)S(1)} %collective-permute-done.2.inner, ...), custom_call_target="tpu_custom_call" | custom-call | flops 1000000000 | bytes 1048576 | tf_op jit(solution)/shard_map/pallas_call | solution.py:100
  42.9 0.0 collective-permute-done.6.inner
  42.9 0.0 copy-start.5
  42.9 1.9 %shard_map.169.own_first = f32[2,8,128]{2,1,0:T(8,128)S(1)} custom-call(s32[41]{0:T(128)S(1)} %concatenate.3.meta, f32[22,8,128]{2,1,0:T(8,128)S(1)} %get-tuple-element.29.geometry, f32[2,8,128]{2,1,0:T(8,128)S(1)} %get-tuple-element.30.own_first, f32[2,8,128]{2,1,0:T(8,128)S(1)} %get-tuple-element.31.own_rest, ...), custom_call_target="tpu_custom_call" | custom-call | flops 100000000 | bytes 1048576 | tf_op jit(solution)/shard_map/pallas_call | solution.py:100
  44.8 0.1 collective-permute-start.8
  44.9 2.7 %collective-permute-start.9 = (f32[2,8,128]{2,1,0:T(8,128)S(1)}, f32[2,8,128]{2,1,0:T(8,128)S(1)}, u32[]{:S(2)}, u32[]{:S(2)}) collective-permute-start(f32[2,8,128]{2,1,0:T(8,128)S(1)} %shard_map.169.own_first), channel_id=1, source_target_pairs={{64,0},{128,64},{192,128},{0,192},{65,1},{129,65},{193,129},{1,193... | collective-permute-start | bytes 24584 | tf_op jit(solution)/shard_map/ppermute | solution.py:600
  47.6 4.0 %collective-permute-start.13 = (f32[8,512]{1,0:T(8,128)S(1)}, f32[8,512]{1,0:T(8,128)S(1)}, u32[]{:S(2)}, u32[]{:S(2)}) collective-permute-start(f32[8,512]{1,0:T(8,128)S(1)} %get-tuple-element.36.mine), channel_id=1, source_target_pairs={{0,1},{1,0},{2,3},{3,2},{4,5},{5,4},{6,7},{7,6},{8,9},{9,8},{10,11... | collective-permute-start | bytes 49160 | tf_op jit(solution)/shard_map/ppermute | solution.py:608
  51.6 0.0 collective-permute-done.9
  51.6 1.6 %collective-permute-start.10 = (f32[3,2,8,128]{3,2,1,0:T(8,128)S(1)}, f32[3,2,8,128]{3,2,1,0:T(8,128)S(1)}, u32[]{:S(2)}, u32[]{:S(2)}) collective-permute-start(f32[3,2,8,128]{3,2,1,0:T(8,128)S(1)} %pad_maximum_fusion.2.straight), channel_id=1, source_target_pairs={{0,1},{1,0},{2,3},{3,2},{4,5},{5,4},{6,7},{7,6},{8,9},{9,8},{10,11... | collective-permute-start | bytes 73736 | tf_op jit(solution)/shard_map/ppermute | solution.py:602
  53.2 0.0 collective-permute-start.11
  53.2 0.0 collective-permute-done.13.beside
  53.3 2.4 %shard_map.172 = (f32[2,2,72,512]{3,2,1,0:T(8,128)S(1)}, f32[2,2,8,512]{3,2,1,0:T(8,128)S(1)}, bf16[2,128,512]{2,1,0:T(8,128)(2,1)S(1)}, bf16[2,128,512]{2,1,0:T(8,128)(2,1)S(1)}, f32[2,128,512]{2,1,0:T(8,128)S(1)}) custom-call(s32[41]{0:T(128)S(1)} %concatenate.3.meta, f32[8,512]{1,0:T(8,128)S(1)} %get-tuple-element.36.mine, ...), custom_call_target="tpu_custom_call" | custom-call | flops 100000000 | bytes 1048576 | tf_op jit(solution)/shard_map/pallas_call | solution.py:100
  55.7 1.9 %shard_map.170.own_rest = f32[2,8,128]{2,1,0:T(8,128)S(1)} custom-call(s32[41]{0:T(128)S(1)} %concatenate.3.meta, f32[22,8,128]{2,1,0:T(8,128)S(1)} %get-tuple-element.29.geometry, f32[2,8,128]{2,1,0:T(8,128)S(1)} %get-tuple-element.30.own_first, f32[2,8,128]{2,1,0:T(8,128)S(1)} %get-tuple-element.31.own_rest, ...), custom_call_target="tpu_custom_call" | custom-call | flops 100000000 | bytes 1048576 | tf_op jit(solution)/shard_map/pallas_call | solution.py:100
  57.7 0.0 collective-permute-done.10.inner
  57.7 0.0 collective-permute-done.11.outer
  57.7 3.6 %shard_map.171 = (f32[4,8,128]{2,1,0:T(8,128)S(1)}, f32[8,512]{1,0:T(8,128)S(1)}) custom-call(s32[41]{0:T(128)S(1)} %concatenate.3.meta, f32[22,8,128]{2,1,0:T(8,128)S(1)} %get-tuple-element.29.geometry, f32[2,8,128]{2,1,0:T(8,128)S(1)} %shard_map.169.own_first, f32[2,8,128]{2,1,0:T(8,128)S(1)} %shard_map.170.own_rest, ...), custom_call_target="tpu_custom_call" | custom-call | flops 100000000 | bytes 1048576 | tf_op jit(solution)/shard_map/pallas_call | solution.py:100
  61.3 3.6 %collective-permute-start.12 = (f32[8,512]{1,0:T(8,128)S(1)}, f32[8,512]{1,0:T(8,128)S(1)}, u32[]{:S(2)}, u32[]{:S(2)}) collective-permute-start(f32[8,512]{1,0:T(8,128)S(1)} %get-tuple-element.34.ordered), channel_id=1, source_target_pairs={{0,1},{1,0},{2,3},{3,2},{4,5},{5,4},{6,7},{7,6},{8,9},{9,8},{10,11... | collective-permute-start | bytes 49160 | tf_op jit(solution)/shard_map/ppermute | solution.py:608
  64.9 1.3 shard_map.173.mine
  66.2 0.0 collective-permute-done.12.ordered
  66.2 2.9 %shard_map.174 = f32[128,8,128]{2,1,0:T(8,128)} custom-call(s32[41]{0:T(128)S(1)} %concatenate.3.meta, f32[8,512]{1,0:T(8,128)S(1)} %collective-permute-done.12.ordered, f32[128,576]{1,0:T(8,128)S(1)} %shard_map.173.mine, f32[2,2,72,512]{3,2,1,0:T(8,128)S(1)} %get-tuple-element.37.tab_x, f32[2,2,8,512]{3,2,1,0:T(8,128)S(1)} %get-tuple-element.38.tab_y, ...), custom_call_target="tpu_custom_call" | custom-call | flops 1000000000 | bytes 1048576 | tf_op jit(solution)/shard_map/pallas_call | solution.py:100
  69.1 7.4 %all-to-all-start = ((f32[128,8,128]{2,1,0:T(8,128)}), f32[128,8,128]{2,1,0:T(8,128)S(1)}, u32[]{:S(2)}, u32[]{:S(2)}) async-start(f32[128,8,128]{2,1,0:T(8,128)} %shard_map.174), calls=%async_computation | async-start | bytes 1048576 | tf_op jit(solution)/shard_map/all_to_all | solution.py:722
  76.5 0.1 fusion.12
  76.6 0.8 collective-permute-start.14
  77.3 2.0 %collective-permute-start.15 = (f32[2,8,128]{2,1,0:T(8,128)S(1)}, f32[2,8,128]{2,1,0:T(8,128)S(1)}, u32[]{:S(2)}, u32[]{:S(2)}) collective-permute-start(f32[2,8,128]{2,1,0:T(8,128)S(1)} %get-tuple-element.46), channel_id=1, source_target_pairs={{64,0},{128,64},{192,128},{0,192},{65,1},{129,65},{193,129},{1,193... | collective-permute-start | bytes 24584 | tf_op jit(solution)/shard_map/ppermute | solution.py:600
  79.6 1.1 collective-permute-done.14
  80.7 1.8 %collective-permute-start.16 = (f32[3,2,8,128]{3,2,1,0:T(8,128)S(1)}, f32[3,2,8,128]{3,2,1,0:T(8,128)S(1)}, u32[]{:S(2)}, u32[]{:S(2)}) collective-permute-start(f32[3,2,8,128]{3,2,1,0:T(8,128)S(1)} %pad_maximum_fusion.3.straight), channel_id=1, source_target_pairs={{0,1},{1,0},{2,3},{3,2},{4,5},{5,4},{6,7},{7,6},{8,9},{9,8},{10,11... | collective-permute-start | bytes 73736 | tf_op jit(solution)/shard_map/ppermute | solution.py:602
  82.5 1.1 collective-permute-start.17
  83.6 0.2 fusion.3.factor
  83.8 5.4 %collective-permute-done.17.outer = f32[3,2,8,128]{3,2,1,0:T(8,128)S(1)} collective-permute-done((f32[3,2,8,128]{3,2,1,0:T(8,128)S(1)}, f32[3,2,8,128]{3,2,1,0:T(8,128)S(1)}, u32[]{:S(2)}, u32[]{:S(2)}) %collective-permute-start.17) | collective-permute-done | bytes 24608 | tf_op jit(solution)/shard_map/ppermute | solution.py:603
  89.2 1.6 %copy-done.1 = f32[2,16,128,128]{3,2,1,0:T(8,128)S(1)} copy-done((f32[2,16,128,128]{3,2,1,0:T(8,128)S(1)}, f32[2,16,128,128]{3,2,1,0:T(8,128)}, u32[]{:S(2)}) %copy-start.1) | copy-done | bytes 2097176
  90.8 3.6 %shard_map.175 = (f32[8,512]{1,0:T(8,128)S(1)}, f32[8,128]{1,0:T(8,128)S(1)}) custom-call(s32[41]{0:T(128)S(1)} %concatenate.3.meta, f32[22,8,128]{2,1,0:T(8,128)S(1)} %get-tuple-element.29.geometry, f32[4,8,128]{2,1,0:T(8,128)S(1)} %get-tuple-element.42.direction, f32[3,2,8,128]{3,2,1,0:T(8,128)S(1)} %pad_maximum_fusion.3.straight, ...), custom_call_target="tpu_custom_call" | custom-call | flops 1000000000 | bytes 1048576 | tf_op jit(solution)/shard_map/pallas_call | solution.py:100
  94.4 1.5 %all-to-all-done.grid = f32[128,8,128]{2,1,0:T(8,128)S(1)} async-done(((f32[128,8,128]{2,1,0:T(8,128)}), f32[128,8,128]{2,1,0:T(8,128)S(1)}, u32[]{:S(2)}, u32[]{:S(2)}) %all-to-all-start) | async-done | bytes 524320 | tf_op jit(solution)/shard_map/all_to_all | solution.py:722
  95.9 0.9 copy-done.12
  96.8 0.9 copy-done.14
  97.8 3.2 %shard_map.176 = f32[128,8,128]{2,1,0:T(8,128)S(1)} custom-call(f32[128,8,128]{2,1,0:T(8,128)S(1)} %all-to-all-done.grid, f32[256,256]{1,0:T(8,128)S(1)} %fusion.3.factor, f32[8,128]{1,0:T(8,128)S(1)} %get-tuple-element.43.sums, bf16[512,256]{1,0:T(8,128)(2,1)S(1)} %copy-done.11, bf16[512,256]{1,0:T(8,128)(2,1)S(1)} %copy-done.12, ...), custom_call_target="tpu_custom_call" | custom-call | flops 1000000000 | bytes 1048576 | tf_op jit(solution)/shard_map/pallas_call | solution.py:100
  101.0 32.8 %all_to_all.10.grid = f32[128,8,128]{2,1,0:T(8,128)S(1)} all-to-all(f32[128,8,128]{2,1,0:T(8,128)S(1)} %shard_map.176), channel_id=1, replica_groups=mesh['slab'=4,'pair'=32,'core'=2] {'slab','pair'}, dimensions={0} | all-to-all | bytes 1048576 | tf_op jit(solution)/shard_map/all_to_all | solution.py:745
  133.9 2.0 %shard_map.178 = f32[8,512]{1,0:T(8,128)S(1)} custom-call(s32[41]{0:T(128)S(1)} %concatenate.3.meta, f32[128,8,128]{2,1,0:T(8,128)S(1)} %all_to_all.10.grid, f32[2,2,72,512]{3,2,1,0:T(8,128)S(1)} %copy-done.18, f32[2,2,8,512]{3,2,1,0:T(8,128)S(1)} %copy-done.26, bf16[2,128,512]{2,1,0:T(8,128)(2,1)S(1)} %copy-done.22, bf16[2,128,512]{2,1,0:T(8,128)(2,1)S(1)} %copy-done.24, ...), custom_call_target="tpu_custom_call" | custom-call | flops 1000000000 | bytes 1048576 | tf_op jit(solution)/shard_map/pallas_call | solution.py:100
  135.9 0.1 collective-permute-start.18
  136.0 2.0 %shard_map.177.mine = f32[8,512]{1,0:T(8,128)S(1)} custom-call(s32[41]{0:T(128)S(1)} %concatenate.3.meta, f32[128,8,128]{2,1,0:T(8,128)S(1)} %all_to_all.10.grid, f32[2,2,72,512]{3,2,1,0:T(8,128)S(1)} %copy-done.18, f32[2,2,8,512]{3,2,1,0:T(8,128)S(1)} %copy-done.26, bf16[2,128,512]{2,1,0:T(8,128)(2,1)S(1)} %copy-done.22, ...), custom_call_target="tpu_custom_call" | custom-call | flops 1000000000 | bytes 1048576 | tf_op jit(solution)/shard_map/pallas_call | solution.py:100
  138.0 0.9 shard_map.179
  (57 shorter events, 0.1 us)
Async XLA Ops:
  0.6 0.7 copy-start.2
  1.3 0.7 copy-start.4
  2.0 0.7 copy-start.6
  2.7 0.7 copy-start.7
  3.4 0.7 copy-start.9
  4.1 0.7 copy-start.10
  5.6 4.4 %collective-permute-start = (f32[2,8,128]{2,1,0:T(8,128)S(1)}, f32[2,8,128]{2,1,0:T(8,128)S(1)}, u32[]{:S(2)}, u32[]{:S(2)}) collective-permute-start(f32[2,8,128]{2,1,0:T(8,128)S(1)} %get-tuple-element.24), channel_id=1, source_target_pairs={{0,64},{64,128},{128,192},{192,0},{1,65},{65,129},{129,193},{193,1... | collective-permute-start | bytes 24584 | tf_op jit(solution)/shard_map/ppermute | solution.py:599
  7.7 2.5 %collective-permute-start.1 = (f32[2,8,128]{2,1,0:T(8,128)S(1)}, f32[2,8,128]{2,1,0:T(8,128)S(1)}, u32[]{:S(2)}, u32[]{:S(2)}) collective-permute-start(f32[2,8,128]{2,1,0:T(8,128)S(1)} %get-tuple-element.24), channel_id=1, source_target_pairs={{64,0},{128,64},{192,128},{0,192},{65,1},{129,65},{193,129},{1,193... | collective-permute-start | bytes 24584 | tf_op jit(solution)/shard_map/ppermute | solution.py:600
  10.2 10.9 %collective-permute-start.2 = (f32[3,2,8,128]{3,2,1,0:T(8,128)S(1)}, f32[3,2,8,128]{3,2,1,0:T(8,128)S(1)}, u32[]{:S(2)}, u32[]{:S(2)}) collective-permute-start(f32[3,2,8,128]{3,2,1,0:T(8,128)S(1)} %pad_maximum_fusion.straight), channel_id=1, source_target_pairs={{0,1},{1,0},{2,3},{3,2},{4,5},{5,4},{6,7},{7,6},{8,9},{9,8},{10,11... | collective-permute-start | bytes 73736 | tf_op jit(solution)/shard_map/ppermute | solution.py:602
  13.8 7.3 %collective-permute-start.3 = (f32[3,2,8,128]{3,2,1,0:T(8,128)S(1)}, f32[3,2,8,128]{3,2,1,0:T(8,128)S(1)}, u32[]{:S(2)}, u32[]{:S(2)}) collective-permute-start(f32[3,2,8,128]{3,2,1,0:T(8,128)S(1)} %pad_maximum_fusion.straight), channel_id=1, source_target_pairs={{0,63},{1,2},{2,1},{3,4},{4,3},{5,6},{6,5},{7,8},{8,7},{9,10},{10,... | collective-permute-start | bytes 73736 | tf_op jit(solution)/shard_map/ppermute | solution.py:603
  24.3 3.8 %collective-permute-start.5 = (f32[2,8,128]{2,1,0:T(8,128)S(1)}, f32[2,8,128]{2,1,0:T(8,128)S(1)}, u32[]{:S(2)}, u32[]{:S(2)}) collective-permute-start(f32[2,8,128]{2,1,0:T(8,128)S(1)} %get-tuple-element.30.own_first), channel_id=1, source_target_pairs={{64,0},{128,64},{192,128},{0,192},{65,1},{129,65},{193,129},{1,193... | collective-permute-start | bytes 24584 | tf_op jit(solution)/shard_map/ppermute | solution.py:600
  27.3 3.7 %collective-permute-start.4 = (f32[2,8,128]{2,1,0:T(8,128)S(1)}, f32[2,8,128]{2,1,0:T(8,128)S(1)}, u32[]{:S(2)}, u32[]{:S(2)}) collective-permute-start(f32[2,8,128]{2,1,0:T(8,128)S(1)} %get-tuple-element.30.own_first), channel_id=1, source_target_pairs={{0,64},{64,128},{128,192},{192,0},{1,65},{65,129},{129,193},{193,1... | collective-permute-start | bytes 24584 | tf_op jit(solution)/shard_map/ppermute | solution.py:599
  31.0 11.9 %collective-permute-start.6 = (f32[3,2,8,128]{3,2,1,0:T(8,128)S(1)}, f32[3,2,8,128]{3,2,1,0:T(8,128)S(1)}, u32[]{:S(2)}, u32[]{:S(2)}) collective-permute-start(f32[3,2,8,128]{3,2,1,0:T(8,128)S(1)} %pad_maximum_fusion.1.straight), channel_id=1, source_target_pairs={{0,1},{1,0},{2,3},{3,2},{4,5},{5,4},{6,7},{7,6},{8,9},{9,8},{10,11... | collective-permute-start | bytes 73736 | tf_op jit(solution)/shard_map/ppermute | solution.py:602
  39.1 3.8 %collective-permute-start.7 = (f32[3,2,8,128]{3,2,1,0:T(8,128)S(1)}, f32[3,2,8,128]{3,2,1,0:T(8,128)S(1)}, u32[]{:S(2)}, u32[]{:S(2)}) collective-permute-start(f32[3,2,8,128]{3,2,1,0:T(8,128)S(1)} %pad_maximum_fusion.1.straight), channel_id=1, source_target_pairs={{0,63},{1,2},{2,1},{3,4},{4,3},{5,6},{6,5},{7,8},{8,7},{9,10},{10,... | collective-permute-start | bytes 73736 | tf_op jit(solution)/shard_map/ppermute | solution.py:603
  42.9 14.8 %copy-start = (f32[2,16,128,128]{3,2,1,0:T(8,128)}, f32[2,16,128,128]{3,2,1,0:T(8,128)S(1)}, u32[]{:S(2)}) copy-start(f32[2,16,128,128]{3,2,1,0:T(8,128)S(1)} %get-tuple-element.33.pairs.pairs_b) | copy-start | bytes 6291460
  42.9 10.4 %copy-start.15 = (bf16[2,128,256]{2,1,0:T(8,128)(2,1)S(1)}, bf16[2,128,256]{2,1,0:T(8,128)(2,1)}, u32[]{:S(2)}) copy-start(bf16[2,128,256]{2,1,0:T(8,128)(2,1)} %constant.155.clone.cas_high) | copy-start | bytes 393220
  42.9 10.4 %copy-start.16 = (bf16[2,128,256]{2,1,0:T(8,128)(2,1)S(1)}, bf16[2,128,256]{2,1,0:T(8,128)(2,1)}, u32[]{:S(2)}) copy-start(bf16[2,128,256]{2,1,0:T(8,128)(2,1)} %constant.156.clone.cas_low) | copy-start | bytes 393220
  42.9 14.8 %copy-start.5 = (s32[1,512]{1,0:T(1,128)S(1)}, s32[1,512]{1,0:T(1,128)}, u32[]{:S(2)}) copy-start(s32[1,512]{1,0:T(1,128)} %order.3) | copy-start | bytes 6148
  44.8 6.8 %collective-permute-start.8 = (f32[2,8,128]{2,1,0:T(8,128)S(1)}, f32[2,8,128]{2,1,0:T(8,128)S(1)}, u32[]{:S(2)}, u32[]{:S(2)}) collective-permute-start(f32[2,8,128]{2,1,0:T(8,128)S(1)} %shard_map.169.own_first), channel_id=1, source_target_pairs={{0,64},{64,128},{128,192},{192,0},{1,65},{65,129},{129,193},{193,1... | collective-permute-start | bytes 24584 | tf_op jit(solution)/shard_map/ppermute | solution.py:599
  44.9 6.7 %collective-permute-start.9 = (f32[2,8,128]{2,1,0:T(8,128)S(1)}, f32[2,8,128]{2,1,0:T(8,128)S(1)}, u32[]{:S(2)}, u32[]{:S(2)}) collective-permute-start(f32[2,8,128]{2,1,0:T(8,128)S(1)} %shard_map.169.own_first), channel_id=1, source_target_pairs={{64,0},{128,64},{192,128},{0,192},{65,1},{129,65},{193,129},{1,193... | collective-permute-start | bytes 24584 | tf_op jit(solution)/shard_map/ppermute | solution.py:600
  47.6 5.6 %collective-permute-start.13 = (f32[8,512]{1,0:T(8,128)S(1)}, f32[8,512]{1,0:T(8,128)S(1)}, u32[]{:S(2)}, u32[]{:S(2)}) collective-permute-start(f32[8,512]{1,0:T(8,128)S(1)} %get-tuple-element.36.mine), channel_id=1, source_target_pairs={{0,1},{1,0},{2,3},{3,2},{4,5},{5,4},{6,7},{7,6},{8,9},{9,8},{10,11... | collective-permute-start | bytes 49160 | tf_op jit(solution)/shard_map/ppermute | solution.py:608
  51.6 6.0 %collective-permute-start.10 = (f32[3,2,8,128]{3,2,1,0:T(8,128)S(1)}, f32[3,2,8,128]{3,2,1,0:T(8,128)S(1)}, u32[]{:S(2)}, u32[]{:S(2)}) collective-permute-start(f32[3,2,8,128]{3,2,1,0:T(8,128)S(1)} %pad_maximum_fusion.2.straight), channel_id=1, source_target_pairs={{0,1},{1,0},{2,3},{3,2},{4,5},{5,4},{6,7},{7,6},{8,9},{9,8},{10,11... | collective-permute-start | bytes 73736 | tf_op jit(solution)/shard_map/ppermute | solution.py:602
  53.2 4.4 %collective-permute-start.11 = (f32[3,2,8,128]{3,2,1,0:T(8,128)S(1)}, f32[3,2,8,128]{3,2,1,0:T(8,128)S(1)}, u32[]{:S(2)}, u32[]{:S(2)}) collective-permute-start(f32[3,2,8,128]{3,2,1,0:T(8,128)S(1)} %pad_maximum_fusion.2.straight), channel_id=1, source_target_pairs={{0,63},{1,2},{2,1},{3,4},{4,3},{5,6},{6,5},{7,8},{8,7},{9,10},{10,... | collective-permute-start | bytes 73736 | tf_op jit(solution)/shard_map/ppermute | solution.py:603
  55.7 10.5 %copy-start.17 = (f32[2,2,72,512]{3,2,1,0:T(8,128)}, f32[2,2,72,512]{3,2,1,0:T(8,128)S(1)}, u32[]{:S(2)}) copy-start(f32[2,2,72,512]{3,2,1,0:T(8,128)S(1)} %get-tuple-element.37.tab_x) | copy-start | bytes 1769476
  55.7 10.5 %copy-start.19 = (f32[2,128,512]{2,1,0:T(8,128)}, f32[2,128,512]{2,1,0:T(8,128)S(1)}, u32[]{:S(2)}) copy-start(f32[2,128,512]{2,1,0:T(8,128)S(1)} %get-tuple-element.41.slope_z) | copy-start | bytes 1572868
  55.7 10.5 %copy-start.21 = (bf16[2,128,512]{2,1,0:T(8,128)(2,1)}, bf16[2,128,512]{2,1,0:T(8,128)(2,1)S(1)}, u32[]{:S(2)}) copy-start(bf16[2,128,512]{2,1,0:T(8,128)(2,1)S(1)} %get-tuple-element.39.w_high) | copy-start | bytes 786436
  55.7 10.5 %copy-start.23 = (bf16[2,128,512]{2,1,0:T(8,128)(2,1)}, bf16[2,128,512]{2,1,0:T(8,128)(2,1)S(1)}, u32[]{:S(2)}) copy-start(bf16[2,128,512]{2,1,0:T(8,128)(2,1)S(1)} %get-tuple-element.40.w_low) | copy-start | bytes 786436
  55.7 10.5 %copy-start.25 = (f32[2,2,8,512]{3,2,1,0:T(8,128)}, f32[2,2,8,512]{3,2,1,0:T(8,128)S(1)}, u32[]{:S(2)}) copy-start(f32[2,2,8,512]{3,2,1,0:T(8,128)S(1)} %get-tuple-element.38.tab_y) | copy-start | bytes 196612
  61.3 4.9 %collective-permute-start.12 = (f32[8,512]{1,0:T(8,128)S(1)}, f32[8,512]{1,0:T(8,128)S(1)}, u32[]{:S(2)}, u32[]{:S(2)}) collective-permute-start(f32[8,512]{1,0:T(8,128)S(1)} %get-tuple-element.34.ordered), channel_id=1, source_target_pairs={{0,1},{1,0},{2,3},{3,2},{4,5},{5,4},{6,7},{7,6},{8,9},{9,8},{10,11... | collective-permute-start | bytes 49160 | tf_op jit(solution)/shard_map/ppermute | solution.py:608
  69.1 26.8 %all-to-all-start = ((f32[128,8,128]{2,1,0:T(8,128)}), f32[128,8,128]{2,1,0:T(8,128)S(1)}, u32[]{:S(2)}, u32[]{:S(2)}) async-start(f32[128,8,128]{2,1,0:T(8,128)} %shard_map.174), calls=%async_computation | async-start | bytes 1048576 | tf_op jit(solution)/shard_map/all_to_all | solution.py:722
  76.6 4.1 %collective-permute-start.14 = (f32[2,8,128]{2,1,0:T(8,128)S(1)}, f32[2,8,128]{2,1,0:T(8,128)S(1)}, u32[]{:S(2)}, u32[]{:S(2)}) collective-permute-start(f32[2,8,128]{2,1,0:T(8,128)S(1)} %get-tuple-element.46), channel_id=1, source_target_pairs={{0,64},{64,128},{128,192},{192,0},{1,65},{65,129},{129,193},{193,1... | collective-permute-start | bytes 24584 | tf_op jit(solution)/shard_map/ppermute | solution.py:599
  77.3 3.4 %collective-permute-start.15 = (f32[2,8,128]{2,1,0:T(8,128)S(1)}, f32[2,8,128]{2,1,0:T(8,128)S(1)}, u32[]{:S(2)}, u32[]{:S(2)}) collective-permute-start(f32[2,8,128]{2,1,0:T(8,128)S(1)} %get-tuple-element.46), channel_id=1, source_target_pairs={{64,0},{128,64},{192,128},{0,192},{65,1},{129,65},{193,129},{1,193... | collective-permute-start | bytes 24584 | tf_op jit(solution)/shard_map/ppermute | solution.py:600
  80.7 3.1 %collective-permute-start.16 = (f32[3,2,8,128]{3,2,1,0:T(8,128)S(1)}, f32[3,2,8,128]{3,2,1,0:T(8,128)S(1)}, u32[]{:S(2)}, u32[]{:S(2)}) collective-permute-start(f32[3,2,8,128]{3,2,1,0:T(8,128)S(1)} %pad_maximum_fusion.3.straight), channel_id=1, source_target_pairs={{0,1},{1,0},{2,3},{3,2},{4,5},{5,4},{6,7},{7,6},{8,9},{9,8},{10,11... | collective-permute-start | bytes 73736 | tf_op jit(solution)/shard_map/ppermute | solution.py:602
  82.5 6.7 %collective-permute-start.17 = (f32[3,2,8,128]{3,2,1,0:T(8,128)S(1)}, f32[3,2,8,128]{3,2,1,0:T(8,128)S(1)}, u32[]{:S(2)}, u32[]{:S(2)}) collective-permute-start(f32[3,2,8,128]{3,2,1,0:T(8,128)S(1)} %pad_maximum_fusion.3.straight), channel_id=1, source_target_pairs={{0,63},{1,2},{2,1},{3,4},{4,3},{5,6},{6,5},{7,8},{8,7},{9,10},{10,... | collective-permute-start | bytes 73736 | tf_op jit(solution)/shard_map/ppermute | solution.py:603
  83.6 12.3 %copy-start.11 = (bf16[512,256]{1,0:T(8,128)(2,1)S(1)}, bf16[512,256]{1,0:T(8,128)(2,1)}, u32[]{:S(2)}) copy-start(bf16[512,256]{1,0:T(8,128)(2,1)} %constant.157.clone.x_high) | copy-start | bytes 786436
  89.2 1.6 %copy-start.1 = (f32[2,16,128,128]{3,2,1,0:T(8,128)S(1)}, f32[2,16,128,128]{3,2,1,0:T(8,128)}, u32[]{:S(2)}) copy-start(f32[2,16,128,128]{3,2,1,0:T(8,128)} %copy-done) | copy-start | bytes 6291460
  90.8 5.1 %copy-start.13 = (bf16[384,256]{1,0:T(8,128)(2,1)S(1)}, bf16[384,256]{1,0:T(8,128)(2,1)}, u32[]{:S(2)}) copy-start(bf16[384,256]{1,0:T(8,128)(2,1)} %constant.159.clone.y_high) | copy-start | bytes 589828
  95.9 1.0 copy-start.12
  96.8 0.9 copy-start.14
  97.8 36.1 %copy-start.18 = (f32[2,2,72,512]{3,2,1,0:T(8,128)S(1)}, f32[2,2,72,512]{3,2,1,0:T(8,128)}, u32[]{:S(2)}) copy-start(f32[2,2,72,512]{3,2,1,0:T(8,128)} %copy-done.17) | copy-start | bytes 1769476
  97.8 36.1 %copy-start.20 = (f32[2,128,512]{2,1,0:T(8,128)S(1)}, f32[2,128,512]{2,1,0:T(8,128)}, u32[]{:S(2)}) copy-start(f32[2,128,512]{2,1,0:T(8,128)} %copy-done.19) | copy-start | bytes 1572868
  97.8 36.1 %copy-start.22 = (bf16[2,128,512]{2,1,0:T(8,128)(2,1)S(1)}, bf16[2,128,512]{2,1,0:T(8,128)(2,1)}, u32[]{:S(2)}) copy-start(bf16[2,128,512]{2,1,0:T(8,128)(2,1)} %copy-done.21) | copy-start | bytes 786436
  97.8 36.1 %copy-start.24 = (bf16[2,128,512]{2,1,0:T(8,128)(2,1)S(1)}, bf16[2,128,512]{2,1,0:T(8,128)(2,1)}, u32[]{:S(2)}) copy-start(bf16[2,128,512]{2,1,0:T(8,128)(2,1)} %copy-done.23) | copy-start | bytes 786436
  97.8 36.1 %copy-start.26 = (f32[2,2,8,512]{3,2,1,0:T(8,128)S(1)}, f32[2,2,8,512]{3,2,1,0:T(8,128)}, u32[]{:S(2)}) copy-start(f32[2,2,8,512]{3,2,1,0:T(8,128)} %copy-done.25) | copy-start | bytes 196612
  135.9 2.1 %copy-start.3 = (f32[3,512]{1,0:T(4,128)S(1)}, f32[3,512]{1,0:T(4,128)}, u32[]{:S(2)}) copy-start(f32[3,512]{1,0:T(4,128)} %residual.1) | copy-start | bytes 18436
  135.9 2.1 %copy-start.8 = (f32[3,512]{1,0:T(4,128)S(1)}, f32[3,512]{1,0:T(4,128)}, u32[]{:S(2)}) copy-start(f32[3,512]{1,0:T(4,128)} %dipoles.1) | copy-start | bytes 18436
  135.9 2.1 %collective-permute-start.18 = (f32[8,512]{1,0:T(8,128)S(1)}, f32[8,512]{1,0:T(8,128)S(1)}, u32[]{:S(2)}, u32[]{:S(2)}) collective-permute-start(f32[8,512]{1,0:T(8,128)S(1)} %shard_map.178), channel_id=1, source_target_pairs={{0,1},{1,0},{2,3},{3,2},{4,5},{5,4},{6,7},{7,6},{8,9},{9,8},{10,11... | collective-permute-start | bytes 49160 | tf_op jit(solution)/shard_map/ppermute | solution.py:608

commit v4 on v3

--- a/solution.py
+++ b/solution.py
@@ -38,7 +38,8 @@
 NT = (((1,), (1,)), ((), ()))
 NN = (((1,), (0,)), ((), ()))
 TN = (((0,), (0,)), ((), ()))
-VMEM_LIMIT = 20 * 1024 * 1024
+SMALL_VMEM = 6 * 1024 * 1024
+LARGE_VMEM = 16 * 1024 * 1024
 
 
 def halves(values):
@@ -50,7 +51,13 @@
     def one(a, b):
         return lax.dot_general(a, b, dims, preferred_element_type=F32)
 
-    return one(left[0], right[0]) + (one(left[0], right[1]) + one(left[1], right[0]))
+    (left_dim,), (right_dim,) = dims[0]
+    if left[0].shape[left_dim] % TILE:
+        return one(left[0], right[0]) + (one(left[0], right[1]) + one(left[1], right[0]))
+    return one(
+        jnp.concatenate([left[0], left[0], left[1]], left_dim),
+        jnp.concatenate([right[0], right[1], right[0]], right_dim),
+    )
 
 
 def thirds(values):
@@ -76,24 +83,36 @@
 PARITY_AT = 40
 
 
-def meta_of(tile_lists, tile_counts, send_tiles, parity):
-    entry = tile_lists.reshape(-1)
-    remote = entry - 4
-    pair = remote // 2
-    pair = pair + (pair >= 4)
-    along = pair // 3
-    across = pair % 3
-    base = jnp.where(across == 1, 4, jnp.where(across == 2 - 2 * parity, 10, 16))
-    slots = jnp.where(entry < 4, entry, base + along * 2 + remote % 2)
-    first, second = (send_tiles[0, 0], send_tiles[0, 1])
+def meta_kernel(lists, counts, send, after, meta):
+    parity = lax.axis_index("core")
+    for tile in range(4):
+
+        def remap(place, carry):
+            entry = lists[0, tile, place]
+            remote = entry - 4
+            pair = lax.shift_right_arithmetic(remote, 1)
+            pair = pair + jnp.where(pair >= 4, 1, 0)
+            along = jnp.where(pair >= 3, 1, 0) + jnp.where(pair >= 6, 1, 0)
+            across = pair - 3 * along
+            base = jnp.where(across == 1, 4, jnp.where(across == 2 - 2 * parity, 10, 16))
+            slot = base + along * 2 + (remote & 1)
+            meta[tile * 8 + place] = jnp.where(entry < 4, entry, slot)
+            return carry
+
+        lax.fori_loop(0, 8, remap, 0)
+        meta[COUNTS_AT + tile] = counts[0, tile]
+    first, second = (send[0, 0], send[0, 1])
     third = jnp.where(
         (first != 0) & (second != 0), 0, jnp.where((first != 1) & (second != 1), 1, 2)
     )
-    rest = jnp.stack([first, second, third, 6 - first - second - third, parity])
-    return jnp.concatenate([slots, tile_counts.reshape(-1), rest]).astype(jnp.int32)
-
-
-def call(kernel, outs, flops, smem=0, scratch=()):
+    meta[ORDER_AT] = first
+    meta[ORDER_AT + 1] = second
+    meta[ORDER_AT + 2] = third
+    meta[ORDER_AT + 3] = 6 - first - second - third
+    meta[PARITY_AT] = parity
+
+
+def call(kernel, outs, flops, smem=0, scratch=(), vmem=SMALL_VMEM):
     def run(*args):
         in_specs = [pl.BlockSpec(memory_space=pltpu.SMEM)] * smem
         in_specs += [pl.BlockSpec(memory_space=pltpu.VMEM)] * (len(args) - smem)
@@ -103,7 +122,7 @@
             in_specs=in_specs,
             out_specs=[pl.BlockSpec(memory_space=pltpu.VMEM)] * len(outs),
             scratch_shapes=list(scratch),
-            compiler_params=pltpu.CompilerParams(vmem_limit_bytes=VMEM_LIMIT),
+            compiler_params=pltpu.CompilerParams(vmem_limit_bytes=vmem),
             cost_estimate=pl.CostEstimate(
                 flops=flops, bytes_accessed=1 << 20, transcendentals=0
             ),
@@ -220,6 +239,7 @@
                     five = keep * (bare_two - (3.0 + 3.0 * damping) * decay * inverse_sq)
                     pairs[0, at * 8 + entry, rows] = five
                     pairs[1, at * 8 + entry, rows] = three
+                    pairs[2, at * 8 + entry, rows] = d_z
                     v = search_rows(other)
                     along = five * (d_x * v[0:1] + d_y * v[1:2] + d_z * v[2:3])
                     sums = (
@@ -267,7 +287,7 @@
 
 def apply_tile(meta, tile, at, pairs, geometry, pool, columns, totals):
     block = geometry[tile]
-    own_columns(columns, block, 3)
+    own_columns(columns, block, 2)
     live = meta[COUNTS_AT + tile]
 
     def chunk_step(chunk, carry):
@@ -281,7 +301,7 @@
                 v = pool[slot]
                 d_x = other[0:1] - columns[0, rows]
                 d_y = other[1:2] - columns[1, rows]
-                d_z = wrap_depth(other[2:3] - columns[2, rows])
+                d_z = pairs[2, at * 8 + entry, rows]
                 three = pairs[1, at * 8 + entry, rows]
                 along = pairs[0, at * 8 + entry, rows] * (d_x * v[0:1] + d_y * v[1:2] + d_z * v[2:3])
                 sums = (
@@ -592,16 +612,24 @@
     return pairs
 
 
-def around(block):
-    n_slab, n_space = (lax.axis_size("slab"), lax.axis_size(SPACE))
+def along_slab(block):
+    n_slab = lax.axis_size("slab")
     up = [(i, (i + 1) % n_slab) for i in range(n_slab)]
     down = [(j, i) for i, j in up]
     before = lax.ppermute(block, "slab", up)
     after = lax.ppermute(block, "slab", down)
-    straight = jnp.stack([before, block, after])
+    return jnp.stack([before, block, after])
+
+
+def across_space(straight):
+    n_slab, n_space = (lax.axis_size("slab"), lax.axis_size(SPACE))
     inner = lax.ppermute(straight, BOTH, swap_pairs(n_slab, n_space, False))
     outer = lax.ppermute(straight, BOTH, swap_pairs(n_slab, n_space, True))
     return (straight, inner, outer)
+
+
+def around(block):
+    return across_space(along_slab(block))
 
 
 def from_core_beside(block):
@@ -625,7 +653,7 @@
     slab_index, space_index = (lax.axis_index("slab"), lax.axis_index(SPACE))
     tile_shape = ((4, 8, TILE), F32)
     two_shape = ((2, 8, TILE), F32)
-    bank_shape = ((2, 16, TILE, TILE), F32)
+    bank_shape = ((3, 16, TILE, TILE), F32)
     pool_scratch = pltpu.VMEM((22, 8, TILE), F32)
     total_scratch = pltpu.VMEM((3, TILE, TILE), F32)
     own, sent, statics = pl.pallas_call(
@@ -645,10 +673,22 @@
             pltpu.VMEM((1, atoms), jnp.int32),
             pltpu.SemaphoreType.DMA((5,)),
         ],
-        compiler_params=pltpu.CompilerParams(vmem_limit_bytes=VMEM_LIMIT),
-    )(send_tiles, residual, cells, fraction, polarizability, tile_order)
-    later = lax.optimization_barrier((tile_lists, tile_counts, send_tiles, sent))
-    meta = meta_of(*later[:3], space_index % 2)
+        compiler_params=pltpu.CompilerParams(vmem_limit_bytes=SMALL_VMEM),
+    )(
+        send_tiles,
+        *[
+            pltpu.with_memory_space_constraint(array, pltpu.HBM)
+            for array in (residual, cells, fraction, polarizability, tile_order)
+        ],
+    )
+    smem, anywhere = (pl.BlockSpec(memory_space=pltpu.SMEM), pl.BlockSpec(memory_space=pltpu.HBM))
+    meta = pl.pallas_call(
+        meta_kernel,
+        out_shape=jax.ShapeDtypeStruct((48,), jnp.int32),
+        in_specs=[smem, smem, smem, pl.BlockSpec(memory_space=pltpu.VMEM)],
+        out_specs=smem,
+        cost_estimate=pl.CostEstimate(flops=10**8, bytes_accessed=1 << 20, transcendentals=0),
+    )(tile_lists, tile_counts, send_tiles, sent)
     first = around(sent)
 
     def pairs_of(first_place):
@@ -708,19 +748,22 @@
         ],
         10**8,
         smem=1,
+        vmem=LARGE_VMEM,
     )(meta, statics, from_core_beside(statics), *split_constant(cas_z))
     message = ((half, 8, TILE), F32)
     flat_scratch = pltpu.VMEM((half, 8 * TILE), F32)
-    spread_own = call(spread_own_kernel, [((half, x_rows * y_rows), F32)], 10**9)(ordered, *tables)[0]
+    spread_own = call(spread_own_kernel, [((half, x_rows * y_rows), F32)], 10**9, vmem=LARGE_VMEM)(ordered, *tables)[0]
     spread = call(
         functools.partial(spread_both_kernel, shift),
         [message],
         10**9,
         smem=1,
         scratch=(flat_scratch,),
+        vmem=LARGE_VMEM,
     )(meta, ordered_beside, spread_own, *tables)[0]
+    spread, straight = lax.optimization_barrier((spread, along_slab(direction[:2])))
     grid = lax.all_to_all(spread, CHIPS, 0, 0, tiled=True)
-    last = around(direction[:2])
+    last = across_space(straight)
     applied, sums = call(
         final_field_kernel,
         [((8, atoms), F32), ((8, TILE), F32)],
@@ -735,6 +778,7 @@
         [message],
         10**9,
         scratch=(flat_scratch,),
+        vmem=LARGE_VMEM,
     )(
         grid,
         factor,
@@ -746,7 +790,7 @@
 
     def probe(side):
         return call(
-            functools.partial(probe_kernel, side, shift), [((8, atoms), F32)], 10**9, smem=1
+            functools.partial(probe_kernel, side, shift), [((8, atoms), F32)], 10**9, smem=1, vmem=LARGE_VMEM
         )(meta, returned, *tables)[0]
 
     beside = from_core_beside(probe(1))

time: 139 us -> 136 us (0.978)
  between operations: 5.11 us -> 1.34 us
  local copies, waits for them, and re-layouts: 11.7 us -> 8.43 us
  starting transfers between devices: 43.2 us -> 46 us
    ppermute x16, starting transfers between devices: 28.2 us -> 32.9 us  [the longest x4 15.7 us: along_slab(): after = lax.ppermute(block, 'slab', down)]
    ppermute x16, waiting for transfers between devices: 10.6 us -> 13 us  [the longest x4 9.92 us: across_space(): outer = lax.ppermute(straight, BOTH, swap_pairs(n_slab, n_space, True))]
    ppermute x3, starting transfers between devices: 7.66 us -> 5.47 us  [from_core_beside(): lax.ppermute(block, BOTH, swap_pairs(lax.axis_size('slab'), lax.axis_size...]
    concatenate x1 -> x0, local copies, waits for them, and re-layouts: 2.02 us -> none  [meta_of(): jnp.concatenate([slots, tile_counts.reshape(-1), rest]).astype(jnp.int32)]
    pallas_call x0 -> x1, Pallas kernels: none -> 1.79 us  [local(): pl.pallas_call(meta_kernel, out_shape=jax.ShapeDtypeStruct((48,), jnp.int...]
    all_to_all x1, waiting for transfers between devices: 1.5 us -> 0.01 us  [local(): grid = lax.all_to_all(spread, CHIPS, 0, 0, tiled=True)]
    unnamed x54 -> x60, local copies, waits for them, and re-layouts: 7.64 us -> 8.43 us
  transfers between devices with their start and end apart: 20 -> 20, of which waited for: 7 -> 6; matrix products, arithmetic and copies ran while one was open for 3% -> 0% of each run, Pallas kernels for 11% -> 12%
where the time goes in v4:
time: 136 us
  starting transfers between devices  46 us (34%)
  Pallas kernels  34.7 us (26%)
  blocking collectives  32.5 us (24%)
  waiting for transfers between devices  13 us (10%)
  local copies, waits for them, and re-layouts  8.43 us (6%)
    all_to_all x1, blocking collectives, local(): returned = lax.all_to_all(planes, CHIPS, 0, 0, tiled=True)  32.5 us
    pallas_call x13, Pallas kernels, run(): pl.pallas_call(kernel, out_shape=[jax.ShapeDtypeStruct(shape, dtype) for...  31.4 us
    ppermute x4, starting transfers between devices, along_slab(): after = lax.ppermute(block, 'slab', down)  15.7 us
    ppermute x4, starting transfers between devices, across_space(): inner = lax.ppermute(straight, BOTH, swap_pairs(n_slab, n_space, False))  14 us
    ppermute x4, waiting for transfers between devices, across_space(): outer = lax.ppermute(straight, BOTH, swap_pairs(n_slab, n_space, True))  9.92 us
    unnamed x60, local copies, waits for them, and re-layouts  8.43 us
    all_to_all x1, starting transfers between devices, local(): grid = lax.all_to_all(spread, CHIPS, 0, 0, tiled=True)  7.62 us
    ppermute x3, starting transfers between devices, from_core_beside(): lax.ppermute(block, BOTH, swap_pairs(lax.axis_size('slab'), lax.axis_size...  5.47 us
  transfers between devices with their start and end apart: 20, of which 6 were waited for; matrix products, arithmetic and copies ran while one was open for 0% of the time, Pallas kernels for 12%

profile of v4, /device:TPU:1, one launch (start us, length us, event | category | flops | bytes accessed | tf_op | source)
XLA Modules:
  0.0 136.2 jit_solution(10903613604763644567)
XLA Ops:
  0.6 0.0 copy-start.13
  0.6 0.6 copy-done.13
  1.3 1.5 %shard_map.166 = (f32[4,8,128]{2,1,0:T(8,128)S(1)}, f32[2,8,128]{2,1,0:T(8,128)S(1)}, f32[8,512]{1,0:T(8,128)S(1)}) custom-call(s32[1,2]{1,0:T(1,128)S(1)} %copy-done.13, f32[3,512]{1,0:T(4,128)} %residual.1, s32[3,512]{1,0:T(4,128)} %refs_1_.1, f32[3,512]{1,0:T(4,128)} %refs_2_.1, f32[512]{0:T(512)} %refs_3_.1, s32[1,512]{1,0:T(1,128)} %order.3), custom_call_target="tpu_custom_call" | custom-call | tf_op jit(solution)/shard_map/pallas_call | solution.py:659
  2.8 0.0 copy-start.10
  2.9 2.1 %collective-permute-start = (f32[2,8,128]{2,1,0:T(8,128)S(1)}, f32[2,8,128]{2,1,0:T(8,128)S(1)}, u32[]{:S(2)}, u32[]{:S(2)}) collective-permute-start(f32[2,8,128]{2,1,0:T(8,128)S(1)} %get-tuple-element.23.after), channel_id=1, source_target_pairs={{0,64},{64,128},{128,192},{192,0},{1,65},{65,129},{129,193},{193,1... | collective-permute-start | bytes 24584 | tf_op jit(solution)/shard_map/ppermute | solution.py:619
  5.0 1.4 collective-permute-start.1
  6.3 0.9 collective-permute-done
  7.3 0.2 collective-permute-done.1
  7.5 3.6 %collective-permute-start.2 = (f32[3,2,8,128]{3,2,1,0:T(8,128)S(1)}, f32[3,2,8,128]{3,2,1,0:T(8,128)S(1)}, u32[]{:S(2)}, u32[]{:S(2)}) collective-permute-start(f32[3,2,8,128]{3,2,1,0:T(8,128)S(1)} %pad_maximum_fusion.straight), channel_id=1, source_target_pairs={{0,1},{1,0},{2,3},{3,2},{4,5},{5,4},{6,7},{7,6},{8,9},{9,8},{10,11... | collective-permute-start | bytes 73736 | tf_op jit(solution)/shard_map/ppermute | solution.py:626
  11.0 0.1 collective-permute-start.3
  11.1 1.8 %shard_map.167.meta = s32[48]{0:T(128)} custom-call(s32[1,4,8]{2,1,0:T(4,128)} %lists.1, s32[1,4]{1,0:T(1,128)} %counts.1, s32[1,2]{1,0:T(1,128)} %send.3, f32[2,8,128]{2,1,0:T(8,128)} %copy-done.10), custom_call_target="tpu_custom_call" | custom-call | flops 100000000 | bytes 1048576 | tf_op jit(solution)/shard_map/pallas_call | solution.py:685
  12.9 0.0 copy-start.12
  12.9 1.4 collective-permute-done.3.outer
  14.3 0.7 copy-done.11
  14.9 3.3 %shard_map.168 = (f32[22,8,128]{2,1,0:T(8,128)S(1)}, f32[3,16,128,128]{3,2,1,0:T(8,128)S(1)}, f32[2,8,128]{2,1,0:T(8,128)S(1)}) custom-call(s32[48]{0:T(128)S(1)} %copy-done.11, f32[4,8,128]{2,1,0:T(8,128)S(1)} %get-tuple-element.24.own, f32[3,2,8,128]{3,2,1,0:T(8,128)S(1)} %pad_maximum_fusion.straight, f32[3,2,8,128]{3,2,1,0:T(8,128)S(1)} %collective-permute-done.2.inner, ...), custom_call_target="tpu_custom_call" | custom-call | flops 1000000000 | bytes 1048576 | tf_op jit(solution)/shard_map/pallas_call | solution.py:119
  18.2 0.1 collective-permute-start.4
  18.3 4.8 %collective-permute-start.5 = (f32[2,8,128]{2,1,0:T(8,128)S(1)}, f32[2,8,128]{2,1,0:T(8,128)S(1)}, u32[]{:S(2)}, u32[]{:S(2)}) collective-permute-start(f32[2,8,128]{2,1,0:T(8,128)S(1)} %get-tuple-element.26.own_first), channel_id=1, source_target_pairs={{64,0},{128,64},{192,128},{0,192},{65,1},{129,65},{193,129},{1,193... | collective-permute-start | bytes 24584 | tf_op jit(solution)/shard_map/ppermute | solution.py:620
  23.1 0.9 collective-permute-done.4
  24.1 0.0 collective-permute-done.5
  24.1 0.0 copy-start.19
  24.1 6.5 %collective-permute-start.6 = (f32[3,2,8,128]{3,2,1,0:T(8,128)S(1)}, f32[3,2,8,128]{3,2,1,0:T(8,128)S(1)}, u32[]{:S(2)}, u32[]{:S(2)}) collective-permute-start(f32[3,2,8,128]{3,2,1,0:T(8,128)S(1)} %pad_maximum_fusion.1.straight), channel_id=1, source_target_pairs={{0,1},{1,0},{2,3},{3,2},{4,5},{5,4},{6,7},{7,6},{8,9},{9,8},{10,11... | collective-permute-start | bytes 73736 | tf_op jit(solution)/shard_map/ppermute | solution.py:626
  30.7 3.8 %shard_map.169 = (f32[22,8,128]{2,1,0:T(8,128)}, f32[3,16,128,128]{3,2,1,0:T(8,128)S(1)}, f32[2,8,128]{2,1,0:T(8,128)S(1)}) custom-call(s32[48]{0:T(128)S(1)} %copy-done.12, f32[4,8,128]{2,1,0:T(8,128)S(1)} %get-tuple-element.24.own, f32[3,2,8,128]{3,2,1,0:T(8,128)S(1)} %pad_maximum_fusion.straight, f32[3,2,8,128]{3,2,1,0:T(8,128)S(1)} %collective-permute-done.2.inner, ...), custom_call_target="tpu_custom_call" | custom-call | flops 1000000000 | bytes 1048576 | tf_op jit(solution)/shard_map/pallas_call | solution.py:119
  34.4 0.0 collective-permute-done.6.inner
  34.4 0.0 collective-permute-done.7.outer
  34.4 0.0 copy-start.4
  34.4 1.7 %shard_map.170.own_first = f32[2,8,128]{2,1,0:T(8,128)S(1)} custom-call(s32[48]{0:T(128)S(1)} %copy-done.12, f32[22,8,128]{2,1,0:T(8,128)S(1)} %get-tuple-element.25.geometry, f32[2,8,128]{2,1,0:T(8,128)S(1)} %get-tuple-element.26.own_first, f32[2,8,128]{2,1,0:T(8,128)S(1)} %get-tuple-element.27.own_rest, f32[3,2,8,128]{3,2,1,0:T(8,128)S(1)} %pad_maximum_fusion.1.straight, ...), custom_call_target="tpu_custom_call" | custom-call | flops 100000000 | bytes 1048576 | tf_op jit(solution)/shard_map/pallas_call | solution.py:119
  36.2 0.1 collective-permute-start.8
  36.3 5.2 %collective-permute-start.9 = (f32[2,8,128]{2,1,0:T(8,128)S(1)}, f32[2,8,128]{2,1,0:T(8,128)S(1)}, u32[]{:S(2)}, u32[]{:S(2)}) collective-permute-start(f32[2,8,128]{2,1,0:T(8,128)S(1)} %shard_map.170.own_first), channel_id=1, source_target_pairs={{64,0},{128,64},{192,128},{0,192},{65,1},{129,65},{193,129},{1,193... | collective-permute-start | bytes 24584 | tf_op jit(solution)/shard_map/ppermute | solution.py:620
  41.5 2.1 %collective-permute-start.13 = (f32[8,512]{1,0:T(8,128)S(1)}, f32[8,512]{1,0:T(8,128)S(1)}, u32[]{:S(2)}, u32[]{:S(2)}) collective-permute-start(f32[8,512]{1,0:T(8,128)S(1)} %get-tuple-element.32.mine), channel_id=1, source_target_pairs={{0,1},{1,0},{2,3},{3,2},{4,5},{5,4},{6,7},{7,6},{8,9},{9,8},{10,11... | collective-permute-start | bytes 49160 | tf_op jit(solution)/shard_map/ppermute | solution.py:636
  43.5 1.6 %collective-permute-start.10 = (f32[3,2,8,128]{3,2,1,0:T(8,128)S(1)}, f32[3,2,8,128]{3,2,1,0:T(8,128)S(1)}, u32[]{:S(2)}, u32[]{:S(2)}) collective-permute-start(f32[3,2,8,128]{3,2,1,0:T(8,128)S(1)} %pad_maximum_fusion.2.straight), channel_id=1, source_target_pairs={{0,1},{1,0},{2,3},{3,2},{4,5},{5,4},{6,7},{7,6},{8,9},{9,8},{10,11... | collective-permute-start | bytes 73736 | tf_op jit(solution)/shard_map/ppermute | solution.py:626
  45.2 0.0 collective-permute-start.11
  45.2 0.0 collective-permute-done.13.beside
  45.2 2.4 %shard_map.173 = (f32[2,2,72,512]{3,2,1,0:T(8,128)S(1)}, f32[2,2,8,512]{3,2,1,0:T(8,128)S(1)}, bf16[2,128,512]{2,1,0:T(8,128)(2,1)S(1)}, bf16[2,128,512]{2,1,0:T(8,128)(2,1)S(1)}, f32[2,128,512]{2,1,0:T(8,128)S(1)}) custom-call(s32[48]{0:T(128)S(1)} %copy-done.12, f32[8,512]{1,0:T(8,128)S(1)} %get-tuple-element.32.mine, ...), custom_call_target="tpu_custom_call" | custom-call | flops 100000000 | bytes 1048576 | tf_op jit(solution)/shard_map/pallas_call | solution.py:119
  47.6 1.7 %shard_map.171.own_rest = f32[2,8,128]{2,1,0:T(8,128)S(1)} custom-call(s32[48]{0:T(128)S(1)} %copy-done.12, f32[22,8,128]{2,1,0:T(8,128)S(1)} %get-tuple-element.25.geometry, f32[2,8,128]{2,1,0:T(8,128)S(1)} %get-tuple-element.26.own_first, f32[2,8,128]{2,1,0:T(8,128)S(1)} %get-tuple-element.27.own_rest, f32[3,2,8,128]{3,2,1,0:T(8,128)S(1)} %pad_maximum_fusion.1.straight, ...), custom_call_target="tpu_custom_call" | custom-call | flops 100000000 | bytes 1048576 | tf_op jit(solution)/shard_map/pallas_call | solution.py:119
  49.4 0.0 collective-permute-done.10.inner
  49.4 0.0 collective-permute-done.11.outer
  49.4 3.2 %shard_map.172 = (f32[4,8,128]{2,1,0:T(8,128)S(1)}, f32[8,512]{1,0:T(8,128)S(1)}) custom-call(s32[48]{0:T(128)S(1)} %copy-done.12, f32[22,8,128]{2,1,0:T(8,128)S(1)} %get-tuple-element.25.geometry, f32[2,8,128]{2,1,0:T(8,128)S(1)} %shard_map.170.own_first, f32[2,8,128]{2,1,0:T(8,128)S(1)} %shard_map.171.own_rest, ...), custom_call_target="tpu_custom_call" | custom-call | flops 100000000 | bytes 1048576 | tf_op jit(solution)/shard_map/pallas_call | solution.py:119
  52.7 4.3 %collective-permute-start.15 = (f32[2,8,128]{2,1,0:T(8,128)S(1)}, f32[2,8,128]{2,1,0:T(8,128)S(1)}, u32[]{:S(2)}, u32[]{:S(2)}) collective-permute-start(f32[2,8,128]{2,1,0:T(8,128)S(1)} %get-tuple-element.44), channel_id=1, source_target_pairs={{64,0},{128,64},{192,128},{0,192},{65,1},{129,65},{193,129},{1,193... | collective-permute-start | bytes 24584 | tf_op jit(solution)/shard_map/ppermute | solution.py:620
  56.9 1.4 %collective-permute-start.12 = (f32[8,512]{1,0:T(8,128)S(1)}, f32[8,512]{1,0:T(8,128)S(1)}, u32[]{:S(2)}, u32[]{:S(2)}) collective-permute-start(f32[8,512]{1,0:T(8,128)S(1)} %get-tuple-element.30.ordered), channel_id=1, source_target_pairs={{0,1},{1,0},{2,3},{3,2},{4,5},{5,4},{6,7},{7,6},{8,9},{9,8},{10,11... | collective-permute-start | bytes 49160 | tf_op jit(solution)/shard_map/ppermute | solution.py:636
  58.3 1.4 shard_map.174.mine
  59.7 1.0 collective-permute-done.14
  60.7 2.2 %shard_map.175 = f32[128,8,128]{2,1,0:T(8,128)S(1)} custom-call(s32[48]{0:T(128)S(1)} %copy-done.12, f32[8,512]{1,0:T(8,128)S(1)} %collective-permute-done.12.ordered, f32[128,576]{1,0:T(8,128)S(1)} %shard_map.174.mine, f32[2,2,72,512]{3,2,1,0:T(8,128)S(1)} %get-tuple-element.33.tab_x, f32[2,2,8,512]{3,2,1,0:T(8,128)S(1)} %get-tuple-element.34.tab_y, ...), custom_call_target="tpu_custom_call" | custom-call | flops 1000000000 | bytes 1048576 | tf_op jit(solution)/shard_map/pallas_call | solution.py:119
  62.9 0.8 copy-done.2
  63.7 7.6 %all-to-all-start = ((f32[128,8,128]{2,1,0:T(8,128)}), f32[128,8,128]{2,1,0:T(8,128)}, u32[]{:S(2)}, u32[]{:S(2)}) async-start(f32[128,8,128]{2,1,0:T(8,128)} %copy-done.2), calls=%async_computation | async-start | bytes 1048576 | tf_op jit(solution)/shard_map/all_to_all | solution.py:765
  71.6 0.1 fusion.12
  71.7 2.3 %collective-permute-start.16 = (f32[3,2,8,128]{3,2,1,0:T(8,128)S(1)}, f32[3,2,8,128]{3,2,1,0:T(8,128)S(1)}, u32[]{:S(2)}, u32[]{:S(2)}) collective-permute-start(f32[3,2,8,128]{3,2,1,0:T(8,128)S(1)} %pad_maximum_fusion.3.straight), channel_id=1, source_target_pairs={{0,1},{1,0},{2,3},{3,2},{4,5},{5,4},{6,7},{7,6},{8,9},{9,8},{10,11... | collective-permute-start | bytes 73736 | tf_op jit(solution)/shard_map/ppermute | solution.py:626
  73.9 0.9 collective-permute-start.17
  74.8 0.2 fusion.3.factor
  75.0 8.6 %collective-permute-done.17.outer = f32[3,2,8,128]{3,2,1,0:T(8,128)S(1)} collective-permute-done((f32[3,2,8,128]{3,2,1,0:T(8,128)S(1)}, f32[3,2,8,128]{3,2,1,0:T(8,128)S(1)}, u32[]{:S(2)}, u32[]{:S(2)}) %collective-permute-start.17) | collective-permute-done | bytes 24608 | tf_op jit(solution)/shard_map/ppermute | solution.py:627
  83.6 1.9 %copy-done.1 = f32[3,16,128,128]{3,2,1,0:T(8,128)S(1)} copy-done((f32[3,16,128,128]{3,2,1,0:T(8,128)S(1)}, f32[3,16,128,128]{3,2,1,0:T(8,128)}, u32[]{:S(2)}) %copy-start.1) | copy-done | bytes 3145752
  85.4 3.2 %shard_map.176 = (f32[8,512]{1,0:T(8,128)S(1)}, f32[8,128]{1,0:T(8,128)S(1)}) custom-call(s32[48]{0:T(128)S(1)} %copy-done.12, f32[22,8,128]{2,1,0:T(8,128)S(1)} %get-tuple-element.25.geometry, f32[4,8,128]{2,1,0:T(8,128)S(1)} %get-tuple-element.38.direction, f32[3,2,8,128]{3,2,1,0:T(8,128)S(1)} %pad_maximum_fusion.3.straight, ...), custom_call_target="tpu_custom_call" | custom-call | flops 1000000000 | bytes 1048576 | tf_op jit(solution)/shard_map/pallas_call | solution.py:119
  88.7 0.6 copy-done.7
  89.3 0.9 copy-done.14
  90.2 0.9 copy-done.15
  91.2 0.9 copy-done.16
  92.1 0.9 copy-done.17
  93.1 4.3 %shard_map.177 = f32[128,8,128]{2,1,0:T(8,128)S(1)} custom-call(f32[128,8,128]{2,1,0:T(8,128)} %all-to-all-done.grid, f32[256,256]{1,0:T(8,128)S(1)} %fusion.3.factor, f32[8,128]{1,0:T(8,128)S(1)} %get-tuple-element.41.sums, bf16[512,256]{1,0:T(8,128)(2,1)S(1)} %copy-done.14, bf16[512,256]{1,0:T(8,128)(2,1)S(1)} %copy-done.15, ...), custom_call_target="tpu_custom_call" | custom-call | flops 1000000000 | bytes 1048576 | tf_op jit(solution)/shard_map/pallas_call | solution.py:119
  97.4 32.5 %all_to_all.10.grid = f32[128,8,128]{2,1,0:T(8,128)S(1)} all-to-all(f32[128,8,128]{2,1,0:T(8,128)S(1)} %shard_map.177), channel_id=1, replica_groups=mesh['slab'=4,'pair'=32,'core'=2] {'slab','pair'}, dimensions={0} | all-to-all | bytes 1048576 | tf_op jit(solution)/shard_map/all_to_all | solution.py:789
  129.9 0.0 copy-start.3
  129.9 0.0 copy-start.9
  129.9 1.7 %shard_map.179 = f32[8,512]{1,0:T(8,128)S(1)} custom-call(s32[48]{0:T(128)S(1)} %copy-done.12, f32[128,8,128]{2,1,0:T(8,128)S(1)} %all_to_all.10.grid, f32[2,2,72,512]{3,2,1,0:T(8,128)S(1)} %copy-done.21, f32[2,2,8,512]{3,2,1,0:T(8,128)S(1)} %copy-done.29, bf16[2,128,512]{2,1,0:T(8,128)(2,1)S(1)} %copy-done.25, bf16[2,128,512]{2,1,0:T(8,128)(2,1)S(1)} %copy-done.27, ...), custom_call_target="tpu_custom_call" | custom-call | flops 1000000000 | bytes 1048576 | tf_op jit(solution)/shard_map/pallas_call | solution.py:119
  131.6 2.0 %collective-permute-start.18 = (f32[8,512]{1,0:T(8,128)S(1)}, f32[8,512]{1,0:T(8,128)S(1)}, u32[]{:S(2)}, u32[]{:S(2)}) collective-permute-start(f32[8,512]{1,0:T(8,128)S(1)} %shard_map.179), channel_id=1, source_target_pairs={{0,1},{1,0},{2,3},{3,2},{4,5},{5,4},{6,7},{7,6},{8,9},{9,8},{10,11... | collective-permute-start | bytes 49160 | tf_op jit(solution)/shard_map/ppermute | solution.py:636
  133.6 1.7 %shard_map.178.mine = f32[8,512]{1,0:T(8,128)S(1)} custom-call(s32[48]{0:T(128)S(1)} %copy-done.12, f32[128,8,128]{2,1,0:T(8,128)S(1)} %all_to_all.10.grid, f32[2,2,72,512]{3,2,1,0:T(8,128)S(1)} %copy-done.21, f32[2,2,8,512]{3,2,1,0:T(8,128)S(1)} %copy-done.29, bf16[2,128,512]{2,1,0:T(8,128)(2,1)S(1)} %copy-done.25, bf16[2,128,512]{2,1,0:T(8,128)(2,1)S(1)} %copy-done.27, ...), custom_call_target="tpu_custom_call" | custom-call | flops 1000000000 | bytes 1048576 | tf_op jit(solution)/shard_map/pallas_call | solution.py:119
  135.3 0.9 shard_map.180
  (60 shorter events, 0.1 us)
Async XLA Ops:
  0.6 0.7 copy-start.13
  2.8 8.3 %copy-start.10 = (f32[2,8,128]{2,1,0:T(8,128)}, f32[2,8,128]{2,1,0:T(8,128)S(1)}, u32[]{:S(2)}) copy-start(f32[2,8,128]{2,1,0:T(8,128)S(1)} %get-tuple-element.23.after) | copy-start | bytes 24580
  2.9 4.4 %collective-permute-start = (f32[2,8,128]{2,1,0:T(8,128)S(1)}, f32[2,8,128]{2,1,0:T(8,128)S(1)}, u32[]{:S(2)}, u32[]{:S(2)}) collective-permute-start(f32[2,8,128]{2,1,0:T(8,128)S(1)} %get-tuple-element.23.after), channel_id=1, source_target_pairs={{0,64},{64,128},{128,192},{192,0},{1,65},{65,129},{129,193},{193,1... | collective-permute-start | bytes 24584 | tf_op jit(solution)/shard_map/ppermute | solution.py:619
  5.0 2.5 %collective-permute-start.1 = (f32[2,8,128]{2,1,0:T(8,128)S(1)}, f32[2,8,128]{2,1,0:T(8,128)S(1)}, u32[]{:S(2)}, u32[]{:S(2)}) collective-permute-start(f32[2,8,128]{2,1,0:T(8,128)S(1)} %get-tuple-element.23.after), channel_id=1, source_target_pairs={{64,0},{128,64},{192,128},{0,192},{65,1},{129,65},{193,129},{1,193... | collective-permute-start | bytes 24584 | tf_op jit(solution)/shard_map/ppermute | solution.py:620
  7.5 5.5 %collective-permute-start.2 = (f32[3,2,8,128]{3,2,1,0:T(8,128)S(1)}, f32[3,2,8,128]{3,2,1,0:T(8,128)S(1)}, u32[]{:S(2)}, u32[]{:S(2)}) collective-permute-start(f32[3,2,8,128]{3,2,1,0:T(8,128)S(1)} %pad_maximum_fusion.straight), channel_id=1, source_target_pairs={{0,1},{1,0},{2,3},{3,2},{4,5},{5,4},{6,7},{7,6},{8,9},{9,8},{10,11... | collective-permute-start | bytes 73736 | tf_op jit(solution)/shard_map/ppermute | solution.py:626
  11.0 3.3 %collective-permute-start.3 = (f32[3,2,8,128]{3,2,1,0:T(8,128)S(1)}, f32[3,2,8,128]{3,2,1,0:T(8,128)S(1)}, u32[]{:S(2)}, u32[]{:S(2)}) collective-permute-start(f32[3,2,8,128]{3,2,1,0:T(8,128)S(1)} %pad_maximum_fusion.straight), channel_id=1, source_target_pairs={{0,63},{1,2},{2,1},{3,4},{4,3},{5,6},{6,5},{7,8},{8,7},{9,10},{10,... | collective-permute-start | bytes 73736 | tf_op jit(solution)/shard_map/ppermute | solution.py:627
  12.9 17.7 %copy-start.12 = (s32[48]{0:T(128)S(1)}, s32[48]{0:T(128)}, u32[]{:S(2)}) copy-start(s32[48]{0:T(128)} %shard_map.167.meta) | copy-start | bytes 580
  14.3 0.7 copy-start.11
  18.2 5.9 %collective-permute-start.4 = (f32[2,8,128]{2,1,0:T(8,128)S(1)}, f32[2,8,128]{2,1,0:T(8,128)S(1)}, u32[]{:S(2)}, u32[]{:S(2)}) collective-permute-start(f32[2,8,128]{2,1,0:T(8,128)S(1)} %get-tuple-element.26.own_first), channel_id=1, source_target_pairs={{0,64},{64,128},{128,192},{192,0},{1,65},{65,129},{129,193},{193,1... | collective-permute-start | bytes 24584 | tf_op jit(solution)/shard_map/ppermute | solution.py:619
  18.3 5.8 %collective-permute-start.5 = (f32[2,8,128]{2,1,0:T(8,128)S(1)}, f32[2,8,128]{2,1,0:T(8,128)S(1)}, u32[]{:S(2)}, u32[]{:S(2)}) collective-permute-start(f32[2,8,128]{2,1,0:T(8,128)S(1)} %get-tuple-element.26.own_first), channel_id=1, source_target_pairs={{64,0},{128,64},{192,128},{0,192},{65,1},{129,65},{193,129},{1,193... | collective-permute-start | bytes 24584 | tf_op jit(solution)/shard_map/ppermute | solution.py:620
  24.1 21.1 %copy-start.18 = (bf16[2,128,256]{2,1,0:T(8,128)(2,1)S(1)}, bf16[2,128,256]{2,1,0:T(8,128)(2,1)}, u32[]{:S(2)}) copy-start(bf16[2,128,256]{2,1,0:T(8,128)(2,1)} %constant.90.clone.cas_high) | copy-start | bytes 393220
  24.1 21.1 %copy-start.19 = (bf16[2,128,256]{2,1,0:T(8,128)(2,1)S(1)}, bf16[2,128,256]{2,1,0:T(8,128)(2,1)}, u32[]{:S(2)}) copy-start(bf16[2,128,256]{2,1,0:T(8,128)(2,1)} %constant.91.clone.cas_low) | copy-start | bytes 393220
  24.1 10.3 %collective-permute-start.6 = (f32[3,2,8,128]{3,2,1,0:T(8,128)S(1)}, f32[3,2,8,128]{3,2,1,0:T(8,128)S(1)}, u32[]{:S(2)}, u32[]{:S(2)}) collective-permute-start(f32[3,2,8,128]{3,2,1,0:T(8,128)S(1)} %pad_maximum_fusion.1.straight), channel_id=1, source_target_pairs={{0,1},{1,0},{2,3},{3,2},{4,5},{5,4},{6,7},{7,6},{8,9},{9,8},{10,11... | collective-permute-start | bytes 73736 | tf_op jit(solution)/shard_map/ppermute | solution.py:626
  30.6 3.8 %collective-permute-start.7 = (f32[3,2,8,128]{3,2,1,0:T(8,128)S(1)}, f32[3,2,8,128]{3,2,1,0:T(8,128)S(1)}, u32[]{:S(2)}, u32[]{:S(2)}) collective-permute-start(f32[3,2,8,128]{3,2,1,0:T(8,128)S(1)} %pad_maximum_fusion.1.straight), channel_id=1, source_target_pairs={{0,63},{1,2},{2,1},{3,4},{4,3},{5,6},{6,5},{7,8},{8,7},{9,10},{10,... | collective-permute-start | bytes 73736 | tf_op jit(solution)/shard_map/ppermute | solution.py:627
  34.4 15.0 %copy-start = (f32[3,16,128,128]{3,2,1,0:T(8,128)}, f32[3,16,128,128]{3,2,1,0:T(8,128)S(1)}, u32[]{:S(2)}) copy-start(f32[3,16,128,128]{3,2,1,0:T(8,128)S(1)} %get-tuple-element.29.pairs.pairs_b) | copy-start | bytes 9437188
  34.4 15.0 %copy-start.4 = (s32[1,512]{1,0:T(1,128)S(1)}, s32[1,512]{1,0:T(1,128)}, u32[]{:S(2)}) copy-start(s32[1,512]{1,0:T(1,128)} %order.3) | copy-start | bytes 6148
  36.2 7.4 %collective-permute-start.8 = (f32[2,8,128]{2,1,0:T(8,128)S(1)}, f32[2,8,128]{2,1,0:T(8,128)S(1)}, u32[]{:S(2)}, u32[]{:S(2)}) collective-permute-start(f32[2,8,128]{2,1,0:T(8,128)S(1)} %shard_map.170.own_first), channel_id=1, source_target_pairs={{0,64},{64,128},{128,192},{192,0},{1,65},{65,129},{129,193},{193,1... | collective-permute-start | bytes 24584 | tf_op jit(solution)/shard_map/ppermute | solution.py:619
  36.3 7.3 %collective-permute-start.9 = (f32[2,8,128]{2,1,0:T(8,128)S(1)}, f32[2,8,128]{2,1,0:T(8,128)S(1)}, u32[]{:S(2)}, u32[]{:S(2)}) collective-permute-start(f32[2,8,128]{2,1,0:T(8,128)S(1)} %shard_map.170.own_first), channel_id=1, source_target_pairs={{64,0},{128,64},{192,128},{0,192},{65,1},{129,65},{193,129},{1,193... | collective-permute-start | bytes 24584 | tf_op jit(solution)/shard_map/ppermute | solution.py:620
  41.5 3.7 %collective-permute-start.13 = (f32[8,512]{1,0:T(8,128)S(1)}, f32[8,512]{1,0:T(8,128)S(1)}, u32[]{:S(2)}, u32[]{:S(2)}) collective-permute-start(f32[8,512]{1,0:T(8,128)S(1)} %get-tuple-element.32.mine), channel_id=1, source_target_pairs={{0,1},{1,0},{2,3},{3,2},{4,5},{5,4},{6,7},{7,6},{8,9},{9,8},{10,11... | collective-permute-start | bytes 49160 | tf_op jit(solution)/shard_map/ppermute | solution.py:636
  43.5 5.8 %collective-permute-start.10 = (f32[3,2,8,128]{3,2,1,0:T(8,128)S(1)}, f32[3,2,8,128]{3,2,1,0:T(8,128)S(1)}, u32[]{:S(2)}, u32[]{:S(2)}) collective-permute-start(f32[3,2,8,128]{3,2,1,0:T(8,128)S(1)} %pad_maximum_fusion.2.straight), channel_id=1, source_target_pairs={{0,1},{1,0},{2,3},{3,2},{4,5},{5,4},{6,7},{7,6},{8,9},{9,8},{10,11... | collective-permute-start | bytes 73736 | tf_op jit(solution)/shard_map/ppermute | solution.py:626
  45.2 4.2 %collective-permute-start.11 = (f32[3,2,8,128]{3,2,1,0:T(8,128)S(1)}, f32[3,2,8,128]{3,2,1,0:T(8,128)S(1)}, u32[]{:S(2)}, u32[]{:S(2)}) collective-permute-start(f32[3,2,8,128]{3,2,1,0:T(8,128)S(1)} %pad_maximum_fusion.2.straight), channel_id=1, source_target_pairs={{0,63},{1,2},{2,1},{3,4},{4,3},{5,6},{6,5},{7,8},{8,7},{9,10},{10,... | collective-permute-start | bytes 73736 | tf_op jit(solution)/shard_map/ppermute | solution.py:627
  47.6 13.1 %copy-start.20 = (f32[2,2,72,512]{3,2,1,0:T(8,128)}, f32[2,2,72,512]{3,2,1,0:T(8,128)S(1)}, u32[]{:S(2)}) copy-start(f32[2,2,72,512]{3,2,1,0:T(8,128)S(1)} %get-tuple-element.33.tab_x) | copy-start | bytes 1769476
  47.6 13.1 %copy-start.22 = (f32[2,128,512]{2,1,0:T(8,128)}, f32[2,128,512]{2,1,0:T(8,128)S(1)}, u32[]{:S(2)}) copy-start(f32[2,128,512]{2,1,0:T(8,128)S(1)} %get-tuple-element.37.slope_z) | copy-start | bytes 1572868
  47.6 13.1 %copy-start.24 = (bf16[2,128,512]{2,1,0:T(8,128)(2,1)}, bf16[2,128,512]{2,1,0:T(8,128)(2,1)S(1)}, u32[]{:S(2)}) copy-start(bf16[2,128,512]{2,1,0:T(8,128)(2,1)S(1)} %get-tuple-element.35.w_high) | copy-start | bytes 786436
  47.6 13.1 %copy-start.26 = (bf16[2,128,512]{2,1,0:T(8,128)(2,1)}, bf16[2,128,512]{2,1,0:T(8,128)(2,1)S(1)}, u32[]{:S(2)}) copy-start(bf16[2,128,512]{2,1,0:T(8,128)(2,1)S(1)} %get-tuple-element.36.w_low) | copy-start | bytes 786436
  47.6 13.1 %copy-start.28 = (f32[2,2,8,512]{3,2,1,0:T(8,128)}, f32[2,2,8,512]{3,2,1,0:T(8,128)S(1)}, u32[]{:S(2)}) copy-start(f32[2,2,8,512]{3,2,1,0:T(8,128)S(1)} %get-tuple-element.34.tab_y) | copy-start | bytes 196612
  52.7 8.0 %copy-start.5 = (f32[8,512]{1,0:T(8,128)}, f32[8,512]{1,0:T(8,128)S(1)}, u32[]{:S(2)}) copy-start(f32[8,512]{1,0:T(8,128)S(1)} %get-tuple-element.30.ordered) | copy-start | bytes 49156
  52.7 7.0 %collective-permute-start.15 = (f32[2,8,128]{2,1,0:T(8,128)S(1)}, f32[2,8,128]{2,1,0:T(8,128)S(1)}, u32[]{:S(2)}, u32[]{:S(2)}) collective-permute-start(f32[2,8,128]{2,1,0:T(8,128)S(1)} %get-tuple-element.44), channel_id=1, source_target_pairs={{64,0},{128,64},{192,128},{0,192},{65,1},{129,65},{193,129},{1,193... | collective-permute-start | bytes 24584 | tf_op jit(solution)/shard_map/ppermute | solution.py:620
  56.9 3.7 %collective-permute-start.14 = (f32[2,8,128]{2,1,0:T(8,128)S(1)}, f32[2,8,128]{2,1,0:T(8,128)S(1)}, u32[]{:S(2)}, u32[]{:S(2)}) collective-permute-start(f32[2,8,128]{2,1,0:T(8,128)S(1)} %get-tuple-element.44), channel_id=1, source_target_pairs={{0,64},{64,128},{128,192},{192,0},{1,65},{65,129},{129,193},{193,1... | collective-permute-start | bytes 24584 | tf_op jit(solution)/shard_map/ppermute | solution.py:619
  56.9 3.7 %collective-permute-start.12 = (f32[8,512]{1,0:T(8,128)S(1)}, f32[8,512]{1,0:T(8,128)S(1)}, u32[]{:S(2)}, u32[]{:S(2)}) collective-permute-start(f32[8,512]{1,0:T(8,128)S(1)} %get-tuple-element.30.ordered), channel_id=1, source_target_pairs={{0,1},{1,0},{2,3},{3,2},{4,5},{5,4},{6,7},{7,6},{8,9},{9,8},{10,11... | collective-permute-start | bytes 49160 | tf_op jit(solution)/shard_map/ppermute | solution.py:636
  62.9 0.8 copy-start.2
  63.7 25.6 %all-to-all-start = ((f32[128,8,128]{2,1,0:T(8,128)}), f32[128,8,128]{2,1,0:T(8,128)}, u32[]{:S(2)}, u32[]{:S(2)}) async-start(f32[128,8,128]{2,1,0:T(8,128)} %copy-done.2), calls=%async_computation | async-start | bytes 1048576 | tf_op jit(solution)/shard_map/all_to_all | solution.py:765
  71.7 3.3 %collective-permute-start.16 = (f32[3,2,8,128]{3,2,1,0:T(8,128)S(1)}, f32[3,2,8,128]{3,2,1,0:T(8,128)S(1)}, u32[]{:S(2)}, u32[]{:S(2)}) collective-permute-start(f32[3,2,8,128]{3,2,1,0:T(8,128)S(1)} %pad_maximum_fusion.3.straight), channel_id=1, source_target_pairs={{0,1},{1,0},{2,3},{3,2},{4,5},{5,4},{6,7},{7,6},{8,9},{9,8},{10,11... | collective-permute-start | bytes 73736 | tf_op jit(solution)/shard_map/ppermute | solution.py:626
  73.9 9.6 %collective-permute-start.17 = (f32[3,2,8,128]{3,2,1,0:T(8,128)S(1)}, f32[3,2,8,128]{3,2,1,0:T(8,128)S(1)}, u32[]{:S(2)}, u32[]{:S(2)}) collective-permute-start(f32[3,2,8,128]{3,2,1,0:T(8,128)S(1)} %pad_maximum_fusion.3.straight), channel_id=1, source_target_pairs={{0,63},{1,2},{2,1},{3,4},{4,3},{5,6},{6,5},{7,8},{8,7},{9,10},{10,... | collective-permute-start | bytes 73736 | tf_op jit(solution)/shard_map/ppermute | solution.py:627
  83.6 1.9 %copy-start.1 = (f32[3,16,128,128]{3,2,1,0:T(8,128)S(1)}, f32[3,16,128,128]{3,2,1,0:T(8,128)}, u32[]{:S(2)}) copy-start(f32[3,16,128,128]{3,2,1,0:T(8,128)} %copy-done) | copy-start | bytes 9437188
  88.7 0.6 copy-start.7
  89.3 1.0 copy-start.14
  90.2 0.9 copy-start.15
  91.2 0.9 copy-start.16
  92.1 0.9 copy-start.17
  93.0 36.8 %copy-start.21 = (f32[2,2,72,512]{3,2,1,0:T(8,128)S(1)}, f32[2,2,72,512]{3,2,1,0:T(8,128)}, u32[]{:S(2)}) copy-start(f32[2,2,72,512]{3,2,1,0:T(8,128)} %copy-done.20) | copy-start | bytes 1769476
  93.0 36.8 %copy-start.23 = (f32[2,128,512]{2,1,0:T(8,128)S(1)}, f32[2,128,512]{2,1,0:T(8,128)}, u32[]{:S(2)}) copy-start(f32[2,128,512]{2,1,0:T(8,128)} %copy-done.22) | copy-start | bytes 1572868
  93.0 36.8 %copy-start.25 = (bf16[2,128,512]{2,1,0:T(8,128)(2,1)S(1)}, bf16[2,128,512]{2,1,0:T(8,128)(2,1)}, u32[]{:S(2)}) copy-start(bf16[2,128,512]{2,1,0:T(8,128)(2,1)} %copy-done.24) | copy-start | bytes 786436
  93.0 36.8 %copy-start.27 = (bf16[2,128,512]{2,1,0:T(8,128)(2,1)S(1)}, bf16[2,128,512]{2,1,0:T(8,128)(2,1)}, u32[]{:S(2)}) copy-start(bf16[2,128,512]{2,1,0:T(8,128)(2,1)} %copy-done.26) | copy-start | bytes 786436
  93.1 36.8 %copy-start.29 = (f32[2,2,8,512]{3,2,1,0:T(8,128)S(1)}, f32[2,2,8,512]{3,2,1,0:T(8,128)}, u32[]{:S(2)}) copy-start(f32[2,2,8,512]{3,2,1,0:T(8,128)} %copy-done.28) | copy-start | bytes 196612
  129.9 5.4 %copy-start.3 = (f32[3,512]{1,0:T(4,128)S(1)}, f32[3,512]{1,0:T(4,128)}, u32[]{:S(2)}) copy-start(f32[3,512]{1,0:T(4,128)} %residual.1) | copy-start | bytes 18436
  129.9 5.4 %copy-start.6 = (f32[8,512]{1,0:T(8,128)S(1)}, f32[8,512]{1,0:T(8,128)}, u32[]{:S(2)}) copy-start(f32[8,512]{1,0:T(8,128)} %copy-done.5) | copy-start | bytes 49156
  129.9 5.4 %copy-start.8 = (f32[8,512]{1,0:T(8,128)S(1)}, f32[8,512]{1,0:T(8,128)}, u32[]{:S(2)}) copy-start(f32[8,512]{1,0:T(8,128)} %copy-done.7) | copy-start | bytes 49156
  129.9 5.4 %copy-start.9 = (f32[3,512]{1,0:T(4,128)S(1)}, f32[3,512]{1,0:T(4,128)}, u32[]{:S(2)}) copy-start(f32[3,512]{1,0:T(4,128)} %dipoles.1) | copy-start | bytes 18436
  131.6 3.7 %collective-permute-start.18 = (f32[8,512]{1,0:T(8,128)S(1)}, f32[8,512]{1,0:T(8,128)S(1)}, u32[]{:S(2)}, u32[]{:S(2)}) collective-permute-start(f32[8,512]{1,0:T(8,128)S(1)} %shard_map.179), channel_id=1, source_target_pairs={{0,1},{1,0},{2,3},{3,2},{4,5},{5,4},{6,7},{7,6},{8,9},{9,8},{10,11... | collective-permute-start | bytes 49160 | tf_op jit(solution)/shard_map/ppermute | solution.py:636

commit v5 on v4

--- a/solution.py
+++ b/solution.py
@@ -112,10 +112,15 @@
     meta[PARITY_AT] = parity
 
 
-def call(kernel, outs, flops, smem=0, scratch=(), vmem=SMALL_VMEM):
+def call(kernel, outs, flops, smem=0, scratch=(), vmem=SMALL_VMEM, hbm=0):
     def run(*args):
+        kept = len(args) - hbm
+        args = args[:kept] + tuple(
+            pltpu.with_memory_space_constraint(array, pltpu.HBM) for array in args[kept:]
+        )
         in_specs = [pl.BlockSpec(memory_space=pltpu.SMEM)] * smem
-        in_specs += [pl.BlockSpec(memory_space=pltpu.VMEM)] * (len(args) - smem)
+        in_specs += [pl.BlockSpec(memory_space=pltpu.VMEM)] * (kept - smem)
+        in_specs += [pl.BlockSpec(memory_space=pltpu.HBM)] * hbm
         return pl.pallas_call(
             kernel,
             out_shape=[jax.ShapeDtypeStruct(shape, dtype) for shape, dtype in outs],
@@ -132,7 +137,7 @@
 
 
 def gather_kernel(send, *refs):
-    sources, (own, sent, statics), held, sems = (refs[:5], refs[5:8], refs[8:13], refs[13])
+    sources, (own, sent, bundle), held, sems = (refs[:5], refs[5:8], refs[8:13], refs[13])
     copies = [
         pltpu.make_async_copy(source, target, sems.at[at])
         for at, (source, target) in enumerate(zip(sources, held))
@@ -144,9 +149,9 @@
     residual, cells, fraction, alphas, order = held
     atoms = residual.shape[1]
     in_cells = cells[...].astype(F32)
-    statics[0:3] = in_cells
-    statics[3:6] = fraction[...]
-    statics[6:8] = jnp.zeros((2, atoms), F32)
+    bundle[0:3, :atoms] = in_cells
+    bundle[3:6, :atoms] = fraction[...]
+    bundle[6:8, :atoms] = jnp.zeros((2, atoms), F32)
     position = in_cells + fraction[...]
     rows = jnp.concatenate(
         [position, alphas[...].reshape(1, atoms), residual[...], jnp.zeros((1, atoms), F32)], 0
@@ -155,27 +160,29 @@
     for tile in range(atoms // TILE):
         own[tile] = picked[:, tile * TILE : (tile + 1) * TILE]
     for place in range(2):
-        sent[place] = own[send[0, place]]
+        block = own[send[0, place]]
+        sent[place] = block
+        bundle[:, atoms + place * TILE : atoms + (place + 1) * TILE] = block
 
 
 def search_rows(block):
     return block[3:4] * block[4:7]
 
 
-def fill_pool(pool, extents, own, straight, inner, outer, meta):
+def fill_pool(pool, extents, own, level, before, after, meta):
     inner_step = jnp.where(meta[PARITY_AT] == 0, 1.0, -1.0)
     rows = lax.broadcasted_iota(jnp.int32, (8, TILE), 0)
     for tile in range(4):
         pool[tile] = own[tile]
-    for base, source, step in ((4, straight, 0.0), (10, inner, inner_step), (16, outer, -inner_step)):
-        for along in range(3):
+    for along, source in enumerate((before, level, after)):
+        for kind, step in enumerate((0.0, inner_step, -inner_step)):
             shift = jnp.where(
                 rows == 0,
                 float((along - 1) * extents[0]),
                 jnp.where(rows == 1, step * float(extents[1]), 0.0),
             )
             for member in range(2):
-                pool[base + 2 * along + member] = source[along, member] + shift
+                pool[4 + 6 * kind + 2 * along + member] = source[kind, member] + shift
 
 
 def own_columns(columns, block, count):
@@ -193,8 +200,8 @@
 GROUP = 4
 
 
-def pair_kernel(first_place, extents, meta, own, straight, inner, outer, pool, pairs, found, columns, totals):
-    fill_pool(pool, extents, own, straight, inner, outer, meta)
+def pair_kernel(first_place, extents, meta, own, level, before, after, pool, pairs, found, columns, totals):
+    fill_pool(pool, extents, own, level, before, after, meta)
 
     def tile_step(at, carry):
         tile = meta[ORDER_AT + first_place + at]
@@ -276,13 +283,24 @@
 APPLY_ROWS = 64
 
 
-def fill_search(pool, own_first, own_rest, straight, inner, outer, meta):
+def fill_search(pool, own_first, own_rest, level, before, after, meta):
     for place in range(4):
         pool[meta[ORDER_AT + place]] = own_first[place] if place < 2 else own_rest[place - 2]
-    for base, source in ((4, straight), (10, inner), (16, outer)):
-        for along in range(3):
+    for along, source in enumerate((before, level, after)):
+        for kind in range(3):
             for member in range(2):
-                pool[base + 2 * along + member] = source[along, member]
+                pool[4 + 6 * kind + 2 * along + member] = source[kind, member]
+
+
+def join_kernel(own, inner, outer, level):
+    for member in range(2):
+        level[0, member] = own[member]
+        if len(inner.shape) == 3:
+            level[1, member] = inner[member]
+        else:
+            start = inner.shape[1] - (2 - member) * TILE
+            level[1, member] = inner[:, start : start + TILE]
+        level[2, member] = outer[member]
 
 
 def apply_tile(meta, tile, at, pairs, geometry, pool, columns, totals):
@@ -336,28 +354,37 @@
 
 
 def sweep_kernel(
-    first_place, meta, geometry, own_first, own_rest, straight, inner, outer, pairs, found, pool, columns, totals
+    first_place, meta, geometry, own_first, own_rest, level, before, after, pairs, found, pool, columns, totals
 ):
-    fill_search(pool, own_first, own_rest, straight, inner, outer, meta)
+    fill_search(pool, own_first, own_rest, level, before, after, meta)
     sweep_tiles(first_place, meta, geometry, (pairs,), found, pool, columns, totals)
 
 
 def direction_kernel(
-    meta, geometry, own_first, own_rest, straight, inner, outer, pairs_a, pairs_b, order, found, ordered, pool, columns, totals, local
+    meta, geometry, own_first, own_rest, level, before, after, pairs_a, pairs_b, order, found, sent, bundle, pool, columns, totals, local
 ):
-    fill_search(pool, own_first, own_rest, straight, inner, outer, meta)
+    atoms = order.shape[1]
+    fill_search(pool, own_first, own_rest, level, before, after, meta)
     sweep_tiles(0, meta, geometry, (pairs_a, pairs_b), found, pool, columns, totals, local)
     in_tiles = jnp.concatenate([local[tile] for tile in range(4)], 1)
-    ordered[...] = selected(in_tiles, order_matrix(order[...], order.shape[1]), NT)
+    bundle[:, :atoms] = selected(in_tiles, order_matrix(order[...], atoms), NT)
+    for place in range(2):
+        block = found[place]
+        sent[place] = block
+        bundle[:, atoms + place * TILE : atoms + (place + 1) * TILE] = block
 
 
 def final_field_kernel(
-    meta, geometry, direction, straight, inner, outer, pairs_a, pairs_b, order, applied, sums, pool, columns, totals, local
+    meta, geometry, direction, level, before, after, pairs_a, order, stored_b, applied, sums, pool, columns, totals, local, pairs_b, sem
 ):
+    copy = pltpu.make_async_copy(stored_b, pairs_b, sem.at[0])
+    copy.start()
     atoms = order.shape[1]
-    fill_search(pool, direction, direction.at[2:4], straight, inner, outer, meta)
+    fill_search(pool, direction, direction.at[2:4], level, before, after, meta)
     both = (jnp.zeros((1, TILE), F32), jnp.zeros((1, TILE), F32))
     for bank, pairs in enumerate((pairs_a, pairs_b)):
+        if bank == 1:
+            copy.wait()
 
         def tile_step(at, both):
             curve, dots = both
@@ -438,12 +465,13 @@
 def tables_kernel(meta, mine, beside, cas_high, cas_low, tab_x, tab_y, w_high, w_low, slope_z):
     cas = (cas_high[meta[PARITY_AT]], cas_low[meta[PARITY_AT]])
     for side, statics in enumerate((mine, beside)):
-        cells = statics[0:3].astype(jnp.int32)
+        atoms = tab_x.shape[3]
+        cells = statics[0:3, :atoms].astype(jnp.int32)
         for dim, out in ((0, tab_x), (1, tab_y)):
-            weights, slopes = spline(statics[3 + dim : 4 + dim])
+            weights, slopes = spline(statics[3 + dim : 4 + dim, :atoms])
             out[side, 0] = table(cells[dim : dim + 1], weights, out.shape[2], False)
             out[side, 1] = table(cells[dim : dim + 1], slopes, out.shape[2], False)
-        weights, slopes = spline(statics[5:6])
+        weights, slopes = spline(statics[5:6, :atoms])
         high, low = halves(product(cas, halves(table(cells[2:3], weights, G, True)), NN))
         w_high[side] = high
         w_low[side] = low
@@ -466,7 +494,7 @@
 
 
 def spread_own_kernel(ordered, tab_x, tab_y, w_high, w_low, slope_z, out):
-    out[...] = spread_part(0, ordered[...], tab_x, tab_y, w_high, w_low, slope_z)
+    out[...] = spread_part(0, ordered[:, : tab_x.shape[3]], tab_x, tab_y, w_high, w_low, slope_z)
 
 
 def put_lanes(out, flat):
@@ -479,7 +507,7 @@
 
 
 def spread_both_kernel(shift, meta, ordered, mine, tab_x, tab_y, w_high, w_low, slope_z, out, flat):
-    theirs = spread_part(1, ordered[...], tab_x, tab_y, w_high, w_low, slope_z)
+    theirs = spread_part(1, ordered[:, : tab_x.shape[3]], tab_x, tab_y, w_high, w_low, slope_z)
     ours = mine[...]
     width = ours.shape[1]
     even = meta[PARITY_AT] == 0
@@ -492,28 +520,46 @@
     put_lanes(out, flat)
 
 
-def plane_kernel(shapes, grid, factor, sums, x_high, x_low, y_high, y_low, out, flat):
+def plane_kernel(shapes, grid, waves, sums, *refs):
+    stored, out, flat, padded = (refs[:6], refs[6], refs[7], refs[8])
+    held, sems = (refs[9:15], refs[15])
+    copies = [
+        pltpu.make_async_copy(source, target, sems.at[at])
+        for at, (source, target) in enumerate(zip(stored, held))
+    ]
+    for copy in copies:
+        copy.start()
+    x_high, x_low, yt_high, yt_low, y_high, y_low = held
     n_slab, n_pair, x_rows, y_rows = shapes
     width = x_rows * y_rows
     flat[...] = get_lanes(grid)
-    along_x = None
+    padded[...] = jnp.zeros(padded.shape, F32)
     for s in range(n_slab):
-        block = jnp.concatenate(
-            [
-                flat[s * n_pair : (s + 1) * n_pair, y * x_rows : (y + 1) * x_rows]
-                for y in range(y_rows)
-            ],
-            0,
-        )
-        rows = slice(s * TILE, s * TILE + x_rows)
-        term = product(halves(block), (x_high[rows], x_low[rows]), NN)
-        along_x = term if along_x is None else along_x + term
-    cas_y = (y_high[...], y_low[...])
-    spectrum = product(cas_y, halves(along_x), TN)
-    scaled = spectrum * factor[...]
+        for y in range(y_rows):
+            padded[y * n_pair : (y + 1) * n_pair, s * TILE : s * TILE + x_rows] = flat[
+                s * n_pair : (s + 1) * n_pair, y * x_rows : (y + 1) * x_rows
+            ]
+    copies[0].wait()
+    copies[1].wait()
+    cas_x = (x_high[...], x_low[...])
+    along_x = product(halves(padded[...]), cas_x, NN)
+    for copy in copies[2:]:
+        copy.wait()
+    spectrum = product((yt_high[...], yt_low[...]), halves(along_x), NN)
+    freq_z = lax.axis_index("slab") * (2 * n_pair) + 2 * lax.axis_index("pair") + lax.axis_index("core")
+    ids_x = lax.broadcasted_iota(jnp.int32, (1, G), 1)
+    by_x = waves[...]
+    by_z = jnp.sum(jnp.where(ids_x == freq_z, by_x, 0.0), axis=1, keepdims=True)
+    by_y = by_x.T
+    anchor = jnp.where(
+        (lax.broadcasted_iota(jnp.int32, (G, G), 0) + lax.broadcasted_iota(jnp.int32, (G, G), 1) + freq_z) == 0, 1.0, 0.0
+    )
+    squares = by_x[0:1] + by_y[:, 0:1] + (by_z[0:1] + anchor)
+    factor = (1.0 - anchor) * (by_x[1:2] * by_z[1:2]) * by_y[:, 1:2] / (math.pi * float(G) ** 3 * squares)
+    scaled = spectrum * factor
     energy = jnp.sum(jnp.sum(spectrum * scaled, axis=0, keepdims=True), axis=1, keepdims=True)
-    back = halves(product(cas_y, halves(scaled), NN))
-    planes = product(back, (x_high[...], x_low[...]), NT)
+    back = halves(product((y_high[...], y_low[...]), halves(scaled), NN))
+    planes = product(back, cas_x, NT)
     for s in range(n_slab):
         for y in range(y_rows):
             flat[s * n_pair : (s + 1) * n_pair, y * x_rows : (y + 1) * x_rows] = planes[
@@ -560,7 +606,7 @@
 def finish_kernel(mine, theirs, ordered, applied, dipoles, residual, next_dipoles, next_residual, direction):
     total = mine[...] + theirs[...]
     step = total[3:4, 2:3] / (total[3:4, 0:1] + total[3:4, 1:2])
-    d = ordered[0:3]
+    d = ordered[0:3, : dipoles.shape[1]]
     next_dipoles[...] = dipoles[...] + step * d
     next_residual[...] = residual[...] - step * (applied[0:3] + total[0:3])
     direction[...] = d
@@ -578,29 +624,15 @@
     return (jnp.asarray(high), jnp.asarray(low))
 
 
-def wave_factors(freq_ids):
-    wrapped = jnp.where(freq_ids > G // 2, freq_ids - G, freq_ids).astype(F32) / G
-    angles = 2.0 * math.pi / G * freq_ids.astype(F32)
-    modulus = 115.0 / 192.0 + 19.0 / 48.0 * jnp.cos(angles) + 1.0 / 192.0 * jnp.cos(2.0 * angles)
-    return (
-        wrapped * wrapped,
-        jnp.exp(-((math.pi / BETA) ** 2) * wrapped * wrapped) / (modulus * modulus),
-    )
-
-
-def multiplier(freq_x, freq_y, freq_z):
-    square_x, factor_x = wave_factors(freq_x)
-    square_y, factor_y = wave_factors(freq_y)
-    square_z, factor_z = wave_factors(freq_z)
-    square_sum = square_x + square_y + square_z
-    anchor = ((freq_x == 0) & (freq_y == 0) & (freq_z == 0)).astype(F32)
-    return (
-        (1.0 - anchor)
-        * factor_x
-        * factor_y
-        * factor_z
-        / (math.pi * float(G) ** 3 * (square_sum + anchor))
-    )
+def wave_factors():
+    freq = np.arange(G)
+    wrapped = np.where(freq > G // 2, freq - G, freq) / G
+    angles = 2.0 * np.pi / G * freq
+    modulus = 115.0 / 192.0 + 19.0 / 48.0 * np.cos(angles) + 1.0 / 192.0 * np.cos(2.0 * angles)
+    rows = np.zeros((8, G), np.float32)
+    rows[0] = wrapped * wrapped
+    rows[1] = np.exp(-((np.pi / BETA) ** 2) * wrapped * wrapped) / (modulus * modulus)
+    return jnp.asarray(rows)
 
 
 def swap_pairs(n_slab, n_space, odd):
@@ -612,30 +644,25 @@
     return pairs
 
 
-def along_slab(block):
+def beside(block, odd):
+    n_slab, n_space = (lax.axis_size("slab"), lax.axis_size(SPACE))
+    return lax.ppermute(block, BOTH, swap_pairs(n_slab, n_space, odd))
+
+
+def along_slab(level):
     n_slab = lax.axis_size("slab")
     up = [(i, (i + 1) % n_slab) for i in range(n_slab)]
     down = [(j, i) for i, j in up]
-    before = lax.ppermute(block, "slab", up)
-    after = lax.ppermute(block, "slab", down)
-    return jnp.stack([before, block, after])
-
-
-def across_space(straight):
-    n_slab, n_space = (lax.axis_size("slab"), lax.axis_size(SPACE))
-    inner = lax.ppermute(straight, BOTH, swap_pairs(n_slab, n_space, False))
-    outer = lax.ppermute(straight, BOTH, swap_pairs(n_slab, n_space, True))
-    return (straight, inner, outer)
-
-
-def around(block):
-    return across_space(along_slab(block))
-
-
-def from_core_beside(block):
-    return lax.ppermute(
-        block, BOTH, swap_pairs(lax.axis_size("slab"), lax.axis_size(SPACE), False)
-    )
+    return (level, lax.ppermute(level, "slab", up), lax.ppermute(level, "slab", down))
+
+
+def joined(block, inner, outer):
+    return call(join_kernel, [((3, 2, 8, TILE), F32)], 10**6)(block, inner, outer)[0]
+
+
+def around(block, bundle=None):
+    inner = beside(block if bundle is None else bundle, False)
+    return along_slab(joined(block, inner, beside(block, True))), inner
 
 
 def local(
@@ -650,7 +677,6 @@
     pair_rows = 2 * extents[1] + 4
     shift = extents[1] * x_rows
     half = G // 2
-    slab_index, space_index = (lax.axis_index("slab"), lax.axis_index(SPACE))
     tile_shape = ((4, 8, TILE), F32)
     two_shape = ((2, 8, TILE), F32)
     bank_shape = ((3, 16, TILE, TILE), F32)
@@ -661,7 +687,7 @@
         out_shape=[
             jax.ShapeDtypeStruct(*tile_shape),
             jax.ShapeDtypeStruct(*two_shape),
-            jax.ShapeDtypeStruct((8, atoms), F32),
+            jax.ShapeDtypeStruct((8, atoms + 2 * TILE), F32),
         ],
         in_specs=[pl.BlockSpec(memory_space=pltpu.SMEM)] + [pl.BlockSpec(memory_space=pltpu.HBM)] * 5,
         out_specs=[pl.BlockSpec(memory_space=pltpu.VMEM)] * 3,
@@ -689,7 +715,7 @@
         out_specs=smem,
         cost_estimate=pl.CostEstimate(flops=10**8, bytes_accessed=1 << 20, transcendentals=0),
     )(tile_lists, tile_counts, send_tiles, sent)
-    first = around(sent)
+    first, statics_beside = around(sent, statics)
 
     def pairs_of(first_place):
         return call(
@@ -703,7 +729,7 @@
     geometry, pairs_a, search_a = pairs_of(0)
     _, pairs_b, search_b = pairs_of(2)
     sweep_scratch = (pool_scratch, pltpu.VMEM((3, TILE, TILE), F32), total_scratch)
-    second = around(search_a)
+    second, _ = around(search_a)
 
     def sweep(first_place, pairs):
         return call(
@@ -716,16 +742,16 @@
 
     next_a = sweep(0, pairs_a)
     next_b = sweep(2, pairs_b)
-    third = around(next_a)
+    third, _ = around(next_a)
     local_scratch = pltpu.VMEM((4, 8, TILE), F32)
-    direction, ordered = call(
+    direction, sent, ordered = call(
         direction_kernel,
-        [tile_shape, ((8, atoms), F32)],
+        [tile_shape, two_shape, ((8, atoms + 2 * TILE), F32)],
         10**8,
         smem=1,
         scratch=sweep_scratch + (local_scratch,),
     )(meta, geometry, next_a, next_b, *third, pairs_a, pairs_b, tile_order)
-    ordered_beside = from_core_beside(ordered)
+    ordered_beside, outer = (beside(ordered, False), beside(sent, True))
     freq = np.arange(G)
     padded_x = np.stack([(s * extents[0] + np.arange(x_rows) - 2) % G for s in range(n_slab)])
     real_x = np.tile(np.arange(x_rows) < extents[0] + 4, n_slab)
@@ -736,7 +762,6 @@
     cas_z = cas_matrix(freq_by_core.reshape(-1), freq).reshape(2, half, G)
     wide_x = np.zeros((n_slab, TILE, G))
     wide_x[:, :x_rows] = cas_x.reshape(n_slab, x_rows, G)
-    statics, _ = lax.optimization_barrier((statics, first[1]))
     tables = call(
         tables_kernel,
         [
@@ -749,7 +774,7 @@
         10**8,
         smem=1,
         vmem=LARGE_VMEM,
-    )(meta, statics, from_core_beside(statics), *split_constant(cas_z))
+    )(meta, statics, statics_beside, *split_constant(cas_z))
     message = ((half, 8, TILE), F32)
     flat_scratch = pltpu.VMEM((half, 8 * TILE), F32)
     spread_own = call(spread_own_kernel, [((half, x_rows * y_rows), F32)], 10**9, vmem=LARGE_VMEM)(ordered, *tables)[0]
@@ -761,29 +786,36 @@
         scratch=(flat_scratch,),
         vmem=LARGE_VMEM,
     )(meta, ordered_beside, spread_own, *tables)[0]
-    spread, straight = lax.optimization_barrier((spread, along_slab(direction[:2])))
+    spread, outer = lax.optimization_barrier((spread, outer))
     grid = lax.all_to_all(spread, CHIPS, 0, 0, tiled=True)
-    last = across_space(straight)
+    last = along_slab(joined(sent, ordered_beside, outer))
     applied, sums = call(
         final_field_kernel,
         [((8, atoms), F32), ((8, TILE), F32)],
         10**9,
         smem=1,
-        scratch=sweep_scratch + (local_scratch,),
-    )(meta, geometry, direction, *last, pairs_a, pairs_b, tile_order)
-    ids = jnp.arange(G, dtype=jnp.int32)
-    factor = multiplier(ids[None, :], ids[:, None], slab_index * n_space + space_index)
+        scratch=sweep_scratch
+        + (local_scratch, pltpu.VMEM(*bank_shape), pltpu.SemaphoreType.DMA((1,))),
+        vmem=LARGE_VMEM,
+        hbm=1,
+    )(meta, geometry, direction, *last, pairs_a, tile_order, pairs_b)
     planes = call(
         functools.partial(plane_kernel, (n_slab, n_pair, x_rows, pair_rows)),
         [message],
         10**9,
-        scratch=(flat_scratch,),
+        scratch=(flat_scratch, pltpu.VMEM((n_pair * pair_rows, n_slab * TILE), F32))
+        + (pltpu.VMEM((n_slab * TILE, G), BF16),) * 2
+        + (pltpu.VMEM((G, n_pair * pair_rows), BF16),) * 2
+        + (pltpu.VMEM((n_pair * pair_rows, G), BF16),) * 2
+        + (pltpu.SemaphoreType.DMA((6,)),),
         vmem=LARGE_VMEM,
+        hbm=6,
     )(
         grid,
-        factor,
+        wave_factors(),
         sums,
         *split_constant(wide_x.reshape(-1, G)),
+        *split_constant(cas_y.T),
         *split_constant(cas_y),
     )[0]
     returned = lax.all_to_all(planes, CHIPS, 0, 0, tiled=True)
@@ -793,11 +825,11 @@
             functools.partial(probe_kernel, side, shift), [((8, atoms), F32)], 10**9, smem=1, vmem=LARGE_VMEM
         )(meta, returned, *tables)[0]
 
-    beside = from_core_beside(probe(1))
+    theirs = beside(probe(1), False)
     three = ((3, atoms), F32)
     return tuple(
         call(finish_kernel, [three, three, three], 10**6)(
-            probe(0), beside, ordered, applied, dipoles, residual
+            probe(0), theirs, ordered, applied, dipoles, residual
         )
     )
 

time: 136 us -> 131 us (0.963)
  blocking collectives: 32.5 us -> 24.4 us
  waiting for transfers between devices: 13 us -> 21.1 us
  Pallas kernels: 34.7 us -> 41.4 us
  local copies, waits for them, and re-layouts: 8.43 us -> 2.24 us
  starting transfers between devices: 46 us -> 40.4 us
    all_to_all x1, waiting for transfers between devices: 0.01 us -> 10 us  [local(): grid = lax.all_to_all(spread, CHIPS, 0, 0, tiled=True)]
    all_to_all x1, blocking collectives: 32.5 us -> 24.4 us  [local(): returned = lax.all_to_all(planes, CHIPS, 0, 0, tiled=True)]
    ppermute x19 -> x17, starting transfers between devices: 38.4 us -> 31.6 us  [the longest x9 20.8 us: beside(): return lax.ppermute(block, BOTH, swap_pairs(n_slab, n_space, odd))]
    pallas_call x13 -> x17, Pallas kernels: 31.4 us -> 38.1 us  [run(): pl.pallas_call(kernel, out_shape=[jax.ShapeDtypeStruct(shape, dtype) for...]
    unnamed x60 -> x40, local copies, waits for them, and re-layouts: 8.43 us -> 2.24 us
    ppermute x19 -> x17, waiting for transfers between devices: 13 us -> 11 us  [the longest x9 9.23 us: beside(): return lax.ppermute(block, BOTH, swap_pairs(n_slab, n_space, odd))]
  transfers between devices with their start and end apart: 20 -> 18, of which waited for: 6 -> 7; matrix products, arithmetic and copies ran while one was open for 0% -> 0% of each run, Pallas kernels for 12% -> 16%
where the time goes in v5:
time: 131 us; the launch traced here: 130 us
  Pallas kernels  41.4 us (32%)
  starting transfers between devices  40.4 us (31%)
  blocking collectives  24.4 us (19%)
  waiting for transfers between devices  21.1 us (16%)
  local copies, waits for them, and re-layouts  2.24 us (2%)
    pallas_call x17, Pallas kernels, run(): pl.pallas_call(kernel, out_shape=[jax.ShapeDtypeStruct(shape, dtype) for...  38.1 us
    all_to_all x1, blocking collectives, local(): returned = lax.all_to_all(planes, CHIPS, 0, 0, tiled=True)  24.4 us
    ppermute x9, starting transfers between devices, beside(): return lax.ppermute(block, BOTH, swap_pairs(n_slab, n_space, odd))  20.8 us
    all_to_all x1, waiting for transfers between devices, local(): grid = lax.all_to_all(spread, CHIPS, 0, 0, tiled=True)  10 us
    ppermute x9, waiting for transfers between devices, beside(): return lax.ppermute(block, BOTH, swap_pairs(n_slab, n_space, odd))  9.23 us
    ppermute x4, starting transfers between devices, along_slab(): lax.ppermute(level, 'slab', down)  8.88 us
    all_to_all x1, starting transfers between devices, local(): grid = lax.all_to_all(spread, CHIPS, 0, 0, tiled=True)  8.81 us
  transfers between devices with their start and end apart: 18, of which 7 were waited for; matrix products, arithmetic and copies ran while one was open for 0% of the time, Pallas kernels for 16%

profile of v5, /device:TPU:1, one launch (start us, length us, event | category | flops | bytes accessed | tf_op | source)
XLA Modules:
  0.0 130.5 jit_solution(11606964182956816238)
XLA Ops:
  0.6 0.0 copy-start.8
  0.6 0.6 copy-done.8
  1.3 1.5 %shard_map.193 = (f32[4,8,128]{2,1,0:T(8,128)S(1)}, f32[2,8,128]{2,1,0:T(8,128)S(1)}, f32[8,768]{1,0:T(8,128)S(1)}) custom-call(s32[1,2]{1,0:T(1,128)S(1)} %copy-done.8, f32[3,512]{1,0:T(4,128)} %residual.1, s32[3,512]{1,0:T(4,128)} %refs_1_.2, f32[3,512]{1,0:T(4,128)} %refs_2_.2, f32[512]{0:T(512)} %refs_3_.2, s32[1,512]{1,0:T(1,128)} %order.3), custom_call_target="tpu_custom_call" | custom-call | tf_op jit(solution)/shard_map/pallas_call | solution.py:685
  2.8 0.0 copy-start.5
  2.9 3.3 %collective-permute-start = (f32[8,768]{1,0:T(8,128)S(1)}, f32[8,768]{1,0:T(8,128)S(1)}, u32[]{:S(2)}, u32[]{:S(2)}) collective-permute-start(f32[8,768]{1,0:T(8,128)S(1)} %get-tuple-element.25.mine), channel_id=1, source_target_pairs={{0,1},{1,0},{2,3},{3,2},{4,5},{5,4},{6,7},{7,6},{8,9},{9,8},{10,11... | collective-permute-start | bytes 73736 | tf_op jit(solution)/shard_map/ppermute | solution.py:649
  6.2 0.0 collective-permute-start.1
  6.2 3.1 %collective-permute-done.1.outer = f32[2,8,128]{2,1,0:T(8,128)S(1)} collective-permute-done((f32[2,8,128]{2,1,0:T(8,128)S(1)}, f32[2,8,128]{2,1,0:T(8,128)S(1)}, u32[]{:S(2)}, u32[]{:S(2)}) %collective-permute-start.1) | collective-permute-done | bytes 8224 | tf_op jit(solution)/shard_map/ppermute | solution.py:649
  9.3 0.0 collective-permute-done.inner.beside
  9.3 0.0 collective-permute-start.2
  9.3 2.7 %collective-permute-start.3 = (f32[3,2,8,128]{3,2,1,0:T(8,128)S(1)}, f32[3,2,8,128]{3,2,1,0:T(8,128)S(1)}, u32[]{:S(2)}, u32[]{:S(2)}) collective-permute-start(f32[3,2,8,128]{3,2,1,0:T(8,128)S(1)} %shard_map.195.level), channel_id=1, source_target_pairs={{64,0},{128,64},{192,128},{0,192},{65,1},{129,65},{193,129},{1,193... | collective-permute-start | bytes 73736 | tf_op jit(solution)/shard_map/ppermute | solution.py:656
  11.9 1.8 %shard_map.194.meta = s32[48]{0:T(128)} custom-call(s32[1,4,8]{2,1,0:T(4,128)} %lists.1, s32[1,4]{1,0:T(1,128)} %counts.1, s32[1,2]{1,0:T(1,128)} %send.3, f32[2,8,128]{2,1,0:T(8,128)} %copy-done.5), custom_call_target="tpu_custom_call" | custom-call | flops 100000000 | bytes 1048576 | tf_op jit(solution)/shard_map/pallas_call | solution.py:711
  13.7 0.0 copy-start.7
  13.8 0.0 collective-permute-done.2.before
  13.8 0.0 collective-permute-done.3.after
  13.8 0.7 copy-done.6
  14.5 5.1 %shard_map.196 = (f32[22,8,128]{2,1,0:T(8,128)S(1)}, f32[3,16,128,128]{3,2,1,0:T(8,128)S(1)}, f32[2,8,128]{2,1,0:T(8,128)S(1)}) custom-call(s32[48]{0:T(128)S(1)} %copy-done.6, f32[4,8,128]{2,1,0:T(8,128)S(1)} %get-tuple-element.24.own, f32[3,2,8,128]{3,2,1,0:T(8,128)S(1)} %shard_map.195.level, f32[3,2,8,128]{3,2,1,0:T(8,128)S(1)} %collective-permute-done.2.before, ...), custom_call_target="tpu_custom_call" | custom-call | flops 1000000000 | bytes 1048576 | tf_op jit(solution)/shard_map/pallas_call | solution.py:124
  19.5 5.8 %collective-permute-start.4 = (f32[2,8,128]{2,1,0:T(8,128)S(1)}, f32[2,8,128]{2,1,0:T(8,128)S(1)}, u32[]{:S(2)}, u32[]{:S(2)}) collective-permute-start(f32[2,8,128]{2,1,0:T(8,128)S(1)} %get-tuple-element.27.own.own_first), channel_id=1, source_target_pairs={{0,1},{1,0},{2,3},{3,2},{4,5},{5,4},{6,7},{7,6},{8,9},{9,8},{10,11... | collective-permute-start | bytes 24584 | tf_op jit(solution)/shard_map/ppermute | solution.py:649
  25.4 0.0 collective-permute-start.5
  25.4 0.8 collective-permute-done.4.inner
  26.2 2.2 %collective-permute-done.5.outer = f32[2,8,128]{2,1,0:T(8,128)S(1)} collective-permute-done((f32[2,8,128]{2,1,0:T(8,128)S(1)}, f32[2,8,128]{2,1,0:T(8,128)S(1)}, u32[]{:S(2)}, u32[]{:S(2)}) %collective-permute-start.5) | collective-permute-done | bytes 8224 | tf_op jit(solution)/shard_map/ppermute | solution.py:649
  28.4 1.3 collective-permute-start.6
  29.7 1.5 %collective-permute-start.7 = (f32[3,2,8,128]{3,2,1,0:T(8,128)S(1)}, f32[3,2,8,128]{3,2,1,0:T(8,128)S(1)}, u32[]{:S(2)}, u32[]{:S(2)}) collective-permute-start(f32[3,2,8,128]{3,2,1,0:T(8,128)S(1)} %shard_map.198.level), channel_id=1, source_target_pairs={{64,0},{128,64},{192,128},{0,192},{65,1},{129,65},{193,129},{1,193... | collective-permute-start | bytes 73736 | tf_op jit(solution)/shard_map/ppermute | solution.py:656
  31.2 0.0 copy-done.7
  31.2 5.5 %shard_map.197 = (f32[22,8,128]{2,1,0:T(8,128)}, f32[3,16,128,128]{3,2,1,0:T(8,128)S(1)}, f32[2,8,128]{2,1,0:T(8,128)S(1)}) custom-call(s32[48]{0:T(128)S(1)} %copy-done.7, f32[4,8,128]{2,1,0:T(8,128)S(1)} %get-tuple-element.24.own, f32[3,2,8,128]{3,2,1,0:T(8,128)S(1)} %shard_map.195.level, f32[3,2,8,128]{3,2,1,0:T(8,128)S(1)} %collective-permute-done.2.before, ...), custom_call_target="tpu_custom_call" | custom-call | flops 1000000000 | bytes 1048576 | tf_op jit(solution)/shard_map/pallas_call | solution.py:124
  36.7 0.0 collective-permute-done.6.before
  36.7 0.0 collective-permute-done.7.after
  36.7 0.0 copy-start.3
  36.7 2.2 %shard_map.199.own.own_first = f32[2,8,128]{2,1,0:T(8,128)S(1)} custom-call(s32[48]{0:T(128)S(1)} %copy-done.7, f32[22,8,128]{2,1,0:T(8,128)S(1)} %get-tuple-element.26.geometry, f32[2,8,128]{2,1,0:T(8,128)S(1)} %get-tuple-element.27.own.own_first, f32[2,8,128]{2,1,0:T(8,128)S(1)} %get-tuple-element.28.own_rest, f32[3,2,8,128]{3,2,1,0:T(8,128)S(1)} %shard_map.198.level, ...), custom_call_target="tpu_custom_call" | custom-call | flops 100000000 | bytes 1048576 | tf_op jit(solution)/shard_map/pallas_call | solution.py:124
  38.9 4.1 %collective-permute-start.8 = (f32[2,8,128]{2,1,0:T(8,128)S(1)}, f32[2,8,128]{2,1,0:T(8,128)S(1)}, u32[]{:S(2)}, u32[]{:S(2)}) collective-permute-start(f32[2,8,128]{2,1,0:T(8,128)S(1)} %shard_map.199.own.own_first), channel_id=1, source_target_pairs={{0,1},{1,0},{2,3},{3,2},{4,5},{5,4},{6,7},{7,6},{8,9},{9,8},{10,11... | collective-permute-start | bytes 24584 | tf_op jit(solution)/shard_map/ppermute | solution.py:649
  43.0 0.0 collective-permute-start.9
  43.0 0.8 collective-permute-done.8.inner
  43.8 2.2 %collective-permute-done.9.outer = f32[2,8,128]{2,1,0:T(8,128)S(1)} collective-permute-done((f32[2,8,128]{2,1,0:T(8,128)S(1)}, f32[2,8,128]{2,1,0:T(8,128)S(1)}, u32[]{:S(2)}, u32[]{:S(2)}) %collective-permute-start.9) | collective-permute-done | bytes 8224 | tf_op jit(solution)/shard_map/ppermute | solution.py:649
  46.0 0.0 collective-permute-start.10
  46.0 2.7 %collective-permute-start.11 = (f32[3,2,8,128]{3,2,1,0:T(8,128)S(1)}, f32[3,2,8,128]{3,2,1,0:T(8,128)S(1)}, u32[]{:S(2)}, u32[]{:S(2)}) collective-permute-start(f32[3,2,8,128]{3,2,1,0:T(8,128)S(1)} %shard_map.201.level), channel_id=1, source_target_pairs={{64,0},{128,64},{192,128},{0,192},{65,1},{129,65},{193,129},{1,193... | collective-permute-start | bytes 73736 | tf_op jit(solution)/shard_map/ppermute | solution.py:656
  48.7 0.0 copy-done.9
  48.7 2.4 %shard_map.203 = (f32[2,2,72,512]{3,2,1,0:T(8,128)S(1)}, f32[2,2,8,512]{3,2,1,0:T(8,128)S(1)}, bf16[2,128,512]{2,1,0:T(8,128)(2,1)S(1)}, bf16[2,128,512]{2,1,0:T(8,128)(2,1)S(1)}, f32[2,128,512]{2,1,0:T(8,128)S(1)}) custom-call(s32[48]{0:T(128)S(1)} %copy-done.7, f32[8,768]{1,0:T(8,128)S(1)} %get-tuple-element.25.mine, ...), custom_call_target="tpu_custom_call" | custom-call | flops 100000000 | bytes 1048576 | tf_op jit(solution)/shard_map/pallas_call | solution.py:124
  51.2 2.2 %shard_map.200.own_rest = f32[2,8,128]{2,1,0:T(8,128)S(1)} custom-call(s32[48]{0:T(128)S(1)} %copy-done.7, f32[22,8,128]{2,1,0:T(8,128)S(1)} %get-tuple-element.26.geometry, f32[2,8,128]{2,1,0:T(8,128)S(1)} %get-tuple-element.27.own.own_first, f32[2,8,128]{2,1,0:T(8,128)S(1)} %get-tuple-element.28.own_rest, f32[3,2,8,128]{3,2,1,0:T(8,128)S(1)} %shard_map.198.level, ...), custom_call_target="tpu_custom_call" | custom-call | flops 100000000 | bytes 1048576 | tf_op jit(solution)/shard_map/pallas_call | solution.py:124
  53.3 0.0 collective-permute-done.10.before
  53.3 0.0 collective-permute-done.11.after
  53.3 0.0 copy-done
  53.4 4.1 %shard_map.202 = (f32[4,8,128]{2,1,0:T(8,128)S(1)}, f32[2,8,128]{2,1,0:T(8,128)S(1)}, f32[8,768]{1,0:T(8,128)S(1)}) custom-call(s32[48]{0:T(128)S(1)} %copy-done.7, f32[22,8,128]{2,1,0:T(8,128)S(1)} %get-tuple-element.26.geometry, f32[2,8,128]{2,1,0:T(8,128)S(1)} %shard_map.199.own.own_first, f32[2,8,128]{2,1,0:T(8,128)S(1)} %shard_map.200.own_rest, ...), custom_call_target="tpu_custom_call" | custom-call | flops 100000000 | bytes 1048576 | tf_op jit(solution)/shard_map/pallas_call | solution.py:124
  57.4 4.1 %collective-permute-start.12 = (f32[8,768]{1,0:T(8,128)S(1)}, f32[8,768]{1,0:T(8,128)S(1)}, u32[]{:S(2)}, u32[]{:S(2)}) collective-permute-start(f32[8,768]{1,0:T(8,128)S(1)} %get-tuple-element.31.ordered), channel_id=1, source_target_pairs={{0,1},{1,0},{2,3},{3,2},{4,5},{5,4},{6,7},{7,6},{8,9},{9,8},{10,11... | collective-permute-start | bytes 73736 | tf_op jit(solution)/shard_map/ppermute | solution.py:649
  61.5 0.0 collective-permute-start.13
  61.5 1.3 %shard_map.204.mine = f32[128,576]{1,0:T(8,128)S(1)} custom-call(f32[8,768]{1,0:T(8,128)S(1)} %get-tuple-element.31.ordered, f32[2,2,72,512]{3,2,1,0:T(8,128)S(1)} %get-tuple-element.32.tab_x, f32[2,2,8,512]{3,2,1,0:T(8,128)S(1)} %get-tuple-element.33.tab_y, bf16[2,128,512]{2,1,0:T(8,128)(2,1)S(1)} %get-tuple-element.34.w_high, ...), custom_call_target="tpu_custom_call" | custom-call | flops 1000000000 | bytes 1048576 | tf_op jit(solution)/shard_map/pallas_call | solution.py:124
  62.9 0.0 collective-permute-done.12.ordered.inner
  62.9 2.2 %shard_map.205 = f32[128,8,128]{2,1,0:T(8,128)S(1)} custom-call(s32[48]{0:T(128)S(1)} %copy-done.7, f32[8,768]{1,0:T(8,128)S(1)} %collective-permute-done.12.ordered.inner, f32[128,576]{1,0:T(8,128)S(1)} %shard_map.204.mine, f32[2,2,72,512]{3,2,1,0:T(8,128)S(1)} %get-tuple-element.32.tab_x, f32[2,2,8,512]{3,2,1,0:T(8,128)S(1)} %get-tuple-element.33.tab_y, ...), custom_call_target="tpu_custom_call" | custom-call | flops 1000000000 | bytes 1048576 | tf_op jit(solution)/shard_map/pallas_call | solution.py:124
  65.1 0.8 copy-done.1
  65.9 0.0 collective-permute-done.13.outer
  65.9 8.8 %all-to-all-start = ((f32[128,8,128]{2,1,0:T(8,128)}), f32[128,8,128]{2,1,0:T(8,128)}, u32[]{:S(2)}, u32[]{:S(2)}) async-start(f32[128,8,128]{2,1,0:T(8,128)} %copy-done.1), calls=%async_computation | async-start | bytes 1048576 | tf_op jit(solution)/shard_map/all_to_all | solution.py:790
  74.7 0.7 collective-permute-start.14
  75.4 2.1 %collective-permute-start.15 = (f32[3,2,8,128]{3,2,1,0:T(8,128)S(1)}, f32[3,2,8,128]{3,2,1,0:T(8,128)S(1)}, u32[]{:S(2)}, u32[]{:S(2)}) collective-permute-start(f32[3,2,8,128]{3,2,1,0:T(8,128)S(1)} %shard_map.206.level), channel_id=1, source_target_pairs={{64,0},{128,64},{192,128},{0,192},{65,1},{129,65},{193,129},{1,193... | collective-permute-start | bytes 73736 | tf_op jit(solution)/shard_map/ppermute | solution.py:656
  77.5 1.8 %collective-permute-done.14.before = f32[3,2,8,128]{3,2,1,0:T(8,128)S(1)} collective-permute-done((f32[3,2,8,128]{3,2,1,0:T(8,128)S(1)}, f32[3,2,8,128]{3,2,1,0:T(8,128)S(1)}, u32[]{:S(2)}, u32[]{:S(2)}) %collective-permute-start.14) | collective-permute-done | bytes 24608 | tf_op jit(solution)/shard_map/ppermute | solution.py:656
  79.3 0.0 collective-permute-done.15.after
  79.3 4.4 %shard_map.207 = (f32[8,512]{1,0:T(8,128)S(1)}, f32[8,128]{1,0:T(8,128)S(1)}) custom-call(s32[48]{0:T(128)S(1)} %copy-done.7, f32[22,8,128]{2,1,0:T(8,128)S(1)} %get-tuple-element.26.geometry, f32[4,8,128]{2,1,0:T(8,128)S(1)} %get-tuple-element.39.direction, f32[3,2,8,128]{3,2,1,0:T(8,128)S(1)} %shard_map.206.level, ...), custom_call_target="tpu_custom_call" | custom-call | flops 1000000000 | bytes 1048576 | tf_op jit(solution)/shard_map/pallas_call | solution.py:124
  83.7 10.0 %all-to-all-done.grid = f32[128,8,128]{2,1,0:T(8,128)} async-done(((f32[128,8,128]{2,1,0:T(8,128)}), f32[128,8,128]{2,1,0:T(8,128)}, u32[]{:S(2)}, u32[]{:S(2)}) %all-to-all-start) | async-done | bytes 524320 | tf_op jit(solution)/shard_map/all_to_all | solution.py:790
  93.7 4.7 %shard_map.208 = f32[128,8,128]{2,1,0:T(8,128)S(1)} custom-call(f32[128,8,128]{2,1,0:T(8,128)} %all-to-all-done.grid, f32[8,256]{1,0:T(8,128)S(1)} %copy-done.11, f32[8,128]{1,0:T(8,128)S(1)} %get-tuple-element.41.sums, bf16[512,256]{1,0:T(8,128)(2,1)} %constant.21.clone.refs_0_, bf16[512,256]{1,0:T(8,128)(2,1)} %constant.22.clone.refs_1_, ...), custom_call_target="tpu_custom_call" | custom-call | flops 1000000000 | bytes 1048576 | tf_op jit(solution)/shard_map/pallas_call | solution.py:124
  98.4 24.4 %all_to_all.10.grid = f32[128,8,128]{2,1,0:T(8,128)S(1)} all-to-all(f32[128,8,128]{2,1,0:T(8,128)S(1)} %shard_map.208), channel_id=1, replica_groups=mesh['slab'=4,'pair'=32,'core'=2] {'slab','pair'}, dimensions={0} | all-to-all | bytes 1048576 | tf_op jit(solution)/shard_map/all_to_all | solution.py:821
  122.8 0.0 copy-start.2
  122.8 0.0 copy-start.4
  122.8 1.7 %shard_map.210 = f32[8,512]{1,0:T(8,128)S(1)} custom-call(s32[48]{0:T(128)S(1)} %copy-done.7, f32[128,8,128]{2,1,0:T(8,128)S(1)} %all_to_all.10.grid, f32[2,2,72,512]{3,2,1,0:T(8,128)S(1)} %copy-done.13, f32[2,2,8,512]{3,2,1,0:T(8,128)S(1)} %get-tuple-element.33.tab_y, bf16[2,128,512]{2,1,0:T(8,128)(2,1)S(1)} %copy-done.17, ...), custom_call_target="tpu_custom_call" | custom-call | flops 1000000000 | bytes 1048576 | tf_op jit(solution)/shard_map/pallas_call | solution.py:124
  124.5 3.5 %collective-permute-start.16 = (f32[8,512]{1,0:T(8,128)S(1)}, f32[8,512]{1,0:T(8,128)S(1)}, u32[]{:S(2)}, u32[]{:S(2)}) collective-permute-start(f32[8,512]{1,0:T(8,128)S(1)} %shard_map.210), channel_id=1, source_target_pairs={{0,1},{1,0},{2,3},{3,2},{4,5},{5,4},{6,7},{7,6},{8,9},{9,8},{10,11... | collective-permute-start | bytes 49160 | tf_op jit(solution)/shard_map/ppermute | solution.py:649
  127.9 1.7 %shard_map.209.mine = f32[8,512]{1,0:T(8,128)S(1)} custom-call(s32[48]{0:T(128)S(1)} %copy-done.7, f32[128,8,128]{2,1,0:T(8,128)S(1)} %all_to_all.10.grid, f32[2,2,72,512]{3,2,1,0:T(8,128)S(1)} %copy-done.13, f32[2,2,8,512]{3,2,1,0:T(8,128)S(1)} %get-tuple-element.33.tab_y, bf16[2,128,512]{2,1,0:T(8,128)(2,1)S(1)} %copy-done.17, ...), custom_call_target="tpu_custom_call" | custom-call | flops 1000000000 | bytes 1048576 | tf_op jit(solution)/shard_map/pallas_call | solution.py:124
  129.6 0.0 collective-permute-done.16.theirs
  129.6 0.9 shard_map.211
  (32 shorter events, 0.1 us)
Async XLA Ops:
  0.6 0.7 copy-start.8
  2.8 9.1 %copy-start.5 = (f32[2,8,128]{2,1,0:T(8,128)}, f32[2,8,128]{2,1,0:T(8,128)S(1)}, u32[]{:S(2)}) copy-start(f32[2,8,128]{2,1,0:T(8,128)S(1)} %get-tuple-element.23.after.own) | copy-start | bytes 24580
  2.9 6.4 %collective-permute-start = (f32[8,768]{1,0:T(8,128)S(1)}, f32[8,768]{1,0:T(8,128)S(1)}, u32[]{:S(2)}, u32[]{:S(2)}) collective-permute-start(f32[8,768]{1,0:T(8,128)S(1)} %get-tuple-element.25.mine), channel_id=1, source_target_pairs={{0,1},{1,0},{2,3},{3,2},{4,5},{5,4},{6,7},{7,6},{8,9},{9,8},{10,11... | collective-permute-start | bytes 73736 | tf_op jit(solution)/shard_map/ppermute | solution.py:649
  6.2 3.1 %collective-permute-start.1 = (f32[2,8,128]{2,1,0:T(8,128)S(1)}, f32[2,8,128]{2,1,0:T(8,128)S(1)}, u32[]{:S(2)}, u32[]{:S(2)}) collective-permute-start(f32[2,8,128]{2,1,0:T(8,128)S(1)} %get-tuple-element.23.after.own), channel_id=1, source_target_pairs={{0,63},{1,2},{2,1},{3,4},{4,3},{5,6},{6,5},{7,8},{8,7},{9,10},{10,... | collective-permute-start | bytes 24584 | tf_op jit(solution)/shard_map/ppermute | solution.py:649
  9.3 4.5 %collective-permute-start.2 = (f32[3,2,8,128]{3,2,1,0:T(8,128)S(1)}, f32[3,2,8,128]{3,2,1,0:T(8,128)S(1)}, u32[]{:S(2)}, u32[]{:S(2)}) collective-permute-start(f32[3,2,8,128]{3,2,1,0:T(8,128)S(1)} %shard_map.195.level), channel_id=1, source_target_pairs={{0,64},{64,128},{128,192},{192,0},{1,65},{65,129},{129,193},{193,1... | collective-permute-start | bytes 73736 | tf_op jit(solution)/shard_map/ppermute | solution.py:656
  9.3 4.5 %collective-permute-start.3 = (f32[3,2,8,128]{3,2,1,0:T(8,128)S(1)}, f32[3,2,8,128]{3,2,1,0:T(8,128)S(1)}, u32[]{:S(2)}, u32[]{:S(2)}) collective-permute-start(f32[3,2,8,128]{3,2,1,0:T(8,128)S(1)} %shard_map.195.level), channel_id=1, source_target_pairs={{64,0},{128,64},{192,128},{0,192},{65,1},{129,65},{193,129},{1,193... | collective-permute-start | bytes 73736 | tf_op jit(solution)/shard_map/ppermute | solution.py:656
  13.7 17.4 %copy-start.7 = (s32[48]{0:T(128)S(1)}, s32[48]{0:T(128)}, u32[]{:S(2)}) copy-start(s32[48]{0:T(128)} %shard_map.194.meta) | copy-start | bytes 580
  13.8 0.7 copy-start.6
  19.5 6.6 %collective-permute-start.4 = (f32[2,8,128]{2,1,0:T(8,128)S(1)}, f32[2,8,128]{2,1,0:T(8,128)S(1)}, u32[]{:S(2)}, u32[]{:S(2)}) collective-permute-start(f32[2,8,128]{2,1,0:T(8,128)S(1)} %get-tuple-element.27.own.own_first), channel_id=1, source_target_pairs={{0,1},{1,0},{2,3},{3,2},{4,5},{5,4},{6,7},{7,6},{8,9},{9,8},{10,11... | collective-permute-start | bytes 24584 | tf_op jit(solution)/shard_map/ppermute | solution.py:649
  25.4 3.1 %collective-permute-start.5 = (f32[2,8,128]{2,1,0:T(8,128)S(1)}, f32[2,8,128]{2,1,0:T(8,128)S(1)}, u32[]{:S(2)}, u32[]{:S(2)}) collective-permute-start(f32[2,8,128]{2,1,0:T(8,128)S(1)} %get-tuple-element.27.own.own_first), channel_id=1, source_target_pairs={{0,63},{1,2},{2,1},{3,4},{4,3},{5,6},{6,5},{7,8},{8,7},{9,10},{10,... | collective-permute-start | bytes 24584 | tf_op jit(solution)/shard_map/ppermute | solution.py:649
  28.4 20.3 %copy-start.9 = (bf16[2,128,256]{2,1,0:T(8,128)(2,1)S(1)}, bf16[2,128,256]{2,1,0:T(8,128)(2,1)}, u32[]{:S(2)}) copy-start(bf16[2,128,256]{2,1,0:T(8,128)(2,1)} %constant.18.clone.cas_high) | copy-start | bytes 393220
  28.4 20.3 %copy-start.10 = (bf16[2,128,256]{2,1,0:T(8,128)(2,1)S(1)}, bf16[2,128,256]{2,1,0:T(8,128)(2,1)}, u32[]{:S(2)}) copy-start(bf16[2,128,256]{2,1,0:T(8,128)(2,1)} %constant.19.clone.cas_low) | copy-start | bytes 393220
  28.4 8.3 %collective-permute-start.6 = (f32[3,2,8,128]{3,2,1,0:T(8,128)S(1)}, f32[3,2,8,128]{3,2,1,0:T(8,128)S(1)}, u32[]{:S(2)}, u32[]{:S(2)}) collective-permute-start(f32[3,2,8,128]{3,2,1,0:T(8,128)S(1)} %shard_map.198.level), channel_id=1, source_target_pairs={{0,64},{64,128},{128,192},{192,0},{1,65},{65,129},{129,193},{193,1... | collective-permute-start | bytes 73736 | tf_op jit(solution)/shard_map/ppermute | solution.py:656
  29.7 7.0 %collective-permute-start.7 = (f32[3,2,8,128]{3,2,1,0:T(8,128)S(1)}, f32[3,2,8,128]{3,2,1,0:T(8,128)S(1)}, u32[]{:S(2)}, u32[]{:S(2)}) collective-permute-start(f32[3,2,8,128]{3,2,1,0:T(8,128)S(1)} %shard_map.198.level), channel_id=1, source_target_pairs={{64,0},{128,64},{192,128},{0,192},{65,1},{129,65},{193,129},{1,193... | collective-permute-start | bytes 73736 | tf_op jit(solution)/shard_map/ppermute | solution.py:656
  36.7 16.6 %copy-start = (f32[3,16,128,128]{3,2,1,0:T(8,128)}, f32[3,16,128,128]{3,2,1,0:T(8,128)S(1)}, u32[]{:S(2)}) copy-start(f32[3,16,128,128]{3,2,1,0:T(8,128)S(1)} %get-tuple-element.30.pairs.pairs_b.stored_b) | copy-start | bytes 9437188
  36.7 16.6 %copy-start.3 = (s32[1,512]{1,0:T(1,128)S(1)}, s32[1,512]{1,0:T(1,128)}, u32[]{:S(2)}) copy-start(s32[1,512]{1,0:T(1,128)} %order.3) | copy-start | bytes 6148
  38.9 4.9 %collective-permute-start.8 = (f32[2,8,128]{2,1,0:T(8,128)S(1)}, f32[2,8,128]{2,1,0:T(8,128)S(1)}, u32[]{:S(2)}, u32[]{:S(2)}) collective-permute-start(f32[2,8,128]{2,1,0:T(8,128)S(1)} %shard_map.199.own.own_first), channel_id=1, source_target_pairs={{0,1},{1,0},{2,3},{3,2},{4,5},{5,4},{6,7},{7,6},{8,9},{9,8},{10,11... | collective-permute-start | bytes 24584 | tf_op jit(solution)/shard_map/ppermute | solution.py:649
  43.0 3.1 %collective-permute-start.9 = (f32[2,8,128]{2,1,0:T(8,128)S(1)}, f32[2,8,128]{2,1,0:T(8,128)S(1)}, u32[]{:S(2)}, u32[]{:S(2)}) collective-permute-start(f32[2,8,128]{2,1,0:T(8,128)S(1)} %shard_map.199.own.own_first), channel_id=1, source_target_pairs={{0,63},{1,2},{2,1},{3,4},{4,3},{5,6},{6,5},{7,8},{8,7},{9,10},{10,... | collective-permute-start | bytes 24584 | tf_op jit(solution)/shard_map/ppermute | solution.py:649
  46.0 7.3 %collective-permute-start.10 = (f32[3,2,8,128]{3,2,1,0:T(8,128)S(1)}, f32[3,2,8,128]{3,2,1,0:T(8,128)S(1)}, u32[]{:S(2)}, u32[]{:S(2)}) collective-permute-start(f32[3,2,8,128]{3,2,1,0:T(8,128)S(1)} %shard_map.201.level), channel_id=1, source_target_pairs={{0,64},{64,128},{128,192},{192,0},{1,65},{65,129},{129,193},{193,1... | collective-permute-start | bytes 73736 | tf_op jit(solution)/shard_map/ppermute | solution.py:656
  46.0 7.3 %collective-permute-start.11 = (f32[3,2,8,128]{3,2,1,0:T(8,128)S(1)}, f32[3,2,8,128]{3,2,1,0:T(8,128)S(1)}, u32[]{:S(2)}, u32[]{:S(2)}) collective-permute-start(f32[3,2,8,128]{3,2,1,0:T(8,128)S(1)} %shard_map.201.level), channel_id=1, source_target_pairs={{64,0},{128,64},{192,128},{0,192},{65,1},{129,65},{193,129},{1,193... | collective-permute-start | bytes 73736 | tf_op jit(solution)/shard_map/ppermute | solution.py:656
  51.1 11.7 %copy-start.12 = (f32[2,2,72,512]{3,2,1,0:T(8,128)}, f32[2,2,72,512]{3,2,1,0:T(8,128)S(1)}, u32[]{:S(2)}) copy-start(f32[2,2,72,512]{3,2,1,0:T(8,128)S(1)} %get-tuple-element.32.tab_x) | copy-start | bytes 1769476
  51.1 11.7 %copy-start.14 = (f32[2,128,512]{2,1,0:T(8,128)}, f32[2,128,512]{2,1,0:T(8,128)S(1)}, u32[]{:S(2)}) copy-start(f32[2,128,512]{2,1,0:T(8,128)S(1)} %get-tuple-element.36.slope_z) | copy-start | bytes 1572868
  51.1 11.7 %copy-start.16 = (bf16[2,128,512]{2,1,0:T(8,128)(2,1)}, bf16[2,128,512]{2,1,0:T(8,128)(2,1)S(1)}, u32[]{:S(2)}) copy-start(bf16[2,128,512]{2,1,0:T(8,128)(2,1)S(1)} %get-tuple-element.34.w_high) | copy-start | bytes 786436
  51.2 11.7 %copy-start.18 = (bf16[2,128,512]{2,1,0:T(8,128)(2,1)}, bf16[2,128,512]{2,1,0:T(8,128)(2,1)S(1)}, u32[]{:S(2)}) copy-start(bf16[2,128,512]{2,1,0:T(8,128)(2,1)S(1)} %get-tuple-element.35.w_low) | copy-start | bytes 786436
  57.4 5.4 %collective-permute-start.12 = (f32[8,768]{1,0:T(8,128)S(1)}, f32[8,768]{1,0:T(8,128)S(1)}, u32[]{:S(2)}, u32[]{:S(2)}) collective-permute-start(f32[8,768]{1,0:T(8,128)S(1)} %get-tuple-element.31.ordered), channel_id=1, source_target_pairs={{0,1},{1,0},{2,3},{3,2},{4,5},{5,4},{6,7},{7,6},{8,9},{9,8},{10,11... | collective-permute-start | bytes 73736 | tf_op jit(solution)/shard_map/ppermute | solution.py:649
  61.5 4.4 %collective-permute-start.13 = (f32[2,8,128]{2,1,0:T(8,128)S(1)}, f32[2,8,128]{2,1,0:T(8,128)S(1)}, u32[]{:S(2)}, u32[]{:S(2)}) collective-permute-start(f32[2,8,128]{2,1,0:T(8,128)S(1)} %get-tuple-element.37.own), channel_id=1, source_target_pairs={{0,63},{1,2},{2,1},{3,4},{4,3},{5,6},{6,5},{7,8},{8,7},{9,10},{10,... | collective-permute-start | bytes 24584 | tf_op jit(solution)/shard_map/ppermute | solution.py:649
  65.1 0.8 copy-start.1
  65.9 27.8 %all-to-all-start = ((f32[128,8,128]{2,1,0:T(8,128)}), f32[128,8,128]{2,1,0:T(8,128)}, u32[]{:S(2)}, u32[]{:S(2)}) async-start(f32[128,8,128]{2,1,0:T(8,128)} %copy-done.1), calls=%async_computation | async-start | bytes 1048576 | tf_op jit(solution)/shard_map/all_to_all | solution.py:790
  74.7 4.5 %collective-permute-start.14 = (f32[3,2,8,128]{3,2,1,0:T(8,128)S(1)}, f32[3,2,8,128]{3,2,1,0:T(8,128)S(1)}, u32[]{:S(2)}, u32[]{:S(2)}) collective-permute-start(f32[3,2,8,128]{3,2,1,0:T(8,128)S(1)} %shard_map.206.level), channel_id=1, source_target_pairs={{0,64},{64,128},{128,192},{192,0},{1,65},{65,129},{129,193},{193,1... | collective-permute-start | bytes 73736 | tf_op jit(solution)/shard_map/ppermute | solution.py:656
  75.4 3.9 %collective-permute-start.15 = (f32[3,2,8,128]{3,2,1,0:T(8,128)S(1)}, f32[3,2,8,128]{3,2,1,0:T(8,128)S(1)}, u32[]{:S(2)}, u32[]{:S(2)}) collective-permute-start(f32[3,2,8,128]{3,2,1,0:T(8,128)S(1)} %shard_map.206.level), channel_id=1, source_target_pairs={{64,0},{128,64},{192,128},{0,192},{65,1},{129,65},{193,129},{1,193... | collective-permute-start | bytes 73736 | tf_op jit(solution)/shard_map/ppermute | solution.py:656
  79.3 14.4 %copy-start.11 = (f32[8,256]{1,0:T(8,128)S(1)}, f32[8,256]{1,0:T(8,128)}, u32[]{:S(2)}) copy-start(f32[8,256]{1,0:T(8,128)} %constant.20.clone.waves) | copy-start | bytes 24580
  83.6 39.1 %copy-start.15 = (f32[2,128,512]{2,1,0:T(8,128)S(1)}, f32[2,128,512]{2,1,0:T(8,128)}, u32[]{:S(2)}) copy-start(f32[2,128,512]{2,1,0:T(8,128)} %copy-done.14) | copy-start | bytes 1572868
  83.7 39.1 %copy-start.17 = (bf16[2,128,512]{2,1,0:T(8,128)(2,1)S(1)}, bf16[2,128,512]{2,1,0:T(8,128)(2,1)}, u32[]{:S(2)}) copy-start(bf16[2,128,512]{2,1,0:T(8,128)(2,1)} %copy-done.16) | copy-start | bytes 786436
  83.7 39.1 %copy-start.19 = (bf16[2,128,512]{2,1,0:T(8,128)(2,1)S(1)}, bf16[2,128,512]{2,1,0:T(8,128)(2,1)}, u32[]{:S(2)}) copy-start(bf16[2,128,512]{2,1,0:T(8,128)(2,1)} %copy-done.18) | copy-start | bytes 786436
  93.7 29.1 %copy-start.13 = (f32[2,2,72,512]{3,2,1,0:T(8,128)S(1)}, f32[2,2,72,512]{3,2,1,0:T(8,128)}, u32[]{:S(2)}) copy-start(f32[2,2,72,512]{3,2,1,0:T(8,128)} %copy-done.12) | copy-start | bytes 1769476
  122.8 6.8 %copy-start.2 = (f32[3,512]{1,0:T(4,128)S(1)}, f32[3,512]{1,0:T(4,128)}, u32[]{:S(2)}) copy-start(f32[3,512]{1,0:T(4,128)} %residual.1) | copy-start | bytes 18436
  122.8 6.8 %copy-start.4 = (f32[3,512]{1,0:T(4,128)S(1)}, f32[3,512]{1,0:T(4,128)}, u32[]{:S(2)}) copy-start(f32[3,512]{1,0:T(4,128)} %dipoles.1) | copy-start | bytes 18436
  124.5 5.1 %collective-permute-start.16 = (f32[8,512]{1,0:T(8,128)S(1)}, f32[8,512]{1,0:T(8,128)S(1)}, u32[]{:S(2)}, u32[]{:S(2)}) collective-permute-start(f32[8,512]{1,0:T(8,128)S(1)} %shard_map.210), channel_id=1, source_target_pairs={{0,1},{1,0},{2,3},{3,2},{4,5},{5,4},{6,7},{7,6},{8,9},{9,8},{10,11... | collective-permute-start | bytes 49160 | tf_op jit(solution)/shard_map/ppermute | solution.py:649

commit v6 on v5

--- a/solution.py
+++ b/solution.py
@@ -200,7 +200,7 @@
 GROUP = 4
 
 
-def pair_kernel(first_place, extents, meta, own, level, before, after, pool, pairs, found, columns, totals):
+def pair_kernel(first_place, count, extents, meta, own, level, before, after, pool, pairs, found, columns, totals):
     fill_pool(pool, extents, own, level, before, after, meta)
 
     def tile_step(at, carry):
@@ -266,7 +266,7 @@
         found[at] = updated(block, totals)
         return carry
 
-    lax.fori_loop(0, 2, tile_step, 0)
+    lax.fori_loop(0, count, tile_step, 0)
 
 
 def field_rows(totals):
@@ -283,9 +283,12 @@
 APPLY_ROWS = 64
 
 
-def fill_search(pool, own_first, own_rest, level, before, after, meta):
-    for place in range(4):
-        pool[meta[ORDER_AT + place]] = own_first[place] if place < 2 else own_rest[place - 2]
+def fill_search(pool, owns, level, before, after, meta):
+    place = 0
+    for own in owns:
+        for at in range(own.shape[0]):
+            pool[meta[ORDER_AT + place]] = own[at]
+            place += 1
     for along, source in enumerate((before, level, after)):
         for kind in range(3):
             for member in range(2):
@@ -338,34 +341,37 @@
     lax.fori_loop(0, TILE // APPLY_ROWS, chunk_step, 0)
 
 
-def sweep_tiles(first_place, meta, geometry, banks, found, pool, columns, totals, local=None):
-    for bank, pairs in enumerate(banks):
+def sweep_tiles(place, meta, geometry, banks, found, pool, columns, totals, local=None):
+    done = 0
+    for pairs in banks:
+        count = pairs.shape[1] // 8
 
         def tile_step(at, carry):
-            tile = meta[ORDER_AT + first_place + 2 * bank + at]
+            tile = meta[ORDER_AT + place + done + at]
             apply_tile(meta, tile, at, pairs, geometry, pool, columns, totals)
             rows = updated(geometry[tile], totals)
-            found[2 * bank + at] = rows
+            found[done + at] = rows
             if local is not None:
                 local[tile] = rows
             return carry
 
-        lax.fori_loop(0, 2, tile_step, 0)
-
-
-def sweep_kernel(
-    first_place, meta, geometry, own_first, own_rest, level, before, after, pairs, found, pool, columns, totals
-):
-    fill_search(pool, own_first, own_rest, level, before, after, meta)
-    sweep_tiles(first_place, meta, geometry, (pairs,), found, pool, columns, totals)
+        lax.fori_loop(0, count, tile_step, 0)
+        done += count
+
+
+def sweep_kernel(place, owns, meta, geometry, *refs):
+    own_refs, (level, before, after) = (refs[:owns], refs[owns : owns + 3])
+    banks, (found, pool, columns, totals) = (refs[owns + 3 : -4], refs[-4:])
+    fill_search(pool, own_refs, level, before, after, meta)
+    sweep_tiles(place, meta, geometry, banks, found, pool, columns, totals)
 
 
 def direction_kernel(
-    meta, geometry, own_first, own_rest, level, before, after, pairs_a, pairs_b, order, found, sent, bundle, pool, columns, totals, local
+    meta, geometry, own_a, own_b, level, before, after, pairs_a, pairs_b, pairs_c, order, found, sent, bundle, pool, columns, totals, local
 ):
     atoms = order.shape[1]
-    fill_search(pool, own_first, own_rest, level, before, after, meta)
-    sweep_tiles(0, meta, geometry, (pairs_a, pairs_b), found, pool, columns, totals, local)
+    fill_search(pool, (own_a, own_b), level, before, after, meta)
+    sweep_tiles(0, meta, geometry, (pairs_a, pairs_b, pairs_c), found, pool, columns, totals, local)
     in_tiles = jnp.concatenate([local[tile] for tile in range(4)], 1)
     bundle[:, :atoms] = selected(in_tiles, order_matrix(order[...], atoms), NT)
     for place in range(2):
@@ -375,20 +381,24 @@
 
 
 def final_field_kernel(
-    meta, geometry, direction, level, before, after, pairs_a, order, stored_b, applied, sums, pool, columns, totals, local, pairs_b, sem
+    meta, geometry, direction, level, before, after, pairs_a, order, stored_b, stored_c, applied, sums, pool, columns, totals, local, pairs_b, pairs_c, sems
 ):
-    copy = pltpu.make_async_copy(stored_b, pairs_b, sem.at[0])
-    copy.start()
+    copies = [
+        pltpu.make_async_copy(source, target, sems.at[at])
+        for at, (source, target) in enumerate(((stored_b, pairs_b), (stored_c, pairs_c)))
+    ]
+    for copy in copies:
+        copy.start()
     atoms = order.shape[1]
-    fill_search(pool, direction, direction.at[2:4], level, before, after, meta)
+    fill_search(pool, (direction,), level, before, after, meta)
     both = (jnp.zeros((1, TILE), F32), jnp.zeros((1, TILE), F32))
-    for bank, pairs in enumerate((pairs_a, pairs_b)):
-        if bank == 1:
-            copy.wait()
+    for first, pairs in ((0, pairs_a), (2, pairs_b), (3, pairs_c)):
+        if first:
+            copies[first - 2].wait()
 
         def tile_step(at, both):
             curve, dots = both
-            place = 2 * bank + at
+            place = first + at
             tile = meta[ORDER_AT + place]
             apply_tile(meta, tile, at, pairs, geometry, pool, columns, totals)
             block = geometry[tile]
@@ -404,7 +414,7 @@
             local[tile] = jnp.concatenate(rows + [jnp.zeros((5, TILE), F32)], 0)
             return (curve, dots)
 
-        both = lax.fori_loop(0, 2, tile_step, both)
+        both = lax.fori_loop(0, pairs.shape[1] // 8, tile_step, both)
     in_tiles = jnp.concatenate([local[tile] for tile in range(4)], 1)
     applied[...] = selected(in_tiles, order_matrix(order[...], atoms), NT)
     lane = lax.broadcasted_iota(jnp.int32, (8, TILE), 1)
@@ -660,9 +670,10 @@
     return call(join_kernel, [((3, 2, 8, TILE), F32)], 10**6)(block, inner, outer)[0]
 
 
-def around(block, bundle=None):
+def around(block, bundle=None, beneath=None):
     inner = beside(block if bundle is None else bundle, False)
-    return along_slab(joined(block, inner, beside(block, True))), inner
+    outer, _ = lax.optimization_barrier((beside(block, True), beneath))
+    return along_slab(joined(block, inner, outer)), inner
 
 
 def local(
@@ -679,7 +690,7 @@
     half = G // 2
     tile_shape = ((4, 8, TILE), F32)
     two_shape = ((2, 8, TILE), F32)
-    bank_shape = ((3, 16, TILE, TILE), F32)
+    one_bank = ((3, 8, TILE, TILE), F32)
     pool_scratch = pltpu.VMEM((22, 8, TILE), F32)
     total_scratch = pltpu.VMEM((3, TILE, TILE), F32)
     own, sent, statics = pl.pallas_call(
@@ -715,43 +726,8 @@
         out_specs=smem,
         cost_estimate=pl.CostEstimate(flops=10**8, bytes_accessed=1 << 20, transcendentals=0),
     )(tile_lists, tile_counts, send_tiles, sent)
-    first, statics_beside = around(sent, statics)
-
-    def pairs_of(first_place):
-        return call(
-            functools.partial(pair_kernel, first_place, extents),
-            [((22, 8, TILE), F32), bank_shape, two_shape],
-            10**9,
-            smem=1,
-            scratch=(pltpu.VMEM((4, TILE, TILE), F32), total_scratch),
-        )(meta, own, *first)
-
-    geometry, pairs_a, search_a = pairs_of(0)
-    _, pairs_b, search_b = pairs_of(2)
-    sweep_scratch = (pool_scratch, pltpu.VMEM((3, TILE, TILE), F32), total_scratch)
-    second, _ = around(search_a)
-
-    def sweep(first_place, pairs):
-        return call(
-            functools.partial(sweep_kernel, first_place),
-            [two_shape],
-            10**8,
-            smem=1,
-            scratch=sweep_scratch,
-        )(meta, geometry, search_a, search_b, *second, pairs)[0]
-
-    next_a = sweep(0, pairs_a)
-    next_b = sweep(2, pairs_b)
-    third, _ = around(next_a)
-    local_scratch = pltpu.VMEM((4, 8, TILE), F32)
-    direction, sent, ordered = call(
-        direction_kernel,
-        [tile_shape, two_shape, ((8, atoms + 2 * TILE), F32)],
-        10**8,
-        smem=1,
-        scratch=sweep_scratch + (local_scratch,),
-    )(meta, geometry, next_a, next_b, *third, pairs_a, pairs_b, tile_order)
-    ordered_beside, outer = (beside(ordered, False), beside(sent, True))
+    first, statics_beside = around(sent, statics, beneath=meta)
+
     freq = np.arange(G)
     padded_x = np.stack([(s * extents[0] + np.arange(x_rows) - 2) % G for s in range(n_slab)])
     real_x = np.tile(np.arange(x_rows) < extents[0] + 4, n_slab)
@@ -775,6 +751,47 @@
         smem=1,
         vmem=LARGE_VMEM,
     )(meta, statics, statics_beside, *split_constant(cas_z))
+    level, before, after = first
+    after, _ = lax.optimization_barrier((after, tables[1]))
+    first = (level, before, after)
+
+    def pairs_of(place, count):
+        return call(
+            functools.partial(pair_kernel, place, count, extents),
+            [((22, 8, TILE), F32), ((3, 8 * count, TILE, TILE), F32), ((count, 8, TILE), F32)],
+            10**9,
+            smem=1,
+            scratch=(pltpu.VMEM((4, TILE, TILE), F32), total_scratch),
+        )(meta, own, *first)
+
+    geometry, pairs_a, search_a = pairs_of(0, 2)
+    _, pairs_b, search_b = pairs_of(2, 1)
+    _, pairs_c, search_c = pairs_of(3, 1)
+    sweep_scratch = (pool_scratch, pltpu.VMEM((3, TILE, TILE), F32), total_scratch)
+    second, _ = around(search_a, beneath=search_b)
+
+    def sweep(place, banks):
+        owns = (search_a, search_b, search_c)
+        return call(
+            functools.partial(sweep_kernel, place, len(owns)),
+            [two_shape],
+            10**8,
+            smem=1,
+            scratch=sweep_scratch,
+        )(meta, geometry, *owns, *second, *banks)[0]
+
+    next_a = sweep(0, (pairs_a,))
+    next_b = sweep(2, (pairs_b, pairs_c))
+    third, _ = around(next_a, beneath=next_b)
+    local_scratch = pltpu.VMEM((4, 8, TILE), F32)
+    direction, sent, ordered = call(
+        direction_kernel,
+        [tile_shape, two_shape, ((8, atoms + 2 * TILE), F32)],
+        10**8,
+        smem=1,
+        scratch=sweep_scratch + (local_scratch,),
+    )(meta, geometry, next_a, next_b, *third, pairs_a, pairs_b, pairs_c, tile_order)
+    ordered_beside = beside(ordered, False)
     message = ((half, 8, TILE), F32)
     flat_scratch = pltpu.VMEM((half, 8 * TILE), F32)
     spread_own = call(spread_own_kernel, [((half, x_rows * y_rows), F32)], 10**9, vmem=LARGE_VMEM)(ordered, *tables)[0]
@@ -786,7 +803,8 @@
         scratch=(flat_scratch,),
         vmem=LARGE_VMEM,
     )(meta, ordered_beside, spread_own, *tables)[0]
-    spread, outer = lax.optimization_barrier((spread, outer))
+    late, _ = lax.optimization_barrier((sent, spread_own))
+    spread, outer = lax.optimization_barrier((spread, beside(late, True)))
     grid = lax.all_to_all(spread, CHIPS, 0, 0, tiled=True)
     last = along_slab(joined(sent, ordered_beside, outer))
     applied, sums = call(
@@ -795,10 +813,10 @@
         10**9,
         smem=1,
         scratch=sweep_scratch
-        + (local_scratch, pltpu.VMEM(*bank_shape), pltpu.SemaphoreType.DMA((1,))),
+        + (local_scratch, pltpu.VMEM(*one_bank), pltpu.VMEM(*one_bank), pltpu.SemaphoreType.DMA((2,))),
         vmem=LARGE_VMEM,
-        hbm=1,
-    )(meta, geometry, direction, *last, pairs_a, tile_order, pairs_b)
+        hbm=2,
+    )(meta, geometry, direction, *last, pairs_a, tile_order, pairs_b, pairs_c)
     planes = call(
         functools.partial(plane_kernel, (n_slab, n_pair, x_rows, pair_rows)),
         [message],

time: 131 us -> 131 us (level)
  starting transfers between devices: 40.4 us -> 49.1 us
  Pallas kernels: 41.4 us -> 35.9 us
  waiting for transfers between devices: 21.1 us -> 16.1 us
  local copies, waits for them, and re-layouts: 2.24 us -> 4.7 us
    ppermute x9, starting transfers between devices: 20.8 us -> 28.9 us  [beside(): return lax.ppermute(block, BOTH, swap_pairs(n_slab, n_space, odd))]
    ppermute x9, waiting for transfers between devices: 9.23 us -> 1.29 us  [beside(): return lax.ppermute(block, BOTH, swap_pairs(n_slab, n_space, odd))]
    pallas_call x17 -> x18, Pallas kernels: 38.1 us -> 32.5 us  [run(): pl.pallas_call(kernel, out_shape=[jax.ShapeDtypeStruct(shape, dtype) for...]
    unnamed x40 -> x44, local copies, waits for them, and re-layouts: 2.24 us -> 4.7 us
    all_to_all x1, waiting for transfers between devices: 10 us -> 11.9 us  [local(): grid = lax.all_to_all(spread, CHIPS, 0, 0, tiled=True)]
    all_to_all x1, starting transfers between devices: 8.81 us -> 10.5 us  [local(): grid = lax.all_to_all(spread, CHIPS, 0, 0, tiled=True)]
  transfers between devices with their start and end apart: 18 -> 18, of which waited for: 7 -> 4; matrix products, arithmetic and copies ran while one was open for 0% -> 0% of each run, Pallas kernels for 16% -> 15%
where the time goes in v6:
time: 131 us
  starting transfers between devices  49.1 us (37%)
  Pallas kernels  35.9 us (27%)
  blocking collectives  24.4 us (19%)
  waiting for transfers between devices  16.1 us (12%)
  local copies, waits for them, and re-layouts  4.7 us (4%)
    pallas_call x18, Pallas kernels, run(): pl.pallas_call(kernel, out_shape=[jax.ShapeDtypeStruct(shape, dtype) for...  32.5 us
    ppermute x9, starting transfers between devices, beside(): return lax.ppermute(block, BOTH, swap_pairs(n_slab, n_space, odd))  28.9 us
    all_to_all x1, blocking collectives, local(): returned = lax.all_to_all(planes, CHIPS, 0, 0, tiled=True)  24.4 us
    all_to_all x1, waiting for transfers between devices, local(): grid = lax.all_to_all(spread, CHIPS, 0, 0, tiled=True)  11.9 us
    all_to_all x1, starting transfers between devices, local(): grid = lax.all_to_all(spread, CHIPS, 0, 0, tiled=True)  10.5 us
    ppermute x4, starting transfers between devices, along_slab(): lax.ppermute(level, 'slab', down)  8.52 us
    unnamed x44, local copies, waits for them, and re-layouts  4.7 us
    ppermute x4, waiting for transfers between devices, along_slab(): lax.ppermute(level, 'slab', up)  2.84 us
  transfers between devices with their start and end apart: 18, of which 4 were waited for; matrix products, arithmetic and copies ran while one was open for 0% of the time, Pallas kernels for 15%

profile of v6, /device:TPU:1, one launch (start us, length us, event | category | flops | bytes accessed | tf_op | source)
XLA Modules:
  0.0 131.1 jit_solution(2631009803176565443)
XLA Ops:
  0.6 0.0 copy-start.10
  0.6 0.6 copy-done.10
  1.3 1.5 %shard_map.193 = (f32[4,8,128]{2,1,0:T(8,128)S(1)}, f32[2,8,128]{2,1,0:T(8,128)S(1)}, f32[8,768]{1,0:T(8,128)S(1)}) custom-call(s32[1,2]{1,0:T(1,128)S(1)} %copy-done.10, f32[3,512]{1,0:T(4,128)} %residual.1, s32[3,512]{1,0:T(4,128)} %refs_1_.2, f32[3,512]{1,0:T(4,128)} %refs_2_.2, f32[512]{0:T(512)} %refs_3_.2, s32[1,512]{1,0:T(1,128)} %order.3), custom_call_target="tpu_custom_call" | custom-call | tf_op jit(solution)/shard_map/pallas_call | solution.py:696
  2.8 0.0 copy-start.6
  2.9 3.3 %collective-permute-start = (f32[8,768]{1,0:T(8,128)S(1)}, f32[8,768]{1,0:T(8,128)S(1)}, u32[]{:S(2)}, u32[]{:S(2)}) collective-permute-start(f32[8,768]{1,0:T(8,128)S(1)} %get-tuple-element.32.mine), channel_id=1, source_target_pairs={{0,1},{1,0},{2,3},{3,2},{4,5},{5,4},{6,7},{7,6},{8,9},{9,8},{10,11... | collective-permute-start | bytes 73736 | tf_op jit(solution)/shard_map/ppermute | solution.py:659
  6.2 0.0 collective-permute-start.1
  6.2 1.8 %shard_map.194.meta = s32[48]{0:T(128)} custom-call(s32[1,4,8]{2,1,0:T(4,128)} %lists.1, s32[1,4]{1,0:T(1,128)} %counts.1, s32[1,2]{1,0:T(1,128)} %send.3, f32[2,8,128]{2,1,0:T(8,128)} %copy-done.6), custom_call_target="tpu_custom_call" | custom-call | flops 100000000 | bytes 1048576 | tf_op jit(solution)/shard_map/pallas_call | solution.py:722
  8.0 1.3 collective-permute-done.1.outer
  9.3 0.0 collective-permute-done.inner.beside
  9.3 0.7 copy-done.7
  10.0 1.1 collective-permute-start.3
  11.1 0.4 collective-permute-start.2
  11.4 0.7 copy-done.8
  12.1 0.9 copy-done.11
  13.0 0.9 copy-done.12
  13.9 2.4 %shard_map.196 = (f32[2,2,72,512]{3,2,1,0:T(8,128)S(1)}, f32[2,2,8,512]{3,2,1,0:T(8,128)S(1)}, bf16[2,128,512]{2,1,0:T(8,128)(2,1)S(1)}, bf16[2,128,512]{2,1,0:T(8,128)(2,1)S(1)}, f32[2,128,512]{2,1,0:T(8,128)S(1)}) custom-call(s32[48]{0:T(128)S(1)} %copy-done.8, f32[8,768]{1,0:T(8,128)S(1)} %get-tuple-element.32.mine, ...), custom_call_target="tpu_custom_call" | custom-call | flops 100000000 | bytes 1048576 | tf_op jit(solution)/shard_map/pallas_call | solution.py:124
  16.3 0.0 copy-start.14
  16.3 0.0 copy-start.16
  16.3 0.0 copy-start.18
  16.3 0.0 collective-permute-done.3.after
  16.3 0.0 collective-permute-done.2.before
  16.3 3.3 %shard_map.197 = (f32[22,8,128]{2,1,0:T(8,128)S(1)}, f32[3,16,128,128]{3,2,1,0:T(8,128)S(1)}, f32[2,8,128]{2,1,0:T(8,128)S(1)}) custom-call(s32[48]{0:T(128)S(1)} %copy-done.8, f32[4,8,128]{2,1,0:T(8,128)S(1)} %get-tuple-element.31.own, f32[3,2,8,128]{3,2,1,0:T(8,128)S(1)} %shard_map.195.level, f32[3,2,8,128]{3,2,1,0:T(8,128)S(1)} %collective-permute-done.2.before, ...), custom_call_target="tpu_custom_call" | custom-call | flops 1000000000 | bytes 1048576 | tf_op jit(solution)/shard_map/pallas_call | solution.py:124
  19.6 1.4 %collective-permute-start.5 = (f32[2,8,128]{2,1,0:T(8,128)S(1)}, f32[2,8,128]{2,1,0:T(8,128)S(1)}, u32[]{:S(2)}, u32[]{:S(2)}) collective-permute-start(f32[2,8,128]{2,1,0:T(8,128)S(1)} %get-tuple-element.37.own.refs_0_), channel_id=1, source_target_pairs={{0,63},{1,2},{2,1},{3,4},{4,3},{5,6},{6,5},{7,8},{8,7},{9,10},{10,... | collective-permute-start | bytes 24584 | tf_op jit(solution)/shard_map/ppermute | solution.py:659
  21.0 11.5 %collective-permute-start.4 = (f32[2,8,128]{2,1,0:T(8,128)S(1)}, f32[2,8,128]{2,1,0:T(8,128)S(1)}, u32[]{:S(2)}, u32[]{:S(2)}) collective-permute-start(f32[2,8,128]{2,1,0:T(8,128)S(1)} %get-tuple-element.37.own.refs_0_), channel_id=1, source_target_pairs={{0,1},{1,0},{2,3},{3,2},{4,5},{5,4},{6,7},{7,6},{8,9},{9,8},{10,11... | collective-permute-start | bytes 24584 | tf_op jit(solution)/shard_map/ppermute | solution.py:659
  32.5 2.4 %shard_map.198 = (f32[22,8,128]{2,1,0:T(8,128)}, f32[3,8,128,128]{3,2,1,0:T(8,128)S(1)}, f32[1,8,128]{2,1,0:T(8,128)S(1)}) custom-call(s32[48]{0:T(128)S(1)} %copy-done.8, f32[4,8,128]{2,1,0:T(8,128)S(1)} %get-tuple-element.31.own, f32[3,2,8,128]{3,2,1,0:T(8,128)S(1)} %shard_map.195.level, f32[3,2,8,128]{3,2,1,0:T(8,128)S(1)} %collective-permute-done.2.before, ...), custom_call_target="tpu_custom_call" | custom-call | flops 1000000000 | bytes 1048576 | tf_op jit(solution)/shard_map/pallas_call | solution.py:124
  34.9 0.0 collective-permute-done.5.outer
  34.9 0.0 collective-permute-done.4.inner
  34.9 0.1 collective-permute-start.6
  35.0 2.7 %collective-permute-start.7 = (f32[3,2,8,128]{3,2,1,0:T(8,128)S(1)}, f32[3,2,8,128]{3,2,1,0:T(8,128)S(1)}, u32[]{:S(2)}, u32[]{:S(2)}) collective-permute-start(f32[3,2,8,128]{3,2,1,0:T(8,128)S(1)} %shard_map.200.refs_3_), channel_id=1, source_target_pairs={{64,0},{128,64},{192,128},{0,192},{65,1},{129,65},{193,129},{1,193... | collective-permute-start | bytes 73736 | tf_op jit(solution)/shard_map/ppermute | solution.py:666
  37.7 2.4 %shard_map.199 = (f32[22,8,128]{2,1,0:T(8,128)}, f32[3,8,128,128]{3,2,1,0:T(8,128)S(1)}, f32[1,8,128]{2,1,0:T(8,128)S(1)}) custom-call(s32[48]{0:T(128)S(1)} %copy-done.8, f32[4,8,128]{2,1,0:T(8,128)S(1)} %get-tuple-element.31.own, f32[3,2,8,128]{3,2,1,0:T(8,128)S(1)} %shard_map.195.level, f32[3,2,8,128]{3,2,1,0:T(8,128)S(1)} %collective-permute-done.2.before, ...), custom_call_target="tpu_custom_call" | custom-call | flops 1000000000 | bytes 1048576 | tf_op jit(solution)/shard_map/pallas_call | solution.py:124
  40.0 0.0 collective-permute-done.6.refs_4_
  40.0 0.0 collective-permute-done.7.refs_5_
  40.1 1.7 %shard_map.201.own.own_a = f32[2,8,128]{2,1,0:T(8,128)S(1)} custom-call(s32[48]{0:T(128)S(1)} %copy-done.8, f32[22,8,128]{2,1,0:T(8,128)S(1)} %get-tuple-element.36.geometry, f32[2,8,128]{2,1,0:T(8,128)S(1)} %get-tuple-element.37.own.refs_0_, f32[1,8,128]{2,1,0:T(8,128)S(1)} %get-tuple-element.38.refs_1_, f32[1,8,128]{2,1,0:T(8,128)S(1)} %get-tuple-element.39.refs_2_, ...), custom_call_target="tpu_custom_call" | custom-call | flops 100000000 | bytes 1048576 | tf_op jit(solution)/shard_map/pallas_call | solution.py:124
  41.8 0.1 collective-permute-start.9
  41.9 5.2 %collective-permute-start.8 = (f32[2,8,128]{2,1,0:T(8,128)S(1)}, f32[2,8,128]{2,1,0:T(8,128)S(1)}, u32[]{:S(2)}, u32[]{:S(2)}) collective-permute-start(f32[2,8,128]{2,1,0:T(8,128)S(1)} %shard_map.201.own.own_a), channel_id=1, source_target_pairs={{0,1},{1,0},{2,3},{3,2},{4,5},{5,4},{6,7},{7,6},{8,9},{9,8},{10,11... | collective-permute-start | bytes 24584 | tf_op jit(solution)/shard_map/ppermute | solution.py:659
  47.1 1.6 %shard_map.202.own_b = f32[2,8,128]{2,1,0:T(8,128)S(1)} custom-call(s32[48]{0:T(128)S(1)} %copy-done.8, f32[22,8,128]{2,1,0:T(8,128)S(1)} %get-tuple-element.36.geometry, f32[2,8,128]{2,1,0:T(8,128)S(1)} %get-tuple-element.37.own.refs_0_, f32[1,8,128]{2,1,0:T(8,128)S(1)} %get-tuple-element.38.refs_1_, f32[1,8,128]{2,1,0:T(8,128)S(1)} %get-tuple-element.39.refs_2_, ...), custom_call_target="tpu_custom_call" | custom-call | flops 100000000 | bytes 1048576 | tf_op jit(solution)/shard_map/pallas_call | solution.py:124
  48.7 0.0 collective-permute-done.9.outer
  48.7 0.0 collective-permute-done.8.inner
  48.8 0.1 collective-permute-start.10
  48.8 2.7 %collective-permute-start.11 = (f32[3,2,8,128]{3,2,1,0:T(8,128)S(1)}, f32[3,2,8,128]{3,2,1,0:T(8,128)S(1)}, u32[]{:S(2)}, u32[]{:S(2)}) collective-permute-start(f32[3,2,8,128]{3,2,1,0:T(8,128)S(1)} %shard_map.203.level), channel_id=1, source_target_pairs={{64,0},{128,64},{192,128},{0,192},{65,1},{129,65},{193,129},{1,193... | collective-permute-start | bytes 73736 | tf_op jit(solution)/shard_map/ppermute | solution.py:666
  51.5 1.2 collective-permute-done.10.before
  52.7 0.0 collective-permute-done.11.after
  52.7 3.0 %shard_map.204 = (f32[4,8,128]{2,1,0:T(8,128)S(1)}, f32[2,8,128]{2,1,0:T(8,128)S(1)}, f32[8,768]{1,0:T(8,128)S(1)}) custom-call(s32[48]{0:T(128)S(1)} %copy-done.8, f32[22,8,128]{2,1,0:T(8,128)S(1)} %get-tuple-element.36.geometry, f32[2,8,128]{2,1,0:T(8,128)S(1)} %shard_map.201.own.own_a, f32[2,8,128]{2,1,0:T(8,128)S(1)} %shard_map.202.own_b, ...), custom_call_target="tpu_custom_call" | custom-call | flops 100000000 | bytes 1048576 | tf_op jit(solution)/shard_map/pallas_call | solution.py:124
  55.7 4.2 %collective-permute-start.12 = (f32[8,768]{1,0:T(8,128)S(1)}, f32[8,768]{1,0:T(8,128)S(1)}, u32[]{:S(2)}, u32[]{:S(2)}) collective-permute-start(f32[8,768]{1,0:T(8,128)S(1)} %get-tuple-element.45.ordered), channel_id=1, source_target_pairs={{0,1},{1,0},{2,3},{3,2},{4,5},{5,4},{6,7},{7,6},{8,9},{9,8},{10,11... | collective-permute-start | bytes 73736 | tf_op jit(solution)/shard_map/ppermute | solution.py:659
  59.9 1.3 %shard_map.205.mine = f32[128,576]{1,0:T(8,128)S(1)} custom-call(f32[8,768]{1,0:T(8,128)S(1)} %get-tuple-element.45.ordered, f32[2,2,72,512]{3,2,1,0:T(8,128)S(1)} %get-tuple-element.46.tab_x, f32[2,2,8,512]{3,2,1,0:T(8,128)S(1)} %get-tuple-element.34.tab_y, bf16[2,128,512]{2,1,0:T(8,128)(2,1)S(1)} %get-tuple-element.47.w_high, ...), custom_call_target="tpu_custom_call" | custom-call | flops 1000000000 | bytes 1048576 | tf_op jit(solution)/shard_map/pallas_call | solution.py:124
  61.3 0.1 collective-permute-start.13
  61.4 0.0 collective-permute-done.12.ordered.inner
  61.4 2.2 %shard_map.206 = f32[128,8,128]{2,1,0:T(8,128)S(1)} custom-call(s32[48]{0:T(128)S(1)} %copy-done.9, f32[8,768]{1,0:T(8,128)S(1)} %collective-permute-done.12.ordered.inner, f32[128,576]{1,0:T(8,128)S(1)} %shard_map.205.mine, f32[2,2,72,512]{3,2,1,0:T(8,128)S(1)} %get-tuple-element.46.tab_x, f32[2,2,8,512]{3,2,1,0:T(8,128)S(1)} %get-tuple-element.34.tab_y, ...), custom_call_target="tpu_custom_call" | custom-call | flops 1000000000 | bytes 1048576 | tf_op jit(solution)/shard_map/pallas_call | solution.py:124
  63.6 0.8 copy-done.2
  64.4 0.0 collective-permute-done.13.outer
  64.4 10.5 %all-to-all-start = ((f32[128,8,128]{2,1,0:T(8,128)}), f32[128,8,128]{2,1,0:T(8,128)}, u32[]{:S(2)}, u32[]{:S(2)}) async-start(f32[128,8,128]{2,1,0:T(8,128)} %copy-done.2), calls=%async_computation | async-start | bytes 1048576 | tf_op jit(solution)/shard_map/all_to_all | solution.py:808
  75.0 0.7 collective-permute-start.14
  75.7 2.1 %collective-permute-start.15 = (f32[3,2,8,128]{3,2,1,0:T(8,128)S(1)}, f32[3,2,8,128]{3,2,1,0:T(8,128)S(1)}, u32[]{:S(2)}, u32[]{:S(2)}) collective-permute-start(f32[3,2,8,128]{3,2,1,0:T(8,128)S(1)} %shard_map.207.level), channel_id=1, source_target_pairs={{64,0},{128,64},{192,128},{0,192},{65,1},{129,65},{193,129},{1,193... | collective-permute-start | bytes 73736 | tf_op jit(solution)/shard_map/ppermute | solution.py:666
  77.7 1.6 %collective-permute-done.14.before = f32[3,2,8,128]{3,2,1,0:T(8,128)S(1)} collective-permute-done((f32[3,2,8,128]{3,2,1,0:T(8,128)S(1)}, f32[3,2,8,128]{3,2,1,0:T(8,128)S(1)}, u32[]{:S(2)}, u32[]{:S(2)}) %collective-permute-start.14) | collective-permute-done | bytes 24608 | tf_op jit(solution)/shard_map/ppermute | solution.py:666
  79.4 0.0 collective-permute-done.15.after
  79.4 3.4 %shard_map.208 = (f32[8,512]{1,0:T(8,128)S(1)}, f32[8,128]{1,0:T(8,128)S(1)}) custom-call(s32[48]{0:T(128)S(1)} %copy-done.9, f32[22,8,128]{2,1,0:T(8,128)S(1)} %get-tuple-element.36.geometry, f32[4,8,128]{2,1,0:T(8,128)S(1)} %get-tuple-element.53.direction, f32[3,2,8,128]{3,2,1,0:T(8,128)S(1)} %shard_map.207.level, ...), custom_call_target="tpu_custom_call" | custom-call | flops 1000000000 | bytes 1048576 | tf_op jit(solution)/shard_map/pallas_call | solution.py:124
  82.8 11.9 %all-to-all-done.grid = f32[128,8,128]{2,1,0:T(8,128)} async-done(((f32[128,8,128]{2,1,0:T(8,128)}), f32[128,8,128]{2,1,0:T(8,128)}, u32[]{:S(2)}, u32[]{:S(2)}) %all-to-all-start) | async-done | bytes 524320 | tf_op jit(solution)/shard_map/all_to_all | solution.py:808
  94.7 4.7 %shard_map.209 = f32[128,8,128]{2,1,0:T(8,128)S(1)} custom-call(f32[128,8,128]{2,1,0:T(8,128)} %all-to-all-done.grid, f32[8,256]{1,0:T(8,128)S(1)} %copy-done.13, f32[8,128]{1,0:T(8,128)S(1)} %get-tuple-element.55.sums, bf16[512,256]{1,0:T(8,128)(2,1)} %constant.21.clone.refs_0_, bf16[512,256]{1,0:T(8,128)(2,1)} %constant.22.clone.refs_1_, ...), custom_call_target="tpu_custom_call" | custom-call | flops 1000000000 | bytes 1048576 | tf_op jit(solution)/shard_map/pallas_call | solution.py:124
  99.4 24.4 %all_to_all.10.grid = f32[128,8,128]{2,1,0:T(8,128)S(1)} all-to-all(f32[128,8,128]{2,1,0:T(8,128)S(1)} %shard_map.209), channel_id=1, replica_groups=mesh['slab'=4,'pair'=32,'core'=2] {'slab','pair'}, dimensions={0} | all-to-all | bytes 1048576 | tf_op jit(solution)/shard_map/all_to_all | solution.py:839
  123.9 1.7 %shard_map.211 = f32[8,512]{1,0:T(8,128)S(1)} custom-call(s32[48]{0:T(128)S(1)} %copy-done.9, f32[128,8,128]{2,1,0:T(8,128)S(1)} %all_to_all.10.grid, f32[2,2,72,512]{3,2,1,0:T(8,128)S(1)} %copy-done.15, f32[2,2,8,512]{3,2,1,0:T(8,128)S(1)} %get-tuple-element.34.tab_y, bf16[2,128,512]{2,1,0:T(8,128)(2,1)S(1)} %copy-done.19, ...), custom_call_target="tpu_custom_call" | custom-call | flops 1000000000 | bytes 1048576 | tf_op jit(solution)/shard_map/pallas_call | solution.py:124
  125.6 3.0 %collective-permute-start.16 = (f32[8,512]{1,0:T(8,128)S(1)}, f32[8,512]{1,0:T(8,128)S(1)}, u32[]{:S(2)}, u32[]{:S(2)}) collective-permute-start(f32[8,512]{1,0:T(8,128)S(1)} %shard_map.211), channel_id=1, source_target_pairs={{0,1},{1,0},{2,3},{3,2},{4,5},{5,4},{6,7},{7,6},{8,9},{9,8},{10,11... | collective-permute-start | bytes 49160 | tf_op jit(solution)/shard_map/ppermute | solution.py:659
  128.6 1.7 %shard_map.210.mine = f32[8,512]{1,0:T(8,128)S(1)} custom-call(s32[48]{0:T(128)S(1)} %copy-done.9, f32[128,8,128]{2,1,0:T(8,128)S(1)} %all_to_all.10.grid, f32[2,2,72,512]{3,2,1,0:T(8,128)S(1)} %copy-done.15, f32[2,2,8,512]{3,2,1,0:T(8,128)S(1)} %get-tuple-element.34.tab_y, bf16[2,128,512]{2,1,0:T(8,128)(2,1)S(1)} %copy-done.19, ...), custom_call_target="tpu_custom_call" | custom-call | flops 1000000000 | bytes 1048576 | tf_op jit(solution)/shard_map/pallas_call | solution.py:124
  130.3 0.0 collective-permute-done.16.theirs
  130.3 0.9 shard_map.212
  (37 shorter events, 0.1 us)
Async XLA Ops:
  0.6 0.7 copy-start.10
  2.8 3.3 %copy-start.6 = (f32[2,8,128]{2,1,0:T(8,128)}, f32[2,8,128]{2,1,0:T(8,128)S(1)}, u32[]{:S(2)}) copy-start(f32[2,8,128]{2,1,0:T(8,128)S(1)} %get-tuple-element.30.after.own) | copy-start | bytes 24580
  2.9 6.4 %collective-permute-start = (f32[8,768]{1,0:T(8,128)S(1)}, f32[8,768]{1,0:T(8,128)S(1)}, u32[]{:S(2)}, u32[]{:S(2)}) collective-permute-start(f32[8,768]{1,0:T(8,128)S(1)} %get-tuple-element.32.mine), channel_id=1, source_target_pairs={{0,1},{1,0},{2,3},{3,2},{4,5},{5,4},{6,7},{7,6},{8,9},{9,8},{10,11... | collective-permute-start | bytes 73736 | tf_op jit(solution)/shard_map/ppermute | solution.py:659
  6.2 3.1 %collective-permute-start.1 = (f32[2,8,128]{2,1,0:T(8,128)S(1)}, f32[2,8,128]{2,1,0:T(8,128)S(1)}, u32[]{:S(2)}, u32[]{:S(2)}) collective-permute-start(f32[2,8,128]{2,1,0:T(8,128)S(1)} %get-tuple-element.30.after.own), channel_id=1, source_target_pairs={{0,63},{1,2},{2,1},{3,4},{4,3},{5,6},{6,5},{7,8},{8,7},{9,10},{10,... | collective-permute-start | bytes 24584 | tf_op jit(solution)/shard_map/ppermute | solution.py:659
  9.3 0.7 copy-start.7
  10.0 6.4 %collective-permute-start.3 = (f32[3,2,8,128]{3,2,1,0:T(8,128)S(1)}, f32[3,2,8,128]{3,2,1,0:T(8,128)S(1)}, u32[]{:S(2)}, u32[]{:S(2)}) collective-permute-start(f32[3,2,8,128]{3,2,1,0:T(8,128)S(1)} %shard_map.195.level), channel_id=1, source_target_pairs={{64,0},{128,64},{192,128},{0,192},{65,1},{129,65},{193,129},{1,193... | collective-permute-start | bytes 73736 | tf_op jit(solution)/shard_map/ppermute | solution.py:666
  11.1 5.3 %collective-permute-start.2 = (f32[3,2,8,128]{3,2,1,0:T(8,128)S(1)}, f32[3,2,8,128]{3,2,1,0:T(8,128)S(1)}, u32[]{:S(2)}, u32[]{:S(2)}) collective-permute-start(f32[3,2,8,128]{3,2,1,0:T(8,128)S(1)} %shard_map.195.level), channel_id=1, source_target_pairs={{0,64},{64,128},{128,192},{192,0},{1,65},{65,129},{129,193},{193,1... | collective-permute-start | bytes 73736 | tf_op jit(solution)/shard_map/ppermute | solution.py:666
  11.4 0.7 copy-start.8
  12.1 0.9 copy-start.11
  13.0 0.9 copy-start.12
  16.3 45.1 %copy-start.14 = (f32[2,2,72,512]{3,2,1,0:T(8,128)}, f32[2,2,72,512]{3,2,1,0:T(8,128)S(1)}, u32[]{:S(2)}) copy-start(f32[2,2,72,512]{3,2,1,0:T(8,128)S(1)} %get-tuple-element.46.tab_x) | copy-start | bytes 1769476
  16.3 45.1 %copy-start.16 = (f32[2,128,512]{2,1,0:T(8,128)}, f32[2,128,512]{2,1,0:T(8,128)S(1)}, u32[]{:S(2)}) copy-start(f32[2,128,512]{2,1,0:T(8,128)S(1)} %get-tuple-element.49.slope_z) | copy-start | bytes 1572868
  16.3 45.1 %copy-start.18 = (bf16[2,128,512]{2,1,0:T(8,128)(2,1)}, bf16[2,128,512]{2,1,0:T(8,128)(2,1)S(1)}, u32[]{:S(2)}) copy-start(bf16[2,128,512]{2,1,0:T(8,128)(2,1)S(1)} %get-tuple-element.47.w_high) | copy-start | bytes 786436
  16.3 45.1 %copy-start.20 = (bf16[2,128,512]{2,1,0:T(8,128)(2,1)}, bf16[2,128,512]{2,1,0:T(8,128)(2,1)S(1)}, u32[]{:S(2)}) copy-start(bf16[2,128,512]{2,1,0:T(8,128)(2,1)S(1)} %get-tuple-element.48.w_low) | copy-start | bytes 786436
  19.6 15.3 %collective-permute-start.5 = (f32[2,8,128]{2,1,0:T(8,128)S(1)}, f32[2,8,128]{2,1,0:T(8,128)S(1)}, u32[]{:S(2)}, u32[]{:S(2)}) collective-permute-start(f32[2,8,128]{2,1,0:T(8,128)S(1)} %get-tuple-element.37.own.refs_0_), channel_id=1, source_target_pairs={{0,63},{1,2},{2,1},{3,4},{4,3},{5,6},{6,5},{7,8},{8,7},{9,10},{10,... | collective-permute-start | bytes 24584 | tf_op jit(solution)/shard_map/ppermute | solution.py:659
  21.0 13.9 %collective-permute-start.4 = (f32[2,8,128]{2,1,0:T(8,128)S(1)}, f32[2,8,128]{2,1,0:T(8,128)S(1)}, u32[]{:S(2)}, u32[]{:S(2)}) collective-permute-start(f32[2,8,128]{2,1,0:T(8,128)S(1)} %get-tuple-element.37.own.refs_0_), channel_id=1, source_target_pairs={{0,1},{1,0},{2,3},{3,2},{4,5},{5,4},{6,7},{7,6},{8,9},{9,8},{10,11... | collective-permute-start | bytes 24584 | tf_op jit(solution)/shard_map/ppermute | solution.py:659
  34.9 17.8 %copy-start = (f32[3,8,128,128]{3,2,1,0:T(8,128)}, f32[3,8,128,128]{3,2,1,0:T(8,128)S(1)}, u32[]{:S(2)}) copy-start(f32[3,8,128,128]{3,2,1,0:T(8,128)S(1)} %get-tuple-element.42.refs_6_.pairs_b.stored_b) | copy-start | bytes 4718596
  34.9 5.1 %collective-permute-start.6 = (f32[3,2,8,128]{3,2,1,0:T(8,128)S(1)}, f32[3,2,8,128]{3,2,1,0:T(8,128)S(1)}, u32[]{:S(2)}, u32[]{:S(2)}) collective-permute-start(f32[3,2,8,128]{3,2,1,0:T(8,128)S(1)} %shard_map.200.refs_3_), channel_id=1, source_target_pairs={{0,64},{64,128},{128,192},{192,0},{1,65},{65,129},{129,193},{193,1... | collective-permute-start | bytes 73736 | tf_op jit(solution)/shard_map/ppermute | solution.py:666
  35.0 5.0 %collective-permute-start.7 = (f32[3,2,8,128]{3,2,1,0:T(8,128)S(1)}, f32[3,2,8,128]{3,2,1,0:T(8,128)S(1)}, u32[]{:S(2)}, u32[]{:S(2)}) collective-permute-start(f32[3,2,8,128]{3,2,1,0:T(8,128)S(1)} %shard_map.200.refs_3_), channel_id=1, source_target_pairs={{64,0},{128,64},{192,128},{0,192},{65,1},{129,65},{193,129},{1,193... | collective-permute-start | bytes 73736 | tf_op jit(solution)/shard_map/ppermute | solution.py:666
  40.0 12.7 %copy-start.1 = (f32[3,8,128,128]{3,2,1,0:T(8,128)}, f32[3,8,128,128]{3,2,1,0:T(8,128)S(1)}, u32[]{:S(2)}) copy-start(f32[3,8,128,128]{3,2,1,0:T(8,128)S(1)} %get-tuple-element.43.refs_7_.pairs_c.stored_c) | copy-start | bytes 4718596
  41.8 6.9 %collective-permute-start.9 = (f32[2,8,128]{2,1,0:T(8,128)S(1)}, f32[2,8,128]{2,1,0:T(8,128)S(1)}, u32[]{:S(2)}, u32[]{:S(2)}) collective-permute-start(f32[2,8,128]{2,1,0:T(8,128)S(1)} %shard_map.201.own.own_a), channel_id=1, source_target_pairs={{0,63},{1,2},{2,1},{3,4},{4,3},{5,6},{6,5},{7,8},{8,7},{9,10},{10,... | collective-permute-start | bytes 24584 | tf_op jit(solution)/shard_map/ppermute | solution.py:659
  41.9 6.8 %collective-permute-start.8 = (f32[2,8,128]{2,1,0:T(8,128)S(1)}, f32[2,8,128]{2,1,0:T(8,128)S(1)}, u32[]{:S(2)}, u32[]{:S(2)}) collective-permute-start(f32[2,8,128]{2,1,0:T(8,128)S(1)} %shard_map.201.own.own_a), channel_id=1, source_target_pairs={{0,1},{1,0},{2,3},{3,2},{4,5},{5,4},{6,7},{7,6},{8,9},{9,8},{10,11... | collective-permute-start | bytes 24584 | tf_op jit(solution)/shard_map/ppermute | solution.py:659
  47.1 5.6 %copy-start.4 = (s32[1,512]{1,0:T(1,128)S(1)}, s32[1,512]{1,0:T(1,128)}, u32[]{:S(2)}) copy-start(s32[1,512]{1,0:T(1,128)} %order.3) | copy-start | bytes 6148
  48.8 4.0 %collective-permute-start.10 = (f32[3,2,8,128]{3,2,1,0:T(8,128)S(1)}, f32[3,2,8,128]{3,2,1,0:T(8,128)S(1)}, u32[]{:S(2)}, u32[]{:S(2)}) collective-permute-start(f32[3,2,8,128]{3,2,1,0:T(8,128)S(1)} %shard_map.203.level), channel_id=1, source_target_pairs={{0,64},{64,128},{128,192},{192,0},{1,65},{65,129},{129,193},{193,1... | collective-permute-start | bytes 73736 | tf_op jit(solution)/shard_map/ppermute | solution.py:666
  48.8 3.9 %collective-permute-start.11 = (f32[3,2,8,128]{3,2,1,0:T(8,128)S(1)}, f32[3,2,8,128]{3,2,1,0:T(8,128)S(1)}, u32[]{:S(2)}, u32[]{:S(2)}) collective-permute-start(f32[3,2,8,128]{3,2,1,0:T(8,128)S(1)} %shard_map.203.level), channel_id=1, source_target_pairs={{64,0},{128,64},{192,128},{0,192},{65,1},{129,65},{193,129},{1,193... | collective-permute-start | bytes 73736 | tf_op jit(solution)/shard_map/ppermute | solution.py:666
  55.7 5.7 %collective-permute-start.12 = (f32[8,768]{1,0:T(8,128)S(1)}, f32[8,768]{1,0:T(8,128)S(1)}, u32[]{:S(2)}, u32[]{:S(2)}) collective-permute-start(f32[8,768]{1,0:T(8,128)S(1)} %get-tuple-element.45.ordered), channel_id=1, source_target_pairs={{0,1},{1,0},{2,3},{3,2},{4,5},{5,4},{6,7},{7,6},{8,9},{9,8},{10,11... | collective-permute-start | bytes 73736 | tf_op jit(solution)/shard_map/ppermute | solution.py:659
  59.9 1.5 %copy-start.9 = (s32[48]{0:T(128)S(1)}, s32[48]{0:T(128)}, u32[]{:S(2)}) copy-start(s32[48]{0:T(128)} %shard_map.194.meta) | copy-start | bytes 580
  61.3 3.2 %collective-permute-start.13 = (f32[2,8,128]{2,1,0:T(8,128)S(1)}, f32[2,8,128]{2,1,0:T(8,128)S(1)}, u32[]{:S(2)}, u32[]{:S(2)}) collective-permute-start(f32[2,8,128]{2,1,0:T(8,128)S(1)} %get-tuple-element.51.own), channel_id=1, source_target_pairs={{0,63},{1,2},{2,1},{3,4},{4,3},{5,6},{6,5},{7,8},{8,7},{9,10},{10,... | collective-permute-start | bytes 24584 | tf_op jit(solution)/shard_map/ppermute | solution.py:659
  63.6 0.8 copy-start.2
  64.4 30.2 %all-to-all-start = ((f32[128,8,128]{2,1,0:T(8,128)}), f32[128,8,128]{2,1,0:T(8,128)}, u32[]{:S(2)}, u32[]{:S(2)}) async-start(f32[128,8,128]{2,1,0:T(8,128)} %copy-done.2), calls=%async_computation | async-start | bytes 1048576 | tf_op jit(solution)/shard_map/all_to_all | solution.py:808
  75.0 4.4 %collective-permute-start.14 = (f32[3,2,8,128]{3,2,1,0:T(8,128)S(1)}, f32[3,2,8,128]{3,2,1,0:T(8,128)S(1)}, u32[]{:S(2)}, u32[]{:S(2)}) collective-permute-start(f32[3,2,8,128]{3,2,1,0:T(8,128)S(1)} %shard_map.207.level), channel_id=1, source_target_pairs={{0,64},{64,128},{128,192},{192,0},{1,65},{65,129},{129,193},{193,1... | collective-permute-start | bytes 73736 | tf_op jit(solution)/shard_map/ppermute | solution.py:666
  75.7 3.7 %collective-permute-start.15 = (f32[3,2,8,128]{3,2,1,0:T(8,128)S(1)}, f32[3,2,8,128]{3,2,1,0:T(8,128)S(1)}, u32[]{:S(2)}, u32[]{:S(2)}) collective-permute-start(f32[3,2,8,128]{3,2,1,0:T(8,128)S(1)} %shard_map.207.level), channel_id=1, source_target_pairs={{64,0},{128,64},{192,128},{0,192},{65,1},{129,65},{193,129},{1,193... | collective-permute-start | bytes 73736 | tf_op jit(solution)/shard_map/ppermute | solution.py:666
  79.4 15.3 %copy-start.13 = (f32[8,256]{1,0:T(8,128)S(1)}, f32[8,256]{1,0:T(8,128)}, u32[]{:S(2)}) copy-start(f32[8,256]{1,0:T(8,128)} %constant.20.clone.waves) | copy-start | bytes 24580
  94.7 29.2 %copy-start.15 = (f32[2,2,72,512]{3,2,1,0:T(8,128)S(1)}, f32[2,2,72,512]{3,2,1,0:T(8,128)}, u32[]{:S(2)}) copy-start(f32[2,2,72,512]{3,2,1,0:T(8,128)} %copy-done.14) | copy-start | bytes 1769476
  94.7 29.2 %copy-start.17 = (f32[2,128,512]{2,1,0:T(8,128)S(1)}, f32[2,128,512]{2,1,0:T(8,128)}, u32[]{:S(2)}) copy-start(f32[2,128,512]{2,1,0:T(8,128)} %copy-done.16) | copy-start | bytes 1572868
  94.7 29.2 %copy-start.19 = (bf16[2,128,512]{2,1,0:T(8,128)(2,1)S(1)}, bf16[2,128,512]{2,1,0:T(8,128)(2,1)}, u32[]{:S(2)}) copy-start(bf16[2,128,512]{2,1,0:T(8,128)(2,1)} %copy-done.18) | copy-start | bytes 786436
  94.7 29.2 %copy-start.21 = (bf16[2,128,512]{2,1,0:T(8,128)(2,1)S(1)}, bf16[2,128,512]{2,1,0:T(8,128)(2,1)}, u32[]{:S(2)}) copy-start(bf16[2,128,512]{2,1,0:T(8,128)(2,1)} %copy-done.20) | copy-start | bytes 786436
  125.6 4.7 %copy-start.3 = (f32[3,512]{1,0:T(4,128)S(1)}, f32[3,512]{1,0:T(4,128)}, u32[]{:S(2)}) copy-start(f32[3,512]{1,0:T(4,128)} %residual.1) | copy-start | bytes 18436
  125.6 4.7 %copy-start.5 = (f32[3,512]{1,0:T(4,128)S(1)}, f32[3,512]{1,0:T(4,128)}, u32[]{:S(2)}) copy-start(f32[3,512]{1,0:T(4,128)} %dipoles.1) | copy-start | bytes 18436
  125.6 4.7 %collective-permute-start.16 = (f32[8,512]{1,0:T(8,128)S(1)}, f32[8,512]{1,0:T(8,128)S(1)}, u32[]{:S(2)}, u32[]{:S(2)}) collective-permute-start(f32[8,512]{1,0:T(8,128)S(1)} %shard_map.211), channel_id=1, source_target_pairs={{0,1},{1,0},{2,3},{3,2},{4,5},{5,4},{6,7},{7,6},{8,9},{9,8},{10,11... | collective-permute-start | bytes 49160 | tf_op jit(solution)/shard_map/ppermute | solution.py:659

commit v7 on v6

--- a/solution.py
+++ b/solution.py
@@ -47,12 +47,12 @@
     return (high, (values - high.astype(F32)).astype(BF16))
 
 
-def product(left, right, dims):
+def product(left, right, dims, stacked=True):
     def one(a, b):
         return lax.dot_general(a, b, dims, preferred_element_type=F32)
 
     (left_dim,), (right_dim,) = dims[0]
-    if left[0].shape[left_dim] % TILE:
+    if not stacked:
         return one(left[0], right[0]) + (one(left[0], right[1]) + one(left[1], right[0]))
     return one(
         jnp.concatenate([left[0], left[0], left[1]], left_dim),
@@ -367,21 +367,21 @@
 
 
 def direction_kernel(
-    meta, geometry, own_a, own_b, level, before, after, pairs_a, pairs_b, pairs_c, order, found, sent, bundle, pool, columns, totals, local
+    meta, geometry, own_a, own_b, level, before, after, sent, pairs_b, pairs_c, order, found, bundle, pool, columns, totals, local
 ):
     atoms = order.shape[1]
     fill_search(pool, (own_a, own_b), level, before, after, meta)
-    sweep_tiles(0, meta, geometry, (pairs_a, pairs_b, pairs_c), found, pool, columns, totals, local)
+    sweep_tiles(2, meta, geometry, (pairs_b, pairs_c), found, pool, columns, totals, local)
+    for place in range(2):
+        block = sent[place]
+        local[meta[ORDER_AT + place]] = block
+        bundle[:, atoms + place * TILE : atoms + (place + 1) * TILE] = block
     in_tiles = jnp.concatenate([local[tile] for tile in range(4)], 1)
     bundle[:, :atoms] = selected(in_tiles, order_matrix(order[...], atoms), NT)
-    for place in range(2):
-        block = found[place]
-        sent[place] = block
-        bundle[:, atoms + place * TILE : atoms + (place + 1) * TILE] = block
 
 
 def final_field_kernel(
-    meta, geometry, direction, level, before, after, pairs_a, order, stored_b, stored_c, applied, sums, pool, columns, totals, local, pairs_b, pairs_c, sems
+    meta, geometry, sent, rest, level, before, after, pairs_a, order, stored_b, stored_c, applied, sums, pool, columns, totals, local, pairs_b, pairs_c, sems
 ):
     copies = [
         pltpu.make_async_copy(source, target, sems.at[at])
@@ -390,7 +390,7 @@
     for copy in copies:
         copy.start()
     atoms = order.shape[1]
-    fill_search(pool, (direction,), level, before, after, meta)
+    fill_search(pool, (sent, rest), level, before, after, meta)
     both = (jnp.zeros((1, TILE), F32), jnp.zeros((1, TILE), F32))
     for first, pairs in ((0, pairs_a), (2, pairs_b), (3, pairs_c)):
         if first:
@@ -402,7 +402,7 @@
             tile = meta[ORDER_AT + place]
             apply_tile(meta, tile, at, pairs, geometry, pool, columns, totals)
             block = geometry[tile]
-            ahead = direction[place]
+            ahead = rest[first - 2 + at] if first else sent[at]
             field = field_rows(totals)
             rows = []
             for part in range(3):
@@ -472,8 +472,19 @@
     return total
 
 
-def tables_kernel(meta, mine, beside, cas_high, cas_low, tab_x, tab_y, w_high, w_low, slope_z):
-    cas = (cas_high[meta[PARITY_AT]], cas_low[meta[PARITY_AT]])
+def tables_kernel(
+    meta, mine, beside, stored_high, stored_low, tab_x, tab_y, w_high, w_low, slope_z, cas_high, cas_low, sems
+):
+    core = meta[PARITY_AT]
+    copies = [
+        pltpu.make_async_copy(stored_high.at[core], cas_high, sems.at[0]),
+        pltpu.make_async_copy(stored_low.at[core], cas_low, sems.at[1]),
+    ]
+    for copy in copies:
+        copy.start()
+    for copy in copies:
+        copy.wait()
+    cas = (cas_high[...], cas_low[...])
     for side, statics in enumerate((mine, beside)):
         atoms = tab_x.shape[3]
         cells = statics[0:3, :atoms].astype(jnp.int32)
@@ -552,10 +563,10 @@
     copies[0].wait()
     copies[1].wait()
     cas_x = (x_high[...], x_low[...])
-    along_x = product(halves(padded[...]), cas_x, NN)
+    along_x = product(halves(padded[...]), cas_x, NN, False)
     for copy in copies[2:]:
         copy.wait()
-    spectrum = product((yt_high[...], yt_low[...]), halves(along_x), NN)
+    spectrum = product((yt_high[...], yt_low[...]), halves(along_x), NN, False)
     freq_z = lax.axis_index("slab") * (2 * n_pair) + 2 * lax.axis_index("pair") + lax.axis_index("core")
     ids_x = lax.broadcasted_iota(jnp.int32, (1, G), 1)
     by_x = waves[...]
@@ -568,8 +579,8 @@
     factor = (1.0 - anchor) * (by_x[1:2] * by_z[1:2]) * by_y[:, 1:2] / (math.pi * float(G) ** 3 * squares)
     scaled = spectrum * factor
     energy = jnp.sum(jnp.sum(spectrum * scaled, axis=0, keepdims=True), axis=1, keepdims=True)
-    back = halves(product((y_high[...], y_low[...]), halves(scaled), NN))
-    planes = product(back, cas_x, NT)
+    back = halves(product((y_high[...], y_low[...]), halves(scaled), NN, False))
+    planes = product(back, cas_x, NT, False)
     for s in range(n_slab):
         for y in range(y_rows):
             flat[s * n_pair : (s + 1) * n_pair, y * x_rows : (y + 1) * x_rows] = planes[
@@ -724,6 +735,7 @@
         out_shape=jax.ShapeDtypeStruct((48,), jnp.int32),
         in_specs=[smem, smem, smem, pl.BlockSpec(memory_space=pltpu.VMEM)],
         out_specs=smem,
+        compiler_params=pltpu.CompilerParams(vmem_limit_bytes=SMALL_VMEM),
         cost_estimate=pl.CostEstimate(flops=10**8, bytes_accessed=1 << 20, transcendentals=0),
     )(tile_lists, tile_counts, send_tiles, sent)
     first, statics_beside = around(sent, statics, beneath=meta)
@@ -738,6 +750,35 @@
     cas_z = cas_matrix(freq_by_core.reshape(-1), freq).reshape(2, half, G)
     wide_x = np.zeros((n_slab, TILE, G))
     wide_x[:, :x_rows] = cas_x.reshape(n_slab, x_rows, G)
+    def pairs_of(place, count):
+        return call(
+            functools.partial(pair_kernel, place, count, extents),
+            [((22, 8, TILE), F32), ((3, 8 * count, TILE, TILE), F32), ((count, 8, TILE), F32)],
+            10**9,
+            smem=1,
+            scratch=(pltpu.VMEM((4, TILE, TILE), F32), total_scratch),
+        )(meta, own, *first)
+
+    geometry, pairs_a, search_a = pairs_of(0, 2)
+    _, pairs_b, search_b = pairs_of(2, 1)
+    _, pairs_c, search_c = pairs_of(3, 1)
+    sweep_scratch = (pool_scratch, pltpu.VMEM((3, TILE, TILE), F32), total_scratch)
+    second, _ = around(search_a, beneath=search_b)
+
+    def sweep(place, owns, received, banks):
+        return call(
+            functools.partial(sweep_kernel, place, len(owns)),
+            [two_shape],
+            10**8,
+            smem=1,
+            scratch=sweep_scratch,
+        )(meta, geometry, *owns, *received, *banks)[0]
+
+    searches = (search_a, search_b, search_c)
+    next_a = sweep(0, searches, second, (pairs_a,))
+    next_b = sweep(2, searches, second, (pairs_b, pairs_c))
+    third, _ = around(next_a, beneath=next_b)
+    statics_beside, _ = lax.optimization_barrier((statics_beside, third[0]))
     tables = call(
         tables_kernel,
         [
@@ -750,47 +791,22 @@
         10**8,
         smem=1,
         vmem=LARGE_VMEM,
+        scratch=(pltpu.VMEM((half, G), BF16),) * 2 + (pltpu.SemaphoreType.DMA((2,)),),
+        hbm=2,
     )(meta, statics, statics_beside, *split_constant(cas_z))
-    level, before, after = first
+    level, before, after = third
     after, _ = lax.optimization_barrier((after, tables[1]))
-    first = (level, before, after)
-
-    def pairs_of(place, count):
-        return call(
-            functools.partial(pair_kernel, place, count, extents),
-            [((22, 8, TILE), F32), ((3, 8 * count, TILE, TILE), F32), ((count, 8, TILE), F32)],
-            10**9,
-            smem=1,
-            scratch=(pltpu.VMEM((4, TILE, TILE), F32), total_scratch),
-        )(meta, own, *first)
-
-    geometry, pairs_a, search_a = pairs_of(0, 2)
-    _, pairs_b, search_b = pairs_of(2, 1)
-    _, pairs_c, search_c = pairs_of(3, 1)
-    sweep_scratch = (pool_scratch, pltpu.VMEM((3, TILE, TILE), F32), total_scratch)
-    second, _ = around(search_a, beneath=search_b)
-
-    def sweep(place, banks):
-        owns = (search_a, search_b, search_c)
-        return call(
-            functools.partial(sweep_kernel, place, len(owns)),
-            [two_shape],
-            10**8,
-            smem=1,
-            scratch=sweep_scratch,
-        )(meta, geometry, *owns, *second, *banks)[0]
-
-    next_a = sweep(0, (pairs_a,))
-    next_b = sweep(2, (pairs_b, pairs_c))
-    third, _ = around(next_a, beneath=next_b)
+    third = (level, before, after)
     local_scratch = pltpu.VMEM((4, 8, TILE), F32)
-    direction, sent, ordered = call(
+    sent = sweep(0, (next_a, next_b), third, (pairs_a,))
+    outer = beside(sent, True)
+    rest, ordered = call(
         direction_kernel,
-        [tile_shape, two_shape, ((8, atoms + 2 * TILE), F32)],
+        [two_shape, ((8, atoms + 2 * TILE), F32)],
         10**8,
         smem=1,
         scratch=sweep_scratch + (local_scratch,),
-    )(meta, geometry, next_a, next_b, *third, pairs_a, pairs_b, pairs_c, tile_order)
+    )(meta, geometry, next_a, next_b, *third, sent, pairs_b, pairs_c, tile_order)
     ordered_beside = beside(ordered, False)
     message = ((half, 8, TILE), F32)
     flat_scratch = pltpu.VMEM((half, 8 * TILE), F32)
@@ -803,8 +819,7 @@
         scratch=(flat_scratch,),
         vmem=LARGE_VMEM,
     )(meta, ordered_beside, spread_own, *tables)[0]
-    late, _ = lax.optimization_barrier((sent, spread_own))
-    spread, outer = lax.optimization_barrier((spread, beside(late, True)))
+    spread, outer = lax.optimization_barrier((spread, outer))
     grid = lax.all_to_all(spread, CHIPS, 0, 0, tiled=True)
     last = along_slab(joined(sent, ordered_beside, outer))
     applied, sums = call(
@@ -816,7 +831,7 @@
         + (local_scratch, pltpu.VMEM(*one_bank), pltpu.VMEM(*one_bank), pltpu.SemaphoreType.DMA((2,))),
         vmem=LARGE_VMEM,
         hbm=2,
-    )(meta, geometry, direction, *last, pairs_a, tile_order, pairs_b, pairs_c)
+    )(meta, geometry, sent, rest, *last, pairs_a, tile_order, pairs_b, pairs_c)
     planes = call(
         functools.partial(plane_kernel, (n_slab, n_pair, x_rows, pair_rows)),
         [message],

time: 131 us -> 128 us (0.977)
  waiting for transfers between devices: 16.1 us -> 14.1 us
  local copies, waits for them, and re-layouts: 4.7 us -> 2.86 us
  Pallas kernels: 35.9 us -> 37.3 us
    ppermute x4, starting transfers between devices: 1.21 us -> 3.49 us  [along_slab(): lax.ppermute(level, 'slab', up)]
    ppermute x4, starting transfers between devices: 8.52 us -> 6.32 us  [along_slab(): lax.ppermute(level, 'slab', down)]
    unnamed x44 -> x36, local copies, waits for them, and re-layouts: 4.7 us -> 2.86 us
    all_to_all x1, starting transfers between devices: 10.5 us -> 8.86 us  [local(): grid = lax.all_to_all(spread, CHIPS, 0, 0, tiled=True)]
    pallas_call x18 -> x19, Pallas kernels: 32.5 us -> 34.1 us  [run(): pl.pallas_call(kernel, out_shape=[jax.ShapeDtypeStruct(shape, dtype) for...]
  transfers between devices with their start and end apart: 18 -> 18, of which waited for: 4 -> 3; matrix products, arithmetic and copies ran while one was open for 0% -> 0% of each run, Pallas kernels for 15% -> 17%
where the time goes in v7:
time: 128 us
  starting transfers between devices  48.2 us (38%)
  Pallas kernels  37.3 us (29%)
  blocking collectives  24.5 us (19%)
  waiting for transfers between devices  14.1 us (11%)
  local copies, waits for them, and re-layouts  2.86 us (2%)
    pallas_call x19, Pallas kernels, run(): pl.pallas_call(kernel, out_shape=[jax.ShapeDtypeStruct(shape, dtype) for...  34.1 us
    ppermute x9, starting transfers between devices, beside(): return lax.ppermute(block, BOTH, swap_pairs(n_slab, n_space, odd))  29.5 us
    all_to_all x1, blocking collectives, local(): returned = lax.all_to_all(planes, CHIPS, 0, 0, tiled=True)  24.5 us
    all_to_all x1, waiting for transfers between devices, local(): grid = lax.all_to_all(spread, CHIPS, 0, 0, tiled=True)  10.8 us
    all_to_all x1, starting transfers between devices, local(): grid = lax.all_to_all(spread, CHIPS, 0, 0, tiled=True)  8.86 us
    ppermute x4, starting transfers between devices, along_slab(): lax.ppermute(level, 'slab', down)  6.32 us
    ppermute x4, starting transfers between devices, along_slab(): lax.ppermute(level, 'slab', up)  3.49 us
    ppermute x4, waiting for transfers between devices, along_slab(): lax.ppermute(level, 'slab', up)  3.3 us
  transfers between devices with their start and end apart: 18, of which 3 were waited for; matrix products, arithmetic and copies ran while one was open for 0% of the time, Pallas kernels for 17%

profile of v7, /device:TPU:1, one launch (start us, length us, event | category | flops | bytes accessed | tf_op | source)
XLA Modules:
  0.0 128.0 jit_solution(11762347531587864388)
XLA Ops:
  0.6 0.6 copy-done.6
  1.3 1.5 %shard_map.193 = (f32[4,8,128]{2,1,0:T(8,128)S(1)}, f32[2,8,128]{2,1,0:T(8,128)S(1)}, f32[8,768]{1,0:T(8,128)S(1)}) custom-call(s32[1,2]{1,0:T(1,128)S(1)} %copy-done.6, f32[3,512]{1,0:T(4,128)} %residual.1, s32[3,512]{1,0:T(4,128)} %refs_1_.2, f32[3,512]{1,0:T(4,128)} %refs_2_.2, f32[512]{0:T(512)} %refs_3_.2, s32[1,512]{1,0:T(1,128)} %order.3), custom_call_target="tpu_custom_call" | custom-call | tf_op jit(solution)/shard_map/pallas_call | solution.py:707
  2.8 3.3 %collective-permute-start = (f32[8,768]{1,0:T(8,128)S(1)}, f32[8,768]{1,0:T(8,128)S(1)}, u32[]{:S(2)}, u32[]{:S(2)}) collective-permute-start(f32[8,768]{1,0:T(8,128)S(1)} %get-tuple-element.31.mine), channel_id=1, source_target_pairs={{0,1},{1,0},{2,3},{3,2},{4,5},{5,4},{6,7},{7,6},{8,9},{9,8},{10,11... | collective-permute-start | bytes 73736 | tf_op jit(solution)/shard_map/ppermute | solution.py:670
  6.2 0.0 collective-permute-start.1
  6.2 0.7 copy-done.7
  6.9 0.7 copy-done.8
  7.5 1.7 %shard_map.194.meta = s32[48]{0:T(128)S(1)} custom-call(s32[1,4,8]{2,1,0:T(4,128)S(1)} %copy-done.7, s32[1,4]{1,0:T(1,128)S(1)} %copy-done.8, s32[1,2]{1,0:T(1,128)S(1)} %copy-done.6, f32[2,8,128]{2,1,0:T(8,128)S(1)} %get-tuple-element.29.after.own), custom_call_target="tpu_custom_call" | custom-call | flops 100000000 | bytes 1048576 | tf_op jit(solution)/shard_map/pallas_call | solution.py:733
  9.3 0.0 collective-permute-done.1.outer
  9.3 0.0 collective-permute-done.inner.beside
  9.3 1.2 collective-permute-start.2
  10.5 1.6 %collective-permute-start.3 = (f32[3,2,8,128]{3,2,1,0:T(8,128)S(1)}, f32[3,2,8,128]{3,2,1,0:T(8,128)S(1)}, u32[]{:S(2)}, u32[]{:S(2)}) collective-permute-start(f32[3,2,8,128]{3,2,1,0:T(8,128)S(1)} %shard_map.195.level), channel_id=1, source_target_pairs={{64,0},{128,64},{192,128},{0,192},{65,1},{129,65},{193,129},{1,193... | collective-permute-start | bytes 73736 | tf_op jit(solution)/shard_map/ppermute | solution.py:677
  12.0 1.5 %collective-permute-done.2.before = f32[3,2,8,128]{3,2,1,0:T(8,128)S(1)} collective-permute-done((f32[3,2,8,128]{3,2,1,0:T(8,128)S(1)}, f32[3,2,8,128]{3,2,1,0:T(8,128)S(1)}, u32[]{:S(2)}, u32[]{:S(2)}) %collective-permute-start.2) | collective-permute-done | bytes 24608 | tf_op jit(solution)/shard_map/ppermute | solution.py:677
  13.5 0.0 collective-permute-done.3.after
  13.5 3.3 %shard_map.196 = (f32[22,8,128]{2,1,0:T(8,128)S(1)}, f32[3,16,128,128]{3,2,1,0:T(8,128)S(1)}, f32[2,8,128]{2,1,0:T(8,128)S(1)}) custom-call(s32[48]{0:T(128)S(1)} %shard_map.194.meta, f32[4,8,128]{2,1,0:T(8,128)S(1)} %get-tuple-element.30.own, f32[3,2,8,128]{3,2,1,0:T(8,128)S(1)} %shard_map.195.level, f32[3,2,8,128]{3,2,1,0:T(8,128)S(1)} %collective-permute-done.2.before, ...), custom_call_target="tpu_custom_call" | custom-call | flops 1000000000 | bytes 1048576 | tf_op jit(solution)/shard_map/pallas_call | solution.py:124
  16.8 2.7 %collective-permute-start.5 = (f32[2,8,128]{2,1,0:T(8,128)S(1)}, f32[2,8,128]{2,1,0:T(8,128)S(1)}, u32[]{:S(2)}, u32[]{:S(2)}) collective-permute-start(f32[2,8,128]{2,1,0:T(8,128)S(1)} %get-tuple-element.34.own.refs_0_), channel_id=1, source_target_pairs={{0,63},{1,2},{2,1},{3,4},{4,3},{5,6},{6,5},{7,8},{8,7},{9,10},{10,... | collective-permute-start | bytes 24584 | tf_op jit(solution)/shard_map/ppermute | solution.py:670
  19.5 8.8 %collective-permute-start.4 = (f32[2,8,128]{2,1,0:T(8,128)S(1)}, f32[2,8,128]{2,1,0:T(8,128)S(1)}, u32[]{:S(2)}, u32[]{:S(2)}) collective-permute-start(f32[2,8,128]{2,1,0:T(8,128)S(1)} %get-tuple-element.34.own.refs_0_), channel_id=1, source_target_pairs={{0,1},{1,0},{2,3},{3,2},{4,5},{5,4},{6,7},{7,6},{8,9},{9,8},{10,11... | collective-permute-start | bytes 24584 | tf_op jit(solution)/shard_map/ppermute | solution.py:670
  28.3 2.4 %shard_map.197 = (f32[22,8,128]{2,1,0:T(8,128)}, f32[3,8,128,128]{3,2,1,0:T(8,128)S(1)}, f32[1,8,128]{2,1,0:T(8,128)S(1)}) custom-call(s32[48]{0:T(128)S(1)} %shard_map.194.meta, f32[4,8,128]{2,1,0:T(8,128)S(1)} %get-tuple-element.30.own, f32[3,2,8,128]{3,2,1,0:T(8,128)S(1)} %shard_map.195.level, f32[3,2,8,128]{3,2,1,0:T(8,128)S(1)} %collective-permute-done.2.before, ...), custom_call_target="tpu_custom_call" | custom-call | flops 1000000000 | bytes 1048576 | tf_op jit(solution)/shard_map/pallas_call | solution.py:124
  30.6 0.0 collective-permute-done.5.outer
  30.6 0.0 collective-permute-done.4.inner
  30.7 0.4 collective-permute-start.6
  31.0 2.4 %collective-permute-start.7 = (f32[3,2,8,128]{3,2,1,0:T(8,128)S(1)}, f32[3,2,8,128]{3,2,1,0:T(8,128)S(1)}, u32[]{:S(2)}, u32[]{:S(2)}) collective-permute-start(f32[3,2,8,128]{3,2,1,0:T(8,128)S(1)} %shard_map.199.refs_3_), channel_id=1, source_target_pairs={{64,0},{128,64},{192,128},{0,192},{65,1},{129,65},{193,129},{1,193... | collective-permute-start | bytes 73736 | tf_op jit(solution)/shard_map/ppermute | solution.py:677
  33.4 2.4 %shard_map.198 = (f32[22,8,128]{2,1,0:T(8,128)}, f32[3,8,128,128]{3,2,1,0:T(8,128)S(1)}, f32[1,8,128]{2,1,0:T(8,128)S(1)}) custom-call(s32[48]{0:T(128)S(1)} %shard_map.194.meta, f32[4,8,128]{2,1,0:T(8,128)S(1)} %get-tuple-element.30.own, f32[3,2,8,128]{3,2,1,0:T(8,128)S(1)} %shard_map.195.level, f32[3,2,8,128]{3,2,1,0:T(8,128)S(1)} %collective-permute-done.2.before, ...), custom_call_target="tpu_custom_call" | custom-call | flops 1000000000 | bytes 1048576 | tf_op jit(solution)/shard_map/pallas_call | solution.py:124
  35.8 0.0 collective-permute-done.6.refs_4_
  35.8 0.0 collective-permute-done.7.refs_5_
  35.8 1.7 %shard_map.200.own.refs_0_.own_a = f32[2,8,128]{2,1,0:T(8,128)S(1)} custom-call(s32[48]{0:T(128)S(1)} %shard_map.194.meta, f32[22,8,128]{2,1,0:T(8,128)S(1)} %get-tuple-element.33.geometry, f32[2,8,128]{2,1,0:T(8,128)S(1)} %get-tuple-element.34.own.refs_0_, f32[1,8,128]{2,1,0:T(8,128)S(1)} %get-tuple-element.35.refs_1_, ...), custom_call_target="tpu_custom_call" | custom-call | flops 100000000 | bytes 1048576 | tf_op jit(solution)/shard_map/pallas_call | solution.py:124
  37.5 0.1 collective-permute-start.9
  37.6 5.5 %collective-permute-start.8 = (f32[2,8,128]{2,1,0:T(8,128)S(1)}, f32[2,8,128]{2,1,0:T(8,128)S(1)}, u32[]{:S(2)}, u32[]{:S(2)}) collective-permute-start(f32[2,8,128]{2,1,0:T(8,128)S(1)} %shard_map.200.own.refs_0_.own_a), channel_id=1, source_target_pairs={{0,1},{1,0},{2,3},{3,2},{4,5},{5,4},{6,7},{7,6},{8,9},{9,8},{10,11... | collective-permute-start | bytes 24584 | tf_op jit(solution)/shard_map/ppermute | solution.py:670
  43.1 1.6 %shard_map.201.refs_1_.own_b = f32[2,8,128]{2,1,0:T(8,128)S(1)} custom-call(s32[48]{0:T(128)S(1)} %shard_map.194.meta, f32[22,8,128]{2,1,0:T(8,128)S(1)} %get-tuple-element.33.geometry, f32[2,8,128]{2,1,0:T(8,128)S(1)} %get-tuple-element.34.own.refs_0_, f32[1,8,128]{2,1,0:T(8,128)S(1)} %get-tuple-element.35.refs_1_, ...), custom_call_target="tpu_custom_call" | custom-call | flops 100000000 | bytes 1048576 | tf_op jit(solution)/shard_map/pallas_call | solution.py:124
  44.7 0.0 collective-permute-done.9.outer
  44.7 0.0 collective-permute-done.8.inner
  44.8 0.3 collective-permute-start.11
  45.0 1.3 collective-permute-start.10
  46.3 3.3 %shard_map.203 = (f32[2,2,72,512]{3,2,1,0:T(8,128)S(1)}, f32[2,2,8,512]{3,2,1,0:T(8,128)S(1)}, bf16[2,128,512]{2,1,0:T(8,128)(2,1)S(1)}, bf16[2,128,512]{2,1,0:T(8,128)(2,1)S(1)}, f32[2,128,512]{2,1,0:T(8,128)S(1)}) custom-call(s32[48]{0:T(128)S(1)} %shard_map.194.meta, f32[8,768]{1,0:T(8,128)S(1)} %get-tuple-element.31.mine, ...), custom_call_target="tpu_custom_call" | custom-call | flops 100000000 | bytes 1048576 | tf_op jit(solution)/shard_map/pallas_call | solution.py:124
  49.6 0.0 collective-permute-done.11.refs_4_.after
  49.6 0.0 copy-start.4
  49.7 0.0 collective-permute-done.10.refs_3_.before
  49.7 1.7 %shard_map.204.sent.own = f32[2,8,128]{2,1,0:T(8,128)S(1)} custom-call(s32[48]{0:T(128)S(1)} %shard_map.194.meta, f32[22,8,128]{2,1,0:T(8,128)S(1)} %get-tuple-element.33.geometry, f32[2,8,128]{2,1,0:T(8,128)S(1)} %shard_map.200.own.refs_0_.own_a, f32[2,8,128]{2,1,0:T(8,128)S(1)} %shard_map.201.refs_1_.own_b, f32[3,2,8,128]{3,2,1,0:T(8,128)S(1)} %shard_map.202.refs_2_.level, ...), custom_call_target="tpu_custom_call" | custom-call | flops 100000000 | bytes 1048576 | tf_op jit(solution)/shard_map/pallas_call | solution.py:124
  51.4 0.1 collective-permute-start.13
  51.5 1.8 %shard_map.205 = (f32[2,8,128]{2,1,0:T(8,128)S(1)}, f32[8,768]{1,0:T(8,128)S(1)}) custom-call(s32[48]{0:T(128)S(1)} %shard_map.194.meta, f32[22,8,128]{2,1,0:T(8,128)S(1)} %get-tuple-element.33.geometry, f32[2,8,128]{2,1,0:T(8,128)S(1)} %shard_map.200.own.refs_0_.own_a, f32[2,8,128]{2,1,0:T(8,128)S(1)} %shard_map.201.refs_1_.own_b, ...), custom_call_target="tpu_custom_call" | custom-call | flops 100000000 | bytes 1048576 | tf_op jit(solution)/shard_map/pallas_call | solution.py:124
  53.3 5.6 %collective-permute-start.12 = (f32[8,768]{1,0:T(8,128)S(1)}, f32[8,768]{1,0:T(8,128)S(1)}, u32[]{:S(2)}, u32[]{:S(2)}) collective-permute-start(f32[8,768]{1,0:T(8,128)S(1)} %get-tuple-element.45.ordered), channel_id=1, source_target_pairs={{0,1},{1,0},{2,3},{3,2},{4,5},{5,4},{6,7},{7,6},{8,9},{9,8},{10,11... | collective-permute-start | bytes 73736 | tf_op jit(solution)/shard_map/ppermute | solution.py:670
  59.0 1.3 %shard_map.206.mine = f32[128,576]{1,0:T(8,128)S(1)} custom-call(f32[8,768]{1,0:T(8,128)S(1)} %get-tuple-element.45.ordered, f32[2,2,72,512]{3,2,1,0:T(8,128)S(1)} %get-tuple-element.46.tab_x, f32[2,2,8,512]{3,2,1,0:T(8,128)S(1)} %get-tuple-element.43.tab_y, bf16[2,128,512]{2,1,0:T(8,128)(2,1)S(1)} %get-tuple-element.47.w_high, ...), custom_call_target="tpu_custom_call" | custom-call | flops 1000000000 | bytes 1048576 | tf_op jit(solution)/shard_map/pallas_call | solution.py:124
  60.3 0.0 collective-permute-done.12.ordered.inner
  60.3 0.0 copy-done.10
  60.3 0.0 copy-done.12
  60.4 0.0 copy-done.14
  60.4 0.0 copy-done.16
  60.4 2.2 %shard_map.207 = f32[128,8,128]{2,1,0:T(8,128)S(1)} custom-call(s32[48]{0:T(128)S(1)} %shard_map.194.meta, f32[8,768]{1,0:T(8,128)S(1)} %collective-permute-done.12.ordered.inner, f32[128,576]{1,0:T(8,128)S(1)} %shard_map.206.mine, f32[2,2,72,512]{3,2,1,0:T(8,128)S(1)} %get-tuple-element.46.tab_x, f32[2,2,8,512]{3,2,1,0:T(8,128)S(1)} %get-tuple-element.43.tab_y, ...), custom_call_target="tpu_custom_call" | custom-call | flops 1000000000 | bytes 1048576 | tf_op jit(solution)/shard_map/pallas_call | solution.py:124
  62.6 0.8 copy-done.2
  63.4 0.0 collective-permute-done.13.outer
  63.4 8.9 %all-to-all-start = ((f32[128,8,128]{2,1,0:T(8,128)}), f32[128,8,128]{2,1,0:T(8,128)}, u32[]{:S(2)}, u32[]{:S(2)}) async-start(f32[128,8,128]{2,1,0:T(8,128)} %copy-done.2), calls=%async_computation | async-start | bytes 1048576 | tf_op jit(solution)/shard_map/all_to_all | solution.py:823
  72.3 0.7 collective-permute-start.14
  72.9 2.1 %collective-permute-start.15 = (f32[3,2,8,128]{3,2,1,0:T(8,128)S(1)}, f32[3,2,8,128]{3,2,1,0:T(8,128)S(1)}, u32[]{:S(2)}, u32[]{:S(2)}) collective-permute-start(f32[3,2,8,128]{3,2,1,0:T(8,128)S(1)} %shard_map.208.level), channel_id=1, source_target_pairs={{64,0},{128,64},{192,128},{0,192},{65,1},{129,65},{193,129},{1,193... | collective-permute-start | bytes 73736 | tf_op jit(solution)/shard_map/ppermute | solution.py:677
  75.0 1.8 %collective-permute-done.14.before = f32[3,2,8,128]{3,2,1,0:T(8,128)S(1)} collective-permute-done((f32[3,2,8,128]{3,2,1,0:T(8,128)S(1)}, f32[3,2,8,128]{3,2,1,0:T(8,128)S(1)}, u32[]{:S(2)}, u32[]{:S(2)}) %collective-permute-start.14) | collective-permute-done | bytes 24608 | tf_op jit(solution)/shard_map/ppermute | solution.py:677
  76.8 0.0 collective-permute-done.15.after
  76.8 3.4 %shard_map.209 = (f32[8,512]{1,0:T(8,128)S(1)}, f32[8,128]{1,0:T(8,128)S(1)}) custom-call(s32[48]{0:T(128)S(1)} %shard_map.194.meta, f32[22,8,128]{2,1,0:T(8,128)S(1)} %get-tuple-element.33.geometry, f32[2,8,128]{2,1,0:T(8,128)S(1)} %shard_map.204.sent.own, f32[2,8,128]{2,1,0:T(8,128)S(1)} %get-tuple-element.51.rest, f32[3,2,8,128]{3,2,1,0:T(8,128)S(1)} %shard_map.208.level, ...), custom_call_target="tpu_custom_call" | custom-call | flops 1000000000 | bytes 1048576 | tf_op jit(solution)/shard_map/pallas_call | solution.py:124
  80.2 10.8 %all-to-all-done.grid = f32[128,8,128]{2,1,0:T(8,128)} async-done(((f32[128,8,128]{2,1,0:T(8,128)}), f32[128,8,128]{2,1,0:T(8,128)}, u32[]{:S(2)}, u32[]{:S(2)}) %all-to-all-start) | async-done | bytes 524320 | tf_op jit(solution)/shard_map/all_to_all | solution.py:823
  91.0 0.0 copy-start.17
  91.0 4.8 %shard_map.210 = f32[128,8,128]{2,1,0:T(8,128)S(1)} custom-call(f32[128,8,128]{2,1,0:T(8,128)} %all-to-all-done.grid, f32[8,256]{1,0:T(8,128)S(1)} %copy-done.9, f32[8,128]{1,0:T(8,128)S(1)} %get-tuple-element.53.sums, bf16[512,256]{1,0:T(8,128)(2,1)} %constant.21.clone.refs_0_, bf16[512,256]{1,0:T(8,128)(2,1)} %constant.22.clone.refs_1_, ...), custom_call_target="tpu_custom_call" | custom-call | flops 1000000000 | bytes 1048576 | tf_op jit(solution)/shard_map/pallas_call | solution.py:124
  95.8 24.5 %all_to_all.10.grid = f32[128,8,128]{2,1,0:T(8,128)S(1)} all-to-all(f32[128,8,128]{2,1,0:T(8,128)S(1)} %shard_map.210), channel_id=1, replica_groups=mesh['slab'=4,'pair'=32,'core'=2] {'slab','pair'}, dimensions={0} | all-to-all | bytes 1048576 | tf_op jit(solution)/shard_map/all_to_all | solution.py:854
  120.4 1.7 %shard_map.212 = f32[8,512]{1,0:T(8,128)S(1)} custom-call(s32[48]{0:T(128)S(1)} %shard_map.194.meta, f32[128,8,128]{2,1,0:T(8,128)S(1)} %all_to_all.10.grid, f32[2,2,72,512]{3,2,1,0:T(8,128)S(1)} %copy-done.11, f32[2,2,8,512]{3,2,1,0:T(8,128)S(1)} %get-tuple-element.43.tab_y, bf16[2,128,512]{2,1,0:T(8,128)(2,1)S(1)} %copy-done.15, ...), custom_call_target="tpu_custom_call" | custom-call | flops 1000000000 | bytes 1048576 | tf_op jit(solution)/shard_map/pallas_call | solution.py:124
  122.0 3.4 %collective-permute-start.16 = (f32[8,512]{1,0:T(8,128)S(1)}, f32[8,512]{1,0:T(8,128)S(1)}, u32[]{:S(2)}, u32[]{:S(2)}) collective-permute-start(f32[8,512]{1,0:T(8,128)S(1)} %shard_map.212), channel_id=1, source_target_pairs={{0,1},{1,0},{2,3},{3,2},{4,5},{5,4},{6,7},{7,6},{8,9},{9,8},{10,11... | collective-permute-start | bytes 49160 | tf_op jit(solution)/shard_map/ppermute | solution.py:670
  125.5 1.7 %shard_map.211.mine = f32[8,512]{1,0:T(8,128)S(1)} custom-call(s32[48]{0:T(128)S(1)} %shard_map.194.meta, f32[128,8,128]{2,1,0:T(8,128)S(1)} %all_to_all.10.grid, f32[2,2,72,512]{3,2,1,0:T(8,128)S(1)} %copy-done.11, f32[2,2,8,512]{3,2,1,0:T(8,128)S(1)} %get-tuple-element.43.tab_y, bf16[2,128,512]{2,1,0:T(8,128)(2,1)S(1)} %copy-done.15, ...), custom_call_target="tpu_custom_call" | custom-call | flops 1000000000 | bytes 1048576 | tf_op jit(solution)/shard_map/pallas_call | solution.py:124
  127.1 0.0 collective-permute-done.16.theirs
  127.1 0.9 shard_map.213
  (30 shorter events, 0.1 us)
Async XLA Ops:
  0.6 0.7 copy-start.6
  2.8 6.4 %collective-permute-start = (f32[8,768]{1,0:T(8,128)S(1)}, f32[8,768]{1,0:T(8,128)S(1)}, u32[]{:S(2)}, u32[]{:S(2)}) collective-permute-start(f32[8,768]{1,0:T(8,128)S(1)} %get-tuple-element.31.mine), channel_id=1, source_target_pairs={{0,1},{1,0},{2,3},{3,2},{4,5},{5,4},{6,7},{7,6},{8,9},{9,8},{10,11... | collective-permute-start | bytes 73736 | tf_op jit(solution)/shard_map/ppermute | solution.py:670
  6.2 3.1 %collective-permute-start.1 = (f32[2,8,128]{2,1,0:T(8,128)S(1)}, f32[2,8,128]{2,1,0:T(8,128)S(1)}, u32[]{:S(2)}, u32[]{:S(2)}) collective-permute-start(f32[2,8,128]{2,1,0:T(8,128)S(1)} %get-tuple-element.29.after.own), channel_id=1, source_target_pairs={{0,63},{1,2},{2,1},{3,4},{4,3},{5,6},{6,5},{7,8},{8,7},{9,10},{10,... | collective-permute-start | bytes 24584 | tf_op jit(solution)/shard_map/ppermute | solution.py:670
  6.2 0.7 copy-start.7
  6.8 0.7 copy-start.8
  9.3 4.3 %collective-permute-start.2 = (f32[3,2,8,128]{3,2,1,0:T(8,128)S(1)}, f32[3,2,8,128]{3,2,1,0:T(8,128)S(1)}, u32[]{:S(2)}, u32[]{:S(2)}) collective-permute-start(f32[3,2,8,128]{3,2,1,0:T(8,128)S(1)} %shard_map.195.level), channel_id=1, source_target_pairs={{0,64},{64,128},{128,192},{192,0},{1,65},{65,129},{129,193},{193,1... | collective-permute-start | bytes 73736 | tf_op jit(solution)/shard_map/ppermute | solution.py:677
  10.5 3.1 %collective-permute-start.3 = (f32[3,2,8,128]{3,2,1,0:T(8,128)S(1)}, f32[3,2,8,128]{3,2,1,0:T(8,128)S(1)}, u32[]{:S(2)}, u32[]{:S(2)}) collective-permute-start(f32[3,2,8,128]{3,2,1,0:T(8,128)S(1)} %shard_map.195.level), channel_id=1, source_target_pairs={{64,0},{128,64},{192,128},{0,192},{65,1},{129,65},{193,129},{1,193... | collective-permute-start | bytes 73736 | tf_op jit(solution)/shard_map/ppermute | solution.py:677
  16.8 13.8 %collective-permute-start.5 = (f32[2,8,128]{2,1,0:T(8,128)S(1)}, f32[2,8,128]{2,1,0:T(8,128)S(1)}, u32[]{:S(2)}, u32[]{:S(2)}) collective-permute-start(f32[2,8,128]{2,1,0:T(8,128)S(1)} %get-tuple-element.34.own.refs_0_), channel_id=1, source_target_pairs={{0,63},{1,2},{2,1},{3,4},{4,3},{5,6},{6,5},{7,8},{8,7},{9,10},{10,... | collective-permute-start | bytes 24584 | tf_op jit(solution)/shard_map/ppermute | solution.py:670
  19.5 11.2 %collective-permute-start.4 = (f32[2,8,128]{2,1,0:T(8,128)S(1)}, f32[2,8,128]{2,1,0:T(8,128)S(1)}, u32[]{:S(2)}, u32[]{:S(2)}) collective-permute-start(f32[2,8,128]{2,1,0:T(8,128)S(1)} %get-tuple-element.34.own.refs_0_), channel_id=1, source_target_pairs={{0,1},{1,0},{2,3},{3,2},{4,5},{5,4},{6,7},{7,6},{8,9},{9,8},{10,11... | collective-permute-start | bytes 24584 | tf_op jit(solution)/shard_map/ppermute | solution.py:670
  30.6 20.9 %copy-start = (f32[3,8,128,128]{3,2,1,0:T(8,128)}, f32[3,8,128,128]{3,2,1,0:T(8,128)S(1)}, u32[]{:S(2)}) copy-start(f32[3,8,128,128]{3,2,1,0:T(8,128)S(1)} %get-tuple-element.39.refs_6_.pairs_b.stored_b) | copy-start | bytes 4718596
  30.7 5.1 %collective-permute-start.6 = (f32[3,2,8,128]{3,2,1,0:T(8,128)S(1)}, f32[3,2,8,128]{3,2,1,0:T(8,128)S(1)}, u32[]{:S(2)}, u32[]{:S(2)}) collective-permute-start(f32[3,2,8,128]{3,2,1,0:T(8,128)S(1)} %shard_map.199.refs_3_), channel_id=1, source_target_pairs={{0,64},{64,128},{128,192},{192,0},{1,65},{65,129},{129,193},{193,1... | collective-permute-start | bytes 73736 | tf_op jit(solution)/shard_map/ppermute | solution.py:677
  31.0 4.8 %collective-permute-start.7 = (f32[3,2,8,128]{3,2,1,0:T(8,128)S(1)}, f32[3,2,8,128]{3,2,1,0:T(8,128)S(1)}, u32[]{:S(2)}, u32[]{:S(2)}) collective-permute-start(f32[3,2,8,128]{3,2,1,0:T(8,128)S(1)} %shard_map.199.refs_3_), channel_id=1, source_target_pairs={{64,0},{128,64},{192,128},{0,192},{65,1},{129,65},{193,129},{1,193... | collective-permute-start | bytes 73736 | tf_op jit(solution)/shard_map/ppermute | solution.py:677
  35.8 15.7 %copy-start.1 = (f32[3,8,128,128]{3,2,1,0:T(8,128)}, f32[3,8,128,128]{3,2,1,0:T(8,128)S(1)}, u32[]{:S(2)}) copy-start(f32[3,8,128,128]{3,2,1,0:T(8,128)S(1)} %get-tuple-element.40.refs_7_.pairs_c.stored_c) | copy-start | bytes 4718596
  37.5 7.2 %collective-permute-start.9 = (f32[2,8,128]{2,1,0:T(8,128)S(1)}, f32[2,8,128]{2,1,0:T(8,128)S(1)}, u32[]{:S(2)}, u32[]{:S(2)}) collective-permute-start(f32[2,8,128]{2,1,0:T(8,128)S(1)} %shard_map.200.own.refs_0_.own_a), channel_id=1, source_target_pairs={{0,63},{1,2},{2,1},{3,4},{4,3},{5,6},{6,5},{7,8},{8,7},{9,10},{10,... | collective-permute-start | bytes 24584 | tf_op jit(solution)/shard_map/ppermute | solution.py:670
  37.6 7.1 %collective-permute-start.8 = (f32[2,8,128]{2,1,0:T(8,128)S(1)}, f32[2,8,128]{2,1,0:T(8,128)S(1)}, u32[]{:S(2)}, u32[]{:S(2)}) collective-permute-start(f32[2,8,128]{2,1,0:T(8,128)S(1)} %shard_map.200.own.refs_0_.own_a), channel_id=1, source_target_pairs={{0,1},{1,0},{2,3},{3,2},{4,5},{5,4},{6,7},{7,6},{8,9},{9,8},{10,11... | collective-permute-start | bytes 24584 | tf_op jit(solution)/shard_map/ppermute | solution.py:670
  44.8 4.9 %collective-permute-start.11 = (f32[3,2,8,128]{3,2,1,0:T(8,128)S(1)}, f32[3,2,8,128]{3,2,1,0:T(8,128)S(1)}, u32[]{:S(2)}, u32[]{:S(2)}) collective-permute-start(f32[3,2,8,128]{3,2,1,0:T(8,128)S(1)} %shard_map.202.refs_2_.level), channel_id=1, source_target_pairs={{64,0},{128,64},{192,128},{0,192},{65,1},{129,65},{193,129},{1,193... | collective-permute-start | bytes 73736 | tf_op jit(solution)/shard_map/ppermute | solution.py:677
  45.0 4.6 %collective-permute-start.10 = (f32[3,2,8,128]{3,2,1,0:T(8,128)S(1)}, f32[3,2,8,128]{3,2,1,0:T(8,128)S(1)}, u32[]{:S(2)}, u32[]{:S(2)}) collective-permute-start(f32[3,2,8,128]{3,2,1,0:T(8,128)S(1)} %shard_map.202.refs_2_.level), channel_id=1, source_target_pairs={{0,64},{64,128},{128,192},{192,0},{1,65},{65,129},{129,193},{193,1... | collective-permute-start | bytes 73736 | tf_op jit(solution)/shard_map/ppermute | solution.py:677
  49.6 10.7 %copy-start.10 = (f32[2,2,72,512]{3,2,1,0:T(8,128)}, f32[2,2,72,512]{3,2,1,0:T(8,128)S(1)}, u32[]{:S(2)}) copy-start(f32[2,2,72,512]{3,2,1,0:T(8,128)S(1)} %get-tuple-element.46.tab_x) | copy-start | bytes 1769476
  49.6 10.7 %copy-start.12 = (f32[2,128,512]{2,1,0:T(8,128)}, f32[2,128,512]{2,1,0:T(8,128)S(1)}, u32[]{:S(2)}) copy-start(f32[2,128,512]{2,1,0:T(8,128)S(1)} %get-tuple-element.49.slope_z) | copy-start | bytes 1572868
  49.6 10.7 %copy-start.14 = (bf16[2,128,512]{2,1,0:T(8,128)(2,1)}, bf16[2,128,512]{2,1,0:T(8,128)(2,1)S(1)}, u32[]{:S(2)}) copy-start(bf16[2,128,512]{2,1,0:T(8,128)(2,1)S(1)} %get-tuple-element.47.w_high) | copy-start | bytes 786436
  49.6 10.7 %copy-start.16 = (bf16[2,128,512]{2,1,0:T(8,128)(2,1)}, bf16[2,128,512]{2,1,0:T(8,128)(2,1)S(1)}, u32[]{:S(2)}) copy-start(bf16[2,128,512]{2,1,0:T(8,128)(2,1)S(1)} %get-tuple-element.48.w_low) | copy-start | bytes 786436
  49.6 1.9 %copy-start.4 = (s32[1,512]{1,0:T(1,128)S(1)}, s32[1,512]{1,0:T(1,128)}, u32[]{:S(2)}) copy-start(s32[1,512]{1,0:T(1,128)} %order.3) | copy-start | bytes 6148
  51.4 12.0 %collective-permute-start.13 = (f32[2,8,128]{2,1,0:T(8,128)S(1)}, f32[2,8,128]{2,1,0:T(8,128)S(1)}, u32[]{:S(2)}, u32[]{:S(2)}) collective-permute-start(f32[2,8,128]{2,1,0:T(8,128)S(1)} %shard_map.204.sent.own), channel_id=1, source_target_pairs={{0,63},{1,2},{2,1},{3,4},{4,3},{5,6},{6,5},{7,8},{8,7},{9,10},{10,... | collective-permute-start | bytes 24584 | tf_op jit(solution)/shard_map/ppermute | solution.py:670
  53.3 7.0 %collective-permute-start.12 = (f32[8,768]{1,0:T(8,128)S(1)}, f32[8,768]{1,0:T(8,128)S(1)}, u32[]{:S(2)}, u32[]{:S(2)}) collective-permute-start(f32[8,768]{1,0:T(8,128)S(1)} %get-tuple-element.45.ordered), channel_id=1, source_target_pairs={{0,1},{1,0},{2,3},{3,2},{4,5},{5,4},{6,7},{7,6},{8,9},{9,8},{10,11... | collective-permute-start | bytes 73736 | tf_op jit(solution)/shard_map/ppermute | solution.py:670
  62.6 0.8 copy-start.2
  63.4 27.6 %all-to-all-start = ((f32[128,8,128]{2,1,0:T(8,128)}), f32[128,8,128]{2,1,0:T(8,128)}, u32[]{:S(2)}, u32[]{:S(2)}) async-start(f32[128,8,128]{2,1,0:T(8,128)} %copy-done.2), calls=%async_computation | async-start | bytes 1048576 | tf_op jit(solution)/shard_map/all_to_all | solution.py:823
  72.3 4.5 %collective-permute-start.14 = (f32[3,2,8,128]{3,2,1,0:T(8,128)S(1)}, f32[3,2,8,128]{3,2,1,0:T(8,128)S(1)}, u32[]{:S(2)}, u32[]{:S(2)}) collective-permute-start(f32[3,2,8,128]{3,2,1,0:T(8,128)S(1)} %shard_map.208.level), channel_id=1, source_target_pairs={{0,64},{64,128},{128,192},{192,0},{1,65},{65,129},{129,193},{193,1... | collective-permute-start | bytes 73736 | tf_op jit(solution)/shard_map/ppermute | solution.py:677
  72.9 3.9 %collective-permute-start.15 = (f32[3,2,8,128]{3,2,1,0:T(8,128)S(1)}, f32[3,2,8,128]{3,2,1,0:T(8,128)S(1)}, u32[]{:S(2)}, u32[]{:S(2)}) collective-permute-start(f32[3,2,8,128]{3,2,1,0:T(8,128)S(1)} %shard_map.208.level), channel_id=1, source_target_pairs={{64,0},{128,64},{192,128},{0,192},{65,1},{129,65},{193,129},{1,193... | collective-permute-start | bytes 73736 | tf_op jit(solution)/shard_map/ppermute | solution.py:677
  76.8 14.2 %copy-start.9 = (f32[8,256]{1,0:T(8,128)S(1)}, f32[8,256]{1,0:T(8,128)}, u32[]{:S(2)}) copy-start(f32[8,256]{1,0:T(8,128)} %constant.20.clone.waves) | copy-start | bytes 24580
  91.0 29.4 %copy-start.11 = (f32[2,2,72,512]{3,2,1,0:T(8,128)S(1)}, f32[2,2,72,512]{3,2,1,0:T(8,128)}, u32[]{:S(2)}) copy-start(f32[2,2,72,512]{3,2,1,0:T(8,128)} %copy-done.10) | copy-start | bytes 1769476
  91.0 29.4 %copy-start.13 = (f32[2,128,512]{2,1,0:T(8,128)S(1)}, f32[2,128,512]{2,1,0:T(8,128)}, u32[]{:S(2)}) copy-start(f32[2,128,512]{2,1,0:T(8,128)} %copy-done.12) | copy-start | bytes 1572868
  91.0 29.4 %copy-start.15 = (bf16[2,128,512]{2,1,0:T(8,128)(2,1)S(1)}, bf16[2,128,512]{2,1,0:T(8,128)(2,1)}, u32[]{:S(2)}) copy-start(bf16[2,128,512]{2,1,0:T(8,128)(2,1)} %copy-done.14) | copy-start | bytes 786436
  91.0 29.4 %copy-start.17 = (bf16[2,128,512]{2,1,0:T(8,128)(2,1)S(1)}, bf16[2,128,512]{2,1,0:T(8,128)(2,1)}, u32[]{:S(2)}) copy-start(bf16[2,128,512]{2,1,0:T(8,128)(2,1)} %copy-done.16) | copy-start | bytes 786436
  122.0 5.1 %copy-start.3 = (f32[3,512]{1,0:T(4,128)S(1)}, f32[3,512]{1,0:T(4,128)}, u32[]{:S(2)}) copy-start(f32[3,512]{1,0:T(4,128)} %residual.1) | copy-start | bytes 18436
  122.0 5.1 %copy-start.5 = (f32[3,512]{1,0:T(4,128)S(1)}, f32[3,512]{1,0:T(4,128)}, u32[]{:S(2)}) copy-start(f32[3,512]{1,0:T(4,128)} %dipoles.1) | copy-start | bytes 18436
  122.0 5.1 %collective-permute-start.16 = (f32[8,512]{1,0:T(8,128)S(1)}, f32[8,512]{1,0:T(8,128)S(1)}, u32[]{:S(2)}, u32[]{:S(2)}) collective-permute-start(f32[8,512]{1,0:T(8,128)S(1)} %shard_map.212), channel_id=1, source_target_pairs={{0,1},{1,0},{2,3},{3,2},{4,5},{5,4},{6,7},{7,6},{8,9},{9,8},{10,11... | collective-permute-start | bytes 49160 | tf_op jit(solution)/shard_map/ppermute | solution.py:670

commit v8 on v7

--- a/solution.py
+++ b/solution.py
@@ -112,7 +112,7 @@
     meta[PARITY_AT] = parity
 
 
-def call(kernel, outs, flops, smem=0, scratch=(), vmem=SMALL_VMEM, hbm=0):
+def call(kernel, outs, flops, smem=0, scratch=(), vmem=SMALL_VMEM, hbm=0, hbm_outs=False):
     def run(*args):
         kept = len(args) - hbm
         args = args[:kept] + tuple(
@@ -123,9 +123,11 @@
         in_specs += [pl.BlockSpec(memory_space=pltpu.HBM)] * hbm
         return pl.pallas_call(
             kernel,
-            out_shape=[jax.ShapeDtypeStruct(shape, dtype) for shape, dtype in outs],
+            out_shape=[
+                (pltpu.HBM if hbm_outs else jax.ShapeDtypeStruct)(shape, dtype) for shape, dtype in outs
+            ],
             in_specs=in_specs,
-            out_specs=[pl.BlockSpec(memory_space=pltpu.VMEM)] * len(outs),
+            out_specs=[pl.BlockSpec(memory_space=pltpu.HBM if hbm_outs else pltpu.VMEM)] * len(outs),
             scratch_shapes=list(scratch),
             compiler_params=pltpu.CompilerParams(vmem_limit_bytes=vmem),
             cost_estimate=pl.CostEstimate(
@@ -136,8 +138,8 @@
     return run
 
 
-def gather_kernel(send, *refs):
-    sources, (own, sent, bundle), held, sems = (refs[:5], refs[5:8], refs[8:13], refs[13])
+def gather_kernel(*refs):
+    sources, (own, sent, bundle), held, sems = (refs[:6], refs[6:9], refs[9:15], refs[15])
     copies = [
         pltpu.make_async_copy(source, target, sems.at[at])
         for at, (source, target) in enumerate(zip(sources, held))
@@ -146,7 +148,7 @@
         copy.start()
     for copy in copies:
         copy.wait()
-    residual, cells, fraction, alphas, order = held
+    residual, cells, fraction, alphas, order, send = held
     atoms = residual.shape[1]
     in_cells = cells[...].astype(F32)
     bundle[0:3, :atoms] = in_cells
@@ -473,9 +475,9 @@
 
 
 def tables_kernel(
-    meta, mine, beside, stored_high, stored_low, tab_x, tab_y, w_high, w_low, slope_z, cas_high, cas_low, sems
+    mine, beside, stored_high, stored_low, tab_x, tab_y, w_high, w_low, slope_z, cas_high, cas_low, sems
 ):
-    core = meta[PARITY_AT]
+    core = lax.axis_index("core")
     copies = [
         pltpu.make_async_copy(stored_high.at[core], cas_high, sems.at[0]),
         pltpu.make_async_copy(stored_low.at[core], cas_low, sems.at[1]),
@@ -527,32 +529,57 @@
     return jnp.concatenate([grid[:, row, :] for row in range(8)], 1)
 
 
-def spread_both_kernel(shift, meta, ordered, mine, tab_x, tab_y, w_high, w_low, slope_z, out, flat):
+def spread_both_kernel(shift, ordered, mine, tab_x, tab_y, w_high, w_low, slope_z, out, flat, message, sems):
     theirs = spread_part(1, ordered[:, : tab_x.shape[3]], tab_x, tab_y, w_high, w_low, slope_z)
     ours = mine[...]
     width = ours.shape[1]
-    even = meta[PARITY_AT] == 0
+    even = lax.axis_index("core") == 0
     lower = jnp.where(even, ours, theirs)
     upper = jnp.where(even, theirs, ours)
     flat[:, :shift] = lower[:, :shift]
     flat[:, shift:width] = lower[:, shift:] + upper[:, : width - shift]
     flat[:, width : width + shift] = upper[:, width - shift :]
     flat[:, width + shift :] = jnp.zeros((flat.shape[0], flat.shape[1] - width - shift), F32)
-    put_lanes(out, flat)
-
-
-def plane_kernel(shapes, grid, waves, sums, *refs):
-    stored, out, flat, padded = (refs[:6], refs[6], refs[7], refs[8])
-    held, sems = (refs[9:15], refs[15])
+    pieces = sems.shape[0]
+    size = flat.shape[0] // pieces
+    copies = []
+    for piece in range(pieces):
+        rows = slice(piece * size, (piece + 1) * size)
+        for row in range(8):
+            message[rows, row, :] = flat[rows, row * TILE : (row + 1) * TILE]
+        copies.append(pltpu.make_async_copy(message.at[rows], out.at[rows], sems.at[piece]))
+        copies[-1].start()
+    for copy in copies:
+        copy.wait()
+
+
+def factor_of(waves, freq_z):
+    ids_x = lax.broadcasted_iota(jnp.int32, (1, G), 1)
+    by_x = waves[...]
+    by_z = jnp.sum(jnp.where(ids_x == freq_z, by_x, 0.0), axis=1, keepdims=True)
+    by_y = by_x.T
+    anchor = jnp.where(
+        (lax.broadcasted_iota(jnp.int32, (G, G), 0) + lax.broadcasted_iota(jnp.int32, (G, G), 1) + freq_z) == 0, 1.0, 0.0
+    )
+    squares = by_x[0:1] + by_y[:, 0:1] + (by_z[0:1] + anchor)
+    return (1.0 - anchor) * (by_x[1:2] * by_z[1:2]) * by_y[:, 1:2] / (math.pi * float(G) ** 3 * squares)
+
+
+def plane_kernel(shapes, waves, sums, *refs):
+    stored, out, flat, padded = (refs[:7], refs[7], refs[8], refs[9])
+    held, sems = (refs[10:17], refs[17])
     copies = [
         pltpu.make_async_copy(source, target, sems.at[at])
         for at, (source, target) in enumerate(zip(stored, held))
     ]
     for copy in copies:
         copy.start()
-    x_high, x_low, yt_high, yt_low, y_high, y_low = held
+    grid, x_high, x_low, yt_high, yt_low, y_high, y_low = held
     n_slab, n_pair, x_rows, y_rows = shapes
     width = x_rows * y_rows
+    freq_z = lax.axis_index("slab") * (2 * n_pair) + 2 * lax.axis_index("pair") + lax.axis_index("core")
+    factor = factor_of(waves, freq_z)
+    copies[0].wait()
     flat[...] = get_lanes(grid)
     padded[...] = jnp.zeros(padded.shape, F32)
     for s in range(n_slab):
@@ -560,23 +587,11 @@
             padded[y * n_pair : (y + 1) * n_pair, s * TILE : s * TILE + x_rows] = flat[
                 s * n_pair : (s + 1) * n_pair, y * x_rows : (y + 1) * x_rows
             ]
-    copies[0].wait()
-    copies[1].wait()
+    for copy in copies[1:]:
+        copy.wait()
     cas_x = (x_high[...], x_low[...])
     along_x = product(halves(padded[...]), cas_x, NN, False)
-    for copy in copies[2:]:
-        copy.wait()
     spectrum = product((yt_high[...], yt_low[...]), halves(along_x), NN, False)
-    freq_z = lax.axis_index("slab") * (2 * n_pair) + 2 * lax.axis_index("pair") + lax.axis_index("core")
-    ids_x = lax.broadcasted_iota(jnp.int32, (1, G), 1)
-    by_x = waves[...]
-    by_z = jnp.sum(jnp.where(ids_x == freq_z, by_x, 0.0), axis=1, keepdims=True)
-    by_y = by_x.T
-    anchor = jnp.where(
-        (lax.broadcasted_iota(jnp.int32, (G, G), 0) + lax.broadcasted_iota(jnp.int32, (G, G), 1) + freq_z) == 0, 1.0, 0.0
-    )
-    squares = by_x[0:1] + by_y[:, 0:1] + (by_z[0:1] + anchor)
-    factor = (1.0 - anchor) * (by_x[1:2] * by_z[1:2]) * by_y[:, 1:2] / (math.pi * float(G) ** 3 * squares)
     scaled = spectrum * factor
     energy = jnp.sum(jnp.sum(spectrum * scaled, axis=0, keepdims=True), axis=1, keepdims=True)
     back = halves(product((y_high[...], y_low[...]), halves(scaled), NN, False))
@@ -610,12 +625,12 @@
     return fields
 
 
-def probe_kernel(side, shift, meta, grid, tab_x, tab_y, w_high, w_low, slope_z, out):
+def probe_kernel(side, shift, grid, tab_x, tab_y, w_high, w_low, slope_z, out):
     matrix = get_lanes(grid)
     width = tab_x.shape[2] * tab_y.shape[2]
     low_side = 0 if side == 0 else 1
     planes = jnp.where(
-        meta[PARITY_AT] == low_side, matrix[:, :width], matrix[:, shift : shift + width]
+        lax.axis_index("core") == low_side, matrix[:, :width], matrix[:, shift : shift + width]
     )
     fields = probe_part(side, halves(planes), tab_x, tab_y, w_high, w_low, slope_z)
     atoms = out.shape[1]
@@ -711,7 +726,7 @@
             jax.ShapeDtypeStruct(*two_shape),
             jax.ShapeDtypeStruct((8, atoms + 2 * TILE), F32),
         ],
-        in_specs=[pl.BlockSpec(memory_space=pltpu.SMEM)] + [pl.BlockSpec(memory_space=pltpu.HBM)] * 5,
+        in_specs=[pl.BlockSpec(memory_space=pltpu.HBM)] * 6,
         out_specs=[pl.BlockSpec(memory_space=pltpu.VMEM)] * 3,
         scratch_shapes=[
             pltpu.VMEM((3, atoms), F32),
@@ -719,14 +734,14 @@
             pltpu.VMEM((3, atoms), F32),
             pltpu.VMEM((atoms,), F32),
             pltpu.VMEM((1, atoms), jnp.int32),
-            pltpu.SemaphoreType.DMA((5,)),
+            pltpu.SMEM((1, 2), jnp.int32),
+            pltpu.SemaphoreType.DMA((6,)),
         ],
         compiler_params=pltpu.CompilerParams(vmem_limit_bytes=SMALL_VMEM),
     )(
-        send_tiles,
         *[
             pltpu.with_memory_space_constraint(array, pltpu.HBM)
-            for array in (residual, cells, fraction, polarizability, tile_order)
+            for array in (residual, cells, fraction, polarizability, tile_order, send_tiles)
         ],
     )
     smem, anywhere = (pl.BlockSpec(memory_space=pltpu.SMEM), pl.BlockSpec(memory_space=pltpu.HBM))
@@ -789,11 +804,10 @@
             ((2, half, atoms), F32),
         ],
         10**8,
-        smem=1,
         vmem=LARGE_VMEM,
         scratch=(pltpu.VMEM((half, G), BF16),) * 2 + (pltpu.SemaphoreType.DMA((2,)),),
         hbm=2,
-    )(meta, statics, statics_beside, *split_constant(cas_z))
+    )(statics, statics_beside, *split_constant(cas_z))
     level, before, after = third
     after, _ = lax.optimization_barrier((after, tables[1]))
     third = (level, before, after)
@@ -815,10 +829,10 @@
         functools.partial(spread_both_kernel, shift),
         [message],
         10**9,
-        smem=1,
-        scratch=(flat_scratch,),
+        scratch=(flat_scratch, pltpu.VMEM(*message), pltpu.SemaphoreType.DMA((4,))),
         vmem=LARGE_VMEM,
-    )(meta, ordered_beside, spread_own, *tables)[0]
+        hbm_outs=True,
+    )(ordered_beside, spread_own, *tables)[0]
     spread, outer = lax.optimization_barrier((spread, outer))
     grid = lax.all_to_all(spread, CHIPS, 0, 0, tiled=True)
     last = along_slab(joined(sent, ordered_beside, outer))
@@ -836,17 +850,17 @@
         functools.partial(plane_kernel, (n_slab, n_pair, x_rows, pair_rows)),
         [message],
         10**9,
-        scratch=(flat_scratch, pltpu.VMEM((n_pair * pair_rows, n_slab * TILE), F32))
+        scratch=(flat_scratch, pltpu.VMEM((n_pair * pair_rows, n_slab * TILE), F32), pltpu.VMEM(*message))
         + (pltpu.VMEM((n_slab * TILE, G), BF16),) * 2
         + (pltpu.VMEM((G, n_pair * pair_rows), BF16),) * 2
         + (pltpu.VMEM((n_pair * pair_rows, G), BF16),) * 2
-        + (pltpu.SemaphoreType.DMA((6,)),),
+        + (pltpu.SemaphoreType.DMA((7,)),),
         vmem=LARGE_VMEM,
-        hbm=6,
+        hbm=7,
     )(
-        grid,
         wave_factors(),
         sums,
+        grid,
         *split_constant(wide_x.reshape(-1, G)),
         *split_constant(cas_y.T),
         *split_constant(cas_y),
@@ -855,8 +869,8 @@
 
     def probe(side):
         return call(
-            functools.partial(probe_kernel, side, shift), [((8, atoms), F32)], 10**9, smem=1, vmem=LARGE_VMEM
-        )(meta, returned, *tables)[0]
+            functools.partial(probe_kernel, side, shift), [((8, atoms), F32)], 10**9, vmem=LARGE_VMEM
+        )(returned, *tables)[0]
 
     theirs = beside(probe(1), False)
     three = ((3, atoms), F32)

time: 128 us -> 125 us (0.977)
  waiting for transfers between devices: 14.1 us -> 16.7 us
  Pallas kernels: 37.3 us -> 34.8 us
  starting transfers between devices: 48.2 us -> 45.9 us
    ppermute x9, waiting for transfers between devices: 0.02 us -> 2.17 us  [beside(): return lax.ppermute(block, BOTH, swap_pairs(n_slab, n_space, odd))]
    pallas_call x19, Pallas kernels: 34.1 us -> 32 us  [run(): pl.pallas_call(kernel, out_shape=[(pltpu.HBM if hbm_outs else jax.ShapeDt...]
    ppermute x9, starting transfers between devices: 29.5 us -> 27.9 us  [beside(): return lax.ppermute(block, BOTH, swap_pairs(n_slab, n_space, odd))]
    unnamed x36 -> x34, local copies, waits for them, and re-layouts: 2.86 us -> 2.05 us
  transfers between devices with their start and end apart: 18 -> 18, of which waited for: 3 -> 6; matrix products, arithmetic and copies ran while one was open for 0% -> 0% of each run, Pallas kernels for 17% -> 17%
where the time goes in v8:
time: 125 us
  starting transfers between devices  45.9 us (37%)
  Pallas kernels  34.8 us (28%)
  blocking collectives  24.5 us (20%)
  waiting for transfers between devices  16.7 us (13%)
  local copies, waits for them, and re-layouts  2.05 us (2%)
    pallas_call x19, Pallas kernels, run(): pl.pallas_call(kernel, out_shape=[(pltpu.HBM if hbm_outs else jax.ShapeDt...  32 us
    ppermute x9, starting transfers between devices, beside(): return lax.ppermute(block, BOTH, swap_pairs(n_slab, n_space, odd))  27.9 us
    all_to_all x1, blocking collectives, local(): returned = lax.all_to_all(planes, CHIPS, 0, 0, tiled=True)  24.5 us
    all_to_all x1, waiting for transfers between devices, local(): grid = lax.all_to_all(spread, CHIPS, 0, 0, tiled=True)  10.8 us
    all_to_all x1, starting transfers between devices, local(): grid = lax.all_to_all(spread, CHIPS, 0, 0, tiled=True)  8.32 us
    ppermute x4, starting transfers between devices, along_slab(): lax.ppermute(level, 'slab', down)  7.4 us
    ppermute x4, waiting for transfers between devices, along_slab(): lax.ppermute(level, 'slab', up)  3.69 us
  transfers between devices with their start and end apart: 18, of which 6 were waited for; matrix products, arithmetic and copies ran while one was open for 0% of the time, Pallas kernels for 17%

profile of v8, /device:TPU:1, one launch (start us, length us, event | category | flops | bytes accessed | tf_op | source)
XLA Modules:
  0.0 124.8 jit_solution(9228094007946870153)
XLA Ops:
  0.6 1.1 shard_map.193
  1.7 3.3 %collective-permute-start = (f32[8,768]{1,0:T(8,128)S(1)}, f32[8,768]{1,0:T(8,128)S(1)}, u32[]{:S(2)}, u32[]{:S(2)}) collective-permute-start(f32[8,768]{1,0:T(8,128)S(1)} %get-tuple-element.31.mine), channel_id=1, source_target_pairs={{0,1},{1,0},{2,3},{3,2},{4,5},{5,4},{6,7},{7,6},{8,9},{9,8},{10,11... | collective-permute-start | bytes 73736 | tf_op jit(solution)/shard_map/ppermute | solution.py:685
  5.0 0.0 collective-permute-start.1
  5.0 0.7 copy-done.5
  5.7 0.7 copy-done.6
  6.4 0.7 copy-done.7
  7.0 1.7 %shard_map.194.meta = s32[48]{0:T(128)S(1)} custom-call(s32[1,4,8]{2,1,0:T(4,128)S(1)} %copy-done.6, s32[1,4]{1,0:T(1,128)S(1)} %copy-done.7, s32[1,2]{1,0:T(1,128)S(1)} %copy-done.5, f32[2,8,128]{2,1,0:T(8,128)S(1)} %get-tuple-element.29.after.own), custom_call_target="tpu_custom_call" | custom-call | flops 100000000 | bytes 1048576 | tf_op jit(solution)/shard_map/pallas_call | solution.py:748
  8.8 0.0 collective-permute-done.1.outer
  8.8 0.0 collective-permute-done.inner.beside
  8.8 1.2 collective-permute-start.2
  10.0 1.6 %collective-permute-start.3 = (f32[3,2,8,128]{3,2,1,0:T(8,128)S(1)}, f32[3,2,8,128]{3,2,1,0:T(8,128)S(1)}, u32[]{:S(2)}, u32[]{:S(2)}) collective-permute-start(f32[3,2,8,128]{3,2,1,0:T(8,128)S(1)} %shard_map.195.level), channel_id=1, source_target_pairs={{64,0},{128,64},{192,128},{0,192},{65,1},{129,65},{193,129},{1,193... | collective-permute-start | bytes 73736 | tf_op jit(solution)/shard_map/ppermute | solution.py:692
  11.6 1.2 collective-permute-done.2.before
  12.8 0.0 collective-permute-done.3.after
  12.8 3.3 %shard_map.196 = (f32[22,8,128]{2,1,0:T(8,128)S(1)}, f32[3,16,128,128]{3,2,1,0:T(8,128)S(1)}, f32[2,8,128]{2,1,0:T(8,128)S(1)}) custom-call(s32[48]{0:T(128)S(1)} %shard_map.194.meta, f32[4,8,128]{2,1,0:T(8,128)S(1)} %get-tuple-element.30.own, f32[3,2,8,128]{3,2,1,0:T(8,128)S(1)} %shard_map.195.level, f32[3,2,8,128]{3,2,1,0:T(8,128)S(1)} %collective-permute-done.2.before, ...), custom_call_target="tpu_custom_call" | custom-call | flops 1000000000 | bytes 1048576 | tf_op jit(solution)/shard_map/pallas_call | solution.py:124
  16.0 10.0 %collective-permute-start.4 = (f32[2,8,128]{2,1,0:T(8,128)S(1)}, f32[2,8,128]{2,1,0:T(8,128)S(1)}, u32[]{:S(2)}, u32[]{:S(2)}) collective-permute-start(f32[2,8,128]{2,1,0:T(8,128)S(1)} %get-tuple-element.34.own.refs_0_), channel_id=1, source_target_pairs={{0,1},{1,0},{2,3},{3,2},{4,5},{5,4},{6,7},{7,6},{8,9},{9,8},{10,11... | collective-permute-start | bytes 24584 | tf_op jit(solution)/shard_map/ppermute | solution.py:685
  26.0 0.0 collective-permute-start.5
  26.0 2.4 %shard_map.197 = (f32[22,8,128]{2,1,0:T(8,128)}, f32[3,8,128,128]{3,2,1,0:T(8,128)S(1)}, f32[1,8,128]{2,1,0:T(8,128)S(1)}) custom-call(s32[48]{0:T(128)S(1)} %shard_map.194.meta, f32[4,8,128]{2,1,0:T(8,128)S(1)} %get-tuple-element.30.own, f32[3,2,8,128]{3,2,1,0:T(8,128)S(1)} %shard_map.195.level, f32[3,2,8,128]{3,2,1,0:T(8,128)S(1)} %collective-permute-done.2.before, ...), custom_call_target="tpu_custom_call" | custom-call | flops 1000000000 | bytes 1048576 | tf_op jit(solution)/shard_map/pallas_call | solution.py:124
  28.4 0.7 collective-permute-done.5.outer
  29.1 0.0 collective-permute-done.4.inner
  29.1 0.0 collective-permute-start.6
  29.1 2.7 %collective-permute-start.7 = (f32[3,2,8,128]{3,2,1,0:T(8,128)S(1)}, f32[3,2,8,128]{3,2,1,0:T(8,128)S(1)}, u32[]{:S(2)}, u32[]{:S(2)}) collective-permute-start(f32[3,2,8,128]{3,2,1,0:T(8,128)S(1)} %shard_map.199.refs_3_), channel_id=1, source_target_pairs={{64,0},{128,64},{192,128},{0,192},{65,1},{129,65},{193,129},{1,193... | collective-permute-start | bytes 73736 | tf_op jit(solution)/shard_map/ppermute | solution.py:692
  31.8 2.4 %shard_map.198 = (f32[22,8,128]{2,1,0:T(8,128)}, f32[3,8,128,128]{3,2,1,0:T(8,128)S(1)}, f32[1,8,128]{2,1,0:T(8,128)S(1)}) custom-call(s32[48]{0:T(128)S(1)} %shard_map.194.meta, f32[4,8,128]{2,1,0:T(8,128)S(1)} %get-tuple-element.30.own, f32[3,2,8,128]{3,2,1,0:T(8,128)S(1)} %shard_map.195.level, f32[3,2,8,128]{3,2,1,0:T(8,128)S(1)} %collective-permute-done.2.before, ...), custom_call_target="tpu_custom_call" | custom-call | flops 1000000000 | bytes 1048576 | tf_op jit(solution)/shard_map/pallas_call | solution.py:124
  34.2 0.0 collective-permute-done.6.refs_4_
  34.2 0.0 collective-permute-done.7.refs_5_
  34.2 1.7 %shard_map.200.own.refs_0_.own_a = f32[2,8,128]{2,1,0:T(8,128)S(1)} custom-call(s32[48]{0:T(128)S(1)} %shard_map.194.meta, f32[22,8,128]{2,1,0:T(8,128)S(1)} %get-tuple-element.33.geometry, f32[2,8,128]{2,1,0:T(8,128)S(1)} %get-tuple-element.34.own.refs_0_, f32[1,8,128]{2,1,0:T(8,128)S(1)} %get-tuple-element.35.refs_1_, ...), custom_call_target="tpu_custom_call" | custom-call | flops 100000000 | bytes 1048576 | tf_op jit(solution)/shard_map/pallas_call | solution.py:124
  35.9 5.4 %collective-permute-start.8 = (f32[2,8,128]{2,1,0:T(8,128)S(1)}, f32[2,8,128]{2,1,0:T(8,128)S(1)}, u32[]{:S(2)}, u32[]{:S(2)}) collective-permute-start(f32[2,8,128]{2,1,0:T(8,128)S(1)} %shard_map.200.own.refs_0_.own_a), channel_id=1, source_target_pairs={{0,1},{1,0},{2,3},{3,2},{4,5},{5,4},{6,7},{7,6},{8,9},{9,8},{10,11... | collective-permute-start | bytes 24584 | tf_op jit(solution)/shard_map/ppermute | solution.py:685
  41.3 0.0 collective-permute-start.9
  41.3 1.6 %shard_map.201.refs_1_.own_b = f32[2,8,128]{2,1,0:T(8,128)S(1)} custom-call(s32[48]{0:T(128)S(1)} %shard_map.194.meta, f32[22,8,128]{2,1,0:T(8,128)S(1)} %get-tuple-element.33.geometry, f32[2,8,128]{2,1,0:T(8,128)S(1)} %get-tuple-element.34.own.refs_0_, f32[1,8,128]{2,1,0:T(8,128)S(1)} %get-tuple-element.35.refs_1_, ...), custom_call_target="tpu_custom_call" | custom-call | flops 100000000 | bytes 1048576 | tf_op jit(solution)/shard_map/pallas_call | solution.py:124
  42.9 1.5 %collective-permute-done.9.outer = f32[2,8,128]{2,1,0:T(8,128)S(1)} collective-permute-done((f32[2,8,128]{2,1,0:T(8,128)S(1)}, f32[2,8,128]{2,1,0:T(8,128)S(1)}, u32[]{:S(2)}, u32[]{:S(2)}) %collective-permute-start.9) | collective-permute-done | bytes 8224 | tf_op jit(solution)/shard_map/ppermute | solution.py:685
  44.4 0.0 collective-permute-done.8.inner
  44.4 1.1 collective-permute-start.11
  45.4 0.4 collective-permute-start.10
  45.8 2.7 %shard_map.203 = (f32[2,2,72,512]{3,2,1,0:T(8,128)S(1)}, f32[2,2,8,512]{3,2,1,0:T(8,128)S(1)}, bf16[2,128,512]{2,1,0:T(8,128)(2,1)S(1)}, bf16[2,128,512]{2,1,0:T(8,128)(2,1)S(1)}, f32[2,128,512]{2,1,0:T(8,128)S(1)}) custom-call(f32[8,768]{1,0:T(8,128)S(1)} %get-tuple-element.31.mine, f32[8,768]{1,0:T(8,128)S(1)} %collective-permute-done.inner.beside, ...), custom_call_target="tpu_custom_call" | custom-call | flops 100000000 | bytes 1048576 | tf_op jit(solution)/shard_map/pallas_call | solution.py:124
  48.6 0.0 copy-start.9
  48.6 0.0 copy-start.11
  48.6 0.0 collective-permute-done.11.refs_4_.after
  48.6 0.0 copy-start.3
  48.6 0.7 collective-permute-done.10.refs_3_.before
  49.3 1.7 %shard_map.204.sent.own = f32[2,8,128]{2,1,0:T(8,128)S(1)} custom-call(s32[48]{0:T(128)S(1)} %shard_map.194.meta, f32[22,8,128]{2,1,0:T(8,128)S(1)} %get-tuple-element.33.geometry, f32[2,8,128]{2,1,0:T(8,128)S(1)} %shard_map.200.own.refs_0_.own_a, f32[2,8,128]{2,1,0:T(8,128)S(1)} %shard_map.201.refs_1_.own_b, f32[3,2,8,128]{3,2,1,0:T(8,128)S(1)} %shard_map.202.refs_2_.level, ...), custom_call_target="tpu_custom_call" | custom-call | flops 100000000 | bytes 1048576 | tf_op jit(solution)/shard_map/pallas_call | solution.py:124
  51.1 1.9 %collective-permute-start.13 = (f32[2,8,128]{2,1,0:T(8,128)S(1)}, f32[2,8,128]{2,1,0:T(8,128)S(1)}, u32[]{:S(2)}, u32[]{:S(2)}) collective-permute-start(f32[2,8,128]{2,1,0:T(8,128)S(1)} %shard_map.204.sent.own), channel_id=1, source_target_pairs={{0,63},{1,2},{2,1},{3,4},{4,3},{5,6},{6,5},{7,8},{8,7},{9,10},{10,... | collective-permute-start | bytes 24584 | tf_op jit(solution)/shard_map/ppermute | solution.py:685
  53.0 0.0 copy-done.1
  53.0 1.8 %shard_map.205 = (f32[2,8,128]{2,1,0:T(8,128)S(1)}, f32[8,768]{1,0:T(8,128)S(1)}) custom-call(s32[48]{0:T(128)S(1)} %shard_map.194.meta, f32[22,8,128]{2,1,0:T(8,128)S(1)} %get-tuple-element.33.geometry, f32[2,8,128]{2,1,0:T(8,128)S(1)} %shard_map.200.own.refs_0_.own_a, f32[2,8,128]{2,1,0:T(8,128)S(1)} %shard_map.201.refs_1_.own_b, ...), custom_call_target="tpu_custom_call" | custom-call | flops 100000000 | bytes 1048576 | tf_op jit(solution)/shard_map/pallas_call | solution.py:124
  54.8 3.9 %collective-permute-start.12 = (f32[8,768]{1,0:T(8,128)S(1)}, f32[8,768]{1,0:T(8,128)S(1)}, u32[]{:S(2)}, u32[]{:S(2)}) collective-permute-start(f32[8,768]{1,0:T(8,128)S(1)} %get-tuple-element.46.ordered), channel_id=1, source_target_pairs={{0,1},{1,0},{2,3},{3,2},{4,5},{5,4},{6,7},{7,6},{8,9},{9,8},{10,11... | collective-permute-start | bytes 73736 | tf_op jit(solution)/shard_map/ppermute | solution.py:685
  58.7 1.4 %shard_map.206.mine = f32[128,576]{1,0:T(8,128)S(1)} custom-call(f32[8,768]{1,0:T(8,128)S(1)} %get-tuple-element.46.ordered, f32[2,2,72,512]{3,2,1,0:T(8,128)S(1)} %get-tuple-element.47.tab_x, f32[2,2,8,512]{3,2,1,0:T(8,128)S(1)} %get-tuple-element.43.tab_y, bf16[2,128,512]{2,1,0:T(8,128)(2,1)S(1)} %get-tuple-element.48.w_high, ...), custom_call_target="tpu_custom_call" | custom-call | flops 1000000000 | bytes 1048576 | tf_op jit(solution)/shard_map/pallas_call | solution.py:124
  60.1 0.0 collective-permute-done.12.ordered.inner
  60.1 2.5 %shard_map.207 = f32[128,8,128]{2,1,0:T(8,128)} custom-call(f32[8,768]{1,0:T(8,128)S(1)} %collective-permute-done.12.ordered.inner, f32[128,576]{1,0:T(8,128)S(1)} %shard_map.206.mine, f32[2,2,72,512]{3,2,1,0:T(8,128)S(1)} %get-tuple-element.47.tab_x, f32[2,2,8,512]{3,2,1,0:T(8,128)S(1)} %get-tuple-element.43.tab_y, ...), custom_call_target="tpu_custom_call" | custom-call | flops 1000000000 | bytes 1048576 | tf_op jit(solution)/shard_map/pallas_call | solution.py:124
  62.6 0.0 collective-permute-done.13.outer
  62.6 8.3 %all-to-all-start = ((f32[128,8,128]{2,1,0:T(8,128)}), f32[128,8,128]{2,1,0:T(8,128)}, u32[]{:S(2)}, u32[]{:S(2)}) async-start(f32[128,8,128]{2,1,0:T(8,128)} %shard_map.207), calls=%async_computation | async-start | bytes 1048576 | tf_op jit(solution)/shard_map/all_to_all | solution.py:837
  70.9 0.7 collective-permute-start.14
  71.6 2.1 %collective-permute-start.15 = (f32[3,2,8,128]{3,2,1,0:T(8,128)S(1)}, f32[3,2,8,128]{3,2,1,0:T(8,128)S(1)}, u32[]{:S(2)}, u32[]{:S(2)}) collective-permute-start(f32[3,2,8,128]{3,2,1,0:T(8,128)S(1)} %shard_map.208.level), channel_id=1, source_target_pairs={{64,0},{128,64},{192,128},{0,192},{65,1},{129,65},{193,129},{1,193... | collective-permute-start | bytes 73736 | tf_op jit(solution)/shard_map/ppermute | solution.py:692
  73.7 1.8 %collective-permute-done.14.before = f32[3,2,8,128]{3,2,1,0:T(8,128)S(1)} collective-permute-done((f32[3,2,8,128]{3,2,1,0:T(8,128)S(1)}, f32[3,2,8,128]{3,2,1,0:T(8,128)S(1)}, u32[]{:S(2)}, u32[]{:S(2)}) %collective-permute-start.14) | collective-permute-done | bytes 24608 | tf_op jit(solution)/shard_map/ppermute | solution.py:692
  75.5 0.0 collective-permute-done.15.after
  75.5 3.4 %shard_map.209 = (f32[8,512]{1,0:T(8,128)S(1)}, f32[8,128]{1,0:T(8,128)S(1)}) custom-call(s32[48]{0:T(128)S(1)} %shard_map.194.meta, f32[22,8,128]{2,1,0:T(8,128)S(1)} %get-tuple-element.33.geometry, f32[2,8,128]{2,1,0:T(8,128)S(1)} %shard_map.204.sent.own, f32[2,8,128]{2,1,0:T(8,128)S(1)} %get-tuple-element.45.rest, f32[3,2,8,128]{3,2,1,0:T(8,128)S(1)} %shard_map.208.level, ...), custom_call_target="tpu_custom_call" | custom-call | flops 1000000000 | bytes 1048576 | tf_op jit(solution)/shard_map/pallas_call | solution.py:124
  78.9 10.8 %all-to-all-done.refs_0_ = f32[128,8,128]{2,1,0:T(8,128)} async-done(((f32[128,8,128]{2,1,0:T(8,128)}), f32[128,8,128]{2,1,0:T(8,128)}, u32[]{:S(2)}, u32[]{:S(2)}) %all-to-all-start) | async-done | bytes 524320 | tf_op jit(solution)/shard_map/all_to_all | solution.py:837
  89.7 4.1 %shard_map.210 = f32[128,8,128]{2,1,0:T(8,128)S(1)} custom-call(f32[8,256]{1,0:T(8,128)S(1)} %copy-done.8, f32[8,128]{1,0:T(8,128)S(1)} %get-tuple-element.52.sums, f32[128,8,128]{2,1,0:T(8,128)} %all-to-all-done.refs_0_, bf16[512,256]{1,0:T(8,128)(2,1)} %constant.21.clone.refs_1_, bf16[512,256]{1,0:T(8,128)(2,1)} %constant.22.clone.refs_2_, ...), custom_call_target="tpu_custom_call" | custom-call | flops 1000000000 | bytes 1048576 | tf_op jit(solution)/shard_map/pallas_call | solution.py:124
  93.8 24.5 %all_to_all.10.grid = f32[128,8,128]{2,1,0:T(8,128)S(1)} all-to-all(f32[128,8,128]{2,1,0:T(8,128)S(1)} %shard_map.210), channel_id=1, replica_groups=mesh['slab'=4,'pair'=32,'core'=2] {'slab','pair'}, dimensions={0} | all-to-all | bytes 1048576 | tf_op jit(solution)/shard_map/all_to_all | solution.py:868
  118.3 0.0 copy-done.10
  118.3 0.0 copy-done.14
  118.3 1.1 shard_map.212
  119.4 3.4 %collective-permute-start.16 = (f32[8,512]{1,0:T(8,128)S(1)}, f32[8,512]{1,0:T(8,128)S(1)}, u32[]{:S(2)}, u32[]{:S(2)}) collective-permute-start(f32[8,512]{1,0:T(8,128)S(1)} %shard_map.212), channel_id=1, source_target_pairs={{0,1},{1,0},{2,3},{3,2},{4,5},{5,4},{6,7},{7,6},{8,9},{9,8},{10,11... | collective-permute-start | bytes 49160 | tf_op jit(solution)/shard_map/ppermute | solution.py:685
  122.8 1.1 shard_map.211.mine
  123.9 0.0 collective-permute-done.16.theirs
  123.9 0.0 copy-done.2
  123.9 0.9 shard_map.213
  (28 shorter events, 0.1 us)
Async XLA Ops:
  1.7 7.1 %collective-permute-start = (f32[8,768]{1,0:T(8,128)S(1)}, f32[8,768]{1,0:T(8,128)S(1)}, u32[]{:S(2)}, u32[]{:S(2)}) collective-permute-start(f32[8,768]{1,0:T(8,128)S(1)} %get-tuple-element.31.mine), channel_id=1, source_target_pairs={{0,1},{1,0},{2,3},{3,2},{4,5},{5,4},{6,7},{7,6},{8,9},{9,8},{10,11... | collective-permute-start | bytes 73736 | tf_op jit(solution)/shard_map/ppermute | solution.py:685
  5.0 3.7 %collective-permute-start.1 = (f32[2,8,128]{2,1,0:T(8,128)S(1)}, f32[2,8,128]{2,1,0:T(8,128)S(1)}, u32[]{:S(2)}, u32[]{:S(2)}) collective-permute-start(f32[2,8,128]{2,1,0:T(8,128)S(1)} %get-tuple-element.29.after.own), channel_id=1, source_target_pairs={{0,63},{1,2},{2,1},{3,4},{4,3},{5,6},{6,5},{7,8},{8,7},{9,10},{10,... | collective-permute-start | bytes 24584 | tf_op jit(solution)/shard_map/ppermute | solution.py:685
  5.0 0.7 copy-start.5
  5.7 0.7 copy-start.6
  6.4 0.7 copy-start.7
  8.8 4.0 %collective-permute-start.2 = (f32[3,2,8,128]{3,2,1,0:T(8,128)S(1)}, f32[3,2,8,128]{3,2,1,0:T(8,128)S(1)}, u32[]{:S(2)}, u32[]{:S(2)}) collective-permute-start(f32[3,2,8,128]{3,2,1,0:T(8,128)S(1)} %shard_map.195.level), channel_id=1, source_target_pairs={{0,64},{64,128},{128,192},{192,0},{1,65},{65,129},{129,193},{193,1... | collective-permute-start | bytes 73736 | tf_op jit(solution)/shard_map/ppermute | solution.py:692
  10.0 2.8 %collective-permute-start.3 = (f32[3,2,8,128]{3,2,1,0:T(8,128)S(1)}, f32[3,2,8,128]{3,2,1,0:T(8,128)S(1)}, u32[]{:S(2)}, u32[]{:S(2)}) collective-permute-start(f32[3,2,8,128]{3,2,1,0:T(8,128)S(1)} %shard_map.195.level), channel_id=1, source_target_pairs={{64,0},{128,64},{192,128},{0,192},{65,1},{129,65},{193,129},{1,193... | collective-permute-start | bytes 73736 | tf_op jit(solution)/shard_map/ppermute | solution.py:692
  16.0 13.1 %collective-permute-start.4 = (f32[2,8,128]{2,1,0:T(8,128)S(1)}, f32[2,8,128]{2,1,0:T(8,128)S(1)}, u32[]{:S(2)}, u32[]{:S(2)}) collective-permute-start(f32[2,8,128]{2,1,0:T(8,128)S(1)} %get-tuple-element.34.own.refs_0_), channel_id=1, source_target_pairs={{0,1},{1,0},{2,3},{3,2},{4,5},{5,4},{6,7},{7,6},{8,9},{9,8},{10,11... | collective-permute-start | bytes 24584 | tf_op jit(solution)/shard_map/ppermute | solution.py:685
  26.0 3.1 %collective-permute-start.5 = (f32[2,8,128]{2,1,0:T(8,128)S(1)}, f32[2,8,128]{2,1,0:T(8,128)S(1)}, u32[]{:S(2)}, u32[]{:S(2)}) collective-permute-start(f32[2,8,128]{2,1,0:T(8,128)S(1)} %get-tuple-element.34.own.refs_0_), channel_id=1, source_target_pairs={{0,63},{1,2},{2,1},{3,4},{4,3},{5,6},{6,5},{7,8},{8,7},{9,10},{10,... | collective-permute-start | bytes 24584 | tf_op jit(solution)/shard_map/ppermute | solution.py:685
  28.4 24.6 %copy-start = (f32[3,8,128,128]{3,2,1,0:T(8,128)}, f32[3,8,128,128]{3,2,1,0:T(8,128)S(1)}, u32[]{:S(2)}) copy-start(f32[3,8,128,128]{3,2,1,0:T(8,128)S(1)} %get-tuple-element.39.refs_6_.pairs_b.stored_b) | copy-start | bytes 4718596
  29.1 5.1 %collective-permute-start.6 = (f32[3,2,8,128]{3,2,1,0:T(8,128)S(1)}, f32[3,2,8,128]{3,2,1,0:T(8,128)S(1)}, u32[]{:S(2)}, u32[]{:S(2)}) collective-permute-start(f32[3,2,8,128]{3,2,1,0:T(8,128)S(1)} %shard_map.199.refs_3_), channel_id=1, source_target_pairs={{0,64},{64,128},{128,192},{192,0},{1,65},{65,129},{129,193},{193,1... | collective-permute-start | bytes 73736 | tf_op jit(solution)/shard_map/ppermute | solution.py:692
  29.1 5.1 %collective-permute-start.7 = (f32[3,2,8,128]{3,2,1,0:T(8,128)S(1)}, f32[3,2,8,128]{3,2,1,0:T(8,128)S(1)}, u32[]{:S(2)}, u32[]{:S(2)}) collective-permute-start(f32[3,2,8,128]{3,2,1,0:T(8,128)S(1)} %shard_map.199.refs_3_), channel_id=1, source_target_pairs={{64,0},{128,64},{192,128},{0,192},{65,1},{129,65},{193,129},{1,193... | collective-permute-start | bytes 73736 | tf_op jit(solution)/shard_map/ppermute | solution.py:692
  34.2 18.8 %copy-start.1 = (f32[3,8,128,128]{3,2,1,0:T(8,128)}, f32[3,8,128,128]{3,2,1,0:T(8,128)S(1)}, u32[]{:S(2)}) copy-start(f32[3,8,128,128]{3,2,1,0:T(8,128)S(1)} %get-tuple-element.40.refs_7_.pairs_c.stored_c) | copy-start | bytes 4718596
  35.9 8.4 %collective-permute-start.8 = (f32[2,8,128]{2,1,0:T(8,128)S(1)}, f32[2,8,128]{2,1,0:T(8,128)S(1)}, u32[]{:S(2)}, u32[]{:S(2)}) collective-permute-start(f32[2,8,128]{2,1,0:T(8,128)S(1)} %shard_map.200.own.refs_0_.own_a), channel_id=1, source_target_pairs={{0,1},{1,0},{2,3},{3,2},{4,5},{5,4},{6,7},{7,6},{8,9},{9,8},{10,11... | collective-permute-start | bytes 24584 | tf_op jit(solution)/shard_map/ppermute | solution.py:685
  41.3 3.1 %collective-permute-start.9 = (f32[2,8,128]{2,1,0:T(8,128)S(1)}, f32[2,8,128]{2,1,0:T(8,128)S(1)}, u32[]{:S(2)}, u32[]{:S(2)}) collective-permute-start(f32[2,8,128]{2,1,0:T(8,128)S(1)} %shard_map.200.own.refs_0_.own_a), channel_id=1, source_target_pairs={{0,63},{1,2},{2,1},{3,4},{4,3},{5,6},{6,5},{7,8},{8,7},{9,10},{10,... | collective-permute-start | bytes 24584 | tf_op jit(solution)/shard_map/ppermute | solution.py:685
  44.4 4.2 %collective-permute-start.11 = (f32[3,2,8,128]{3,2,1,0:T(8,128)S(1)}, f32[3,2,8,128]{3,2,1,0:T(8,128)S(1)}, u32[]{:S(2)}, u32[]{:S(2)}) collective-permute-start(f32[3,2,8,128]{3,2,1,0:T(8,128)S(1)} %shard_map.202.refs_2_.level), channel_id=1, source_target_pairs={{64,0},{128,64},{192,128},{0,192},{65,1},{129,65},{193,129},{1,193... | collective-permute-start | bytes 73736 | tf_op jit(solution)/shard_map/ppermute | solution.py:692
  45.4 3.9 %collective-permute-start.10 = (f32[3,2,8,128]{3,2,1,0:T(8,128)S(1)}, f32[3,2,8,128]{3,2,1,0:T(8,128)S(1)}, u32[]{:S(2)}, u32[]{:S(2)}) collective-permute-start(f32[3,2,8,128]{3,2,1,0:T(8,128)S(1)} %shard_map.202.refs_2_.level), channel_id=1, source_target_pairs={{0,64},{64,128},{128,192},{192,0},{1,65},{65,129},{129,193},{193,1... | collective-permute-start | bytes 73736 | tf_op jit(solution)/shard_map/ppermute | solution.py:692
  48.6 11.5 %copy-start.9 = (f32[2,2,72,512]{3,2,1,0:T(8,128)}, f32[2,2,72,512]{3,2,1,0:T(8,128)S(1)}, u32[]{:S(2)}) copy-start(f32[2,2,72,512]{3,2,1,0:T(8,128)S(1)} %get-tuple-element.47.tab_x) | copy-start | bytes 1769476
  48.6 11.5 %copy-start.11 = (f32[2,128,512]{2,1,0:T(8,128)}, f32[2,128,512]{2,1,0:T(8,128)S(1)}, u32[]{:S(2)}) copy-start(f32[2,128,512]{2,1,0:T(8,128)S(1)} %get-tuple-element.50.slope_z) | copy-start | bytes 1572868
  48.6 11.5 %copy-start.13 = (bf16[2,128,512]{2,1,0:T(8,128)(2,1)}, bf16[2,128,512]{2,1,0:T(8,128)(2,1)S(1)}, u32[]{:S(2)}) copy-start(bf16[2,128,512]{2,1,0:T(8,128)(2,1)S(1)} %get-tuple-element.48.w_high) | copy-start | bytes 786436
  48.6 11.5 %copy-start.15 = (bf16[2,128,512]{2,1,0:T(8,128)(2,1)}, bf16[2,128,512]{2,1,0:T(8,128)(2,1)S(1)}, u32[]{:S(2)}) copy-start(bf16[2,128,512]{2,1,0:T(8,128)(2,1)S(1)} %get-tuple-element.49.w_low) | copy-start | bytes 786436
  48.6 4.4 %copy-start.3 = (s32[1,512]{1,0:T(1,128)S(1)}, s32[1,512]{1,0:T(1,128)}, u32[]{:S(2)}) copy-start(s32[1,512]{1,0:T(1,128)} %order.3) | copy-start | bytes 6148
  51.1 11.5 %collective-permute-start.13 = (f32[2,8,128]{2,1,0:T(8,128)S(1)}, f32[2,8,128]{2,1,0:T(8,128)S(1)}, u32[]{:S(2)}, u32[]{:S(2)}) collective-permute-start(f32[2,8,128]{2,1,0:T(8,128)S(1)} %shard_map.204.sent.own), channel_id=1, source_target_pairs={{0,63},{1,2},{2,1},{3,4},{4,3},{5,6},{6,5},{7,8},{8,7},{9,10},{10,... | collective-permute-start | bytes 24584 | tf_op jit(solution)/shard_map/ppermute | solution.py:685
  54.8 5.3 %collective-permute-start.12 = (f32[8,768]{1,0:T(8,128)S(1)}, f32[8,768]{1,0:T(8,128)S(1)}, u32[]{:S(2)}, u32[]{:S(2)}) collective-permute-start(f32[8,768]{1,0:T(8,128)S(1)} %get-tuple-element.46.ordered), channel_id=1, source_target_pairs={{0,1},{1,0},{2,3},{3,2},{4,5},{5,4},{6,7},{7,6},{8,9},{9,8},{10,11... | collective-permute-start | bytes 73736 | tf_op jit(solution)/shard_map/ppermute | solution.py:685
  62.6 27.1 %all-to-all-start = ((f32[128,8,128]{2,1,0:T(8,128)}), f32[128,8,128]{2,1,0:T(8,128)}, u32[]{:S(2)}, u32[]{:S(2)}) async-start(f32[128,8,128]{2,1,0:T(8,128)} %shard_map.207), calls=%async_computation | async-start | bytes 1048576 | tf_op jit(solution)/shard_map/all_to_all | solution.py:837
  70.9 4.5 %collective-permute-start.14 = (f32[3,2,8,128]{3,2,1,0:T(8,128)S(1)}, f32[3,2,8,128]{3,2,1,0:T(8,128)S(1)}, u32[]{:S(2)}, u32[]{:S(2)}) collective-permute-start(f32[3,2,8,128]{3,2,1,0:T(8,128)S(1)} %shard_map.208.level), channel_id=1, source_target_pairs={{0,64},{64,128},{128,192},{192,0},{1,65},{65,129},{129,193},{193,1... | collective-permute-start | bytes 73736 | tf_op jit(solution)/shard_map/ppermute | solution.py:692
  71.6 3.9 %collective-permute-start.15 = (f32[3,2,8,128]{3,2,1,0:T(8,128)S(1)}, f32[3,2,8,128]{3,2,1,0:T(8,128)S(1)}, u32[]{:S(2)}, u32[]{:S(2)}) collective-permute-start(f32[3,2,8,128]{3,2,1,0:T(8,128)S(1)} %shard_map.208.level), channel_id=1, source_target_pairs={{64,0},{128,64},{192,128},{0,192},{65,1},{129,65},{193,129},{1,193... | collective-permute-start | bytes 73736 | tf_op jit(solution)/shard_map/ppermute | solution.py:692
  75.5 14.2 %copy-start.8 = (f32[8,256]{1,0:T(8,128)S(1)}, f32[8,256]{1,0:T(8,128)}, u32[]{:S(2)}) copy-start(f32[8,256]{1,0:T(8,128)} %constant.20.clone.waves) | copy-start | bytes 24580
  89.7 28.6 %copy-start.10 = (f32[2,2,72,512]{3,2,1,0:T(8,128)S(1)}, f32[2,2,72,512]{3,2,1,0:T(8,128)}, u32[]{:S(2)}) copy-start(f32[2,2,72,512]{3,2,1,0:T(8,128)} %copy-done.9) | copy-start | bytes 1769476
  89.7 28.6 %copy-start.12 = (f32[2,128,512]{2,1,0:T(8,128)S(1)}, f32[2,128,512]{2,1,0:T(8,128)}, u32[]{:S(2)}) copy-start(f32[2,128,512]{2,1,0:T(8,128)} %copy-done.11) | copy-start | bytes 1572868
  89.7 28.6 %copy-start.14 = (bf16[2,128,512]{2,1,0:T(8,128)(2,1)S(1)}, bf16[2,128,512]{2,1,0:T(8,128)(2,1)}, u32[]{:S(2)}) copy-start(bf16[2,128,512]{2,1,0:T(8,128)(2,1)} %copy-done.13) | copy-start | bytes 786436
  89.7 28.6 %copy-start.16 = (bf16[2,128,512]{2,1,0:T(8,128)(2,1)S(1)}, bf16[2,128,512]{2,1,0:T(8,128)(2,1)}, u32[]{:S(2)}) copy-start(bf16[2,128,512]{2,1,0:T(8,128)(2,1)} %copy-done.15) | copy-start | bytes 786436
  119.4 4.5 %copy-start.2 = (f32[3,512]{1,0:T(4,128)S(1)}, f32[3,512]{1,0:T(4,128)}, u32[]{:S(2)}) copy-start(f32[3,512]{1,0:T(4,128)} %residual.1) | copy-start | bytes 18436
  119.4 4.5 %copy-start.4 = (f32[3,512]{1,0:T(4,128)S(1)}, f32[3,512]{1,0:T(4,128)}, u32[]{:S(2)}) copy-start(f32[3,512]{1,0:T(4,128)} %dipoles.1) | copy-start | bytes 18436
  119.4 4.5 %collective-permute-start.16 = (f32[8,512]{1,0:T(8,128)S(1)}, f32[8,512]{1,0:T(8,128)S(1)}, u32[]{:S(2)}, u32[]{:S(2)}) collective-permute-start(f32[8,512]{1,0:T(8,128)S(1)} %shard_map.212), channel_id=1, source_target_pairs={{0,1},{1,0},{2,3},{3,2},{4,5},{5,4},{6,7},{7,6},{8,9},{9,8},{10,11... | collective-permute-start | bytes 49160 | tf_op jit(solution)/shard_map/ppermute | solution.py:685

commit v9 on v8

--- a/solution.py
+++ b/solution.py
@@ -565,8 +565,14 @@
     return (1.0 - anchor) * (by_x[1:2] * by_z[1:2]) * by_y[:, 1:2] / (math.pi * float(G) ** 3 * squares)
 
 
+def rolled(flat, rows, start, size, amount):
+    low = start // TILE * TILE
+    high = -(-(start + size) // TILE) * TILE
+    return pltpu.roll(flat[rows, low:high], amount, 0)[:, start - low : start - low + size]
+
+
 def plane_kernel(shapes, waves, sums, *refs):
-    stored, out, flat, padded = (refs[:7], refs[7], refs[8], refs[9])
+    stored, out, flat, plane = (refs[:7], refs[7], refs[8], refs[9])
     held, sems = (refs[10:17], refs[17])
     copies = [
         pltpu.make_async_copy(source, target, sems.at[at])
@@ -576,31 +582,56 @@
         copy.start()
     grid, x_high, x_low, yt_high, yt_low, y_high, y_low = held
     n_slab, n_pair, x_rows, y_rows = shapes
+    x_own, y_own = (G // n_slab, y_rows - 4)
     width = x_rows * y_rows
     freq_z = lax.axis_index("slab") * (2 * n_pair) + 2 * lax.axis_index("pair") + lax.axis_index("core")
     factor = factor_of(waves, freq_z)
     copies[0].wait()
     flat[...] = get_lanes(grid)
-    padded[...] = jnp.zeros(padded.shape, F32)
-    for s in range(n_slab):
-        for y in range(y_rows):
-            padded[y * n_pair : (y + 1) * n_pair, s * TILE : s * TILE + x_rows] = flat[
-                s * n_pair : (s + 1) * n_pair, y * x_rows : (y + 1) * x_rows
-            ]
+    two = 2 * x_rows
+    first_own, last_own = (slice(two, 2 * two), slice(y_own * x_rows, y_own * x_rows + two))
+    slabs = [slice(s * n_pair, (s + 1) * n_pair) for s in range(n_slab)]
+    for rows in slabs:
+        from_next = rolled(flat, rows, 0, two, n_pair - 1)
+        from_last = rolled(flat, rows, width - two, two, 1)
+        flat[rows, last_own] = flat[rows, last_own] + from_next
+        flat[rows, first_own] = flat[rows, first_own] + from_last
+    padded = [
+        jnp.concatenate(
+            [flat[rows, (y + 2) * x_rows : (y + 3) * x_rows] for y in range(y_own)], 0
+        )
+        for rows in slabs
+    ]
+    for s, block in enumerate(padded):
+        plane[:, s * x_own : (s + 1) * x_own] = block[:, 2 : x_own + 2]
+    for s, block in enumerate(padded):
+        for at, part in (
+            ((s * x_own - 2) % G, block[:, :2]),
+            ((s + 1) * x_own % G, block[:, x_own + 2 : x_own + 4]),
+        ):
+            plane[:, at : at + 2] = plane[:, at : at + 2] + part
     for copy in copies[1:]:
         copy.wait()
     cas_x = (x_high[...], x_low[...])
-    along_x = product(halves(padded[...]), cas_x, NN, False)
+    along_x = product(halves(plane[...]), cas_x, NN, False)
     spectrum = product((yt_high[...], yt_low[...]), halves(along_x), NN, False)
     scaled = spectrum * factor
     energy = jnp.sum(jnp.sum(spectrum * scaled, axis=0, keepdims=True), axis=1, keepdims=True)
     back = halves(product((y_high[...], y_low[...]), halves(scaled), NN, False))
-    planes = product(back, cas_x, NT, False)
-    for s in range(n_slab):
-        for y in range(y_rows):
-            flat[s * n_pair : (s + 1) * n_pair, y * x_rows : (y + 1) * x_rows] = planes[
-                y * n_pair : (y + 1) * n_pair, s * TILE : s * TILE + x_rows
-            ]
+    plane[...] = product(back, cas_x, NN, False)
+    for s, rows in enumerate(slabs):
+        start, stop = (s * x_own - 2, (s + 1) * x_own + 2)
+        pieces = [plane[:, max(start, 0) : min(stop, G)]]
+        if start < 0:
+            pieces = [plane[:, G + start :]] + pieces
+        if stop > G:
+            pieces = pieces + [plane[:, : stop - G]]
+        block = pieces[0] if len(pieces) == 1 else jnp.concatenate(pieces, 1)
+        for y in range(y_own):
+            at = (y + 2) * x_rows
+            flat[rows, at : at + x_own + 4] = block[y * n_pair : (y + 1) * n_pair]
+        flat[rows, :two] = rolled(flat, rows, y_own * x_rows, two, 1)
+        flat[rows, width - two : width] = rolled(flat, rows, two, two, n_pair - 1)
     spare = flat.shape[1] - width
     lane = lax.broadcasted_iota(jnp.int32, (1, spare), 1)
     known = jnp.concatenate([sums[0:1], jnp.zeros((1, spare - TILE), F32)], 1)
@@ -756,15 +787,10 @@
     first, statics_beside = around(sent, statics, beneath=meta)
 
     freq = np.arange(G)
-    padded_x = np.stack([(s * extents[0] + np.arange(x_rows) - 2) % G for s in range(n_slab)])
-    real_x = np.tile(np.arange(x_rows) < extents[0] + 4, n_slab)
-    cas_x = cas_matrix(padded_x.reshape(-1), freq) * real_x[:, None]
-    rows_y = (np.arange(n_pair)[None] * 2 * extents[1] + np.arange(pair_rows)[:, None] - 2) % G
+    rows_y = np.arange(n_pair)[None] * 2 * extents[1] + np.arange(2 * extents[1])[:, None]
     cas_y = cas_matrix(rows_y.reshape(-1), freq)
     freq_by_core = np.stack([freq[0::2], freq[1::2]])
     cas_z = cas_matrix(freq_by_core.reshape(-1), freq).reshape(2, half, G)
-    wide_x = np.zeros((n_slab, TILE, G))
-    wide_x[:, :x_rows] = cas_x.reshape(n_slab, x_rows, G)
     def pairs_of(place, count):
         return call(
             functools.partial(pair_kernel, place, count, extents),
@@ -850,10 +876,8 @@
         functools.partial(plane_kernel, (n_slab, n_pair, x_rows, pair_rows)),
         [message],
         10**9,
-        scratch=(flat_scratch, pltpu.VMEM((n_pair * pair_rows, n_slab * TILE), F32), pltpu.VMEM(*message))
-        + (pltpu.VMEM((n_slab * TILE, G), BF16),) * 2
-        + (pltpu.VMEM((G, n_pair * pair_rows), BF16),) * 2
-        + (pltpu.VMEM((n_pair * pair_rows, G), BF16),) * 2
+        scratch=(flat_scratch, pltpu.VMEM((G, G), F32), pltpu.VMEM(*message))
+        + (pltpu.VMEM((G, G), BF16),) * 6
         + (pltpu.SemaphoreType.DMA((7,)),),
         vmem=LARGE_VMEM,
         hbm=7,
@@ -861,7 +885,7 @@
         wave_factors(),
         sums,
         grid,
-        *split_constant(wide_x.reshape(-1, G)),
+        *split_constant(cas_matrix(freq, freq)),
         *split_constant(cas_y.T),
         *split_constant(cas_y),
     )[0]

time: 125 us -> 125 us (level)
  no operation moved by 1% of the time
where the time goes in v9:
time: 125 us
  starting transfers between devices  46.3 us (37%)
  Pallas kernels  34.6 us (28%)
  blocking collectives  24.5 us (20%)
  waiting for transfers between devices  16.7 us (13%)
  local copies, waits for them, and re-layouts  2.05 us (2%)
    pallas_call x19, Pallas kernels, run(): pl.pallas_call(kernel, out_shape=[(pltpu.HBM if hbm_outs else jax.ShapeDt...  31.8 us
    ppermute x9, starting transfers between devices, beside(): return lax.ppermute(block, BOTH, swap_pairs(n_slab, n_space, odd))  27.9 us
    all_to_all x1, blocking collectives, local(): returned = lax.all_to_all(planes, CHIPS, 0, 0, tiled=True)  24.5 us
    all_to_all x1, waiting for transfers between devices, local(): grid = lax.all_to_all(spread, CHIPS, 0, 0, tiled=True)  10.8 us
    all_to_all x1, starting transfers between devices, local(): grid = lax.all_to_all(spread, CHIPS, 0, 0, tiled=True)  8.69 us
    ppermute x4, starting transfers between devices, along_slab(): lax.ppermute(level, 'slab', down)  7.38 us
    ppermute x4, waiting for transfers between devices, along_slab(): lax.ppermute(level, 'slab', up)  3.67 us
  transfers between devices with their start and end apart: 18, of which 6 were waited for; matrix products, arithmetic and copies ran while one was open for 0% of the time, Pallas kernels for 17%

profile of v9, /device:TPU:1, one launch (start us, length us, event | category | flops | bytes accessed | tf_op | source)
XLA Modules:
  0.0 125.0 jit_solution(3635798917140536341)
XLA Ops:
  0.6 1.1 shard_map.193
  1.7 3.3 %collective-permute-start = (f32[8,768]{1,0:T(8,128)S(1)}, f32[8,768]{1,0:T(8,128)S(1)}, u32[]{:S(2)}, u32[]{:S(2)}) collective-permute-start(f32[8,768]{1,0:T(8,128)S(1)} %get-tuple-element.31.mine), channel_id=1, source_target_pairs={{0,1},{1,0},{2,3},{3,2},{4,5},{5,4},{6,7},{7,6},{8,9},{9,8},{10,11... | collective-permute-start | bytes 73736 | tf_op jit(solution)/shard_map/ppermute | solution.py:716
  5.0 0.0 collective-permute-start.1
  5.0 0.7 copy-done.5
  5.7 0.7 copy-done.6
  6.4 0.7 copy-done.7
  7.0 1.7 %shard_map.194.meta = s32[48]{0:T(128)S(1)} custom-call(s32[1,4,8]{2,1,0:T(4,128)S(1)} %copy-done.6, s32[1,4]{1,0:T(1,128)S(1)} %copy-done.7, s32[1,2]{1,0:T(1,128)S(1)} %copy-done.5, f32[2,8,128]{2,1,0:T(8,128)S(1)} %get-tuple-element.29.after.own), custom_call_target="tpu_custom_call" | custom-call | flops 100000000 | bytes 1048576 | tf_op jit(solution)/shard_map/pallas_call | solution.py:779
  8.8 0.0 collective-permute-done.1.outer
  8.8 0.0 collective-permute-done.inner.beside
  8.8 1.2 collective-permute-start.2
  10.0 1.6 %collective-permute-start.3 = (f32[3,2,8,128]{3,2,1,0:T(8,128)S(1)}, f32[3,2,8,128]{3,2,1,0:T(8,128)S(1)}, u32[]{:S(2)}, u32[]{:S(2)}) collective-permute-start(f32[3,2,8,128]{3,2,1,0:T(8,128)S(1)} %shard_map.195.level), channel_id=1, source_target_pairs={{64,0},{128,64},{192,128},{0,192},{65,1},{129,65},{193,129},{1,193... | collective-permute-start | bytes 73736 | tf_op jit(solution)/shard_map/ppermute | solution.py:723
  11.6 1.2 collective-permute-done.2.before
  12.8 0.0 collective-permute-done.3.after
  12.8 3.3 %shard_map.196 = (f32[22,8,128]{2,1,0:T(8,128)S(1)}, f32[3,16,128,128]{3,2,1,0:T(8,128)S(1)}, f32[2,8,128]{2,1,0:T(8,128)S(1)}) custom-call(s32[48]{0:T(128)S(1)} %shard_map.194.meta, f32[4,8,128]{2,1,0:T(8,128)S(1)} %get-tuple-element.30.own, f32[3,2,8,128]{3,2,1,0:T(8,128)S(1)} %shard_map.195.level, f32[3,2,8,128]{3,2,1,0:T(8,128)S(1)} %collective-permute-done.2.before, ...), custom_call_target="tpu_custom_call" | custom-call | flops 1000000000 | bytes 1048576 | tf_op jit(solution)/shard_map/pallas_call | solution.py:124
  16.0 10.0 %collective-permute-start.4 = (f32[2,8,128]{2,1,0:T(8,128)S(1)}, f32[2,8,128]{2,1,0:T(8,128)S(1)}, u32[]{:S(2)}, u32[]{:S(2)}) collective-permute-start(f32[2,8,128]{2,1,0:T(8,128)S(1)} %get-tuple-element.34.own.refs_0_), channel_id=1, source_target_pairs={{0,1},{1,0},{2,3},{3,2},{4,5},{5,4},{6,7},{7,6},{8,9},{9,8},{10,11... | collective-permute-start | bytes 24584 | tf_op jit(solution)/shard_map/ppermute | solution.py:716
  26.0 0.0 collective-permute-start.5
  26.0 2.4 %shard_map.197 = (f32[22,8,128]{2,1,0:T(8,128)}, f32[3,8,128,128]{3,2,1,0:T(8,128)S(1)}, f32[1,8,128]{2,1,0:T(8,128)S(1)}) custom-call(s32[48]{0:T(128)S(1)} %shard_map.194.meta, f32[4,8,128]{2,1,0:T(8,128)S(1)} %get-tuple-element.30.own, f32[3,2,8,128]{3,2,1,0:T(8,128)S(1)} %shard_map.195.level, f32[3,2,8,128]{3,2,1,0:T(8,128)S(1)} %collective-permute-done.2.before, ...), custom_call_target="tpu_custom_call" | custom-call | flops 1000000000 | bytes 1048576 | tf_op jit(solution)/shard_map/pallas_call | solution.py:124
  28.4 0.7 collective-permute-done.5.outer
  29.1 0.0 collective-permute-done.4.inner
  29.1 0.0 collective-permute-start.6
  29.1 2.7 %collective-permute-start.7 = (f32[3,2,8,128]{3,2,1,0:T(8,128)S(1)}, f32[3,2,8,128]{3,2,1,0:T(8,128)S(1)}, u32[]{:S(2)}, u32[]{:S(2)}) collective-permute-start(f32[3,2,8,128]{3,2,1,0:T(8,128)S(1)} %shard_map.199.refs_3_), channel_id=1, source_target_pairs={{64,0},{128,64},{192,128},{0,192},{65,1},{129,65},{193,129},{1,193... | collective-permute-start | bytes 73736 | tf_op jit(solution)/shard_map/ppermute | solution.py:723
  31.8 2.4 %shard_map.198 = (f32[22,8,128]{2,1,0:T(8,128)}, f32[3,8,128,128]{3,2,1,0:T(8,128)S(1)}, f32[1,8,128]{2,1,0:T(8,128)S(1)}) custom-call(s32[48]{0:T(128)S(1)} %shard_map.194.meta, f32[4,8,128]{2,1,0:T(8,128)S(1)} %get-tuple-element.30.own, f32[3,2,8,128]{3,2,1,0:T(8,128)S(1)} %shard_map.195.level, f32[3,2,8,128]{3,2,1,0:T(8,128)S(1)} %collective-permute-done.2.before, ...), custom_call_target="tpu_custom_call" | custom-call | flops 1000000000 | bytes 1048576 | tf_op jit(solution)/shard_map/pallas_call | solution.py:124
  34.2 0.0 collective-permute-done.6.refs_4_
  34.2 0.0 collective-permute-done.7.refs_5_
  34.2 1.7 %shard_map.200.own.refs_0_.own_a = f32[2,8,128]{2,1,0:T(8,128)S(1)} custom-call(s32[48]{0:T(128)S(1)} %shard_map.194.meta, f32[22,8,128]{2,1,0:T(8,128)S(1)} %get-tuple-element.33.geometry, f32[2,8,128]{2,1,0:T(8,128)S(1)} %get-tuple-element.34.own.refs_0_, f32[1,8,128]{2,1,0:T(8,128)S(1)} %get-tuple-element.35.refs_1_, ...), custom_call_target="tpu_custom_call" | custom-call | flops 100000000 | bytes 1048576 | tf_op jit(solution)/shard_map/pallas_call | solution.py:124
  35.9 5.4 %collective-permute-start.8 = (f32[2,8,128]{2,1,0:T(8,128)S(1)}, f32[2,8,128]{2,1,0:T(8,128)S(1)}, u32[]{:S(2)}, u32[]{:S(2)}) collective-permute-start(f32[2,8,128]{2,1,0:T(8,128)S(1)} %shard_map.200.own.refs_0_.own_a), channel_id=1, source_target_pairs={{0,1},{1,0},{2,3},{3,2},{4,5},{5,4},{6,7},{7,6},{8,9},{9,8},{10,11... | collective-permute-start | bytes 24584 | tf_op jit(solution)/shard_map/ppermute | solution.py:716
  41.3 0.0 collective-permute-start.9
  41.3 1.6 %shard_map.201.refs_1_.own_b = f32[2,8,128]{2,1,0:T(8,128)S(1)} custom-call(s32[48]{0:T(128)S(1)} %shard_map.194.meta, f32[22,8,128]{2,1,0:T(8,128)S(1)} %get-tuple-element.33.geometry, f32[2,8,128]{2,1,0:T(8,128)S(1)} %get-tuple-element.34.own.refs_0_, f32[1,8,128]{2,1,0:T(8,128)S(1)} %get-tuple-element.35.refs_1_, ...), custom_call_target="tpu_custom_call" | custom-call | flops 100000000 | bytes 1048576 | tf_op jit(solution)/shard_map/pallas_call | solution.py:124
  42.9 1.5 %collective-permute-done.9.outer = f32[2,8,128]{2,1,0:T(8,128)S(1)} collective-permute-done((f32[2,8,128]{2,1,0:T(8,128)S(1)}, f32[2,8,128]{2,1,0:T(8,128)S(1)}, u32[]{:S(2)}, u32[]{:S(2)}) %collective-permute-start.9) | collective-permute-done | bytes 8224 | tf_op jit(solution)/shard_map/ppermute | solution.py:716
  44.4 0.0 collective-permute-done.8.inner
  44.4 1.1 collective-permute-start.11
  45.4 0.4 collective-permute-start.10
  45.8 2.7 %shard_map.203 = (f32[2,2,72,512]{3,2,1,0:T(8,128)S(1)}, f32[2,2,8,512]{3,2,1,0:T(8,128)S(1)}, bf16[2,128,512]{2,1,0:T(8,128)(2,1)S(1)}, bf16[2,128,512]{2,1,0:T(8,128)(2,1)S(1)}, f32[2,128,512]{2,1,0:T(8,128)S(1)}) custom-call(f32[8,768]{1,0:T(8,128)S(1)} %get-tuple-element.31.mine, f32[8,768]{1,0:T(8,128)S(1)} %collective-permute-done.inner.beside, ...), custom_call_target="tpu_custom_call" | custom-call | flops 100000000 | bytes 1048576 | tf_op jit(solution)/shard_map/pallas_call | solution.py:124
  48.6 0.0 collective-permute-done.11.refs_4_.after
  48.6 0.0 copy-start.3
  48.6 0.7 collective-permute-done.10.refs_3_.before
  49.3 1.7 %shard_map.204.sent.own = f32[2,8,128]{2,1,0:T(8,128)S(1)} custom-call(s32[48]{0:T(128)S(1)} %shard_map.194.meta, f32[22,8,128]{2,1,0:T(8,128)S(1)} %get-tuple-element.33.geometry, f32[2,8,128]{2,1,0:T(8,128)S(1)} %shard_map.200.own.refs_0_.own_a, f32[2,8,128]{2,1,0:T(8,128)S(1)} %shard_map.201.refs_1_.own_b, f32[3,2,8,128]{3,2,1,0:T(8,128)S(1)} %shard_map.202.refs_2_.level, ...), custom_call_target="tpu_custom_call" | custom-call | flops 100000000 | bytes 1048576 | tf_op jit(solution)/shard_map/pallas_call | solution.py:124
  51.1 1.9 %collective-permute-start.13 = (f32[2,8,128]{2,1,0:T(8,128)S(1)}, f32[2,8,128]{2,1,0:T(8,128)S(1)}, u32[]{:S(2)}, u32[]{:S(2)}) collective-permute-start(f32[2,8,128]{2,1,0:T(8,128)S(1)} %shard_map.204.sent.own), channel_id=1, source_target_pairs={{0,63},{1,2},{2,1},{3,4},{4,3},{5,6},{6,5},{7,8},{8,7},{9,10},{10,... | collective-permute-start | bytes 24584 | tf_op jit(solution)/shard_map/ppermute | solution.py:716
  53.0 1.8 %shard_map.205 = (f32[2,8,128]{2,1,0:T(8,128)S(1)}, f32[8,768]{1,0:T(8,128)S(1)}) custom-call(s32[48]{0:T(128)S(1)} %shard_map.194.meta, f32[22,8,128]{2,1,0:T(8,128)S(1)} %get-tuple-element.33.geometry, f32[2,8,128]{2,1,0:T(8,128)S(1)} %shard_map.200.own.refs_0_.own_a, f32[2,8,128]{2,1,0:T(8,128)S(1)} %shard_map.201.refs_1_.own_b, ...), custom_call_target="tpu_custom_call" | custom-call | flops 100000000 | bytes 1048576 | tf_op jit(solution)/shard_map/pallas_call | solution.py:124
  54.8 3.9 %collective-permute-start.12 = (f32[8,768]{1,0:T(8,128)S(1)}, f32[8,768]{1,0:T(8,128)S(1)}, u32[]{:S(2)}, u32[]{:S(2)}) collective-permute-start(f32[8,768]{1,0:T(8,128)S(1)} %get-tuple-element.46.ordered), channel_id=1, source_target_pairs={{0,1},{1,0},{2,3},{3,2},{4,5},{5,4},{6,7},{7,6},{8,9},{9,8},{10,11... | collective-permute-start | bytes 73736 | tf_op jit(solution)/shard_map/ppermute | solution.py:716
  58.7 1.4 %shard_map.206.mine = f32[128,576]{1,0:T(8,128)S(1)} custom-call(f32[8,768]{1,0:T(8,128)S(1)} %get-tuple-element.46.ordered, f32[2,2,72,512]{3,2,1,0:T(8,128)S(1)} %get-tuple-element.47.tab_x, f32[2,2,8,512]{3,2,1,0:T(8,128)S(1)} %get-tuple-element.43.tab_y, bf16[2,128,512]{2,1,0:T(8,128)(2,1)S(1)} %get-tuple-element.48.w_high, ...), custom_call_target="tpu_custom_call" | custom-call | flops 1000000000 | bytes 1048576 | tf_op jit(solution)/shard_map/pallas_call | solution.py:124
  60.1 0.0 collective-permute-done.12.ordered.inner
  60.1 0.0 copy-done.9
  60.1 0.0 copy-done.11
  60.1 0.0 copy-done.13
  60.1 0.0 copy-done.15
  60.1 2.5 %shard_map.207 = f32[128,8,128]{2,1,0:T(8,128)} custom-call(f32[8,768]{1,0:T(8,128)S(1)} %collective-permute-done.12.ordered.inner, f32[128,576]{1,0:T(8,128)S(1)} %shard_map.206.mine, f32[2,2,72,512]{3,2,1,0:T(8,128)S(1)} %get-tuple-element.47.tab_x, f32[2,2,8,512]{3,2,1,0:T(8,128)S(1)} %get-tuple-element.43.tab_y, ...), custom_call_target="tpu_custom_call" | custom-call | flops 1000000000 | bytes 1048576 | tf_op jit(solution)/shard_map/pallas_call | solution.py:124
  62.6 0.0 collective-permute-done.13.outer
  62.6 8.7 %all-to-all-start = ((f32[128,8,128]{2,1,0:T(8,128)}), f32[128,8,128]{2,1,0:T(8,128)}, u32[]{:S(2)}, u32[]{:S(2)}) async-start(f32[128,8,128]{2,1,0:T(8,128)} %shard_map.207), calls=%async_computation | async-start | bytes 1048576 | tf_op jit(solution)/shard_map/all_to_all | solution.py:863
  71.3 0.7 collective-permute-start.14
  72.0 2.1 %collective-permute-start.15 = (f32[3,2,8,128]{3,2,1,0:T(8,128)S(1)}, f32[3,2,8,128]{3,2,1,0:T(8,128)S(1)}, u32[]{:S(2)}, u32[]{:S(2)}) collective-permute-start(f32[3,2,8,128]{3,2,1,0:T(8,128)S(1)} %shard_map.208.level), channel_id=1, source_target_pairs={{64,0},{128,64},{192,128},{0,192},{65,1},{129,65},{193,129},{1,193... | collective-permute-start | bytes 73736 | tf_op jit(solution)/shard_map/ppermute | solution.py:723
  74.1 1.8 %collective-permute-done.14.before = f32[3,2,8,128]{3,2,1,0:T(8,128)S(1)} collective-permute-done((f32[3,2,8,128]{3,2,1,0:T(8,128)S(1)}, f32[3,2,8,128]{3,2,1,0:T(8,128)S(1)}, u32[]{:S(2)}, u32[]{:S(2)}) %collective-permute-start.14) | collective-permute-done | bytes 24608 | tf_op jit(solution)/shard_map/ppermute | solution.py:723
  75.9 0.0 collective-permute-done.15.after
  75.9 3.4 %shard_map.209 = (f32[8,512]{1,0:T(8,128)S(1)}, f32[8,128]{1,0:T(8,128)S(1)}) custom-call(s32[48]{0:T(128)S(1)} %shard_map.194.meta, f32[22,8,128]{2,1,0:T(8,128)S(1)} %get-tuple-element.33.geometry, f32[2,8,128]{2,1,0:T(8,128)S(1)} %shard_map.204.sent.own, f32[2,8,128]{2,1,0:T(8,128)S(1)} %get-tuple-element.45.rest, f32[3,2,8,128]{3,2,1,0:T(8,128)S(1)} %shard_map.208.level, ...), custom_call_target="tpu_custom_call" | custom-call | flops 1000000000 | bytes 1048576 | tf_op jit(solution)/shard_map/pallas_call | solution.py:124
  79.2 10.8 %all-to-all-done.refs_0_ = f32[128,8,128]{2,1,0:T(8,128)} async-done(((f32[128,8,128]{2,1,0:T(8,128)}), f32[128,8,128]{2,1,0:T(8,128)}, u32[]{:S(2)}, u32[]{:S(2)}) %all-to-all-start) | async-done | bytes 524320 | tf_op jit(solution)/shard_map/all_to_all | solution.py:863
  90.1 0.0 copy-start.16
  90.1 3.9 %shard_map.210 = f32[128,8,128]{2,1,0:T(8,128)S(1)} custom-call(f32[8,256]{1,0:T(8,128)S(1)} %copy-done.8, f32[8,128]{1,0:T(8,128)S(1)} %get-tuple-element.52.sums, f32[128,8,128]{2,1,0:T(8,128)} %all-to-all-done.refs_0_, bf16[256,256]{1,0:T(8,128)(2,1)} %constant.21.clone.refs_1_, bf16[256,256]{1,0:T(8,128)(2,1)} %constant.22.clone.refs_2_, ...), custom_call_target="tpu_custom_call" | custom-call | flops 1000000000 | bytes 1048576 | tf_op jit(solution)/shard_map/pallas_call | solution.py:124
  94.0 24.5 %all_to_all.10.grid = f32[128,8,128]{2,1,0:T(8,128)S(1)} all-to-all(f32[128,8,128]{2,1,0:T(8,128)S(1)} %shard_map.210), channel_id=1, replica_groups=mesh['slab'=4,'pair'=32,'core'=2] {'slab','pair'}, dimensions={0} | all-to-all | bytes 1048576 | tf_op jit(solution)/shard_map/all_to_all | solution.py:892
  118.5 0.0 copy-done.10
  118.5 1.1 shard_map.212
  119.6 3.4 %collective-permute-start.16 = (f32[8,512]{1,0:T(8,128)S(1)}, f32[8,512]{1,0:T(8,128)S(1)}, u32[]{:S(2)}, u32[]{:S(2)}) collective-permute-start(f32[8,512]{1,0:T(8,128)S(1)} %shard_map.212), channel_id=1, source_target_pairs={{0,1},{1,0},{2,3},{3,2},{4,5},{5,4},{6,7},{7,6},{8,9},{9,8},{10,11... | collective-permute-start | bytes 49160 | tf_op jit(solution)/shard_map/ppermute | solution.py:716
  123.0 1.1 shard_map.211.mine
  124.1 0.0 collective-permute-done.16.theirs
  124.1 0.9 shard_map.213
  (28 shorter events, 0.1 us)
Async XLA Ops:
  1.7 7.1 %collective-permute-start = (f32[8,768]{1,0:T(8,128)S(1)}, f32[8,768]{1,0:T(8,128)S(1)}, u32[]{:S(2)}, u32[]{:S(2)}) collective-permute-start(f32[8,768]{1,0:T(8,128)S(1)} %get-tuple-element.31.mine), channel_id=1, source_target_pairs={{0,1},{1,0},{2,3},{3,2},{4,5},{5,4},{6,7},{7,6},{8,9},{9,8},{10,11... | collective-permute-start | bytes 73736 | tf_op jit(solution)/shard_map/ppermute | solution.py:716
  5.0 3.7 %collective-permute-start.1 = (f32[2,8,128]{2,1,0:T(8,128)S(1)}, f32[2,8,128]{2,1,0:T(8,128)S(1)}, u32[]{:S(2)}, u32[]{:S(2)}) collective-permute-start(f32[2,8,128]{2,1,0:T(8,128)S(1)} %get-tuple-element.29.after.own), channel_id=1, source_target_pairs={{0,63},{1,2},{2,1},{3,4},{4,3},{5,6},{6,5},{7,8},{8,7},{9,10},{10,... | collective-permute-start | bytes 24584 | tf_op jit(solution)/shard_map/ppermute | solution.py:716
  5.0 0.7 copy-start.5
  5.7 0.7 copy-start.6
  6.4 0.7 copy-start.7
  8.8 4.0 %collective-permute-start.2 = (f32[3,2,8,128]{3,2,1,0:T(8,128)S(1)}, f32[3,2,8,128]{3,2,1,0:T(8,128)S(1)}, u32[]{:S(2)}, u32[]{:S(2)}) collective-permute-start(f32[3,2,8,128]{3,2,1,0:T(8,128)S(1)} %shard_map.195.level), channel_id=1, source_target_pairs={{0,64},{64,128},{128,192},{192,0},{1,65},{65,129},{129,193},{193,1... | collective-permute-start | bytes 73736 | tf_op jit(solution)/shard_map/ppermute | solution.py:723
  10.0 2.8 %collective-permute-start.3 = (f32[3,2,8,128]{3,2,1,0:T(8,128)S(1)}, f32[3,2,8,128]{3,2,1,0:T(8,128)S(1)}, u32[]{:S(2)}, u32[]{:S(2)}) collective-permute-start(f32[3,2,8,128]{3,2,1,0:T(8,128)S(1)} %shard_map.195.level), channel_id=1, source_target_pairs={{64,0},{128,64},{192,128},{0,192},{65,1},{129,65},{193,129},{1,193... | collective-permute-start | bytes 73736 | tf_op jit(solution)/shard_map/ppermute | solution.py:723
  16.0 13.1 %collective-permute-start.4 = (f32[2,8,128]{2,1,0:T(8,128)S(1)}, f32[2,8,128]{2,1,0:T(8,128)S(1)}, u32[]{:S(2)}, u32[]{:S(2)}) collective-permute-start(f32[2,8,128]{2,1,0:T(8,128)S(1)} %get-tuple-element.34.own.refs_0_), channel_id=1, source_target_pairs={{0,1},{1,0},{2,3},{3,2},{4,5},{5,4},{6,7},{7,6},{8,9},{9,8},{10,11... | collective-permute-start | bytes 24584 | tf_op jit(solution)/shard_map/ppermute | solution.py:716
  26.0 3.1 %collective-permute-start.5 = (f32[2,8,128]{2,1,0:T(8,128)S(1)}, f32[2,8,128]{2,1,0:T(8,128)S(1)}, u32[]{:S(2)}, u32[]{:S(2)}) collective-permute-start(f32[2,8,128]{2,1,0:T(8,128)S(1)} %get-tuple-element.34.own.refs_0_), channel_id=1, source_target_pairs={{0,63},{1,2},{2,1},{3,4},{4,3},{5,6},{6,5},{7,8},{8,7},{9,10},{10,... | collective-permute-start | bytes 24584 | tf_op jit(solution)/shard_map/ppermute | solution.py:716
  28.4 24.6 %copy-start = (f32[3,8,128,128]{3,2,1,0:T(8,128)}, f32[3,8,128,128]{3,2,1,0:T(8,128)S(1)}, u32[]{:S(2)}) copy-start(f32[3,8,128,128]{3,2,1,0:T(8,128)S(1)} %get-tuple-element.39.refs_6_.pairs_b.stored_b) | copy-start | bytes 4718596
  29.1 5.1 %collective-permute-start.6 = (f32[3,2,8,128]{3,2,1,0:T(8,128)S(1)}, f32[3,2,8,128]{3,2,1,0:T(8,128)S(1)}, u32[]{:S(2)}, u32[]{:S(2)}) collective-permute-start(f32[3,2,8,128]{3,2,1,0:T(8,128)S(1)} %shard_map.199.refs_3_), channel_id=1, source_target_pairs={{0,64},{64,128},{128,192},{192,0},{1,65},{65,129},{129,193},{193,1... | collective-permute-start | bytes 73736 | tf_op jit(solution)/shard_map/ppermute | solution.py:723
  29.1 5.1 %collective-permute-start.7 = (f32[3,2,8,128]{3,2,1,0:T(8,128)S(1)}, f32[3,2,8,128]{3,2,1,0:T(8,128)S(1)}, u32[]{:S(2)}, u32[]{:S(2)}) collective-permute-start(f32[3,2,8,128]{3,2,1,0:T(8,128)S(1)} %shard_map.199.refs_3_), channel_id=1, source_target_pairs={{64,0},{128,64},{192,128},{0,192},{65,1},{129,65},{193,129},{1,193... | collective-permute-start | bytes 73736 | tf_op jit(solution)/shard_map/ppermute | solution.py:723
  34.2 18.8 %copy-start.1 = (f32[3,8,128,128]{3,2,1,0:T(8,128)}, f32[3,8,128,128]{3,2,1,0:T(8,128)S(1)}, u32[]{:S(2)}) copy-start(f32[3,8,128,128]{3,2,1,0:T(8,128)S(1)} %get-tuple-element.40.refs_7_.pairs_c.stored_c) | copy-start | bytes 4718596
  35.9 8.5 %collective-permute-start.8 = (f32[2,8,128]{2,1,0:T(8,128)S(1)}, f32[2,8,128]{2,1,0:T(8,128)S(1)}, u32[]{:S(2)}, u32[]{:S(2)}) collective-permute-start(f32[2,8,128]{2,1,0:T(8,128)S(1)} %shard_map.200.own.refs_0_.own_a), channel_id=1, source_target_pairs={{0,1},{1,0},{2,3},{3,2},{4,5},{5,4},{6,7},{7,6},{8,9},{9,8},{10,11... | collective-permute-start | bytes 24584 | tf_op jit(solution)/shard_map/ppermute | solution.py:716
  41.3 3.1 %collective-permute-start.9 = (f32[2,8,128]{2,1,0:T(8,128)S(1)}, f32[2,8,128]{2,1,0:T(8,128)S(1)}, u32[]{:S(2)}, u32[]{:S(2)}) collective-permute-start(f32[2,8,128]{2,1,0:T(8,128)S(1)} %shard_map.200.own.refs_0_.own_a), channel_id=1, source_target_pairs={{0,63},{1,2},{2,1},{3,4},{4,3},{5,6},{6,5},{7,8},{8,7},{9,10},{10,... | collective-permute-start | bytes 24584 | tf_op jit(solution)/shard_map/ppermute | solution.py:716
  44.4 4.3 %collective-permute-start.11 = (f32[3,2,8,128]{3,2,1,0:T(8,128)S(1)}, f32[3,2,8,128]{3,2,1,0:T(8,128)S(1)}, u32[]{:S(2)}, u32[]{:S(2)}) collective-permute-start(f32[3,2,8,128]{3,2,1,0:T(8,128)S(1)} %shard_map.202.refs_2_.level), channel_id=1, source_target_pairs={{64,0},{128,64},{192,128},{0,192},{65,1},{129,65},{193,129},{1,193... | collective-permute-start | bytes 73736 | tf_op jit(solution)/shard_map/ppermute | solution.py:723
  45.4 3.9 %collective-permute-start.10 = (f32[3,2,8,128]{3,2,1,0:T(8,128)S(1)}, f32[3,2,8,128]{3,2,1,0:T(8,128)S(1)}, u32[]{:S(2)}, u32[]{:S(2)}) collective-permute-start(f32[3,2,8,128]{3,2,1,0:T(8,128)S(1)} %shard_map.202.refs_2_.level), channel_id=1, source_target_pairs={{0,64},{64,128},{128,192},{192,0},{1,65},{65,129},{129,193},{193,1... | collective-permute-start | bytes 73736 | tf_op jit(solution)/shard_map/ppermute | solution.py:723
  48.6 11.5 %copy-start.9 = (f32[2,2,72,512]{3,2,1,0:T(8,128)}, f32[2,2,72,512]{3,2,1,0:T(8,128)S(1)}, u32[]{:S(2)}) copy-start(f32[2,2,72,512]{3,2,1,0:T(8,128)S(1)} %get-tuple-element.47.tab_x) | copy-start | bytes 1769476
  48.6 11.5 %copy-start.11 = (f32[2,128,512]{2,1,0:T(8,128)}, f32[2,128,512]{2,1,0:T(8,128)S(1)}, u32[]{:S(2)}) copy-start(f32[2,128,512]{2,1,0:T(8,128)S(1)} %get-tuple-element.50.slope_z) | copy-start | bytes 1572868
  48.6 11.5 %copy-start.13 = (bf16[2,128,512]{2,1,0:T(8,128)(2,1)}, bf16[2,128,512]{2,1,0:T(8,128)(2,1)S(1)}, u32[]{:S(2)}) copy-start(bf16[2,128,512]{2,1,0:T(8,128)(2,1)S(1)} %get-tuple-element.48.w_high) | copy-start | bytes 786436
  48.6 11.5 %copy-start.15 = (bf16[2,128,512]{2,1,0:T(8,128)(2,1)}, bf16[2,128,512]{2,1,0:T(8,128)(2,1)S(1)}, u32[]{:S(2)}) copy-start(bf16[2,128,512]{2,1,0:T(8,128)(2,1)S(1)} %get-tuple-element.49.w_low) | copy-start | bytes 786436
  48.6 4.3 %copy-start.3 = (s32[1,512]{1,0:T(1,128)S(1)}, s32[1,512]{1,0:T(1,128)}, u32[]{:S(2)}) copy-start(s32[1,512]{1,0:T(1,128)} %order.3) | copy-start | bytes 6148
  51.1 11.5 %collective-permute-start.13 = (f32[2,8,128]{2,1,0:T(8,128)S(1)}, f32[2,8,128]{2,1,0:T(8,128)S(1)}, u32[]{:S(2)}, u32[]{:S(2)}) collective-permute-start(f32[2,8,128]{2,1,0:T(8,128)S(1)} %shard_map.204.sent.own), channel_id=1, source_target_pairs={{0,63},{1,2},{2,1},{3,4},{4,3},{5,6},{6,5},{7,8},{8,7},{9,10},{10,... | collective-permute-start | bytes 24584 | tf_op jit(solution)/shard_map/ppermute | solution.py:716
  54.8 5.3 %collective-permute-start.12 = (f32[8,768]{1,0:T(8,128)S(1)}, f32[8,768]{1,0:T(8,128)S(1)}, u32[]{:S(2)}, u32[]{:S(2)}) collective-permute-start(f32[8,768]{1,0:T(8,128)S(1)} %get-tuple-element.46.ordered), channel_id=1, source_target_pairs={{0,1},{1,0},{2,3},{3,2},{4,5},{5,4},{6,7},{7,6},{8,9},{9,8},{10,11... | collective-permute-start | bytes 73736 | tf_op jit(solution)/shard_map/ppermute | solution.py:716
  62.6 27.5 %all-to-all-start = ((f32[128,8,128]{2,1,0:T(8,128)}), f32[128,8,128]{2,1,0:T(8,128)}, u32[]{:S(2)}, u32[]{:S(2)}) async-start(f32[128,8,128]{2,1,0:T(8,128)} %shard_map.207), calls=%async_computation | async-start | bytes 1048576 | tf_op jit(solution)/shard_map/all_to_all | solution.py:863
  71.3 4.5 %collective-permute-start.14 = (f32[3,2,8,128]{3,2,1,0:T(8,128)S(1)}, f32[3,2,8,128]{3,2,1,0:T(8,128)S(1)}, u32[]{:S(2)}, u32[]{:S(2)}) collective-permute-start(f32[3,2,8,128]{3,2,1,0:T(8,128)S(1)} %shard_map.208.level), channel_id=1, source_target_pairs={{0,64},{64,128},{128,192},{192,0},{1,65},{65,129},{129,193},{193,1... | collective-permute-start | bytes 73736 | tf_op jit(solution)/shard_map/ppermute | solution.py:723
  72.0 3.9 %collective-permute-start.15 = (f32[3,2,8,128]{3,2,1,0:T(8,128)S(1)}, f32[3,2,8,128]{3,2,1,0:T(8,128)S(1)}, u32[]{:S(2)}, u32[]{:S(2)}) collective-permute-start(f32[3,2,8,128]{3,2,1,0:T(8,128)S(1)} %shard_map.208.level), channel_id=1, source_target_pairs={{64,0},{128,64},{192,128},{0,192},{65,1},{129,65},{193,129},{1,193... | collective-permute-start | bytes 73736 | tf_op jit(solution)/shard_map/ppermute | solution.py:723
  75.9 14.2 %copy-start.8 = (f32[8,256]{1,0:T(8,128)S(1)}, f32[8,256]{1,0:T(8,128)}, u32[]{:S(2)}) copy-start(f32[8,256]{1,0:T(8,128)} %constant.20.clone.waves) | copy-start | bytes 24580
  90.1 28.4 %copy-start.10 = (f32[2,2,72,512]{3,2,1,0:T(8,128)S(1)}, f32[2,2,72,512]{3,2,1,0:T(8,128)}, u32[]{:S(2)}) copy-start(f32[2,2,72,512]{3,2,1,0:T(8,128)} %copy-done.9) | copy-start | bytes 1769476
  90.1 28.4 %copy-start.12 = (f32[2,128,512]{2,1,0:T(8,128)S(1)}, f32[2,128,512]{2,1,0:T(8,128)}, u32[]{:S(2)}) copy-start(f32[2,128,512]{2,1,0:T(8,128)} %copy-done.11) | copy-start | bytes 1572868
  90.1 28.4 %copy-start.14 = (bf16[2,128,512]{2,1,0:T(8,128)(2,1)S(1)}, bf16[2,128,512]{2,1,0:T(8,128)(2,1)}, u32[]{:S(2)}) copy-start(bf16[2,128,512]{2,1,0:T(8,128)(2,1)} %copy-done.13) | copy-start | bytes 786436
  90.1 28.4 %copy-start.16 = (bf16[2,128,512]{2,1,0:T(8,128)(2,1)S(1)}, bf16[2,128,512]{2,1,0:T(8,128)(2,1)}, u32[]{:S(2)}) copy-start(bf16[2,128,512]{2,1,0:T(8,128)(2,1)} %copy-done.15) | copy-start | bytes 786436
  119.6 4.5 %copy-start.2 = (f32[3,512]{1,0:T(4,128)S(1)}, f32[3,512]{1,0:T(4,128)}, u32[]{:S(2)}) copy-start(f32[3,512]{1,0:T(4,128)} %residual.1) | copy-start | bytes 18436
  119.6 4.5 %copy-start.4 = (f32[3,512]{1,0:T(4,128)S(1)}, f32[3,512]{1,0:T(4,128)}, u32[]{:S(2)}) copy-start(f32[3,512]{1,0:T(4,128)} %dipoles.1) | copy-start | bytes 18436
  119.6 4.5 %collective-permute-start.16 = (f32[8,512]{1,0:T(8,128)S(1)}, f32[8,512]{1,0:T(8,128)S(1)}, u32[]{:S(2)}, u32[]{:S(2)}) collective-permute-start(f32[8,512]{1,0:T(8,128)S(1)} %shard_map.212), channel_id=1, source_target_pairs={{0,1},{1,0},{2,3},{3,2},{4,5},{5,4},{6,7},{7,6},{8,9},{9,8},{10,11... | collective-permute-start | bytes 49160 | tf_op jit(solution)/shard_map/ppermute | solution.py:716

commit v10 on v9

--- a/solution.py
+++ b/solution.py
@@ -83,7 +83,17 @@
 PARITY_AT = 40
 
 
-def meta_kernel(lists, counts, send, after, meta):
+def meta_kernel(stored_lists, stored_counts, stored_send, after, meta, lists, counts, send, sems):
+    copies = [
+        pltpu.make_async_copy(source, target, sems.at[at])
+        for at, (source, target) in enumerate(
+            ((stored_lists, lists), (stored_counts, counts), (stored_send, send))
+        )
+    ]
+    for copy in copies:
+        copy.start()
+    for copy in copies:
+        copy.wait()
     parity = lax.axis_index("core")
     for tile in range(4):
 
@@ -202,12 +212,15 @@
 GROUP = 4
 
 
-def pair_kernel(first_place, count, extents, meta, own, level, before, after, pool, pairs, found, columns, totals):
+def pair_kernel(extents, meta, own, level, before, after, pool, pairs, found, columns, totals):
     fill_pool(pool, extents, own, level, before, after, meta)
-
+    pair_tiles(0, meta, pool, pairs, found, columns, totals)
+
+
+def pair_tiles(first_place, meta, pool, pairs, found, columns, totals):
     def tile_step(at, carry):
         tile = meta[ORDER_AT + first_place + at]
-        block = own[tile]
+        block = pool[tile]
         own_columns(columns, jnp.concatenate([block[:3], lax.rsqrt(block[3:4]), block[4:]], 0), 4)
         live = meta[COUNTS_AT + tile]
 
@@ -268,7 +281,7 @@
         found[at] = updated(block, totals)
         return carry
 
-    lax.fori_loop(0, count, tile_step, 0)
+    lax.fori_loop(0, found.shape[0], tile_step, 0)
 
 
 def field_rows(totals):
@@ -727,10 +740,10 @@
     return call(join_kernel, [((3, 2, 8, TILE), F32)], 10**6)(block, inner, outer)[0]
 
 
-def around(block, bundle=None, beneath=None):
-    inner = beside(block if bundle is None else bundle, False)
+def around(block, inner=None, beneath=None):
+    inner = beside(block, False) if inner is None else inner
     outer, _ = lax.optimization_barrier((beside(block, True), beneath))
-    return along_slab(joined(block, inner, outer)), inner
+    return along_slab(joined(block, inner, outer))
 
 
 def local(
@@ -779,47 +792,29 @@
     meta = pl.pallas_call(
         meta_kernel,
         out_shape=jax.ShapeDtypeStruct((48,), jnp.int32),
-        in_specs=[smem, smem, smem, pl.BlockSpec(memory_space=pltpu.VMEM)],
+        in_specs=[anywhere, anywhere, anywhere, pl.BlockSpec(memory_space=pltpu.VMEM)],
         out_specs=smem,
+        scratch_shapes=[
+            pltpu.SMEM(tile_lists.shape, jnp.int32),
+            pltpu.SMEM(tile_counts.shape, jnp.int32),
+            pltpu.SMEM(send_tiles.shape, jnp.int32),
+            pltpu.SemaphoreType.DMA((3,)),
+        ],
         compiler_params=pltpu.CompilerParams(vmem_limit_bytes=SMALL_VMEM),
         cost_estimate=pl.CostEstimate(flops=10**8, bytes_accessed=1 << 20, transcendentals=0),
-    )(tile_lists, tile_counts, send_tiles, sent)
-    first, statics_beside = around(sent, statics, beneath=meta)
-
+    )(
+        *[
+            pltpu.with_memory_space_constraint(array, pltpu.HBM)
+            for array in (tile_lists, tile_counts, send_tiles)
+        ],
+        sent,
+    )
+    statics_beside = beside(statics, False)
     freq = np.arange(G)
     rows_y = np.arange(n_pair)[None] * 2 * extents[1] + np.arange(2 * extents[1])[:, None]
     cas_y = cas_matrix(rows_y.reshape(-1), freq)
     freq_by_core = np.stack([freq[0::2], freq[1::2]])
     cas_z = cas_matrix(freq_by_core.reshape(-1), freq).reshape(2, half, G)
-    def pairs_of(place, count):
-        return call(
-            functools.partial(pair_kernel, place, count, extents),
-            [((22, 8, TILE), F32), ((3, 8 * count, TILE, TILE), F32), ((count, 8, TILE), F32)],
-            10**9,
-            smem=1,
-            scratch=(pltpu.VMEM((4, TILE, TILE), F32), total_scratch),
-        )(meta, own, *first)
-
-    geometry, pairs_a, search_a = pairs_of(0, 2)
-    _, pairs_b, search_b = pairs_of(2, 1)
-    _, pairs_c, search_c = pairs_of(3, 1)
-    sweep_scratch = (pool_scratch, pltpu.VMEM((3, TILE, TILE), F32), total_scratch)
-    second, _ = around(search_a, beneath=search_b)
-
-    def sweep(place, owns, received, banks):
-        return call(
-            functools.partial(sweep_kernel, place, len(owns)),
-            [two_shape],
-            10**8,
-            smem=1,
-            scratch=sweep_scratch,
-        )(meta, geometry, *owns, *received, *banks)[0]
-
-    searches = (search_a, search_b, search_c)
-    next_a = sweep(0, searches, second, (pairs_a,))
-    next_b = sweep(2, searches, second, (pairs_b, pairs_c))
-    third, _ = around(next_a, beneath=next_b)
-    statics_beside, _ = lax.optimization_barrier((statics_beside, third[0]))
     tables = call(
         tables_kernel,
         [
@@ -834,9 +829,44 @@
         scratch=(pltpu.VMEM((half, G), BF16),) * 2 + (pltpu.SemaphoreType.DMA((2,)),),
         hbm=2,
     )(statics, statics_beside, *split_constant(cas_z))
-    level, before, after = third
-    after, _ = lax.optimization_barrier((after, tables[1]))
-    third = (level, before, after)
+    first = around(sent, statics_beside, beneath=(meta, tables[1]))
+
+    pair_scratch = (pltpu.VMEM((4, TILE, TILE), F32), total_scratch)
+    geometry, pairs_a, search_a = call(
+        functools.partial(pair_kernel, extents),
+        [((22, 8, TILE), F32), ((3, 16, TILE, TILE), F32), two_shape],
+        10**9,
+        smem=1,
+        scratch=pair_scratch,
+    )(meta, own, *first)
+
+    def pairs_of(place):
+        return call(
+            functools.partial(pair_tiles, place),
+            [one_bank, ((1, 8, TILE), F32)],
+            10**9,
+            smem=1,
+            scratch=pair_scratch,
+        )(meta, geometry)
+
+    pairs_b, search_b = pairs_of(2)
+    pairs_c, search_c = pairs_of(3)
+    sweep_scratch = (pool_scratch, pltpu.VMEM((3, TILE, TILE), F32), total_scratch)
+    second = around(search_a, beneath=search_b)
+
+    def sweep(place, owns, received, banks):
+        return call(
+            functools.partial(sweep_kernel, place, len(owns)),
+            [two_shape],
+            10**8,
+            smem=1,
+            scratch=sweep_scratch,
+        )(meta, geometry, *owns, *received, *banks)[0]
+
+    searches = (search_a, search_b, search_c)
+    next_a = sweep(0, searches, second, (pairs_a,))
+    next_b = sweep(2, searches, second, (pairs_b, pairs_c))
+    third = around(next_a, beneath=next_b)
     local_scratch = pltpu.VMEM((4, 8, TILE), F32)
     sent = sweep(0, (next_a, next_b), third, (pairs_a,))
     outer = beside(sent, True)

time: 125 us -> 127 us (1.016)
  Pallas kernels: 34.6 us -> 39.6 us
  local copies, waits for them, and re-layouts: 2.05 us -> 0.05 us
    pallas_call x19, Pallas kernels: 31.8 us -> 36.6 us  [run(): pl.pallas_call(kernel, out_shape=[(pltpu.HBM if hbm_outs else jax.ShapeDt...]
    ppermute x9, starting transfers between devices: 27.9 us -> 23.8 us  [beside(): return lax.ppermute(block, BOTH, swap_pairs(n_slab, n_space, odd))]
    all_to_all x1, starting transfers between devices: 8.69 us -> 10.9 us  [local(): grid = lax.all_to_all(spread, CHIPS, 0, 0, tiled=True)]
    unnamed x34 -> x28, local copies, waits for them, and re-layouts: 2.05 us -> 0.05 us
    ppermute x4, starting transfers between devices: 7.38 us -> 9 us  [along_slab(): lax.ppermute(level, 'slab', down)]
  transfers between devices with their start and end apart: 18 -> 18, of which waited for: 6 -> 6; matrix products, arithmetic and copies ran while one was open for 0% -> 0% of each run, Pallas kernels for 17% -> 18%
where the time goes in v10:
time: 127 us; the launch traced here: 126 us
  starting transfers between devices  45.7 us (36%)
  Pallas kernels  39.6 us (31%)
  blocking collectives  24.5 us (19%)
  waiting for transfers between devices  15.7 us (12%)
    pallas_call x19, Pallas kernels, run(): pl.pallas_call(kernel, out_shape=[(pltpu.HBM if hbm_outs else jax.ShapeDt...  36.6 us
    all_to_all x1, blocking collectives, local(): returned = lax.all_to_all(planes, CHIPS, 0, 0, tiled=True)  24.5 us
    ppermute x9, starting transfers between devices, beside(): return lax.ppermute(block, BOTH, swap_pairs(n_slab, n_space, odd))  23.8 us
    all_to_all x1, starting transfers between devices, local(): grid = lax.all_to_all(spread, CHIPS, 0, 0, tiled=True)  10.9 us
    all_to_all x1, waiting for transfers between devices, local(): grid = lax.all_to_all(spread, CHIPS, 0, 0, tiled=True)  10.2 us
    ppermute x4, starting transfers between devices, along_slab(): lax.ppermute(level, 'slab', down)  9 us
    ppermute x4, waiting for transfers between devices, along_slab(): lax.ppermute(level, 'slab', up)  4.21 us
  transfers between devices with their start and end apart: 18, of which 6 were waited for; matrix products, arithmetic and copies ran while one was open for 0% of the time, Pallas kernels for 18%

profile of v10, /device:TPU:1, one launch (start us, length us, event | category | flops | bytes accessed | tf_op | source)
XLA Modules:
  0.0 126.4 jit_solution(12971704135977699929)
XLA Ops:
  0.6 1.1 shard_map.193
  1.7 3.3 %collective-permute-start = (f32[8,768]{1,0:T(8,128)S(1)}, f32[8,768]{1,0:T(8,128)S(1)}, u32[]{:S(2)}, u32[]{:S(2)}) collective-permute-start(f32[8,768]{1,0:T(8,128)S(1)} %get-tuple-element.29.mine), channel_id=1, source_target_pairs={{0,1},{1,0},{2,3},{3,2},{4,5},{5,4},{6,7},{7,6},{8,9},{9,8},{10,11... | collective-permute-start | bytes 73736 | tf_op jit(solution)/shard_map/ppermute | solution.py:729
  5.0 0.0 collective-permute-start.1
  5.0 1.9 %shard_map.194.meta = s32[48]{0:T(128)S(1)} custom-call(s32[1,4,8]{2,1,0:T(4,128)} %stored_lists.1, s32[1,4]{1,0:T(1,128)} %stored_counts.1, s32[1,2]{1,0:T(1,128)} %stored_send.1, f32[2,8,128]{2,1,0:T(8,128)S(1)} %get-tuple-element.27.after.own), custom_call_target="tpu_custom_call" | custom-call | flops 100000000 | bytes 1048576 | tf_op jit(solution)/shard_map/pallas_call | solution.py:792
  6.9 0.0 collective-permute-done.beside.inner
  6.9 2.7 %shard_map.195 = (f32[2,2,72,512]{3,2,1,0:T(8,128)S(1)}, f32[2,2,8,512]{3,2,1,0:T(8,128)S(1)}, bf16[2,128,512]{2,1,0:T(8,128)(2,1)S(1)}, bf16[2,128,512]{2,1,0:T(8,128)(2,1)S(1)}, f32[2,128,512]{2,1,0:T(8,128)S(1)}) custom-call(f32[8,768]{1,0:T(8,128)S(1)} %get-tuple-element.29.mine, f32[8,768]{1,0:T(8,128)S(1)} %collective-permute-done.beside.inner, ...), custom_call_target="tpu_custom_call" | custom-call | flops 100000000 | bytes 1048576 | tf_op jit(solution)/shard_map/pallas_call | solution.py:134
  9.7 0.0 copy-start.6
  9.7 0.0 copy-start.8
  9.7 0.0 copy-start.10
  9.7 0.0 copy-start.12
  9.7 0.0 collective-permute-done.1.outer
  9.8 1.2 collective-permute-start.2
  10.9 1.6 %collective-permute-start.3 = (f32[3,2,8,128]{3,2,1,0:T(8,128)S(1)}, f32[3,2,8,128]{3,2,1,0:T(8,128)S(1)}, u32[]{:S(2)}, u32[]{:S(2)}) collective-permute-start(f32[3,2,8,128]{3,2,1,0:T(8,128)S(1)} %shard_map.196.level), channel_id=1, source_target_pairs={{64,0},{128,64},{192,128},{0,192},{65,1},{129,65},{193,129},{1,193... | collective-permute-start | bytes 73736 | tf_op jit(solution)/shard_map/ppermute | solution.py:736
  12.5 1.2 collective-permute-done.2.before
  13.7 0.0 collective-permute-done.3.after
  13.7 5.0 %shard_map.197 = (f32[22,8,128]{2,1,0:T(8,128)S(1)}, f32[3,16,128,128]{3,2,1,0:T(8,128)S(1)}, f32[2,8,128]{2,1,0:T(8,128)S(1)}) custom-call(s32[48]{0:T(128)S(1)} %shard_map.194.meta, f32[4,8,128]{2,1,0:T(8,128)S(1)} %get-tuple-element.28.own, f32[3,2,8,128]{3,2,1,0:T(8,128)S(1)} %shard_map.196.level, f32[3,2,8,128]{3,2,1,0:T(8,128)S(1)} %collective-permute-done.2.before, ...), custom_call_target="tpu_custom_call" | custom-call | flops 1000000000 | bytes 1048576 | tf_op jit(solution)/shard_map/pallas_call | solution.py:134
  18.8 8.2 %collective-permute-start.4 = (f32[2,8,128]{2,1,0:T(8,128)S(1)}, f32[2,8,128]{2,1,0:T(8,128)S(1)}, u32[]{:S(2)}, u32[]{:S(2)}) collective-permute-start(f32[2,8,128]{2,1,0:T(8,128)S(1)} %get-tuple-element.33.own.refs_0_), channel_id=1, source_target_pairs={{0,1},{1,0},{2,3},{3,2},{4,5},{5,4},{6,7},{7,6},{8,9},{9,8},{10,11... | collective-permute-start | bytes 24584 | tf_op jit(solution)/shard_map/ppermute | solution.py:729
  27.0 0.0 collective-permute-start.5
  27.0 2.8 %shard_map.198 = (f32[3,8,128,128]{3,2,1,0:T(8,128)S(1)}, f32[1,8,128]{2,1,0:T(8,128)S(1)}) custom-call(s32[48]{0:T(128)S(1)} %shard_map.194.meta, f32[22,8,128]{2,1,0:T(8,128)S(1)} %get-tuple-element.32.pool.geometry), custom_call_target="tpu_custom_call" | custom-call | flops 1000000000 | bytes 1048576 | tf_op jit(solution)/shard_map/pallas_call | solution.py:134
  29.8 0.3 collective-permute-done.5.outer
  30.0 0.0 collective-permute-done.4.inner
  30.1 0.0 collective-permute-start.6
  30.1 2.7 %collective-permute-start.7 = (f32[3,2,8,128]{3,2,1,0:T(8,128)S(1)}, f32[3,2,8,128]{3,2,1,0:T(8,128)S(1)}, u32[]{:S(2)}, u32[]{:S(2)}) collective-permute-start(f32[3,2,8,128]{3,2,1,0:T(8,128)S(1)} %shard_map.200.refs_3_), channel_id=1, source_target_pairs={{64,0},{128,64},{192,128},{0,192},{65,1},{129,65},{193,129},{1,193... | collective-permute-start | bytes 73736 | tf_op jit(solution)/shard_map/ppermute | solution.py:736
  32.7 2.8 %shard_map.199 = (f32[3,8,128,128]{3,2,1,0:T(8,128)S(1)}, f32[1,8,128]{2,1,0:T(8,128)S(1)}) custom-call(s32[48]{0:T(128)S(1)} %shard_map.194.meta, f32[22,8,128]{2,1,0:T(8,128)S(1)} %get-tuple-element.32.pool.geometry), custom_call_target="tpu_custom_call" | custom-call | flops 1000000000 | bytes 1048576 | tf_op jit(solution)/shard_map/pallas_call | solution.py:134
  35.5 0.0 collective-permute-done.6.refs_4_
  35.5 0.0 collective-permute-done.7.refs_5_
  35.5 2.2 %shard_map.201.own.refs_0_.own_a = f32[2,8,128]{2,1,0:T(8,128)S(1)} custom-call(s32[48]{0:T(128)S(1)} %shard_map.194.meta, f32[22,8,128]{2,1,0:T(8,128)S(1)} %get-tuple-element.32.pool.geometry, f32[2,8,128]{2,1,0:T(8,128)S(1)} %get-tuple-element.33.own.refs_0_, f32[1,8,128]{2,1,0:T(8,128)S(1)} %get-tuple-element.34.refs_1_, ...), custom_call_target="tpu_custom_call" | custom-call | flops 100000000 | bytes 1048576 | tf_op jit(solution)/shard_map/pallas_call | solution.py:134
  37.7 4.1 %collective-permute-start.8 = (f32[2,8,128]{2,1,0:T(8,128)S(1)}, f32[2,8,128]{2,1,0:T(8,128)S(1)}, u32[]{:S(2)}, u32[]{:S(2)}) collective-permute-start(f32[2,8,128]{2,1,0:T(8,128)S(1)} %shard_map.201.own.refs_0_.own_a), channel_id=1, source_target_pairs={{0,1},{1,0},{2,3},{3,2},{4,5},{5,4},{6,7},{7,6},{8,9},{9,8},{10,11... | collective-permute-start | bytes 24584 | tf_op jit(solution)/shard_map/ppermute | solution.py:729
  41.8 0.0 collective-permute-start.9
  41.8 2.0 %shard_map.202.refs_1_.own_b = f32[2,8,128]{2,1,0:T(8,128)S(1)} custom-call(s32[48]{0:T(128)S(1)} %shard_map.194.meta, f32[22,8,128]{2,1,0:T(8,128)S(1)} %get-tuple-element.32.pool.geometry, f32[2,8,128]{2,1,0:T(8,128)S(1)} %get-tuple-element.33.own.refs_0_, f32[1,8,128]{2,1,0:T(8,128)S(1)} %get-tuple-element.34.refs_1_, ...), custom_call_target="tpu_custom_call" | custom-call | flops 100000000 | bytes 1048576 | tf_op jit(solution)/shard_map/pallas_call | solution.py:134
  43.8 1.0 collective-permute-done.9.outer
  44.8 0.0 collective-permute-done.8.inner
  44.8 0.1 collective-permute-start.10
  44.9 2.7 %collective-permute-start.11 = (f32[3,2,8,128]{3,2,1,0:T(8,128)S(1)}, f32[3,2,8,128]{3,2,1,0:T(8,128)S(1)}, u32[]{:S(2)}, u32[]{:S(2)}) collective-permute-start(f32[3,2,8,128]{3,2,1,0:T(8,128)S(1)} %shard_map.203.refs_2_.level), channel_id=1, source_target_pairs={{64,0},{128,64},{192,128},{0,192},{65,1},{129,65},{193,129},{1,193... | collective-permute-start | bytes 73736 | tf_op jit(solution)/shard_map/ppermute | solution.py:736
  47.6 1.2 collective-permute-done.10.refs_3_.before
  48.8 0.0 collective-permute-done.11.refs_4_.after
  48.8 2.2 %shard_map.204.sent.own = f32[2,8,128]{2,1,0:T(8,128)S(1)} custom-call(s32[48]{0:T(128)S(1)} %shard_map.194.meta, f32[22,8,128]{2,1,0:T(8,128)S(1)} %get-tuple-element.32.pool.geometry, f32[2,8,128]{2,1,0:T(8,128)S(1)} %shard_map.201.own.refs_0_.own_a, f32[2,8,128]{2,1,0:T(8,128)S(1)} %shard_map.202.refs_1_.own_b, ...), custom_call_target="tpu_custom_call" | custom-call | flops 100000000 | bytes 1048576 | tf_op jit(solution)/shard_map/pallas_call | solution.py:134
  51.0 1.1 collective-permute-start.13
  52.1 0.0 copy-done
  52.1 0.0 copy-done.1
  52.1 0.0 copy-done.3
  52.1 2.2 %shard_map.205 = (f32[2,8,128]{2,1,0:T(8,128)S(1)}, f32[8,768]{1,0:T(8,128)S(1)}) custom-call(s32[48]{0:T(128)S(1)} %shard_map.194.meta, f32[22,8,128]{2,1,0:T(8,128)S(1)} %get-tuple-element.32.pool.geometry, f32[2,8,128]{2,1,0:T(8,128)S(1)} %shard_map.201.own.refs_0_.own_a, f32[2,8,128]{2,1,0:T(8,128)S(1)} %shard_map.202.refs_1_.own_b, ...), custom_call_target="tpu_custom_call" | custom-call | flops 100000000 | bytes 1048576 | tf_op jit(solution)/shard_map/pallas_call | solution.py:134
  54.3 3.6 %collective-permute-start.12 = (f32[8,768]{1,0:T(8,128)S(1)}, f32[8,768]{1,0:T(8,128)S(1)}, u32[]{:S(2)}, u32[]{:S(2)}) collective-permute-start(f32[8,768]{1,0:T(8,128)S(1)} %get-tuple-element.42.ordered), channel_id=1, source_target_pairs={{0,1},{1,0},{2,3},{3,2},{4,5},{5,4},{6,7},{7,6},{8,9},{9,8},{10,11... | collective-permute-start | bytes 73736 | tf_op jit(solution)/shard_map/ppermute | solution.py:729
  57.9 1.4 %shard_map.206.mine = f32[128,576]{1,0:T(8,128)S(1)} custom-call(f32[8,768]{1,0:T(8,128)S(1)} %get-tuple-element.42.ordered, f32[2,2,72,512]{3,2,1,0:T(8,128)S(1)} %get-tuple-element.43.tab_x, f32[2,2,8,512]{3,2,1,0:T(8,128)S(1)} %get-tuple-element.30.tab_y, bf16[2,128,512]{2,1,0:T(8,128)(2,1)S(1)} %get-tuple-element.44.w_high, ...), custom_call_target="tpu_custom_call" | custom-call | flops 1000000000 | bytes 1048576 | tf_op jit(solution)/shard_map/pallas_call | solution.py:134
  59.3 0.0 collective-permute-done.12.ordered.inner
  59.3 0.0 copy-done.6
  59.3 2.4 %shard_map.207 = f32[128,8,128]{2,1,0:T(8,128)} custom-call(f32[8,768]{1,0:T(8,128)S(1)} %collective-permute-done.12.ordered.inner, f32[128,576]{1,0:T(8,128)S(1)} %shard_map.206.mine, f32[2,2,72,512]{3,2,1,0:T(8,128)S(1)} %get-tuple-element.43.tab_x, f32[2,2,8,512]{3,2,1,0:T(8,128)S(1)} %get-tuple-element.30.tab_y, ...), custom_call_target="tpu_custom_call" | custom-call | flops 1000000000 | bytes 1048576 | tf_op jit(solution)/shard_map/pallas_call | solution.py:134
  61.8 0.0 collective-permute-done.13.outer
  61.8 10.9 %all-to-all-start = ((f32[128,8,128]{2,1,0:T(8,128)}), f32[128,8,128]{2,1,0:T(8,128)}, u32[]{:S(2)}, u32[]{:S(2)}) async-start(f32[128,8,128]{2,1,0:T(8,128)} %shard_map.207), calls=%async_computation | async-start | bytes 1048576 | tf_op jit(solution)/shard_map/all_to_all | solution.py:893
  72.8 0.7 collective-permute-start.14
  73.4 2.1 %collective-permute-start.15 = (f32[3,2,8,128]{3,2,1,0:T(8,128)S(1)}, f32[3,2,8,128]{3,2,1,0:T(8,128)S(1)}, u32[]{:S(2)}, u32[]{:S(2)}) collective-permute-start(f32[3,2,8,128]{3,2,1,0:T(8,128)S(1)} %shard_map.208.level), channel_id=1, source_target_pairs={{64,0},{128,64},{192,128},{0,192},{65,1},{129,65},{193,129},{1,193... | collective-permute-start | bytes 73736 | tf_op jit(solution)/shard_map/ppermute | solution.py:736
  75.5 1.8 %collective-permute-done.14.before = f32[3,2,8,128]{3,2,1,0:T(8,128)S(1)} collective-permute-done((f32[3,2,8,128]{3,2,1,0:T(8,128)S(1)}, f32[3,2,8,128]{3,2,1,0:T(8,128)S(1)}, u32[]{:S(2)}, u32[]{:S(2)}) %collective-permute-start.14) | collective-permute-done | bytes 24608 | tf_op jit(solution)/shard_map/ppermute | solution.py:736
  77.3 0.0 collective-permute-done.15.after
  77.3 4.0 %shard_map.209 = (f32[8,512]{1,0:T(8,128)S(1)}, f32[8,128]{1,0:T(8,128)S(1)}) custom-call(s32[48]{0:T(128)S(1)} %shard_map.194.meta, f32[22,8,128]{2,1,0:T(8,128)S(1)} %get-tuple-element.32.pool.geometry, f32[2,8,128]{2,1,0:T(8,128)S(1)} %shard_map.204.sent.own, f32[2,8,128]{2,1,0:T(8,128)S(1)} %get-tuple-element.41.rest, ...), custom_call_target="tpu_custom_call" | custom-call | flops 1000000000 | bytes 1048576 | tf_op jit(solution)/shard_map/pallas_call | solution.py:134
  81.3 10.2 %all-to-all-done.refs_0_ = f32[128,8,128]{2,1,0:T(8,128)} async-done(((f32[128,8,128]{2,1,0:T(8,128)}), f32[128,8,128]{2,1,0:T(8,128)}, u32[]{:S(2)}, u32[]{:S(2)}) %all-to-all-start) | async-done | bytes 524320 | tf_op jit(solution)/shard_map/all_to_all | solution.py:893
  91.5 0.0 copy-start.13
  91.5 3.9 %shard_map.210 = f32[128,8,128]{2,1,0:T(8,128)S(1)} custom-call(f32[8,256]{1,0:T(8,128)S(1)} %copy-done.5, f32[8,128]{1,0:T(8,128)S(1)} %get-tuple-element.48.sums, f32[128,8,128]{2,1,0:T(8,128)} %all-to-all-done.refs_0_, bf16[256,256]{1,0:T(8,128)(2,1)} %constant.21.clone.refs_1_, bf16[256,256]{1,0:T(8,128)(2,1)} %constant.22.clone.refs_2_, ...), custom_call_target="tpu_custom_call" | custom-call | flops 1000000000 | bytes 1048576 | tf_op jit(solution)/shard_map/pallas_call | solution.py:134
  95.4 24.5 %all_to_all.10.grid = f32[128,8,128]{2,1,0:T(8,128)S(1)} all-to-all(f32[128,8,128]{2,1,0:T(8,128)S(1)} %shard_map.210), channel_id=1, replica_groups=mesh['slab'=4,'pair'=32,'core'=2] {'slab','pair'}, dimensions={0} | all-to-all | bytes 1048576 | tf_op jit(solution)/shard_map/all_to_all | solution.py:922
  119.9 0.0 copy-done.9
  119.9 1.1 shard_map.212
  121.0 3.5 %collective-permute-start.16 = (f32[8,512]{1,0:T(8,128)S(1)}, f32[8,512]{1,0:T(8,128)S(1)}, u32[]{:S(2)}, u32[]{:S(2)}) collective-permute-start(f32[8,512]{1,0:T(8,128)S(1)} %shard_map.212), channel_id=1, source_target_pairs={{0,1},{1,0},{2,3},{3,2},{4,5},{5,4},{6,7},{7,6},{8,9},{9,8},{10,11... | collective-permute-start | bytes 49160 | tf_op jit(solution)/shard_map/ppermute | solution.py:729
  124.5 1.1 shard_map.211.mine
  125.5 0.0 collective-permute-done.16.theirs
  125.6 0.9 shard_map.213
  (22 shorter events, 0.0 us)
Async XLA Ops:
  1.7 5.2 %collective-permute-start = (f32[8,768]{1,0:T(8,128)S(1)}, f32[8,768]{1,0:T(8,128)S(1)}, u32[]{:S(2)}, u32[]{:S(2)}) collective-permute-start(f32[8,768]{1,0:T(8,128)S(1)} %get-tuple-element.29.mine), channel_id=1, source_target_pairs={{0,1},{1,0},{2,3},{3,2},{4,5},{5,4},{6,7},{7,6},{8,9},{9,8},{10,11... | collective-permute-start | bytes 73736 | tf_op jit(solution)/shard_map/ppermute | solution.py:729
  5.0 4.7 %collective-permute-start.1 = (f32[2,8,128]{2,1,0:T(8,128)S(1)}, f32[2,8,128]{2,1,0:T(8,128)S(1)}, u32[]{:S(2)}, u32[]{:S(2)}) collective-permute-start(f32[2,8,128]{2,1,0:T(8,128)S(1)} %get-tuple-element.27.after.own), channel_id=1, source_target_pairs={{0,63},{1,2},{2,1},{3,4},{4,3},{5,6},{6,5},{7,8},{8,7},{9,10},{10,... | collective-permute-start | bytes 24584 | tf_op jit(solution)/shard_map/ppermute | solution.py:729
  9.7 49.6 %copy-start.6 = (f32[2,2,72,512]{3,2,1,0:T(8,128)}, f32[2,2,72,512]{3,2,1,0:T(8,128)S(1)}, u32[]{:S(2)}) copy-start(f32[2,2,72,512]{3,2,1,0:T(8,128)S(1)} %get-tuple-element.43.tab_x) | copy-start | bytes 1769476
  9.7 49.6 %copy-start.8 = (f32[2,128,512]{2,1,0:T(8,128)}, f32[2,128,512]{2,1,0:T(8,128)S(1)}, u32[]{:S(2)}) copy-start(f32[2,128,512]{2,1,0:T(8,128)S(1)} %get-tuple-element.46.slope_z) | copy-start | bytes 1572868
  9.7 49.6 %copy-start.10 = (bf16[2,128,512]{2,1,0:T(8,128)(2,1)}, bf16[2,128,512]{2,1,0:T(8,128)(2,1)S(1)}, u32[]{:S(2)}) copy-start(bf16[2,128,512]{2,1,0:T(8,128)(2,1)S(1)} %get-tuple-element.44.w_high) | copy-start | bytes 786436
  9.7 49.6 %copy-start.12 = (bf16[2,128,512]{2,1,0:T(8,128)(2,1)}, bf16[2,128,512]{2,1,0:T(8,128)(2,1)S(1)}, u32[]{:S(2)}) copy-start(bf16[2,128,512]{2,1,0:T(8,128)(2,1)S(1)} %get-tuple-element.45.w_low) | copy-start | bytes 786436
  9.8 4.0 %collective-permute-start.2 = (f32[3,2,8,128]{3,2,1,0:T(8,128)S(1)}, f32[3,2,8,128]{3,2,1,0:T(8,128)S(1)}, u32[]{:S(2)}, u32[]{:S(2)}) collective-permute-start(f32[3,2,8,128]{3,2,1,0:T(8,128)S(1)} %shard_map.196.level), channel_id=1, source_target_pairs={{0,64},{64,128},{128,192},{192,0},{1,65},{65,129},{129,193},{193,1... | collective-permute-start | bytes 73736 | tf_op jit(solution)/shard_map/ppermute | solution.py:736
  10.9 2.8 %collective-permute-start.3 = (f32[3,2,8,128]{3,2,1,0:T(8,128)S(1)}, f32[3,2,8,128]{3,2,1,0:T(8,128)S(1)}, u32[]{:S(2)}, u32[]{:S(2)}) collective-permute-start(f32[3,2,8,128]{3,2,1,0:T(8,128)S(1)} %shard_map.196.level), channel_id=1, source_target_pairs={{64,0},{128,64},{192,128},{0,192},{65,1},{129,65},{193,129},{1,193... | collective-permute-start | bytes 73736 | tf_op jit(solution)/shard_map/ppermute | solution.py:736
  18.8 11.3 %collective-permute-start.4 = (f32[2,8,128]{2,1,0:T(8,128)S(1)}, f32[2,8,128]{2,1,0:T(8,128)S(1)}, u32[]{:S(2)}, u32[]{:S(2)}) collective-permute-start(f32[2,8,128]{2,1,0:T(8,128)S(1)} %get-tuple-element.33.own.refs_0_), channel_id=1, source_target_pairs={{0,1},{1,0},{2,3},{3,2},{4,5},{5,4},{6,7},{7,6},{8,9},{9,8},{10,11... | collective-permute-start | bytes 24584 | tf_op jit(solution)/shard_map/ppermute | solution.py:729
  27.0 3.1 %collective-permute-start.5 = (f32[2,8,128]{2,1,0:T(8,128)S(1)}, f32[2,8,128]{2,1,0:T(8,128)S(1)}, u32[]{:S(2)}, u32[]{:S(2)}) collective-permute-start(f32[2,8,128]{2,1,0:T(8,128)S(1)} %get-tuple-element.33.own.refs_0_), channel_id=1, source_target_pairs={{0,63},{1,2},{2,1},{3,4},{4,3},{5,6},{6,5},{7,8},{8,7},{9,10},{10,... | collective-permute-start | bytes 24584 | tf_op jit(solution)/shard_map/ppermute | solution.py:729
  29.8 22.4 %copy-start = (f32[3,8,128,128]{3,2,1,0:T(8,128)}, f32[3,8,128,128]{3,2,1,0:T(8,128)S(1)}, u32[]{:S(2)}) copy-start(f32[3,8,128,128]{3,2,1,0:T(8,128)S(1)} %get-tuple-element.38.refs_6_.pairs_b.stored_b) | copy-start | bytes 4718596
  30.1 5.5 %collective-permute-start.6 = (f32[3,2,8,128]{3,2,1,0:T(8,128)S(1)}, f32[3,2,8,128]{3,2,1,0:T(8,128)S(1)}, u32[]{:S(2)}, u32[]{:S(2)}) collective-permute-start(f32[3,2,8,128]{3,2,1,0:T(8,128)S(1)} %shard_map.200.refs_3_), channel_id=1, source_target_pairs={{0,64},{64,128},{128,192},{192,0},{1,65},{65,129},{129,193},{193,1... | collective-permute-start | bytes 73736 | tf_op jit(solution)/shard_map/ppermute | solution.py:736
  30.1 5.5 %collective-permute-start.7 = (f32[3,2,8,128]{3,2,1,0:T(8,128)S(1)}, f32[3,2,8,128]{3,2,1,0:T(8,128)S(1)}, u32[]{:S(2)}, u32[]{:S(2)}) collective-permute-start(f32[3,2,8,128]{3,2,1,0:T(8,128)S(1)} %shard_map.200.refs_3_), channel_id=1, source_target_pairs={{64,0},{128,64},{192,128},{0,192},{65,1},{129,65},{193,129},{1,193... | collective-permute-start | bytes 73736 | tf_op jit(solution)/shard_map/ppermute | solution.py:736
  35.5 16.6 %copy-start.1 = (f32[3,8,128,128]{3,2,1,0:T(8,128)}, f32[3,8,128,128]{3,2,1,0:T(8,128)S(1)}, u32[]{:S(2)}) copy-start(f32[3,8,128,128]{3,2,1,0:T(8,128)S(1)} %get-tuple-element.39.refs_7_.pairs_c.stored_c) | copy-start | bytes 4718596
  37.7 7.1 %collective-permute-start.8 = (f32[2,8,128]{2,1,0:T(8,128)S(1)}, f32[2,8,128]{2,1,0:T(8,128)S(1)}, u32[]{:S(2)}, u32[]{:S(2)}) collective-permute-start(f32[2,8,128]{2,1,0:T(8,128)S(1)} %shard_map.201.own.refs_0_.own_a), channel_id=1, source_target_pairs={{0,1},{1,0},{2,3},{3,2},{4,5},{5,4},{6,7},{7,6},{8,9},{9,8},{10,11... | collective-permute-start | bytes 24584 | tf_op jit(solution)/shard_map/ppermute | solution.py:729
  41.8 3.1 %collective-permute-start.9 = (f32[2,8,128]{2,1,0:T(8,128)S(1)}, f32[2,8,128]{2,1,0:T(8,128)S(1)}, u32[]{:S(2)}, u32[]{:S(2)}) collective-permute-start(f32[2,8,128]{2,1,0:T(8,128)S(1)} %shard_map.201.own.refs_0_.own_a), channel_id=1, source_target_pairs={{0,63},{1,2},{2,1},{3,4},{4,3},{5,6},{6,5},{7,8},{8,7},{9,10},{10,... | collective-permute-start | bytes 24584 | tf_op jit(solution)/shard_map/ppermute | solution.py:729
  44.8 7.3 %copy-start.3 = (s32[1,512]{1,0:T(1,128)S(1)}, s32[1,512]{1,0:T(1,128)}, u32[]{:S(2)}) copy-start(s32[1,512]{1,0:T(1,128)} %order.3) | copy-start | bytes 6148
  44.8 4.0 %collective-permute-start.10 = (f32[3,2,8,128]{3,2,1,0:T(8,128)S(1)}, f32[3,2,8,128]{3,2,1,0:T(8,128)S(1)}, u32[]{:S(2)}, u32[]{:S(2)}) collective-permute-start(f32[3,2,8,128]{3,2,1,0:T(8,128)S(1)} %shard_map.203.refs_2_.level), channel_id=1, source_target_pairs={{0,64},{64,128},{128,192},{192,0},{1,65},{65,129},{129,193},{193,1... | collective-permute-start | bytes 73736 | tf_op jit(solution)/shard_map/ppermute | solution.py:736
  44.9 3.9 %collective-permute-start.11 = (f32[3,2,8,128]{3,2,1,0:T(8,128)S(1)}, f32[3,2,8,128]{3,2,1,0:T(8,128)S(1)}, u32[]{:S(2)}, u32[]{:S(2)}) collective-permute-start(f32[3,2,8,128]{3,2,1,0:T(8,128)S(1)} %shard_map.203.refs_2_.level), channel_id=1, source_target_pairs={{64,0},{128,64},{192,128},{0,192},{65,1},{129,65},{193,129},{1,193... | collective-permute-start | bytes 73736 | tf_op jit(solution)/shard_map/ppermute | solution.py:736
  51.0 10.8 %collective-permute-start.13 = (f32[2,8,128]{2,1,0:T(8,128)S(1)}, f32[2,8,128]{2,1,0:T(8,128)S(1)}, u32[]{:S(2)}, u32[]{:S(2)}) collective-permute-start(f32[2,8,128]{2,1,0:T(8,128)S(1)} %shard_map.204.sent.own), channel_id=1, source_target_pairs={{0,63},{1,2},{2,1},{3,4},{4,3},{5,6},{6,5},{7,8},{8,7},{9,10},{10,... | collective-permute-start | bytes 24584 | tf_op jit(solution)/shard_map/ppermute | solution.py:729
  54.3 4.9 %collective-permute-start.12 = (f32[8,768]{1,0:T(8,128)S(1)}, f32[8,768]{1,0:T(8,128)S(1)}, u32[]{:S(2)}, u32[]{:S(2)}) collective-permute-start(f32[8,768]{1,0:T(8,128)S(1)} %get-tuple-element.42.ordered), channel_id=1, source_target_pairs={{0,1},{1,0},{2,3},{3,2},{4,5},{5,4},{6,7},{7,6},{8,9},{9,8},{10,11... | collective-permute-start | bytes 73736 | tf_op jit(solution)/shard_map/ppermute | solution.py:729
  61.8 29.7 %all-to-all-start = ((f32[128,8,128]{2,1,0:T(8,128)}), f32[128,8,128]{2,1,0:T(8,128)}, u32[]{:S(2)}, u32[]{:S(2)}) async-start(f32[128,8,128]{2,1,0:T(8,128)} %shard_map.207), calls=%async_computation | async-start | bytes 1048576 | tf_op jit(solution)/shard_map/all_to_all | solution.py:893
  72.8 4.5 %collective-permute-start.14 = (f32[3,2,8,128]{3,2,1,0:T(8,128)S(1)}, f32[3,2,8,128]{3,2,1,0:T(8,128)S(1)}, u32[]{:S(2)}, u32[]{:S(2)}) collective-permute-start(f32[3,2,8,128]{3,2,1,0:T(8,128)S(1)} %shard_map.208.level), channel_id=1, source_target_pairs={{0,64},{64,128},{128,192},{192,0},{1,65},{65,129},{129,193},{193,1... | collective-permute-start | bytes 73736 | tf_op jit(solution)/shard_map/ppermute | solution.py:736
  73.4 3.9 %collective-permute-start.15 = (f32[3,2,8,128]{3,2,1,0:T(8,128)S(1)}, f32[3,2,8,128]{3,2,1,0:T(8,128)S(1)}, u32[]{:S(2)}, u32[]{:S(2)}) collective-permute-start(f32[3,2,8,128]{3,2,1,0:T(8,128)S(1)} %shard_map.208.level), channel_id=1, source_target_pairs={{64,0},{128,64},{192,128},{0,192},{65,1},{129,65},{193,129},{1,193... | collective-permute-start | bytes 73736 | tf_op jit(solution)/shard_map/ppermute | solution.py:736
  77.3 14.2 %copy-start.5 = (f32[8,256]{1,0:T(8,128)S(1)}, f32[8,256]{1,0:T(8,128)}, u32[]{:S(2)}) copy-start(f32[8,256]{1,0:T(8,128)} %constant.20.clone.waves) | copy-start | bytes 24580
  91.5 28.4 %copy-start.7 = (f32[2,2,72,512]{3,2,1,0:T(8,128)S(1)}, f32[2,2,72,512]{3,2,1,0:T(8,128)}, u32[]{:S(2)}) copy-start(f32[2,2,72,512]{3,2,1,0:T(8,128)} %copy-done.6) | copy-start | bytes 1769476
  91.5 28.4 %copy-start.9 = (f32[2,128,512]{2,1,0:T(8,128)S(1)}, f32[2,128,512]{2,1,0:T(8,128)}, u32[]{:S(2)}) copy-start(f32[2,128,512]{2,1,0:T(8,128)} %copy-done.8) | copy-start | bytes 1572868
  91.5 28.4 %copy-start.11 = (bf16[2,128,512]{2,1,0:T(8,128)(2,1)S(1)}, bf16[2,128,512]{2,1,0:T(8,128)(2,1)}, u32[]{:S(2)}) copy-start(bf16[2,128,512]{2,1,0:T(8,128)(2,1)} %copy-done.10) | copy-start | bytes 786436
  91.5 28.4 %copy-start.13 = (bf16[2,128,512]{2,1,0:T(8,128)(2,1)S(1)}, bf16[2,128,512]{2,1,0:T(8,128)(2,1)}, u32[]{:S(2)}) copy-start(bf16[2,128,512]{2,1,0:T(8,128)(2,1)} %copy-done.12) | copy-start | bytes 786436
  121.0 4.6 %copy-start.2 = (f32[3,512]{1,0:T(4,128)S(1)}, f32[3,512]{1,0:T(4,128)}, u32[]{:S(2)}) copy-start(f32[3,512]{1,0:T(4,128)} %residual.1) | copy-start | bytes 18436
  121.0 4.6 %copy-start.4 = (f32[3,512]{1,0:T(4,128)S(1)}, f32[3,512]{1,0:T(4,128)}, u32[]{:S(2)}) copy-start(f32[3,512]{1,0:T(4,128)} %dipoles.1) | copy-start | bytes 18436
  121.0 4.6 %collective-permute-start.16 = (f32[8,512]{1,0:T(8,128)S(1)}, f32[8,512]{1,0:T(8,128)S(1)}, u32[]{:S(2)}, u32[]{:S(2)}) collective-permute-start(f32[8,512]{1,0:T(8,128)S(1)} %shard_map.212), channel_id=1, source_target_pairs={{0,1},{1,0},{2,3},{3,2},{4,5},{5,4},{6,7},{7,6},{8,9},{9,8},{10,11... | collective-permute-start | bytes 49160 | tf_op jit(solution)/shard_map/ppermute | solution.py:729

commit v11 on v10

--- a/solution.py
+++ b/solution.py
@@ -382,15 +382,14 @@
 
 
 def direction_kernel(
-    meta, geometry, own_a, own_b, level, before, after, sent, pairs_b, pairs_c, order, found, bundle, pool, columns, totals, local
+    meta, geometry, own_a, own_b, level, before, after, pairs_a, pairs_b, pairs_c, order, sent, rest, bundle, pool, columns, totals, local
 ):
     atoms = order.shape[1]
     fill_search(pool, (own_a, own_b), level, before, after, meta)
-    sweep_tiles(2, meta, geometry, (pairs_b, pairs_c), found, pool, columns, totals, local)
+    sweep_tiles(0, meta, geometry, (pairs_a,), sent, pool, columns, totals, local)
+    sweep_tiles(2, meta, geometry, (pairs_b, pairs_c), rest, pool, columns, totals, local)
     for place in range(2):
-        block = sent[place]
-        local[meta[ORDER_AT + place]] = block
-        bundle[:, atoms + place * TILE : atoms + (place + 1) * TILE] = block
+        bundle[:, atoms + place * TILE : atoms + (place + 1) * TILE] = sent[place]
     in_tiles = jnp.concatenate([local[tile] for tile in range(4)], 1)
     bundle[:, :atoms] = selected(in_tiles, order_matrix(order[...], atoms), NT)
 
@@ -868,15 +867,13 @@
     next_b = sweep(2, searches, second, (pairs_b, pairs_c))
     third = around(next_a, beneath=next_b)
     local_scratch = pltpu.VMEM((4, 8, TILE), F32)
-    sent = sweep(0, (next_a, next_b), third, (pairs_a,))
-    outer = beside(sent, True)
-    rest, ordered = call(
+    sent, rest, ordered = call(
         direction_kernel,
-        [two_shape, ((8, atoms + 2 * TILE), F32)],
+        [two_shape, two_shape, ((8, atoms + 2 * TILE), F32)],
         10**8,
         smem=1,
         scratch=sweep_scratch + (local_scratch,),
-    )(meta, geometry, next_a, next_b, *third, sent, pairs_b, pairs_c, tile_order)
+    )(meta, geometry, next_a, next_b, *third, pairs_a, pairs_b, pairs_c, tile_order)
     ordered_beside = beside(ordered, False)
     message = ((half, 8, TILE), F32)
     flat_scratch = pltpu.VMEM((half, 8 * TILE), F32)
@@ -889,9 +886,9 @@
         vmem=LARGE_VMEM,
         hbm_outs=True,
     )(ordered_beside, spread_own, *tables)[0]
-    spread, outer = lax.optimization_barrier((spread, outer))
+    late, _ = lax.optimization_barrier((sent, spread))
     grid = lax.all_to_all(spread, CHIPS, 0, 0, tiled=True)
-    last = along_slab(joined(sent, ordered_beside, outer))
+    last = along_slab(joined(sent, ordered_beside, beside(late, True)))
     applied, sums = call(
         final_field_kernel,
         [((8, atoms), F32), ((8, TILE), F32)],

time: 127 us -> 130 us (1.024)
  blocking collectives: 24.5 us -> 31.7 us
  Pallas kernels: 39.6 us -> 33.2 us
  waiting for transfers between devices: 15.7 us -> 18 us
    ppermute x9, waiting for transfers between devices: 1.35 us -> 13.9 us  [beside(): return lax.ppermute(block, BOTH, swap_pairs(n_slab, n_space, odd))]
    all_to_all x1, waiting for transfers between devices: 10.2 us -> 0.01 us  [local(): grid = lax.all_to_all(spread, CHIPS, 0, 0, tiled=True)]
    all_to_all x1, blocking collectives: 24.5 us -> 31.7 us  [local(): returned = lax.all_to_all(planes, CHIPS, 0, 0, tiled=True)]
    pallas_call x19 -> x18, Pallas kernels: 36.6 us -> 30.3 us  [run(): pl.pallas_call(kernel, out_shape=[(pltpu.HBM if hbm_outs else jax.ShapeDt...]
    all_to_all x1, starting transfers between devices: 10.9 us -> 7.31 us  [local(): grid = lax.all_to_all(spread, CHIPS, 0, 0, tiled=True)]
    ppermute x9, starting transfers between devices: 23.8 us -> 27.4 us  [beside(): return lax.ppermute(block, BOTH, swap_pairs(n_slab, n_space, odd))]
  transfers between devices with their start and end apart: 18 -> 18, of which waited for: 6 -> 6; matrix products, arithmetic and copies ran while one was open for 0% -> 0% of each run, Pallas kernels for 18% -> 12%
where the time goes in v11:
time: 130 us
  starting transfers between devices  45.8 us (35%)
  Pallas kernels  33.2 us (26%)
  blocking collectives  31.7 us (24%)
  waiting for transfers between devices  18 us (14%)
    all_to_all x1, blocking collectives, local(): returned = lax.all_to_all(planes, CHIPS, 0, 0, tiled=True)  31.7 us
    pallas_call x18, Pallas kernels, run(): pl.pallas_call(kernel, out_shape=[(pltpu.HBM if hbm_outs else jax.ShapeDt...  30.3 us
    ppermute x9, starting transfers between devices, beside(): return lax.ppermute(block, BOTH, swap_pairs(n_slab, n_space, odd))  27.4 us
    ppermute x9, waiting for transfers between devices, beside(): return lax.ppermute(block, BOTH, swap_pairs(n_slab, n_space, odd))  13.9 us
    ppermute x4, starting transfers between devices, along_slab(): lax.ppermute(level, 'slab', down)  8.58 us
    all_to_all x1, starting transfers between devices, local(): grid = lax.all_to_all(spread, CHIPS, 0, 0, tiled=True)  7.31 us
    ppermute x4, waiting for transfers between devices, along_slab(): lax.ppermute(level, 'slab', up)  4.08 us
  transfers between devices with their start and end apart: 18, of which 6 were waited for; matrix products, arithmetic and copies ran while one was open for 0% of the time, Pallas kernels for 12%

profile of v11, /device:TPU:1, one launch (start us, length us, event | category | flops | bytes accessed | tf_op | source)
XLA Modules:
  0.0 129.8 jit_solution(4685916357148357837)
XLA Ops:
  0.6 1.1 shard_map.193
  1.7 3.3 %collective-permute-start = (f32[8,768]{1,0:T(8,128)S(1)}, f32[8,768]{1,0:T(8,128)S(1)}, u32[]{:S(2)}, u32[]{:S(2)}) collective-permute-start(f32[8,768]{1,0:T(8,128)S(1)} %get-tuple-element.29.mine), channel_id=1, source_target_pairs={{0,1},{1,0},{2,3},{3,2},{4,5},{5,4},{6,7},{7,6},{8,9},{9,8},{10,11... | collective-permute-start | bytes 73736 | tf_op jit(solution)/shard_map/ppermute | solution.py:728
  5.0 0.0 collective-permute-start.1
  5.0 1.9 %shard_map.194.meta = s32[48]{0:T(128)S(1)} custom-call(s32[1,4,8]{2,1,0:T(4,128)} %stored_lists.1, s32[1,4]{1,0:T(1,128)} %stored_counts.1, s32[1,2]{1,0:T(1,128)} %stored_send.1, f32[2,8,128]{2,1,0:T(8,128)S(1)} %get-tuple-element.27.after.own), custom_call_target="tpu_custom_call" | custom-call | flops 100000000 | bytes 1048576 | tf_op jit(solution)/shard_map/pallas_call | solution.py:791
  6.9 0.0 collective-permute-done.beside.inner
  6.9 2.8 %shard_map.195 = (f32[2,2,72,512]{3,2,1,0:T(8,128)S(1)}, f32[2,2,8,512]{3,2,1,0:T(8,128)S(1)}, bf16[2,128,512]{2,1,0:T(8,128)(2,1)S(1)}, bf16[2,128,512]{2,1,0:T(8,128)(2,1)S(1)}, f32[2,128,512]{2,1,0:T(8,128)S(1)}) custom-call(f32[8,768]{1,0:T(8,128)S(1)} %get-tuple-element.29.mine, f32[8,768]{1,0:T(8,128)S(1)} %collective-permute-done.beside.inner, ...), custom_call_target="tpu_custom_call" | custom-call | flops 100000000 | bytes 1048576 | tf_op jit(solution)/shard_map/pallas_call | solution.py:134
  9.7 0.0 copy-start.6
  9.7 0.0 copy-start.8
  9.7 0.0 copy-start.10
  9.7 0.0 copy-start.12
  9.8 0.0 collective-permute-done.1.outer
  9.8 1.2 collective-permute-start.2
  10.9 1.6 %collective-permute-start.3 = (f32[3,2,8,128]{3,2,1,0:T(8,128)S(1)}, f32[3,2,8,128]{3,2,1,0:T(8,128)S(1)}, u32[]{:S(2)}, u32[]{:S(2)}) collective-permute-start(f32[3,2,8,128]{3,2,1,0:T(8,128)S(1)} %shard_map.196.level), channel_id=1, source_target_pairs={{64,0},{128,64},{192,128},{0,192},{65,1},{129,65},{193,129},{1,193... | collective-permute-start | bytes 73736 | tf_op jit(solution)/shard_map/ppermute | solution.py:735
  12.5 1.2 collective-permute-done.2.before
  13.7 0.0 collective-permute-done.3.after
  13.7 3.3 %shard_map.197 = (f32[22,8,128]{2,1,0:T(8,128)S(1)}, f32[3,16,128,128]{3,2,1,0:T(8,128)S(1)}, f32[2,8,128]{2,1,0:T(8,128)S(1)}) custom-call(s32[48]{0:T(128)S(1)} %shard_map.194.meta, f32[4,8,128]{2,1,0:T(8,128)S(1)} %get-tuple-element.28.own, f32[3,2,8,128]{3,2,1,0:T(8,128)S(1)} %shard_map.196.level, f32[3,2,8,128]{3,2,1,0:T(8,128)S(1)} %collective-permute-done.2.before, ...), custom_call_target="tpu_custom_call" | custom-call | flops 1000000000 | bytes 1048576 | tf_op jit(solution)/shard_map/pallas_call | solution.py:134
  17.0 10.0 %collective-permute-start.4 = (f32[2,8,128]{2,1,0:T(8,128)S(1)}, f32[2,8,128]{2,1,0:T(8,128)S(1)}, u32[]{:S(2)}, u32[]{:S(2)}) collective-permute-start(f32[2,8,128]{2,1,0:T(8,128)S(1)} %get-tuple-element.33.own.refs_0_), channel_id=1, source_target_pairs={{0,1},{1,0},{2,3},{3,2},{4,5},{5,4},{6,7},{7,6},{8,9},{9,8},{10,11... | collective-permute-start | bytes 24584 | tf_op jit(solution)/shard_map/ppermute | solution.py:728
  27.0 0.0 collective-permute-start.5
  27.0 1.9 %shard_map.198 = (f32[3,8,128,128]{3,2,1,0:T(8,128)S(1)}, f32[1,8,128]{2,1,0:T(8,128)S(1)}) custom-call(s32[48]{0:T(128)S(1)} %shard_map.194.meta, f32[22,8,128]{2,1,0:T(8,128)S(1)} %get-tuple-element.32.pool.geometry), custom_call_target="tpu_custom_call" | custom-call | flops 1000000000 | bytes 1048576 | tf_op jit(solution)/shard_map/pallas_call | solution.py:134
  28.9 1.2 collective-permute-done.5.outer
  30.1 0.0 collective-permute-done.4.inner
  30.1 0.0 collective-permute-start.6
  30.1 2.7 %collective-permute-start.7 = (f32[3,2,8,128]{3,2,1,0:T(8,128)S(1)}, f32[3,2,8,128]{3,2,1,0:T(8,128)S(1)}, u32[]{:S(2)}, u32[]{:S(2)}) collective-permute-start(f32[3,2,8,128]{3,2,1,0:T(8,128)S(1)} %shard_map.200.refs_3_), channel_id=1, source_target_pairs={{64,0},{128,64},{192,128},{0,192},{65,1},{129,65},{193,129},{1,193... | collective-permute-start | bytes 73736 | tf_op jit(solution)/shard_map/ppermute | solution.py:735
  32.7 1.9 %shard_map.199 = (f32[3,8,128,128]{3,2,1,0:T(8,128)S(1)}, f32[1,8,128]{2,1,0:T(8,128)S(1)}) custom-call(s32[48]{0:T(128)S(1)} %shard_map.194.meta, f32[22,8,128]{2,1,0:T(8,128)S(1)} %get-tuple-element.32.pool.geometry), custom_call_target="tpu_custom_call" | custom-call | flops 1000000000 | bytes 1048576 | tf_op jit(solution)/shard_map/pallas_call | solution.py:134
  34.6 0.0 collective-permute-done.6.refs_4_
  34.7 0.0 collective-permute-done.7.refs_5_
  34.7 1.7 %shard_map.201.own.own_a = f32[2,8,128]{2,1,0:T(8,128)S(1)} custom-call(s32[48]{0:T(128)S(1)} %shard_map.194.meta, f32[22,8,128]{2,1,0:T(8,128)S(1)} %get-tuple-element.32.pool.geometry, f32[2,8,128]{2,1,0:T(8,128)S(1)} %get-tuple-element.33.own.refs_0_, f32[1,8,128]{2,1,0:T(8,128)S(1)} %get-tuple-element.34.refs_1_, ...), custom_call_target="tpu_custom_call" | custom-call | flops 100000000 | bytes 1048576 | tf_op jit(solution)/shard_map/pallas_call | solution.py:134
  36.4 5.4 %collective-permute-start.8 = (f32[2,8,128]{2,1,0:T(8,128)S(1)}, f32[2,8,128]{2,1,0:T(8,128)S(1)}, u32[]{:S(2)}, u32[]{:S(2)}) collective-permute-start(f32[2,8,128]{2,1,0:T(8,128)S(1)} %shard_map.201.own.own_a), channel_id=1, source_target_pairs={{0,1},{1,0},{2,3},{3,2},{4,5},{5,4},{6,7},{7,6},{8,9},{9,8},{10,11... | collective-permute-start | bytes 24584 | tf_op jit(solution)/shard_map/ppermute | solution.py:728
  41.8 0.0 collective-permute-start.9
  41.8 1.6 %shard_map.202.own_b = f32[2,8,128]{2,1,0:T(8,128)S(1)} custom-call(s32[48]{0:T(128)S(1)} %shard_map.194.meta, f32[22,8,128]{2,1,0:T(8,128)S(1)} %get-tuple-element.32.pool.geometry, f32[2,8,128]{2,1,0:T(8,128)S(1)} %get-tuple-element.33.own.refs_0_, f32[1,8,128]{2,1,0:T(8,128)S(1)} %get-tuple-element.34.refs_1_, ...), custom_call_target="tpu_custom_call" | custom-call | flops 100000000 | bytes 1048576 | tf_op jit(solution)/shard_map/pallas_call | solution.py:134
  43.4 1.5 %collective-permute-done.9.outer = f32[2,8,128]{2,1,0:T(8,128)S(1)} collective-permute-done((f32[2,8,128]{2,1,0:T(8,128)S(1)}, f32[2,8,128]{2,1,0:T(8,128)S(1)}, u32[]{:S(2)}, u32[]{:S(2)}) %collective-permute-start.9) | collective-permute-done | bytes 8224 | tf_op jit(solution)/shard_map/ppermute | solution.py:728
  44.9 0.0 collective-permute-done.8.inner
  44.9 0.0 collective-permute-start.10
  44.9 2.7 %collective-permute-start.11 = (f32[3,2,8,128]{3,2,1,0:T(8,128)S(1)}, f32[3,2,8,128]{3,2,1,0:T(8,128)S(1)}, u32[]{:S(2)}, u32[]{:S(2)}) collective-permute-start(f32[3,2,8,128]{3,2,1,0:T(8,128)S(1)} %shard_map.203.level), channel_id=1, source_target_pairs={{64,0},{128,64},{192,128},{0,192},{65,1},{129,65},{193,129},{1,193... | collective-permute-start | bytes 73736 | tf_op jit(solution)/shard_map/ppermute | solution.py:735
  47.5 1.2 collective-permute-done.10.before
  48.8 0.0 collective-permute-done.11.after
  48.8 0.0 copy-done.3
  48.8 3.0 %shard_map.204 = (f32[2,8,128]{2,1,0:T(8,128)S(1)}, f32[2,8,128]{2,1,0:T(8,128)S(1)}, f32[8,768]{1,0:T(8,128)S(1)}) custom-call(s32[48]{0:T(128)S(1)} %shard_map.194.meta, f32[22,8,128]{2,1,0:T(8,128)S(1)} %get-tuple-element.32.pool.geometry, f32[2,8,128]{2,1,0:T(8,128)S(1)} %shard_map.201.own.own_a, f32[2,8,128]{2,1,0:T(8,128)S(1)} %shard_map.202.own_b, ...), custom_call_target="tpu_custom_call" | custom-call | flops 100000000 | bytes 1048576 | tf_op jit(solution)/shard_map/pallas_call | solution.py:134
  51.7 5.4 %collective-permute-start.12 = (f32[8,768]{1,0:T(8,128)S(1)}, f32[8,768]{1,0:T(8,128)S(1)}, u32[]{:S(2)}, u32[]{:S(2)}) collective-permute-start(f32[8,768]{1,0:T(8,128)S(1)} %get-tuple-element.43.ordered), channel_id=1, source_target_pairs={{0,1},{1,0},{2,3},{3,2},{4,5},{5,4},{6,7},{7,6},{8,9},{9,8},{10,11... | collective-permute-start | bytes 73736 | tf_op jit(solution)/shard_map/ppermute | solution.py:728
  57.2 1.4 %shard_map.205.mine = f32[128,576]{1,0:T(8,128)S(1)} custom-call(f32[8,768]{1,0:T(8,128)S(1)} %get-tuple-element.43.ordered, f32[2,2,72,512]{3,2,1,0:T(8,128)S(1)} %get-tuple-element.44.tab_x, f32[2,2,8,512]{3,2,1,0:T(8,128)S(1)} %get-tuple-element.30.tab_y, bf16[2,128,512]{2,1,0:T(8,128)(2,1)S(1)} %get-tuple-element.45.w_high, ...), custom_call_target="tpu_custom_call" | custom-call | flops 1000000000 | bytes 1048576 | tf_op jit(solution)/shard_map/pallas_call | solution.py:134
  58.5 0.0 collective-permute-done.12.ordered.inner
  58.5 0.0 copy-done.6
  58.6 0.0 copy-done.8
  58.6 0.0 copy-done.10
  58.6 0.0 copy-done.12
  58.6 2.5 %shard_map.206 = f32[128,8,128]{2,1,0:T(8,128)} custom-call(f32[8,768]{1,0:T(8,128)S(1)} %collective-permute-done.12.ordered.inner, f32[128,576]{1,0:T(8,128)S(1)} %shard_map.205.mine, f32[2,2,72,512]{3,2,1,0:T(8,128)S(1)} %get-tuple-element.44.tab_x, f32[2,2,8,512]{3,2,1,0:T(8,128)S(1)} %get-tuple-element.30.tab_y, ...), custom_call_target="tpu_custom_call" | custom-call | flops 1000000000 | bytes 1048576 | tf_op jit(solution)/shard_map/pallas_call | solution.py:134
  61.1 7.3 %all-to-all-start = ((f32[128,8,128]{2,1,0:T(8,128)}), f32[128,8,128]{2,1,0:T(8,128)}, u32[]{:S(2)}, u32[]{:S(2)}) async-start(f32[128,8,128]{2,1,0:T(8,128)} %shard_map.206), calls=%async_computation | async-start | bytes 1048576 | tf_op jit(solution)/shard_map/all_to_all | solution.py:890
  68.4 0.6 collective-permute-start.13
  69.0 11.3 %collective-permute-done.13.outer = f32[2,8,128]{2,1,0:T(8,128)S(1)} collective-permute-done((f32[2,8,128]{2,1,0:T(8,128)S(1)}, f32[2,8,128]{2,1,0:T(8,128)S(1)}, u32[]{:S(2)}, u32[]{:S(2)}) %collective-permute-start.13) | collective-permute-done | bytes 8224 | tf_op jit(solution)/shard_map/ppermute | solution.py:728
  80.3 1.4 %collective-permute-start.14 = (f32[3,2,8,128]{3,2,1,0:T(8,128)S(1)}, f32[3,2,8,128]{3,2,1,0:T(8,128)S(1)}, u32[]{:S(2)}, u32[]{:S(2)}) collective-permute-start(f32[3,2,8,128]{3,2,1,0:T(8,128)S(1)} %shard_map.207.level), channel_id=1, source_target_pairs={{0,64},{64,128},{128,192},{192,0},{1,65},{65,129},{129,193},{193,1... | collective-permute-start | bytes 73736 | tf_op jit(solution)/shard_map/ppermute | solution.py:735
  81.7 1.7 %collective-permute-start.15 = (f32[3,2,8,128]{3,2,1,0:T(8,128)S(1)}, f32[3,2,8,128]{3,2,1,0:T(8,128)S(1)}, u32[]{:S(2)}, u32[]{:S(2)}) collective-permute-start(f32[3,2,8,128]{3,2,1,0:T(8,128)S(1)} %shard_map.207.level), channel_id=1, source_target_pairs={{64,0},{128,64},{192,128},{0,192},{65,1},{129,65},{193,129},{1,193... | collective-permute-start | bytes 73736 | tf_op jit(solution)/shard_map/ppermute | solution.py:735
  83.4 1.7 %collective-permute-done.14.before = f32[3,2,8,128]{3,2,1,0:T(8,128)S(1)} collective-permute-done((f32[3,2,8,128]{3,2,1,0:T(8,128)S(1)}, f32[3,2,8,128]{3,2,1,0:T(8,128)S(1)}, u32[]{:S(2)}, u32[]{:S(2)}) %collective-permute-start.14) | collective-permute-done | bytes 24608 | tf_op jit(solution)/shard_map/ppermute | solution.py:735
  85.0 0.0 collective-permute-done.15.after
  85.0 3.4 %shard_map.208 = (f32[8,512]{1,0:T(8,128)S(1)}, f32[8,128]{1,0:T(8,128)S(1)}) custom-call(s32[48]{0:T(128)S(1)} %shard_map.194.meta, f32[22,8,128]{2,1,0:T(8,128)S(1)} %get-tuple-element.32.pool.geometry, f32[2,8,128]{2,1,0:T(8,128)S(1)} %get-tuple-element.48.own.sent, f32[2,8,128]{2,1,0:T(8,128)S(1)} %get-tuple-element.42.rest, ...), custom_call_target="tpu_custom_call" | custom-call | flops 1000000000 | bytes 1048576 | tf_op jit(solution)/shard_map/pallas_call | solution.py:134
  88.4 0.0 all-to-all-done.refs_0_
  88.5 3.9 %shard_map.209 = f32[128,8,128]{2,1,0:T(8,128)S(1)} custom-call(f32[8,256]{1,0:T(8,128)S(1)} %copy-done.5, f32[8,128]{1,0:T(8,128)S(1)} %get-tuple-element.49.sums, f32[128,8,128]{2,1,0:T(8,128)} %all-to-all-done.refs_0_, bf16[256,256]{1,0:T(8,128)(2,1)} %constant.21.clone.refs_1_, bf16[256,256]{1,0:T(8,128)(2,1)} %constant.22.clone.refs_2_, ...), custom_call_target="tpu_custom_call" | custom-call | flops 1000000000 | bytes 1048576 | tf_op jit(solution)/shard_map/pallas_call | solution.py:134
  92.4 31.7 %all_to_all.10.grid = f32[128,8,128]{2,1,0:T(8,128)S(1)} all-to-all(f32[128,8,128]{2,1,0:T(8,128)S(1)} %shard_map.209), channel_id=1, replica_groups=mesh['slab'=4,'pair'=32,'core'=2] {'slab','pair'}, dimensions={0} | all-to-all | bytes 1048576 | tf_op jit(solution)/shard_map/all_to_all | solution.py:919
  124.1 0.0 copy-done.11
  124.1 1.1 shard_map.211
  125.2 2.6 %collective-permute-start.16 = (f32[8,512]{1,0:T(8,128)S(1)}, f32[8,512]{1,0:T(8,128)S(1)}, u32[]{:S(2)}, u32[]{:S(2)}) collective-permute-start(f32[8,512]{1,0:T(8,128)S(1)} %shard_map.211), channel_id=1, source_target_pairs={{0,1},{1,0},{2,3},{3,2},{4,5},{5,4},{6,7},{7,6},{8,9},{9,8},{10,11... | collective-permute-start | bytes 49160 | tf_op jit(solution)/shard_map/ppermute | solution.py:728
  127.8 1.1 shard_map.210.mine
  128.9 0.0 collective-permute-done.16.theirs
  128.9 0.0 copy-done.4
  128.9 0.9 shard_map.212
  (21 shorter events, 0.0 us)
Async XLA Ops:
  1.7 5.2 %collective-permute-start = (f32[8,768]{1,0:T(8,128)S(1)}, f32[8,768]{1,0:T(8,128)S(1)}, u32[]{:S(2)}, u32[]{:S(2)}) collective-permute-start(f32[8,768]{1,0:T(8,128)S(1)} %get-tuple-element.29.mine), channel_id=1, source_target_pairs={{0,1},{1,0},{2,3},{3,2},{4,5},{5,4},{6,7},{7,6},{8,9},{9,8},{10,11... | collective-permute-start | bytes 73736 | tf_op jit(solution)/shard_map/ppermute | solution.py:728
  5.0 4.7 %collective-permute-start.1 = (f32[2,8,128]{2,1,0:T(8,128)S(1)}, f32[2,8,128]{2,1,0:T(8,128)S(1)}, u32[]{:S(2)}, u32[]{:S(2)}) collective-permute-start(f32[2,8,128]{2,1,0:T(8,128)S(1)} %get-tuple-element.27.after.own), channel_id=1, source_target_pairs={{0,63},{1,2},{2,1},{3,4},{4,3},{5,6},{6,5},{7,8},{8,7},{9,10},{10,... | collective-permute-start | bytes 24584 | tf_op jit(solution)/shard_map/ppermute | solution.py:728
  9.7 48.8 %copy-start.6 = (f32[2,2,72,512]{3,2,1,0:T(8,128)}, f32[2,2,72,512]{3,2,1,0:T(8,128)S(1)}, u32[]{:S(2)}) copy-start(f32[2,2,72,512]{3,2,1,0:T(8,128)S(1)} %get-tuple-element.44.tab_x) | copy-start | bytes 1769476
  9.7 48.8 %copy-start.8 = (f32[2,128,512]{2,1,0:T(8,128)}, f32[2,128,512]{2,1,0:T(8,128)S(1)}, u32[]{:S(2)}) copy-start(f32[2,128,512]{2,1,0:T(8,128)S(1)} %get-tuple-element.47.slope_z) | copy-start | bytes 1572868
  9.7 48.8 %copy-start.10 = (bf16[2,128,512]{2,1,0:T(8,128)(2,1)}, bf16[2,128,512]{2,1,0:T(8,128)(2,1)S(1)}, u32[]{:S(2)}) copy-start(bf16[2,128,512]{2,1,0:T(8,128)(2,1)S(1)} %get-tuple-element.45.w_high) | copy-start | bytes 786436
  9.7 48.8 %copy-start.12 = (bf16[2,128,512]{2,1,0:T(8,128)(2,1)}, bf16[2,128,512]{2,1,0:T(8,128)(2,1)S(1)}, u32[]{:S(2)}) copy-start(bf16[2,128,512]{2,1,0:T(8,128)(2,1)S(1)} %get-tuple-element.46.w_low) | copy-start | bytes 786436
  9.8 4.0 %collective-permute-start.2 = (f32[3,2,8,128]{3,2,1,0:T(8,128)S(1)}, f32[3,2,8,128]{3,2,1,0:T(8,128)S(1)}, u32[]{:S(2)}, u32[]{:S(2)}) collective-permute-start(f32[3,2,8,128]{3,2,1,0:T(8,128)S(1)} %shard_map.196.level), channel_id=1, source_target_pairs={{0,64},{64,128},{128,192},{192,0},{1,65},{65,129},{129,193},{193,1... | collective-permute-start | bytes 73736 | tf_op jit(solution)/shard_map/ppermute | solution.py:735
  10.9 2.8 %collective-permute-start.3 = (f32[3,2,8,128]{3,2,1,0:T(8,128)S(1)}, f32[3,2,8,128]{3,2,1,0:T(8,128)S(1)}, u32[]{:S(2)}, u32[]{:S(2)}) collective-permute-start(f32[3,2,8,128]{3,2,1,0:T(8,128)S(1)} %shard_map.196.level), channel_id=1, source_target_pairs={{64,0},{128,64},{192,128},{0,192},{65,1},{129,65},{193,129},{1,193... | collective-permute-start | bytes 73736 | tf_op jit(solution)/shard_map/ppermute | solution.py:735
  17.0 13.1 %collective-permute-start.4 = (f32[2,8,128]{2,1,0:T(8,128)S(1)}, f32[2,8,128]{2,1,0:T(8,128)S(1)}, u32[]{:S(2)}, u32[]{:S(2)}) collective-permute-start(f32[2,8,128]{2,1,0:T(8,128)S(1)} %get-tuple-element.33.own.refs_0_), channel_id=1, source_target_pairs={{0,1},{1,0},{2,3},{3,2},{4,5},{5,4},{6,7},{7,6},{8,9},{9,8},{10,11... | collective-permute-start | bytes 24584 | tf_op jit(solution)/shard_map/ppermute | solution.py:728
  27.0 3.1 %collective-permute-start.5 = (f32[2,8,128]{2,1,0:T(8,128)S(1)}, f32[2,8,128]{2,1,0:T(8,128)S(1)}, u32[]{:S(2)}, u32[]{:S(2)}) collective-permute-start(f32[2,8,128]{2,1,0:T(8,128)S(1)} %get-tuple-element.33.own.refs_0_), channel_id=1, source_target_pairs={{0,63},{1,2},{2,1},{3,4},{4,3},{5,6},{6,5},{7,8},{8,7},{9,10},{10,... | collective-permute-start | bytes 24584 | tf_op jit(solution)/shard_map/ppermute | solution.py:728
  28.9 19.9 %copy-start = (f32[3,8,128,128]{3,2,1,0:T(8,128)}, f32[3,8,128,128]{3,2,1,0:T(8,128)S(1)}, u32[]{:S(2)}) copy-start(f32[3,8,128,128]{3,2,1,0:T(8,128)S(1)} %get-tuple-element.38.refs_6_.pairs_b.stored_b) | copy-start | bytes 4718596
  30.1 4.6 %collective-permute-start.6 = (f32[3,2,8,128]{3,2,1,0:T(8,128)S(1)}, f32[3,2,8,128]{3,2,1,0:T(8,128)S(1)}, u32[]{:S(2)}, u32[]{:S(2)}) collective-permute-start(f32[3,2,8,128]{3,2,1,0:T(8,128)S(1)} %shard_map.200.refs_3_), channel_id=1, source_target_pairs={{0,64},{64,128},{128,192},{192,0},{1,65},{65,129},{129,193},{193,1... | collective-permute-start | bytes 73736 | tf_op jit(solution)/shard_map/ppermute | solution.py:735
  30.1 4.6 %collective-permute-start.7 = (f32[3,2,8,128]{3,2,1,0:T(8,128)S(1)}, f32[3,2,8,128]{3,2,1,0:T(8,128)S(1)}, u32[]{:S(2)}, u32[]{:S(2)}) collective-permute-start(f32[3,2,8,128]{3,2,1,0:T(8,128)S(1)} %shard_map.200.refs_3_), channel_id=1, source_target_pairs={{64,0},{128,64},{192,128},{0,192},{65,1},{129,65},{193,129},{1,193... | collective-permute-start | bytes 73736 | tf_op jit(solution)/shard_map/ppermute | solution.py:735
  34.6 14.1 %copy-start.1 = (f32[3,8,128,128]{3,2,1,0:T(8,128)}, f32[3,8,128,128]{3,2,1,0:T(8,128)S(1)}, u32[]{:S(2)}) copy-start(f32[3,8,128,128]{3,2,1,0:T(8,128)S(1)} %get-tuple-element.39.refs_7_.pairs_c.stored_c) | copy-start | bytes 4718596
  36.4 8.5 %collective-permute-start.8 = (f32[2,8,128]{2,1,0:T(8,128)S(1)}, f32[2,8,128]{2,1,0:T(8,128)S(1)}, u32[]{:S(2)}, u32[]{:S(2)}) collective-permute-start(f32[2,8,128]{2,1,0:T(8,128)S(1)} %shard_map.201.own.own_a), channel_id=1, source_target_pairs={{0,1},{1,0},{2,3},{3,2},{4,5},{5,4},{6,7},{7,6},{8,9},{9,8},{10,11... | collective-permute-start | bytes 24584 | tf_op jit(solution)/shard_map/ppermute | solution.py:728
  41.8 3.1 %collective-permute-start.9 = (f32[2,8,128]{2,1,0:T(8,128)S(1)}, f32[2,8,128]{2,1,0:T(8,128)S(1)}, u32[]{:S(2)}, u32[]{:S(2)}) collective-permute-start(f32[2,8,128]{2,1,0:T(8,128)S(1)} %shard_map.201.own.own_a), channel_id=1, source_target_pairs={{0,63},{1,2},{2,1},{3,4},{4,3},{5,6},{6,5},{7,8},{8,7},{9,10},{10,... | collective-permute-start | bytes 24584 | tf_op jit(solution)/shard_map/ppermute | solution.py:728
  41.8 7.0 %copy-start.3 = (s32[1,512]{1,0:T(1,128)S(1)}, s32[1,512]{1,0:T(1,128)}, u32[]{:S(2)}) copy-start(s32[1,512]{1,0:T(1,128)} %order.3) | copy-start | bytes 6148
  44.9 3.9 %collective-permute-start.10 = (f32[3,2,8,128]{3,2,1,0:T(8,128)S(1)}, f32[3,2,8,128]{3,2,1,0:T(8,128)S(1)}, u32[]{:S(2)}, u32[]{:S(2)}) collective-permute-start(f32[3,2,8,128]{3,2,1,0:T(8,128)S(1)} %shard_map.203.level), channel_id=1, source_target_pairs={{0,64},{64,128},{128,192},{192,0},{1,65},{65,129},{129,193},{193,1... | collective-permute-start | bytes 73736 | tf_op jit(solution)/shard_map/ppermute | solution.py:735
  44.9 3.9 %collective-permute-start.11 = (f32[3,2,8,128]{3,2,1,0:T(8,128)S(1)}, f32[3,2,8,128]{3,2,1,0:T(8,128)S(1)}, u32[]{:S(2)}, u32[]{:S(2)}) collective-permute-start(f32[3,2,8,128]{3,2,1,0:T(8,128)S(1)} %shard_map.203.level), channel_id=1, source_target_pairs={{64,0},{128,64},{192,128},{0,192},{65,1},{129,65},{193,129},{1,193... | collective-permute-start | bytes 73736 | tf_op jit(solution)/shard_map/ppermute | solution.py:735
  51.7 6.8 %collective-permute-start.12 = (f32[8,768]{1,0:T(8,128)S(1)}, f32[8,768]{1,0:T(8,128)S(1)}, u32[]{:S(2)}, u32[]{:S(2)}) collective-permute-start(f32[8,768]{1,0:T(8,128)S(1)} %get-tuple-element.43.ordered), channel_id=1, source_target_pairs={{0,1},{1,0},{2,3},{3,2},{4,5},{5,4},{6,7},{7,6},{8,9},{9,8},{10,11... | collective-permute-start | bytes 73736 | tf_op jit(solution)/shard_map/ppermute | solution.py:728
  61.1 27.4 %all-to-all-start = ((f32[128,8,128]{2,1,0:T(8,128)}), f32[128,8,128]{2,1,0:T(8,128)}, u32[]{:S(2)}, u32[]{:S(2)}) async-start(f32[128,8,128]{2,1,0:T(8,128)} %shard_map.206), calls=%async_computation | async-start | bytes 1048576 | tf_op jit(solution)/shard_map/all_to_all | solution.py:890
  68.4 11.9 %collective-permute-start.13 = (f32[2,8,128]{2,1,0:T(8,128)S(1)}, f32[2,8,128]{2,1,0:T(8,128)S(1)}, u32[]{:S(2)}, u32[]{:S(2)}) collective-permute-start(f32[2,8,128]{2,1,0:T(8,128)S(1)} %get-tuple-element.48.own.sent), channel_id=1, source_target_pairs={{0,63},{1,2},{2,1},{3,4},{4,3},{5,6},{6,5},{7,8},{8,7},{9,10},{10,... | collective-permute-start | bytes 24584 | tf_op jit(solution)/shard_map/ppermute | solution.py:728
  80.3 4.7 %collective-permute-start.14 = (f32[3,2,8,128]{3,2,1,0:T(8,128)S(1)}, f32[3,2,8,128]{3,2,1,0:T(8,128)S(1)}, u32[]{:S(2)}, u32[]{:S(2)}) collective-permute-start(f32[3,2,8,128]{3,2,1,0:T(8,128)S(1)} %shard_map.207.level), channel_id=1, source_target_pairs={{0,64},{64,128},{128,192},{192,0},{1,65},{65,129},{129,193},{193,1... | collective-permute-start | bytes 73736 | tf_op jit(solution)/shard_map/ppermute | solution.py:735
  81.7 3.3 %collective-permute-start.15 = (f32[3,2,8,128]{3,2,1,0:T(8,128)S(1)}, f32[3,2,8,128]{3,2,1,0:T(8,128)S(1)}, u32[]{:S(2)}, u32[]{:S(2)}) collective-permute-start(f32[3,2,8,128]{3,2,1,0:T(8,128)S(1)} %shard_map.207.level), channel_id=1, source_target_pairs={{64,0},{128,64},{192,128},{0,192},{65,1},{129,65},{193,129},{1,193... | collective-permute-start | bytes 73736 | tf_op jit(solution)/shard_map/ppermute | solution.py:735
  85.0 3.4 %copy-start.5 = (f32[8,256]{1,0:T(8,128)S(1)}, f32[8,256]{1,0:T(8,128)}, u32[]{:S(2)}) copy-start(f32[8,256]{1,0:T(8,128)} %constant.20.clone.waves) | copy-start | bytes 24580
  88.4 35.6 %copy-start.7 = (f32[2,2,72,512]{3,2,1,0:T(8,128)S(1)}, f32[2,2,72,512]{3,2,1,0:T(8,128)}, u32[]{:S(2)}) copy-start(f32[2,2,72,512]{3,2,1,0:T(8,128)} %copy-done.6) | copy-start | bytes 1769476
  88.4 35.6 %copy-start.9 = (f32[2,128,512]{2,1,0:T(8,128)S(1)}, f32[2,128,512]{2,1,0:T(8,128)}, u32[]{:S(2)}) copy-start(f32[2,128,512]{2,1,0:T(8,128)} %copy-done.8) | copy-start | bytes 1572868
  88.4 35.6 %copy-start.11 = (bf16[2,128,512]{2,1,0:T(8,128)(2,1)S(1)}, bf16[2,128,512]{2,1,0:T(8,128)(2,1)}, u32[]{:S(2)}) copy-start(bf16[2,128,512]{2,1,0:T(8,128)(2,1)} %copy-done.10) | copy-start | bytes 786436
  88.5 35.6 %copy-start.13 = (bf16[2,128,512]{2,1,0:T(8,128)(2,1)S(1)}, bf16[2,128,512]{2,1,0:T(8,128)(2,1)}, u32[]{:S(2)}) copy-start(bf16[2,128,512]{2,1,0:T(8,128)(2,1)} %copy-done.12) | copy-start | bytes 786436
  125.2 3.7 %copy-start.2 = (f32[3,512]{1,0:T(4,128)S(1)}, f32[3,512]{1,0:T(4,128)}, u32[]{:S(2)}) copy-start(f32[3,512]{1,0:T(4,128)} %residual.1) | copy-start | bytes 18436
  125.2 3.7 %copy-start.4 = (f32[3,512]{1,0:T(4,128)S(1)}, f32[3,512]{1,0:T(4,128)}, u32[]{:S(2)}) copy-start(f32[3,512]{1,0:T(4,128)} %dipoles.1) | copy-start | bytes 18436
  125.2 3.7 %collective-permute-start.16 = (f32[8,512]{1,0:T(8,128)S(1)}, f32[8,512]{1,0:T(8,128)S(1)}, u32[]{:S(2)}, u32[]{:S(2)}) collective-permute-start(f32[8,512]{1,0:T(8,128)S(1)} %shard_map.211), channel_id=1, source_target_pairs={{0,1},{1,0},{2,3},{3,2},{4,5},{5,4},{6,7},{7,6},{8,9},{9,8},{10,11... | collective-permute-start | bytes 49160 | tf_op jit(solution)/shard_map/ppermute | solution.py:728

commit v12 on v11

--- a/solution.py
+++ b/solution.py
@@ -874,7 +874,7 @@
         smem=1,
         scratch=sweep_scratch + (local_scratch,),
     )(meta, geometry, next_a, next_b, *third, pairs_a, pairs_b, pairs_c, tile_order)
-    ordered_beside = beside(ordered, False)
+    ordered_beside, outer = (beside(ordered, False), beside(sent, True))
     message = ((half, 8, TILE), F32)
     flat_scratch = pltpu.VMEM((half, 8 * TILE), F32)
     spread_own = call(spread_own_kernel, [((half, x_rows * y_rows), F32)], 10**9, vmem=LARGE_VMEM)(ordered, *tables)[0]
@@ -886,9 +886,9 @@
         vmem=LARGE_VMEM,
         hbm_outs=True,
     )(ordered_beside, spread_own, *tables)[0]
-    late, _ = lax.optimization_barrier((sent, spread))
+    spread, outer = lax.optimization_barrier((spread, outer))
     grid = lax.all_to_all(spread, CHIPS, 0, 0, tiled=True)
-    last = along_slab(joined(sent, ordered_beside, beside(late, True)))
+    last = along_slab(joined(sent, ordered_beside, outer))
     applied, sums = call(
         final_field_kernel,
         [((8, atoms), F32), ((8, TILE), F32)],

time: 130 us -> 127 us (0.977)
  blocking collectives: 31.7 us -> 26.1 us
  starting transfers between devices: 45.8 us -> 47.8 us
    all_to_all x1, waiting for transfers between devices: 0.01 us -> 11.6 us  [local(): grid = lax.all_to_all(spread, CHIPS, 0, 0, tiled=True)]
    ppermute x9, waiting for transfers between devices: 13.9 us -> 2.64 us  [beside(): return lax.ppermute(block, BOTH, swap_pairs(n_slab, n_space, odd))]
    all_to_all x1, blocking collectives: 31.7 us -> 26.1 us  [local(): returned = lax.all_to_all(planes, CHIPS, 0, 0, tiled=True)]
    all_to_all x1, starting transfers between devices: 7.31 us -> 11.5 us  [local(): grid = lax.all_to_all(spread, CHIPS, 0, 0, tiled=True)]
    ppermute x9, starting transfers between devices: 27.4 us -> 25.4 us  [beside(): return lax.ppermute(block, BOTH, swap_pairs(n_slab, n_space, odd))]
  transfers between devices with their start and end apart: 18 -> 18, of which waited for: 6 -> 6; matrix products, arithmetic and copies ran while one was open for 0% -> 0% of each run, Pallas kernels for 12% -> 14%
where the time goes in v12:
time: 127 us; the launch traced here: 126 us
  starting transfers between devices  47.8 us (38%)
  Pallas kernels  33.2 us (26%)
  blocking collectives  26.1 us (21%)
  waiting for transfers between devices  18.3 us (14%)
    pallas_call x18, Pallas kernels, run(): pl.pallas_call(kernel, out_shape=[(pltpu.HBM if hbm_outs else jax.ShapeDt...  30.2 us
    all_to_all x1, blocking collectives, local(): returned = lax.all_to_all(planes, CHIPS, 0, 0, tiled=True)  26.1 us
    ppermute x9, starting transfers between devices, beside(): return lax.ppermute(block, BOTH, swap_pairs(n_slab, n_space, odd))  25.4 us
    all_to_all x1, waiting for transfers between devices, local(): grid = lax.all_to_all(spread, CHIPS, 0, 0, tiled=True)  11.6 us
    all_to_all x1, starting transfers between devices, local(): grid = lax.all_to_all(spread, CHIPS, 0, 0, tiled=True)  11.5 us
    ppermute x4, starting transfers between devices, along_slab(): lax.ppermute(level, 'slab', down)  9.1 us
    ppermute x4, waiting for transfers between devices, along_slab(): lax.ppermute(level, 'slab', up)  4.08 us
    ppermute x9, waiting for transfers between devices, beside(): return lax.ppermute(block, BOTH, swap_pairs(n_slab, n_space, odd))  2.64 us
  transfers between devices with their start and end apart: 18, of which 6 were waited for; matrix products, arithmetic and copies ran while one was open for 0% of the time, Pallas kernels for 14%

profile of v12, /device:TPU:1, one launch (start us, length us, event | category | flops | bytes accessed | tf_op | source)
XLA Modules:
  0.0 126.4 jit_solution(16776328745076332283)
XLA Ops:
  0.6 1.1 shard_map.193
  1.7 3.3 %collective-permute-start = (f32[8,768]{1,0:T(8,128)S(1)}, f32[8,768]{1,0:T(8,128)S(1)}, u32[]{:S(2)}, u32[]{:S(2)}) collective-permute-start(f32[8,768]{1,0:T(8,128)S(1)} %get-tuple-element.30.mine), channel_id=1, source_target_pairs={{0,1},{1,0},{2,3},{3,2},{4,5},{5,4},{6,7},{7,6},{8,9},{9,8},{10,11... | collective-permute-start | bytes 73736 | tf_op jit(solution)/shard_map/ppermute | solution.py:728
  5.0 0.0 collective-permute-start.1
  5.0 1.9 %shard_map.194.meta = s32[48]{0:T(128)S(1)} custom-call(s32[1,4,8]{2,1,0:T(4,128)} %stored_lists.1, s32[1,4]{1,0:T(1,128)} %stored_counts.1, s32[1,2]{1,0:T(1,128)} %stored_send.1, f32[2,8,128]{2,1,0:T(8,128)S(1)} %get-tuple-element.28.after.own), custom_call_target="tpu_custom_call" | custom-call | flops 100000000 | bytes 1048576 | tf_op jit(solution)/shard_map/pallas_call | solution.py:791
  6.9 0.0 collective-permute-done.beside.inner
  6.9 2.7 %shard_map.195 = (f32[2,2,72,512]{3,2,1,0:T(8,128)S(1)}, f32[2,2,8,512]{3,2,1,0:T(8,128)S(1)}, bf16[2,128,512]{2,1,0:T(8,128)(2,1)S(1)}, bf16[2,128,512]{2,1,0:T(8,128)(2,1)S(1)}, f32[2,128,512]{2,1,0:T(8,128)S(1)}) custom-call(f32[8,768]{1,0:T(8,128)S(1)} %get-tuple-element.30.mine, f32[8,768]{1,0:T(8,128)S(1)} %collective-permute-done.beside.inner, ...), custom_call_target="tpu_custom_call" | custom-call | flops 100000000 | bytes 1048576 | tf_op jit(solution)/shard_map/pallas_call | solution.py:134
  9.7 0.0 copy-start.6
  9.7 0.0 copy-start.8
  9.7 0.0 copy-start.10
  9.7 0.0 copy-start.12
  9.7 0.0 collective-permute-done.1.outer
  9.8 1.2 collective-permute-start.2
  10.9 1.6 %collective-permute-start.3 = (f32[3,2,8,128]{3,2,1,0:T(8,128)S(1)}, f32[3,2,8,128]{3,2,1,0:T(8,128)S(1)}, u32[]{:S(2)}, u32[]{:S(2)}) collective-permute-start(f32[3,2,8,128]{3,2,1,0:T(8,128)S(1)} %shard_map.196.level), channel_id=1, source_target_pairs={{64,0},{128,64},{192,128},{0,192},{65,1},{129,65},{193,129},{1,193... | collective-permute-start | bytes 73736 | tf_op jit(solution)/shard_map/ppermute | solution.py:735
  12.5 1.2 collective-permute-done.2.before
  13.7 0.0 collective-permute-done.3.after
  13.7 3.3 %shard_map.197 = (f32[22,8,128]{2,1,0:T(8,128)S(1)}, f32[3,16,128,128]{3,2,1,0:T(8,128)S(1)}, f32[2,8,128]{2,1,0:T(8,128)S(1)}) custom-call(s32[48]{0:T(128)S(1)} %shard_map.194.meta, f32[4,8,128]{2,1,0:T(8,128)S(1)} %get-tuple-element.29.own, f32[3,2,8,128]{3,2,1,0:T(8,128)S(1)} %shard_map.196.level, f32[3,2,8,128]{3,2,1,0:T(8,128)S(1)} %collective-permute-done.2.before, ...), custom_call_target="tpu_custom_call" | custom-call | flops 1000000000 | bytes 1048576 | tf_op jit(solution)/shard_map/pallas_call | solution.py:134
  17.0 10.0 %collective-permute-start.4 = (f32[2,8,128]{2,1,0:T(8,128)S(1)}, f32[2,8,128]{2,1,0:T(8,128)S(1)}, u32[]{:S(2)}, u32[]{:S(2)}) collective-permute-start(f32[2,8,128]{2,1,0:T(8,128)S(1)} %get-tuple-element.34.own.refs_0_), channel_id=1, source_target_pairs={{0,1},{1,0},{2,3},{3,2},{4,5},{5,4},{6,7},{7,6},{8,9},{9,8},{10,11... | collective-permute-start | bytes 24584 | tf_op jit(solution)/shard_map/ppermute | solution.py:728
  27.0 0.0 collective-permute-start.5
  27.0 1.9 %shard_map.198 = (f32[3,8,128,128]{3,2,1,0:T(8,128)S(1)}, f32[1,8,128]{2,1,0:T(8,128)S(1)}) custom-call(s32[48]{0:T(128)S(1)} %shard_map.194.meta, f32[22,8,128]{2,1,0:T(8,128)S(1)} %get-tuple-element.33.pool.geometry), custom_call_target="tpu_custom_call" | custom-call | flops 1000000000 | bytes 1048576 | tf_op jit(solution)/shard_map/pallas_call | solution.py:134
  28.9 1.2 collective-permute-done.5.outer
  30.0 0.0 collective-permute-done.4.inner
  30.0 0.0 collective-permute-start.6
  30.1 2.8 %collective-permute-start.7 = (f32[3,2,8,128]{3,2,1,0:T(8,128)S(1)}, f32[3,2,8,128]{3,2,1,0:T(8,128)S(1)}, u32[]{:S(2)}, u32[]{:S(2)}) collective-permute-start(f32[3,2,8,128]{3,2,1,0:T(8,128)S(1)} %shard_map.200.refs_3_), channel_id=1, source_target_pairs={{64,0},{128,64},{192,128},{0,192},{65,1},{129,65},{193,129},{1,193... | collective-permute-start | bytes 73736 | tf_op jit(solution)/shard_map/ppermute | solution.py:735
  32.8 1.9 %shard_map.199 = (f32[3,8,128,128]{3,2,1,0:T(8,128)S(1)}, f32[1,8,128]{2,1,0:T(8,128)S(1)}) custom-call(s32[48]{0:T(128)S(1)} %shard_map.194.meta, f32[22,8,128]{2,1,0:T(8,128)S(1)} %get-tuple-element.33.pool.geometry), custom_call_target="tpu_custom_call" | custom-call | flops 1000000000 | bytes 1048576 | tf_op jit(solution)/shard_map/pallas_call | solution.py:134
  34.7 0.0 collective-permute-done.6.refs_4_
  34.7 0.0 collective-permute-done.7.refs_5_
  34.7 1.7 %shard_map.201.own.own_a = f32[2,8,128]{2,1,0:T(8,128)S(1)} custom-call(s32[48]{0:T(128)S(1)} %shard_map.194.meta, f32[22,8,128]{2,1,0:T(8,128)S(1)} %get-tuple-element.33.pool.geometry, f32[2,8,128]{2,1,0:T(8,128)S(1)} %get-tuple-element.34.own.refs_0_, f32[1,8,128]{2,1,0:T(8,128)S(1)} %get-tuple-element.35.refs_1_, ...), custom_call_target="tpu_custom_call" | custom-call | flops 100000000 | bytes 1048576 | tf_op jit(solution)/shard_map/pallas_call | solution.py:134
  36.5 5.3 %collective-permute-start.8 = (f32[2,8,128]{2,1,0:T(8,128)S(1)}, f32[2,8,128]{2,1,0:T(8,128)S(1)}, u32[]{:S(2)}, u32[]{:S(2)}) collective-permute-start(f32[2,8,128]{2,1,0:T(8,128)S(1)} %shard_map.201.own.own_a), channel_id=1, source_target_pairs={{0,1},{1,0},{2,3},{3,2},{4,5},{5,4},{6,7},{7,6},{8,9},{9,8},{10,11... | collective-permute-start | bytes 24584 | tf_op jit(solution)/shard_map/ppermute | solution.py:728
  41.8 0.0 collective-permute-start.9
  41.8 1.6 %shard_map.202.own_b = f32[2,8,128]{2,1,0:T(8,128)S(1)} custom-call(s32[48]{0:T(128)S(1)} %shard_map.194.meta, f32[22,8,128]{2,1,0:T(8,128)S(1)} %get-tuple-element.33.pool.geometry, f32[2,8,128]{2,1,0:T(8,128)S(1)} %get-tuple-element.34.own.refs_0_, f32[1,8,128]{2,1,0:T(8,128)S(1)} %get-tuple-element.35.refs_1_, ...), custom_call_target="tpu_custom_call" | custom-call | flops 100000000 | bytes 1048576 | tf_op jit(solution)/shard_map/pallas_call | solution.py:134
  43.4 1.4 %collective-permute-done.9.outer = f32[2,8,128]{2,1,0:T(8,128)S(1)} collective-permute-done((f32[2,8,128]{2,1,0:T(8,128)S(1)}, f32[2,8,128]{2,1,0:T(8,128)S(1)}, u32[]{:S(2)}, u32[]{:S(2)}) %collective-permute-start.9) | collective-permute-done | bytes 8224 | tf_op jit(solution)/shard_map/ppermute | solution.py:728
  44.8 0.0 collective-permute-done.8.inner
  44.8 0.0 collective-permute-start.10
  44.8 2.7 %collective-permute-start.11 = (f32[3,2,8,128]{3,2,1,0:T(8,128)S(1)}, f32[3,2,8,128]{3,2,1,0:T(8,128)S(1)}, u32[]{:S(2)}, u32[]{:S(2)}) collective-permute-start(f32[3,2,8,128]{3,2,1,0:T(8,128)S(1)} %shard_map.203.level), channel_id=1, source_target_pairs={{64,0},{128,64},{192,128},{0,192},{65,1},{129,65},{193,129},{1,193... | collective-permute-start | bytes 73736 | tf_op jit(solution)/shard_map/ppermute | solution.py:735
  47.5 1.2 collective-permute-done.10.before
  48.7 0.0 collective-permute-done.11.after
  48.7 0.0 copy-done
  48.7 0.0 copy-done.1
  48.7 0.0 copy-done.3
  48.7 3.0 %shard_map.204 = (f32[2,8,128]{2,1,0:T(8,128)S(1)}, f32[2,8,128]{2,1,0:T(8,128)S(1)}, f32[8,768]{1,0:T(8,128)S(1)}) custom-call(s32[48]{0:T(128)S(1)} %shard_map.194.meta, f32[22,8,128]{2,1,0:T(8,128)S(1)} %get-tuple-element.33.pool.geometry, f32[2,8,128]{2,1,0:T(8,128)S(1)} %shard_map.201.own.own_a, f32[2,8,128]{2,1,0:T(8,128)S(1)} %shard_map.202.own_b, ...), custom_call_target="tpu_custom_call" | custom-call | flops 100000000 | bytes 1048576 | tf_op jit(solution)/shard_map/pallas_call | solution.py:134
  51.7 5.4 %collective-permute-start.12 = (f32[8,768]{1,0:T(8,128)S(1)}, f32[8,768]{1,0:T(8,128)S(1)}, u32[]{:S(2)}, u32[]{:S(2)}) collective-permute-start(f32[8,768]{1,0:T(8,128)S(1)} %get-tuple-element.44.ordered), channel_id=1, source_target_pairs={{0,1},{1,0},{2,3},{3,2},{4,5},{5,4},{6,7},{7,6},{8,9},{9,8},{10,11... | collective-permute-start | bytes 73736 | tf_op jit(solution)/shard_map/ppermute | solution.py:728
  57.1 0.0 collective-permute-start.13
  57.1 1.4 %shard_map.205.mine = f32[128,576]{1,0:T(8,128)S(1)} custom-call(f32[8,768]{1,0:T(8,128)S(1)} %get-tuple-element.44.ordered, f32[2,2,72,512]{3,2,1,0:T(8,128)S(1)} %get-tuple-element.45.tab_x, f32[2,2,8,512]{3,2,1,0:T(8,128)S(1)} %get-tuple-element.31.tab_y, bf16[2,128,512]{2,1,0:T(8,128)(2,1)S(1)} %get-tuple-element.46.w_high, ...), custom_call_target="tpu_custom_call" | custom-call | flops 1000000000 | bytes 1048576 | tf_op jit(solution)/shard_map/pallas_call | solution.py:134
  58.5 0.0 collective-permute-done.12.ordered.inner
  58.5 0.0 copy-done.6
  58.5 2.4 %shard_map.206 = f32[128,8,128]{2,1,0:T(8,128)} custom-call(f32[8,768]{1,0:T(8,128)S(1)} %collective-permute-done.12.ordered.inner, f32[128,576]{1,0:T(8,128)S(1)} %shard_map.205.mine, f32[2,2,72,512]{3,2,1,0:T(8,128)S(1)} %get-tuple-element.45.tab_x, f32[2,2,8,512]{3,2,1,0:T(8,128)S(1)} %get-tuple-element.31.tab_y, ...), custom_call_target="tpu_custom_call" | custom-call | flops 1000000000 | bytes 1048576 | tf_op jit(solution)/shard_map/pallas_call | solution.py:134
  61.0 0.0 collective-permute-done.13.outer
  61.0 11.5 %all-to-all-start = ((f32[128,8,128]{2,1,0:T(8,128)}), f32[128,8,128]{2,1,0:T(8,128)}, u32[]{:S(2)}, u32[]{:S(2)}) async-start(f32[128,8,128]{2,1,0:T(8,128)} %shard_map.206), calls=%async_computation | async-start | bytes 1048576 | tf_op jit(solution)/shard_map/all_to_all | solution.py:890
  72.5 0.7 collective-permute-start.14
  73.2 2.1 %collective-permute-start.15 = (f32[3,2,8,128]{3,2,1,0:T(8,128)S(1)}, f32[3,2,8,128]{3,2,1,0:T(8,128)S(1)}, u32[]{:S(2)}, u32[]{:S(2)}) collective-permute-start(f32[3,2,8,128]{3,2,1,0:T(8,128)S(1)} %shard_map.207.level), channel_id=1, source_target_pairs={{64,0},{128,64},{192,128},{0,192},{65,1},{129,65},{193,129},{1,193... | collective-permute-start | bytes 73736 | tf_op jit(solution)/shard_map/ppermute | solution.py:735
  75.3 1.7 %collective-permute-done.14.before = f32[3,2,8,128]{3,2,1,0:T(8,128)S(1)} collective-permute-done((f32[3,2,8,128]{3,2,1,0:T(8,128)S(1)}, f32[3,2,8,128]{3,2,1,0:T(8,128)S(1)}, u32[]{:S(2)}, u32[]{:S(2)}) %collective-permute-start.14) | collective-permute-done | bytes 24608 | tf_op jit(solution)/shard_map/ppermute | solution.py:735
  76.9 0.0 collective-permute-done.15.after
  76.9 3.4 %shard_map.208 = (f32[8,512]{1,0:T(8,128)S(1)}, f32[8,128]{1,0:T(8,128)S(1)}) custom-call(s32[48]{0:T(128)S(1)} %shard_map.194.meta, f32[22,8,128]{2,1,0:T(8,128)S(1)} %get-tuple-element.33.pool.geometry, f32[2,8,128]{2,1,0:T(8,128)S(1)} %get-tuple-element.42.own.sent, f32[2,8,128]{2,1,0:T(8,128)S(1)} %get-tuple-element.43.rest, ...), custom_call_target="tpu_custom_call" | custom-call | flops 1000000000 | bytes 1048576 | tf_op jit(solution)/shard_map/pallas_call | solution.py:134
  80.3 11.6 %all-to-all-done.refs_0_ = f32[128,8,128]{2,1,0:T(8,128)} async-done(((f32[128,8,128]{2,1,0:T(8,128)}), f32[128,8,128]{2,1,0:T(8,128)}, u32[]{:S(2)}, u32[]{:S(2)}) %all-to-all-start) | async-done | bytes 524320 | tf_op jit(solution)/shard_map/all_to_all | solution.py:890
  91.9 0.0 copy-done.5
  91.9 3.9 %shard_map.209 = f32[128,8,128]{2,1,0:T(8,128)S(1)} custom-call(f32[8,256]{1,0:T(8,128)S(1)} %copy-done.5, f32[8,128]{1,0:T(8,128)S(1)} %get-tuple-element.50.sums, f32[128,8,128]{2,1,0:T(8,128)} %all-to-all-done.refs_0_, bf16[256,256]{1,0:T(8,128)(2,1)} %constant.21.clone.refs_1_, bf16[256,256]{1,0:T(8,128)(2,1)} %constant.22.clone.refs_2_, ...), custom_call_target="tpu_custom_call" | custom-call | flops 1000000000 | bytes 1048576 | tf_op jit(solution)/shard_map/pallas_call | solution.py:134
  95.8 26.1 %all_to_all.10.grid = f32[128,8,128]{2,1,0:T(8,128)S(1)} all-to-all(f32[128,8,128]{2,1,0:T(8,128)S(1)} %shard_map.209), channel_id=1, replica_groups=mesh['slab'=4,'pair'=32,'core'=2] {'slab','pair'}, dimensions={0} | all-to-all | bytes 1048576 | tf_op jit(solution)/shard_map/all_to_all | solution.py:919
  121.9 0.0 copy-done.9
  121.9 1.1 shard_map.211
  123.0 1.4 %collective-permute-start.16 = (f32[8,512]{1,0:T(8,128)S(1)}, f32[8,512]{1,0:T(8,128)S(1)}, u32[]{:S(2)}, u32[]{:S(2)}) collective-permute-start(f32[8,512]{1,0:T(8,128)S(1)} %shard_map.211), channel_id=1, source_target_pairs={{0,1},{1,0},{2,3},{3,2},{4,5},{5,4},{6,7},{7,6},{8,9},{9,8},{10,11... | collective-permute-start | bytes 49160 | tf_op jit(solution)/shard_map/ppermute | solution.py:728
  124.4 1.1 shard_map.210.mine
  125.5 0.0 collective-permute-done.16.theirs
  125.5 0.0 copy-done.2
  125.5 0.9 shard_map.212
  (21 shorter events, 0.0 us)
Async XLA Ops:
  1.7 5.2 %collective-permute-start = (f32[8,768]{1,0:T(8,128)S(1)}, f32[8,768]{1,0:T(8,128)S(1)}, u32[]{:S(2)}, u32[]{:S(2)}) collective-permute-start(f32[8,768]{1,0:T(8,128)S(1)} %get-tuple-element.30.mine), channel_id=1, source_target_pairs={{0,1},{1,0},{2,3},{3,2},{4,5},{5,4},{6,7},{7,6},{8,9},{9,8},{10,11... | collective-permute-start | bytes 73736 | tf_op jit(solution)/shard_map/ppermute | solution.py:728
  5.0 4.7 %collective-permute-start.1 = (f32[2,8,128]{2,1,0:T(8,128)S(1)}, f32[2,8,128]{2,1,0:T(8,128)S(1)}, u32[]{:S(2)}, u32[]{:S(2)}) collective-permute-start(f32[2,8,128]{2,1,0:T(8,128)S(1)} %get-tuple-element.28.after.own), channel_id=1, source_target_pairs={{0,63},{1,2},{2,1},{3,4},{4,3},{5,6},{6,5},{7,8},{8,7},{9,10},{10,... | collective-permute-start | bytes 24584 | tf_op jit(solution)/shard_map/ppermute | solution.py:728
  9.7 48.8 %copy-start.6 = (f32[2,2,72,512]{3,2,1,0:T(8,128)}, f32[2,2,72,512]{3,2,1,0:T(8,128)S(1)}, u32[]{:S(2)}) copy-start(f32[2,2,72,512]{3,2,1,0:T(8,128)S(1)} %get-tuple-element.45.tab_x) | copy-start | bytes 1769476
  9.7 48.8 %copy-start.8 = (f32[2,128,512]{2,1,0:T(8,128)}, f32[2,128,512]{2,1,0:T(8,128)S(1)}, u32[]{:S(2)}) copy-start(f32[2,128,512]{2,1,0:T(8,128)S(1)} %get-tuple-element.48.slope_z) | copy-start | bytes 1572868
  9.7 48.8 %copy-start.10 = (bf16[2,128,512]{2,1,0:T(8,128)(2,1)}, bf16[2,128,512]{2,1,0:T(8,128)(2,1)S(1)}, u32[]{:S(2)}) copy-start(bf16[2,128,512]{2,1,0:T(8,128)(2,1)S(1)} %get-tuple-element.46.w_high) | copy-start | bytes 786436
  9.7 48.8 %copy-start.12 = (bf16[2,128,512]{2,1,0:T(8,128)(2,1)}, bf16[2,128,512]{2,1,0:T(8,128)(2,1)S(1)}, u32[]{:S(2)}) copy-start(bf16[2,128,512]{2,1,0:T(8,128)(2,1)S(1)} %get-tuple-element.47.w_low) | copy-start | bytes 786436
  9.8 4.0 %collective-permute-start.2 = (f32[3,2,8,128]{3,2,1,0:T(8,128)S(1)}, f32[3,2,8,128]{3,2,1,0:T(8,128)S(1)}, u32[]{:S(2)}, u32[]{:S(2)}) collective-permute-start(f32[3,2,8,128]{3,2,1,0:T(8,128)S(1)} %shard_map.196.level), channel_id=1, source_target_pairs={{0,64},{64,128},{128,192},{192,0},{1,65},{65,129},{129,193},{193,1... | collective-permute-start | bytes 73736 | tf_op jit(solution)/shard_map/ppermute | solution.py:735
  10.9 2.8 %collective-permute-start.3 = (f32[3,2,8,128]{3,2,1,0:T(8,128)S(1)}, f32[3,2,8,128]{3,2,1,0:T(8,128)S(1)}, u32[]{:S(2)}, u32[]{:S(2)}) collective-permute-start(f32[3,2,8,128]{3,2,1,0:T(8,128)S(1)} %shard_map.196.level), channel_id=1, source_target_pairs={{64,0},{128,64},{192,128},{0,192},{65,1},{129,65},{193,129},{1,193... | collective-permute-start | bytes 73736 | tf_op jit(solution)/shard_map/ppermute | solution.py:735
  17.0 13.0 %collective-permute-start.4 = (f32[2,8,128]{2,1,0:T(8,128)S(1)}, f32[2,8,128]{2,1,0:T(8,128)S(1)}, u32[]{:S(2)}, u32[]{:S(2)}) collective-permute-start(f32[2,8,128]{2,1,0:T(8,128)S(1)} %get-tuple-element.34.own.refs_0_), channel_id=1, source_target_pairs={{0,1},{1,0},{2,3},{3,2},{4,5},{5,4},{6,7},{7,6},{8,9},{9,8},{10,11... | collective-permute-start | bytes 24584 | tf_op jit(solution)/shard_map/ppermute | solution.py:728
  27.0 3.1 %collective-permute-start.5 = (f32[2,8,128]{2,1,0:T(8,128)S(1)}, f32[2,8,128]{2,1,0:T(8,128)S(1)}, u32[]{:S(2)}, u32[]{:S(2)}) collective-permute-start(f32[2,8,128]{2,1,0:T(8,128)S(1)} %get-tuple-element.34.own.refs_0_), channel_id=1, source_target_pairs={{0,63},{1,2},{2,1},{3,4},{4,3},{5,6},{6,5},{7,8},{8,7},{9,10},{10,... | collective-permute-start | bytes 24584 | tf_op jit(solution)/shard_map/ppermute | solution.py:728
  28.9 19.9 %copy-start = (f32[3,8,128,128]{3,2,1,0:T(8,128)}, f32[3,8,128,128]{3,2,1,0:T(8,128)S(1)}, u32[]{:S(2)}) copy-start(f32[3,8,128,128]{3,2,1,0:T(8,128)S(1)} %get-tuple-element.39.refs_6_.pairs_b.stored_b) | copy-start | bytes 4718596
  30.0 4.7 %collective-permute-start.6 = (f32[3,2,8,128]{3,2,1,0:T(8,128)S(1)}, f32[3,2,8,128]{3,2,1,0:T(8,128)S(1)}, u32[]{:S(2)}, u32[]{:S(2)}) collective-permute-start(f32[3,2,8,128]{3,2,1,0:T(8,128)S(1)} %shard_map.200.refs_3_), channel_id=1, source_target_pairs={{0,64},{64,128},{128,192},{192,0},{1,65},{65,129},{129,193},{193,1... | collective-permute-start | bytes 73736 | tf_op jit(solution)/shard_map/ppermute | solution.py:735
  30.1 4.7 %collective-permute-start.7 = (f32[3,2,8,128]{3,2,1,0:T(8,128)S(1)}, f32[3,2,8,128]{3,2,1,0:T(8,128)S(1)}, u32[]{:S(2)}, u32[]{:S(2)}) collective-permute-start(f32[3,2,8,128]{3,2,1,0:T(8,128)S(1)} %shard_map.200.refs_3_), channel_id=1, source_target_pairs={{64,0},{128,64},{192,128},{0,192},{65,1},{129,65},{193,129},{1,193... | collective-permute-start | bytes 73736 | tf_op jit(solution)/shard_map/ppermute | solution.py:735
  34.7 14.0 %copy-start.1 = (f32[3,8,128,128]{3,2,1,0:T(8,128)}, f32[3,8,128,128]{3,2,1,0:T(8,128)S(1)}, u32[]{:S(2)}) copy-start(f32[3,8,128,128]{3,2,1,0:T(8,128)S(1)} %get-tuple-element.40.refs_7_.pairs_c.stored_c) | copy-start | bytes 4718596
  36.5 8.3 %collective-permute-start.8 = (f32[2,8,128]{2,1,0:T(8,128)S(1)}, f32[2,8,128]{2,1,0:T(8,128)S(1)}, u32[]{:S(2)}, u32[]{:S(2)}) collective-permute-start(f32[2,8,128]{2,1,0:T(8,128)S(1)} %shard_map.201.own.own_a), channel_id=1, source_target_pairs={{0,1},{1,0},{2,3},{3,2},{4,5},{5,4},{6,7},{7,6},{8,9},{9,8},{10,11... | collective-permute-start | bytes 24584 | tf_op jit(solution)/shard_map/ppermute | solution.py:728
  41.8 3.1 %collective-permute-start.9 = (f32[2,8,128]{2,1,0:T(8,128)S(1)}, f32[2,8,128]{2,1,0:T(8,128)S(1)}, u32[]{:S(2)}, u32[]{:S(2)}) collective-permute-start(f32[2,8,128]{2,1,0:T(8,128)S(1)} %shard_map.201.own.own_a), channel_id=1, source_target_pairs={{0,63},{1,2},{2,1},{3,4},{4,3},{5,6},{6,5},{7,8},{8,7},{9,10},{10,... | collective-permute-start | bytes 24584 | tf_op jit(solution)/shard_map/ppermute | solution.py:728
  41.8 7.0 %copy-start.3 = (s32[1,512]{1,0:T(1,128)S(1)}, s32[1,512]{1,0:T(1,128)}, u32[]{:S(2)}) copy-start(s32[1,512]{1,0:T(1,128)} %order.3) | copy-start | bytes 6148
  44.8 3.9 %collective-permute-start.10 = (f32[3,2,8,128]{3,2,1,0:T(8,128)S(1)}, f32[3,2,8,128]{3,2,1,0:T(8,128)S(1)}, u32[]{:S(2)}, u32[]{:S(2)}) collective-permute-start(f32[3,2,8,128]{3,2,1,0:T(8,128)S(1)} %shard_map.203.level), channel_id=1, source_target_pairs={{0,64},{64,128},{128,192},{192,0},{1,65},{65,129},{129,193},{193,1... | collective-permute-start | bytes 73736 | tf_op jit(solution)/shard_map/ppermute | solution.py:735
  44.8 3.9 %collective-permute-start.11 = (f32[3,2,8,128]{3,2,1,0:T(8,128)S(1)}, f32[3,2,8,128]{3,2,1,0:T(8,128)S(1)}, u32[]{:S(2)}, u32[]{:S(2)}) collective-permute-start(f32[3,2,8,128]{3,2,1,0:T(8,128)S(1)} %shard_map.203.level), channel_id=1, source_target_pairs={{64,0},{128,64},{192,128},{0,192},{65,1},{129,65},{193,129},{1,193... | collective-permute-start | bytes 73736 | tf_op jit(solution)/shard_map/ppermute | solution.py:735
  51.7 6.8 %collective-permute-start.12 = (f32[8,768]{1,0:T(8,128)S(1)}, f32[8,768]{1,0:T(8,128)S(1)}, u32[]{:S(2)}, u32[]{:S(2)}) collective-permute-start(f32[8,768]{1,0:T(8,128)S(1)} %get-tuple-element.44.ordered), channel_id=1, source_target_pairs={{0,1},{1,0},{2,3},{3,2},{4,5},{5,4},{6,7},{7,6},{8,9},{9,8},{10,11... | collective-permute-start | bytes 73736 | tf_op jit(solution)/shard_map/ppermute | solution.py:728
  57.1 3.9 %collective-permute-start.13 = (f32[2,8,128]{2,1,0:T(8,128)S(1)}, f32[2,8,128]{2,1,0:T(8,128)S(1)}, u32[]{:S(2)}, u32[]{:S(2)}) collective-permute-start(f32[2,8,128]{2,1,0:T(8,128)S(1)} %get-tuple-element.42.own.sent), channel_id=1, source_target_pairs={{0,63},{1,2},{2,1},{3,4},{4,3},{5,6},{6,5},{7,8},{8,7},{9,10},{10,... | collective-permute-start | bytes 24584 | tf_op jit(solution)/shard_map/ppermute | solution.py:728
  61.0 30.9 %all-to-all-start = ((f32[128,8,128]{2,1,0:T(8,128)}), f32[128,8,128]{2,1,0:T(8,128)}, u32[]{:S(2)}, u32[]{:S(2)}) async-start(f32[128,8,128]{2,1,0:T(8,128)} %shard_map.206), calls=%async_computation | async-start | bytes 1048576 | tf_op jit(solution)/shard_map/all_to_all | solution.py:890
  72.5 4.4 %collective-permute-start.14 = (f32[3,2,8,128]{3,2,1,0:T(8,128)S(1)}, f32[3,2,8,128]{3,2,1,0:T(8,128)S(1)}, u32[]{:S(2)}, u32[]{:S(2)}) collective-permute-start(f32[3,2,8,128]{3,2,1,0:T(8,128)S(1)} %shard_map.207.level), channel_id=1, source_target_pairs={{0,64},{64,128},{128,192},{192,0},{1,65},{65,129},{129,193},{193,1... | collective-permute-start | bytes 73736 | tf_op jit(solution)/shard_map/ppermute | solution.py:735
  73.2 3.7 %collective-permute-start.15 = (f32[3,2,8,128]{3,2,1,0:T(8,128)S(1)}, f32[3,2,8,128]{3,2,1,0:T(8,128)S(1)}, u32[]{:S(2)}, u32[]{:S(2)}) collective-permute-start(f32[3,2,8,128]{3,2,1,0:T(8,128)S(1)} %shard_map.207.level), channel_id=1, source_target_pairs={{64,0},{128,64},{192,128},{0,192},{65,1},{129,65},{193,129},{1,193... | collective-permute-start | bytes 73736 | tf_op jit(solution)/shard_map/ppermute | solution.py:735
  76.9 15.0 %copy-start.5 = (f32[8,256]{1,0:T(8,128)S(1)}, f32[8,256]{1,0:T(8,128)}, u32[]{:S(2)}) copy-start(f32[8,256]{1,0:T(8,128)} %constant.20.clone.waves) | copy-start | bytes 24580
  91.9 30.0 %copy-start.7 = (f32[2,2,72,512]{3,2,1,0:T(8,128)S(1)}, f32[2,2,72,512]{3,2,1,0:T(8,128)}, u32[]{:S(2)}) copy-start(f32[2,2,72,512]{3,2,1,0:T(8,128)} %copy-done.6) | copy-start | bytes 1769476
  91.9 30.0 %copy-start.9 = (f32[2,128,512]{2,1,0:T(8,128)S(1)}, f32[2,128,512]{2,1,0:T(8,128)}, u32[]{:S(2)}) copy-start(f32[2,128,512]{2,1,0:T(8,128)} %copy-done.8) | copy-start | bytes 1572868
  91.9 30.0 %copy-start.11 = (bf16[2,128,512]{2,1,0:T(8,128)(2,1)S(1)}, bf16[2,128,512]{2,1,0:T(8,128)(2,1)}, u32[]{:S(2)}) copy-start(bf16[2,128,512]{2,1,0:T(8,128)(2,1)} %copy-done.10) | copy-start | bytes 786436
  91.9 30.0 %copy-start.13 = (bf16[2,128,512]{2,1,0:T(8,128)(2,1)S(1)}, bf16[2,128,512]{2,1,0:T(8,128)(2,1)}, u32[]{:S(2)}) copy-start(bf16[2,128,512]{2,1,0:T(8,128)(2,1)} %copy-done.12) | copy-start | bytes 786436
  123.0 2.5 %copy-start.2 = (f32[3,512]{1,0:T(4,128)S(1)}, f32[3,512]{1,0:T(4,128)}, u32[]{:S(2)}) copy-start(f32[3,512]{1,0:T(4,128)} %residual.1) | copy-start | bytes 18436
  123.0 2.5 %copy-start.4 = (f32[3,512]{1,0:T(4,128)S(1)}, f32[3,512]{1,0:T(4,128)}, u32[]{:S(2)}) copy-start(f32[3,512]{1,0:T(4,128)} %dipoles.1) | copy-start | bytes 18436
  123.0 2.5 %collective-permute-start.16 = (f32[8,512]{1,0:T(8,128)S(1)}, f32[8,512]{1,0:T(8,128)S(1)}, u32[]{:S(2)}, u32[]{:S(2)}) collective-permute-start(f32[8,512]{1,0:T(8,128)S(1)} %shard_map.211), channel_id=1, source_target_pairs={{0,1},{1,0},{2,3},{3,2},{4,5},{5,4},{6,7},{7,6},{8,9},{9,8},{10,11... | collective-permute-start | bytes 49160 | tf_op jit(solution)/shard_map/ppermute | solution.py:728

commit v13 on v8

--- a/solution.py
+++ b/solution.py
@@ -198,7 +198,7 @@
     return jnp.where(depth > half, depth - G, jnp.where(depth < -half, depth + G, depth))
 
 
-PAIR_ROWS = 32
+PAIR_ROWS = 64
 GROUP = 4
 
 

time: 125 us -> 125 us (level)
  no operation moved by 1% of the time
where the time goes in v13:
time: 125 us
  starting transfers between devices  46.1 us (37%)
  Pallas kernels  34.4 us (28%)
  blocking collectives  24.5 us (20%)
  waiting for transfers between devices  16.9 us (14%)
  local copies, waits for them, and re-layouts  2.05 us (2%)
    pallas_call x19, Pallas kernels, run(): pl.pallas_call(kernel, out_shape=[(pltpu.HBM if hbm_outs else jax.ShapeDt...  31.6 us
    ppermute x9, starting transfers between devices, beside(): return lax.ppermute(block, BOTH, swap_pairs(n_slab, n_space, odd))  27.7 us
    all_to_all x1, blocking collectives, local(): returned = lax.all_to_all(planes, CHIPS, 0, 0, tiled=True)  24.5 us
    all_to_all x1, waiting for transfers between devices, local(): grid = lax.all_to_all(spread, CHIPS, 0, 0, tiled=True)  10.8 us
    all_to_all x1, starting transfers between devices, local(): grid = lax.all_to_all(spread, CHIPS, 0, 0, tiled=True)  8.74 us
    ppermute x4, starting transfers between devices, along_slab(): lax.ppermute(level, 'slab', down)  7.54 us
    ppermute x4, waiting for transfers between devices, along_slab(): lax.ppermute(level, 'slab', up)  3.82 us
  transfers between devices with their start and end apart: 18, of which 6 were waited for; matrix products, arithmetic and copies ran while one was open for 0% of the time, Pallas kernels for 17%

profile of v13, /device:TPU:1, one launch (start us, length us, event | category | flops | bytes accessed | tf_op | source)
XLA Modules:
  0.0 124.9 jit_solution(5779274156258558410)
XLA Ops:
  0.6 1.1 shard_map.193
  1.7 3.3 %collective-permute-start = (f32[8,768]{1,0:T(8,128)S(1)}, f32[8,768]{1,0:T(8,128)S(1)}, u32[]{:S(2)}, u32[]{:S(2)}) collective-permute-start(f32[8,768]{1,0:T(8,128)S(1)} %get-tuple-element.31.mine), channel_id=1, source_target_pairs={{0,1},{1,0},{2,3},{3,2},{4,5},{5,4},{6,7},{7,6},{8,9},{9,8},{10,11... | collective-permute-start | bytes 73736 | tf_op jit(solution)/shard_map/ppermute | solution.py:685
  5.0 0.0 collective-permute-start.1
  5.0 0.7 copy-done.5
  5.7 0.7 copy-done.6
  6.4 0.7 copy-done.7
  7.0 1.7 %shard_map.194.meta = s32[48]{0:T(128)S(1)} custom-call(s32[1,4,8]{2,1,0:T(4,128)S(1)} %copy-done.6, s32[1,4]{1,0:T(1,128)S(1)} %copy-done.7, s32[1,2]{1,0:T(1,128)S(1)} %copy-done.5, f32[2,8,128]{2,1,0:T(8,128)S(1)} %get-tuple-element.29.after.own), custom_call_target="tpu_custom_call" | custom-call | flops 100000000 | bytes 1048576 | tf_op jit(solution)/shard_map/pallas_call | solution.py:748
  8.8 0.0 collective-permute-done.1.outer
  8.8 0.0 collective-permute-done.inner.beside
  8.8 1.2 collective-permute-start.2
  10.0 1.6 %collective-permute-start.3 = (f32[3,2,8,128]{3,2,1,0:T(8,128)S(1)}, f32[3,2,8,128]{3,2,1,0:T(8,128)S(1)}, u32[]{:S(2)}, u32[]{:S(2)}) collective-permute-start(f32[3,2,8,128]{3,2,1,0:T(8,128)S(1)} %shard_map.195.level), channel_id=1, source_target_pairs={{64,0},{128,64},{192,128},{0,192},{65,1},{129,65},{193,129},{1,193... | collective-permute-start | bytes 73736 | tf_op jit(solution)/shard_map/ppermute | solution.py:692
  11.6 1.2 collective-permute-done.2.before
  12.8 0.0 collective-permute-done.3.after
  12.8 3.1 %shard_map.196 = (f32[22,8,128]{2,1,0:T(8,128)S(1)}, f32[3,16,128,128]{3,2,1,0:T(8,128)S(1)}, f32[2,8,128]{2,1,0:T(8,128)S(1)}) custom-call(s32[48]{0:T(128)S(1)} %shard_map.194.meta, f32[4,8,128]{2,1,0:T(8,128)S(1)} %get-tuple-element.30.own, f32[3,2,8,128]{3,2,1,0:T(8,128)S(1)} %shard_map.195.level, f32[3,2,8,128]{3,2,1,0:T(8,128)S(1)} %collective-permute-done.2.before, ...), custom_call_target="tpu_custom_call" | custom-call | flops 1000000000 | bytes 1048576 | tf_op jit(solution)/shard_map/pallas_call | solution.py:124
  15.9 9.8 %collective-permute-start.4 = (f32[2,8,128]{2,1,0:T(8,128)S(1)}, f32[2,8,128]{2,1,0:T(8,128)S(1)}, u32[]{:S(2)}, u32[]{:S(2)}) collective-permute-start(f32[2,8,128]{2,1,0:T(8,128)S(1)} %get-tuple-element.34.own.refs_0_), channel_id=1, source_target_pairs={{0,1},{1,0},{2,3},{3,2},{4,5},{5,4},{6,7},{7,6},{8,9},{9,8},{10,11... | collective-permute-start | bytes 24584 | tf_op jit(solution)/shard_map/ppermute | solution.py:685
  25.7 0.0 collective-permute-start.5
  25.7 2.3 %shard_map.197 = (f32[22,8,128]{2,1,0:T(8,128)}, f32[3,8,128,128]{3,2,1,0:T(8,128)S(1)}, f32[1,8,128]{2,1,0:T(8,128)S(1)}) custom-call(s32[48]{0:T(128)S(1)} %shard_map.194.meta, f32[4,8,128]{2,1,0:T(8,128)S(1)} %get-tuple-element.30.own, f32[3,2,8,128]{3,2,1,0:T(8,128)S(1)} %shard_map.195.level, f32[3,2,8,128]{3,2,1,0:T(8,128)S(1)} %collective-permute-done.2.before, ...), custom_call_target="tpu_custom_call" | custom-call | flops 1000000000 | bytes 1048576 | tf_op jit(solution)/shard_map/pallas_call | solution.py:124
  28.0 0.8 collective-permute-done.5.outer
  28.8 0.0 collective-permute-done.4.inner
  28.8 0.0 collective-permute-start.6
  28.8 2.7 %collective-permute-start.7 = (f32[3,2,8,128]{3,2,1,0:T(8,128)S(1)}, f32[3,2,8,128]{3,2,1,0:T(8,128)S(1)}, u32[]{:S(2)}, u32[]{:S(2)}) collective-permute-start(f32[3,2,8,128]{3,2,1,0:T(8,128)S(1)} %shard_map.199.refs_3_), channel_id=1, source_target_pairs={{64,0},{128,64},{192,128},{0,192},{65,1},{129,65},{193,129},{1,193... | collective-permute-start | bytes 73736 | tf_op jit(solution)/shard_map/ppermute | solution.py:692
  31.5 2.3 %shard_map.198 = (f32[22,8,128]{2,1,0:T(8,128)}, f32[3,8,128,128]{3,2,1,0:T(8,128)S(1)}, f32[1,8,128]{2,1,0:T(8,128)S(1)}) custom-call(s32[48]{0:T(128)S(1)} %shard_map.194.meta, f32[4,8,128]{2,1,0:T(8,128)S(1)} %get-tuple-element.30.own, f32[3,2,8,128]{3,2,1,0:T(8,128)S(1)} %shard_map.195.level, f32[3,2,8,128]{3,2,1,0:T(8,128)S(1)} %collective-permute-done.2.before, ...), custom_call_target="tpu_custom_call" | custom-call | flops 1000000000 | bytes 1048576 | tf_op jit(solution)/shard_map/pallas_call | solution.py:124
  33.8 0.0 collective-permute-done.6.refs_4_
  33.8 0.0 collective-permute-done.7.refs_5_
  33.8 1.7 %shard_map.200.own.refs_0_.own_a = f32[2,8,128]{2,1,0:T(8,128)S(1)} custom-call(s32[48]{0:T(128)S(1)} %shard_map.194.meta, f32[22,8,128]{2,1,0:T(8,128)S(1)} %get-tuple-element.33.geometry, f32[2,8,128]{2,1,0:T(8,128)S(1)} %get-tuple-element.34.own.refs_0_, f32[1,8,128]{2,1,0:T(8,128)S(1)} %get-tuple-element.35.refs_1_, ...), custom_call_target="tpu_custom_call" | custom-call | flops 100000000 | bytes 1048576 | tf_op jit(solution)/shard_map/pallas_call | solution.py:124
  35.5 5.3 %collective-permute-start.8 = (f32[2,8,128]{2,1,0:T(8,128)S(1)}, f32[2,8,128]{2,1,0:T(8,128)S(1)}, u32[]{:S(2)}, u32[]{:S(2)}) collective-permute-start(f32[2,8,128]{2,1,0:T(8,128)S(1)} %shard_map.200.own.refs_0_.own_a), channel_id=1, source_target_pairs={{0,1},{1,0},{2,3},{3,2},{4,5},{5,4},{6,7},{7,6},{8,9},{9,8},{10,11... | collective-permute-start | bytes 24584 | tf_op jit(solution)/shard_map/ppermute | solution.py:685
  40.8 0.0 collective-permute-start.9
  40.8 1.6 %shard_map.201.refs_1_.own_b = f32[2,8,128]{2,1,0:T(8,128)S(1)} custom-call(s32[48]{0:T(128)S(1)} %shard_map.194.meta, f32[22,8,128]{2,1,0:T(8,128)S(1)} %get-tuple-element.33.geometry, f32[2,8,128]{2,1,0:T(8,128)S(1)} %get-tuple-element.34.own.refs_0_, f32[1,8,128]{2,1,0:T(8,128)S(1)} %get-tuple-element.35.refs_1_, ...), custom_call_target="tpu_custom_call" | custom-call | flops 100000000 | bytes 1048576 | tf_op jit(solution)/shard_map/pallas_call | solution.py:124
  42.5 1.5 %collective-permute-done.9.outer = f32[2,8,128]{2,1,0:T(8,128)S(1)} collective-permute-done((f32[2,8,128]{2,1,0:T(8,128)S(1)}, f32[2,8,128]{2,1,0:T(8,128)S(1)}, u32[]{:S(2)}, u32[]{:S(2)}) %collective-permute-start.9) | collective-permute-done | bytes 8224 | tf_op jit(solution)/shard_map/ppermute | solution.py:685
  43.9 0.0 collective-permute-done.8.inner
  43.9 1.2 collective-permute-start.11
  45.1 0.3 collective-permute-start.10
  45.4 2.7 %shard_map.203 = (f32[2,2,72,512]{3,2,1,0:T(8,128)S(1)}, f32[2,2,8,512]{3,2,1,0:T(8,128)S(1)}, bf16[2,128,512]{2,1,0:T(8,128)(2,1)S(1)}, bf16[2,128,512]{2,1,0:T(8,128)(2,1)S(1)}, f32[2,128,512]{2,1,0:T(8,128)S(1)}) custom-call(f32[8,768]{1,0:T(8,128)S(1)} %get-tuple-element.31.mine, f32[8,768]{1,0:T(8,128)S(1)} %collective-permute-done.inner.beside, ...), custom_call_target="tpu_custom_call" | custom-call | flops 100000000 | bytes 1048576 | tf_op jit(solution)/shard_map/pallas_call | solution.py:124
  48.1 0.0 copy-start.9
  48.1 0.0 copy-start.11
  48.2 0.0 copy-start.13
  48.2 0.0 copy-start.15
  48.2 0.0 collective-permute-done.11.refs_4_.after
  48.2 0.0 copy-start.3
  48.2 0.8 collective-permute-done.10.refs_3_.before
  49.0 1.7 %shard_map.204.sent.own = f32[2,8,128]{2,1,0:T(8,128)S(1)} custom-call(s32[48]{0:T(128)S(1)} %shard_map.194.meta, f32[22,8,128]{2,1,0:T(8,128)S(1)} %get-tuple-element.33.geometry, f32[2,8,128]{2,1,0:T(8,128)S(1)} %shard_map.200.own.refs_0_.own_a, f32[2,8,128]{2,1,0:T(8,128)S(1)} %shard_map.201.refs_1_.own_b, f32[3,2,8,128]{3,2,1,0:T(8,128)S(1)} %shard_map.202.refs_2_.level, ...), custom_call_target="tpu_custom_call" | custom-call | flops 100000000 | bytes 1048576 | tf_op jit(solution)/shard_map/pallas_call | solution.py:124
  50.8 2.3 %collective-permute-start.13 = (f32[2,8,128]{2,1,0:T(8,128)S(1)}, f32[2,8,128]{2,1,0:T(8,128)S(1)}, u32[]{:S(2)}, u32[]{:S(2)}) collective-permute-start(f32[2,8,128]{2,1,0:T(8,128)S(1)} %shard_map.204.sent.own), channel_id=1, source_target_pairs={{0,63},{1,2},{2,1},{3,4},{4,3},{5,6},{6,5},{7,8},{8,7},{9,10},{10,... | collective-permute-start | bytes 24584 | tf_op jit(solution)/shard_map/ppermute | solution.py:685
  53.1 0.0 copy-done
  53.1 1.8 %shard_map.205 = (f32[2,8,128]{2,1,0:T(8,128)S(1)}, f32[8,768]{1,0:T(8,128)S(1)}) custom-call(s32[48]{0:T(128)S(1)} %shard_map.194.meta, f32[22,8,128]{2,1,0:T(8,128)S(1)} %get-tuple-element.33.geometry, f32[2,8,128]{2,1,0:T(8,128)S(1)} %shard_map.200.own.refs_0_.own_a, f32[2,8,128]{2,1,0:T(8,128)S(1)} %shard_map.201.refs_1_.own_b, ...), custom_call_target="tpu_custom_call" | custom-call | flops 100000000 | bytes 1048576 | tf_op jit(solution)/shard_map/pallas_call | solution.py:124
  54.9 3.5 %collective-permute-start.12 = (f32[8,768]{1,0:T(8,128)S(1)}, f32[8,768]{1,0:T(8,128)S(1)}, u32[]{:S(2)}, u32[]{:S(2)}) collective-permute-start(f32[8,768]{1,0:T(8,128)S(1)} %get-tuple-element.46.ordered), channel_id=1, source_target_pairs={{0,1},{1,0},{2,3},{3,2},{4,5},{5,4},{6,7},{7,6},{8,9},{9,8},{10,11... | collective-permute-start | bytes 73736 | tf_op jit(solution)/shard_map/ppermute | solution.py:685
  58.4 1.4 %shard_map.206.mine = f32[128,576]{1,0:T(8,128)S(1)} custom-call(f32[8,768]{1,0:T(8,128)S(1)} %get-tuple-element.46.ordered, f32[2,2,72,512]{3,2,1,0:T(8,128)S(1)} %get-tuple-element.47.tab_x, f32[2,2,8,512]{3,2,1,0:T(8,128)S(1)} %get-tuple-element.43.tab_y, bf16[2,128,512]{2,1,0:T(8,128)(2,1)S(1)} %get-tuple-element.48.w_high, ...), custom_call_target="tpu_custom_call" | custom-call | flops 1000000000 | bytes 1048576 | tf_op jit(solution)/shard_map/pallas_call | solution.py:124
  59.8 0.0 collective-permute-done.12.ordered.inner
  59.8 2.5 %shard_map.207 = f32[128,8,128]{2,1,0:T(8,128)} custom-call(f32[8,768]{1,0:T(8,128)S(1)} %collective-permute-done.12.ordered.inner, f32[128,576]{1,0:T(8,128)S(1)} %shard_map.206.mine, f32[2,2,72,512]{3,2,1,0:T(8,128)S(1)} %get-tuple-element.47.tab_x, f32[2,2,8,512]{3,2,1,0:T(8,128)S(1)} %get-tuple-element.43.tab_y, ...), custom_call_target="tpu_custom_call" | custom-call | flops 1000000000 | bytes 1048576 | tf_op jit(solution)/shard_map/pallas_call | solution.py:124
  62.3 0.0 collective-permute-done.13.outer
  62.3 8.7 %all-to-all-start = ((f32[128,8,128]{2,1,0:T(8,128)}), f32[128,8,128]{2,1,0:T(8,128)}, u32[]{:S(2)}, u32[]{:S(2)}) async-start(f32[128,8,128]{2,1,0:T(8,128)} %shard_map.207), calls=%async_computation | async-start | bytes 1048576 | tf_op jit(solution)/shard_map/all_to_all | solution.py:837
  71.1 0.7 collective-permute-start.14
  71.7 2.1 %collective-permute-start.15 = (f32[3,2,8,128]{3,2,1,0:T(8,128)S(1)}, f32[3,2,8,128]{3,2,1,0:T(8,128)S(1)}, u32[]{:S(2)}, u32[]{:S(2)}) collective-permute-start(f32[3,2,8,128]{3,2,1,0:T(8,128)S(1)} %shard_map.208.level), channel_id=1, source_target_pairs={{64,0},{128,64},{192,128},{0,192},{65,1},{129,65},{193,129},{1,193... | collective-permute-start | bytes 73736 | tf_op jit(solution)/shard_map/ppermute | solution.py:692
  73.8 1.8 %collective-permute-done.14.before = f32[3,2,8,128]{3,2,1,0:T(8,128)S(1)} collective-permute-done((f32[3,2,8,128]{3,2,1,0:T(8,128)S(1)}, f32[3,2,8,128]{3,2,1,0:T(8,128)S(1)}, u32[]{:S(2)}, u32[]{:S(2)}) %collective-permute-start.14) | collective-permute-done | bytes 24608 | tf_op jit(solution)/shard_map/ppermute | solution.py:692
  75.6 0.0 collective-permute-done.15.after
  75.6 3.4 %shard_map.209 = (f32[8,512]{1,0:T(8,128)S(1)}, f32[8,128]{1,0:T(8,128)S(1)}) custom-call(s32[48]{0:T(128)S(1)} %shard_map.194.meta, f32[22,8,128]{2,1,0:T(8,128)S(1)} %get-tuple-element.33.geometry, f32[2,8,128]{2,1,0:T(8,128)S(1)} %shard_map.204.sent.own, f32[2,8,128]{2,1,0:T(8,128)S(1)} %get-tuple-element.45.rest, f32[3,2,8,128]{3,2,1,0:T(8,128)S(1)} %shard_map.208.level, ...), custom_call_target="tpu_custom_call" | custom-call | flops 1000000000 | bytes 1048576 | tf_op jit(solution)/shard_map/pallas_call | solution.py:124
  79.0 10.8 %all-to-all-done.refs_0_ = f32[128,8,128]{2,1,0:T(8,128)} async-done(((f32[128,8,128]{2,1,0:T(8,128)}), f32[128,8,128]{2,1,0:T(8,128)}, u32[]{:S(2)}, u32[]{:S(2)}) %all-to-all-start) | async-done | bytes 524320 | tf_op jit(solution)/shard_map/all_to_all | solution.py:837
  89.8 4.1 %shard_map.210 = f32[128,8,128]{2,1,0:T(8,128)S(1)} custom-call(f32[8,256]{1,0:T(8,128)S(1)} %copy-done.8, f32[8,128]{1,0:T(8,128)S(1)} %get-tuple-element.52.sums, f32[128,8,128]{2,1,0:T(8,128)} %all-to-all-done.refs_0_, bf16[512,256]{1,0:T(8,128)(2,1)} %constant.21.clone.refs_1_, bf16[512,256]{1,0:T(8,128)(2,1)} %constant.22.clone.refs_2_, ...), custom_call_target="tpu_custom_call" | custom-call | flops 1000000000 | bytes 1048576 | tf_op jit(solution)/shard_map/pallas_call | solution.py:124
  93.9 24.5 %all_to_all.10.grid = f32[128,8,128]{2,1,0:T(8,128)S(1)} all-to-all(f32[128,8,128]{2,1,0:T(8,128)S(1)} %shard_map.210), channel_id=1, replica_groups=mesh['slab'=4,'pair'=32,'core'=2] {'slab','pair'}, dimensions={0} | all-to-all | bytes 1048576 | tf_op jit(solution)/shard_map/all_to_all | solution.py:868
  118.4 1.1 shard_map.212
  119.5 3.4 %collective-permute-start.16 = (f32[8,512]{1,0:T(8,128)S(1)}, f32[8,512]{1,0:T(8,128)S(1)}, u32[]{:S(2)}, u32[]{:S(2)}) collective-permute-start(f32[8,512]{1,0:T(8,128)S(1)} %shard_map.212), channel_id=1, source_target_pairs={{0,1},{1,0},{2,3},{3,2},{4,5},{5,4},{6,7},{7,6},{8,9},{9,8},{10,11... | collective-permute-start | bytes 49160 | tf_op jit(solution)/shard_map/ppermute | solution.py:685
  122.9 1.1 shard_map.211.mine
  124.0 0.0 collective-permute-done.16.theirs
  124.0 0.0 copy-done.4
  124.0 0.9 shard_map.213
  (28 shorter events, 0.1 us)
Async XLA Ops:
  1.7 7.1 %collective-permute-start = (f32[8,768]{1,0:T(8,128)S(1)}, f32[8,768]{1,0:T(8,128)S(1)}, u32[]{:S(2)}, u32[]{:S(2)}) collective-permute-start(f32[8,768]{1,0:T(8,128)S(1)} %get-tuple-element.31.mine), channel_id=1, source_target_pairs={{0,1},{1,0},{2,3},{3,2},{4,5},{5,4},{6,7},{7,6},{8,9},{9,8},{10,11... | collective-permute-start | bytes 73736 | tf_op jit(solution)/shard_map/ppermute | solution.py:685
  5.0 3.7 %collective-permute-start.1 = (f32[2,8,128]{2,1,0:T(8,128)S(1)}, f32[2,8,128]{2,1,0:T(8,128)S(1)}, u32[]{:S(2)}, u32[]{:S(2)}) collective-permute-start(f32[2,8,128]{2,1,0:T(8,128)S(1)} %get-tuple-element.29.after.own), channel_id=1, source_target_pairs={{0,63},{1,2},{2,1},{3,4},{4,3},{5,6},{6,5},{7,8},{8,7},{9,10},{10,... | collective-permute-start | bytes 24584 | tf_op jit(solution)/shard_map/ppermute | solution.py:685
  5.0 0.7 copy-start.5
  5.7 0.7 copy-start.6
  6.4 0.7 copy-start.7
  8.8 4.0 %collective-permute-start.2 = (f32[3,2,8,128]{3,2,1,0:T(8,128)S(1)}, f32[3,2,8,128]{3,2,1,0:T(8,128)S(1)}, u32[]{:S(2)}, u32[]{:S(2)}) collective-permute-start(f32[3,2,8,128]{3,2,1,0:T(8,128)S(1)} %shard_map.195.level), channel_id=1, source_target_pairs={{0,64},{64,128},{128,192},{192,0},{1,65},{65,129},{129,193},{193,1... | collective-permute-start | bytes 73736 | tf_op jit(solution)/shard_map/ppermute | solution.py:692
  10.0 2.8 %collective-permute-start.3 = (f32[3,2,8,128]{3,2,1,0:T(8,128)S(1)}, f32[3,2,8,128]{3,2,1,0:T(8,128)S(1)}, u32[]{:S(2)}, u32[]{:S(2)}) collective-permute-start(f32[3,2,8,128]{3,2,1,0:T(8,128)S(1)} %shard_map.195.level), channel_id=1, source_target_pairs={{64,0},{128,64},{192,128},{0,192},{65,1},{129,65},{193,129},{1,193... | collective-permute-start | bytes 73736 | tf_op jit(solution)/shard_map/ppermute | solution.py:692
  15.9 12.9 %collective-permute-start.4 = (f32[2,8,128]{2,1,0:T(8,128)S(1)}, f32[2,8,128]{2,1,0:T(8,128)S(1)}, u32[]{:S(2)}, u32[]{:S(2)}) collective-permute-start(f32[2,8,128]{2,1,0:T(8,128)S(1)} %get-tuple-element.34.own.refs_0_), channel_id=1, source_target_pairs={{0,1},{1,0},{2,3},{3,2},{4,5},{5,4},{6,7},{7,6},{8,9},{9,8},{10,11... | collective-permute-start | bytes 24584 | tf_op jit(solution)/shard_map/ppermute | solution.py:685
  25.7 3.1 %collective-permute-start.5 = (f32[2,8,128]{2,1,0:T(8,128)S(1)}, f32[2,8,128]{2,1,0:T(8,128)S(1)}, u32[]{:S(2)}, u32[]{:S(2)}) collective-permute-start(f32[2,8,128]{2,1,0:T(8,128)S(1)} %get-tuple-element.34.own.refs_0_), channel_id=1, source_target_pairs={{0,63},{1,2},{2,1},{3,4},{4,3},{5,6},{6,5},{7,8},{8,7},{9,10},{10,... | collective-permute-start | bytes 24584 | tf_op jit(solution)/shard_map/ppermute | solution.py:685
  28.0 25.1 %copy-start = (f32[3,8,128,128]{3,2,1,0:T(8,128)}, f32[3,8,128,128]{3,2,1,0:T(8,128)S(1)}, u32[]{:S(2)}) copy-start(f32[3,8,128,128]{3,2,1,0:T(8,128)S(1)} %get-tuple-element.39.refs_6_.pairs_b.stored_b) | copy-start | bytes 4718596
  28.8 5.0 %collective-permute-start.6 = (f32[3,2,8,128]{3,2,1,0:T(8,128)S(1)}, f32[3,2,8,128]{3,2,1,0:T(8,128)S(1)}, u32[]{:S(2)}, u32[]{:S(2)}) collective-permute-start(f32[3,2,8,128]{3,2,1,0:T(8,128)S(1)} %shard_map.199.refs_3_), channel_id=1, source_target_pairs={{0,64},{64,128},{128,192},{192,0},{1,65},{65,129},{129,193},{193,1... | collective-permute-start | bytes 73736 | tf_op jit(solution)/shard_map/ppermute | solution.py:692
  28.8 5.0 %collective-permute-start.7 = (f32[3,2,8,128]{3,2,1,0:T(8,128)S(1)}, f32[3,2,8,128]{3,2,1,0:T(8,128)S(1)}, u32[]{:S(2)}, u32[]{:S(2)}) collective-permute-start(f32[3,2,8,128]{3,2,1,0:T(8,128)S(1)} %shard_map.199.refs_3_), channel_id=1, source_target_pairs={{64,0},{128,64},{192,128},{0,192},{65,1},{129,65},{193,129},{1,193... | collective-permute-start | bytes 73736 | tf_op jit(solution)/shard_map/ppermute | solution.py:692
  33.8 19.3 %copy-start.1 = (f32[3,8,128,128]{3,2,1,0:T(8,128)}, f32[3,8,128,128]{3,2,1,0:T(8,128)S(1)}, u32[]{:S(2)}) copy-start(f32[3,8,128,128]{3,2,1,0:T(8,128)S(1)} %get-tuple-element.40.refs_7_.pairs_c.stored_c) | copy-start | bytes 4718596
  35.5 8.4 %collective-permute-start.8 = (f32[2,8,128]{2,1,0:T(8,128)S(1)}, f32[2,8,128]{2,1,0:T(8,128)S(1)}, u32[]{:S(2)}, u32[]{:S(2)}) collective-permute-start(f32[2,8,128]{2,1,0:T(8,128)S(1)} %shard_map.200.own.refs_0_.own_a), channel_id=1, source_target_pairs={{0,1},{1,0},{2,3},{3,2},{4,5},{5,4},{6,7},{7,6},{8,9},{9,8},{10,11... | collective-permute-start | bytes 24584 | tf_op jit(solution)/shard_map/ppermute | solution.py:685
  40.8 3.1 %collective-permute-start.9 = (f32[2,8,128]{2,1,0:T(8,128)S(1)}, f32[2,8,128]{2,1,0:T(8,128)S(1)}, u32[]{:S(2)}, u32[]{:S(2)}) collective-permute-start(f32[2,8,128]{2,1,0:T(8,128)S(1)} %shard_map.200.own.refs_0_.own_a), channel_id=1, source_target_pairs={{0,63},{1,2},{2,1},{3,4},{4,3},{5,6},{6,5},{7,8},{8,7},{9,10},{10,... | collective-permute-start | bytes 24584 | tf_op jit(solution)/shard_map/ppermute | solution.py:685
  43.9 4.3 %collective-permute-start.11 = (f32[3,2,8,128]{3,2,1,0:T(8,128)S(1)}, f32[3,2,8,128]{3,2,1,0:T(8,128)S(1)}, u32[]{:S(2)}, u32[]{:S(2)}) collective-permute-start(f32[3,2,8,128]{3,2,1,0:T(8,128)S(1)} %shard_map.202.refs_2_.level), channel_id=1, source_target_pairs={{64,0},{128,64},{192,128},{0,192},{65,1},{129,65},{193,129},{1,193... | collective-permute-start | bytes 73736 | tf_op jit(solution)/shard_map/ppermute | solution.py:692
  45.1 3.9 %collective-permute-start.10 = (f32[3,2,8,128]{3,2,1,0:T(8,128)S(1)}, f32[3,2,8,128]{3,2,1,0:T(8,128)S(1)}, u32[]{:S(2)}, u32[]{:S(2)}) collective-permute-start(f32[3,2,8,128]{3,2,1,0:T(8,128)S(1)} %shard_map.202.refs_2_.level), channel_id=1, source_target_pairs={{0,64},{64,128},{128,192},{192,0},{1,65},{65,129},{129,193},{193,1... | collective-permute-start | bytes 73736 | tf_op jit(solution)/shard_map/ppermute | solution.py:692
  48.1 11.6 %copy-start.9 = (f32[2,2,72,512]{3,2,1,0:T(8,128)}, f32[2,2,72,512]{3,2,1,0:T(8,128)S(1)}, u32[]{:S(2)}) copy-start(f32[2,2,72,512]{3,2,1,0:T(8,128)S(1)} %get-tuple-element.47.tab_x) | copy-start | bytes 1769476
  48.1 11.6 %copy-start.11 = (f32[2,128,512]{2,1,0:T(8,128)}, f32[2,128,512]{2,1,0:T(8,128)S(1)}, u32[]{:S(2)}) copy-start(f32[2,128,512]{2,1,0:T(8,128)S(1)} %get-tuple-element.50.slope_z) | copy-start | bytes 1572868
  48.2 11.6 %copy-start.13 = (bf16[2,128,512]{2,1,0:T(8,128)(2,1)}, bf16[2,128,512]{2,1,0:T(8,128)(2,1)S(1)}, u32[]{:S(2)}) copy-start(bf16[2,128,512]{2,1,0:T(8,128)(2,1)S(1)} %get-tuple-element.48.w_high) | copy-start | bytes 786436
  48.2 11.6 %copy-start.15 = (bf16[2,128,512]{2,1,0:T(8,128)(2,1)}, bf16[2,128,512]{2,1,0:T(8,128)(2,1)S(1)}, u32[]{:S(2)}) copy-start(bf16[2,128,512]{2,1,0:T(8,128)(2,1)S(1)} %get-tuple-element.49.w_low) | copy-start | bytes 786436
  48.2 4.9 %copy-start.3 = (s32[1,512]{1,0:T(1,128)S(1)}, s32[1,512]{1,0:T(1,128)}, u32[]{:S(2)}) copy-start(s32[1,512]{1,0:T(1,128)} %order.3) | copy-start | bytes 6148
  50.8 11.5 %collective-permute-start.13 = (f32[2,8,128]{2,1,0:T(8,128)S(1)}, f32[2,8,128]{2,1,0:T(8,128)S(1)}, u32[]{:S(2)}, u32[]{:S(2)}) collective-permute-start(f32[2,8,128]{2,1,0:T(8,128)S(1)} %shard_map.204.sent.own), channel_id=1, source_target_pairs={{0,63},{1,2},{2,1},{3,4},{4,3},{5,6},{6,5},{7,8},{8,7},{9,10},{10,... | collective-permute-start | bytes 24584 | tf_op jit(solution)/shard_map/ppermute | solution.py:685
  54.9 4.9 %collective-permute-start.12 = (f32[8,768]{1,0:T(8,128)S(1)}, f32[8,768]{1,0:T(8,128)S(1)}, u32[]{:S(2)}, u32[]{:S(2)}) collective-permute-start(f32[8,768]{1,0:T(8,128)S(1)} %get-tuple-element.46.ordered), channel_id=1, source_target_pairs={{0,1},{1,0},{2,3},{3,2},{4,5},{5,4},{6,7},{7,6},{8,9},{9,8},{10,11... | collective-permute-start | bytes 73736 | tf_op jit(solution)/shard_map/ppermute | solution.py:685
  62.3 27.5 %all-to-all-start = ((f32[128,8,128]{2,1,0:T(8,128)}), f32[128,8,128]{2,1,0:T(8,128)}, u32[]{:S(2)}, u32[]{:S(2)}) async-start(f32[128,8,128]{2,1,0:T(8,128)} %shard_map.207), calls=%async_computation | async-start | bytes 1048576 | tf_op jit(solution)/shard_map/all_to_all | solution.py:837
  71.1 4.5 %collective-permute-start.14 = (f32[3,2,8,128]{3,2,1,0:T(8,128)S(1)}, f32[3,2,8,128]{3,2,1,0:T(8,128)S(1)}, u32[]{:S(2)}, u32[]{:S(2)}) collective-permute-start(f32[3,2,8,128]{3,2,1,0:T(8,128)S(1)} %shard_map.208.level), channel_id=1, source_target_pairs={{0,64},{64,128},{128,192},{192,0},{1,65},{65,129},{129,193},{193,1... | collective-permute-start | bytes 73736 | tf_op jit(solution)/shard_map/ppermute | solution.py:692
  71.7 3.9 %collective-permute-start.15 = (f32[3,2,8,128]{3,2,1,0:T(8,128)S(1)}, f32[3,2,8,128]{3,2,1,0:T(8,128)S(1)}, u32[]{:S(2)}, u32[]{:S(2)}) collective-permute-start(f32[3,2,8,128]{3,2,1,0:T(8,128)S(1)} %shard_map.208.level), channel_id=1, source_target_pairs={{64,0},{128,64},{192,128},{0,192},{65,1},{129,65},{193,129},{1,193... | collective-permute-start | bytes 73736 | tf_op jit(solution)/shard_map/ppermute | solution.py:692
  75.6 14.2 %copy-start.8 = (f32[8,256]{1,0:T(8,128)S(1)}, f32[8,256]{1,0:T(8,128)}, u32[]{:S(2)}) copy-start(f32[8,256]{1,0:T(8,128)} %constant.20.clone.waves) | copy-start | bytes 24580
  89.8 28.6 %copy-start.10 = (f32[2,2,72,512]{3,2,1,0:T(8,128)S(1)}, f32[2,2,72,512]{3,2,1,0:T(8,128)}, u32[]{:S(2)}) copy-start(f32[2,2,72,512]{3,2,1,0:T(8,128)} %copy-done.9) | copy-start | bytes 1769476
  89.8 28.6 %copy-start.12 = (f32[2,128,512]{2,1,0:T(8,128)S(1)}, f32[2,128,512]{2,1,0:T(8,128)}, u32[]{:S(2)}) copy-start(f32[2,128,512]{2,1,0:T(8,128)} %copy-done.11) | copy-start | bytes 1572868
  89.8 28.6 %copy-start.14 = (bf16[2,128,512]{2,1,0:T(8,128)(2,1)S(1)}, bf16[2,128,512]{2,1,0:T(8,128)(2,1)}, u32[]{:S(2)}) copy-start(bf16[2,128,512]{2,1,0:T(8,128)(2,1)} %copy-done.13) | copy-start | bytes 786436
  89.8 28.6 %copy-start.16 = (bf16[2,128,512]{2,1,0:T(8,128)(2,1)S(1)}, bf16[2,128,512]{2,1,0:T(8,128)(2,1)}, u32[]{:S(2)}) copy-start(bf16[2,128,512]{2,1,0:T(8,128)(2,1)} %copy-done.15) | copy-start | bytes 786436
  119.5 4.5 %copy-start.2 = (f32[3,512]{1,0:T(4,128)S(1)}, f32[3,512]{1,0:T(4,128)}, u32[]{:S(2)}) copy-start(f32[3,512]{1,0:T(4,128)} %residual.1) | copy-start | bytes 18436
  119.5 4.5 %copy-start.4 = (f32[3,512]{1,0:T(4,128)S(1)}, f32[3,512]{1,0:T(4,128)}, u32[]{:S(2)}) copy-start(f32[3,512]{1,0:T(4,128)} %dipoles.1) | copy-start | bytes 18436
  119.5 4.5 %collective-permute-start.16 = (f32[8,512]{1,0:T(8,128)S(1)}, f32[8,512]{1,0:T(8,128)S(1)}, u32[]{:S(2)}, u32[]{:S(2)}) collective-permute-start(f32[8,512]{1,0:T(8,128)S(1)} %shard_map.212), channel_id=1, source_target_pairs={{0,1},{1,0},{2,3},{3,2},{4,5},{5,4},{6,7},{7,6},{8,9},{9,8},{10,11... | collective-permute-start | bytes 49160 | tf_op jit(solution)/shard_map/ppermute | solution.py:685
